TPU v7x, 32 devices: a whole 2x2x4 slice. The times are simulated.
32 devices in a mesh: seq: 8 (over y, x, core), head: 4 (over z).
Axes of the slice: x: 2, y: 2, z: 4, core: 2. Of those that a mesh axis runs over, the one named last changes fastest.
Arguments:
- tokens: bfloat16 [3, 2048, 2048], P(None, ('seq', 'head')), may hold values from -6 to 6
- starts: int32 [3, 32], P(None, 'seq'), may hold values from 0 to 1, as said below
- cotangent: bfloat16 [3, 2048, 2048], P(None, ('seq', 'head')), may hold values from -6 to 6
- mix_in: bfloat16 [2048, 6144], P('seq'), may hold values from -0.125 to 0.125
- mix_out: bfloat16 [2048, 2048], P('seq'), may hold values from -0.25 to 0.25
- gate_up: bfloat16 [2048, 2, 5632], P('seq', None, 'head'), may hold values from -0.125 to 0.125
- down_proj: bfloat16 [2048, 5632], P('seq', 'head'), may hold values from -0.15625 to 0.15625
- norm_gain: float32 [2048], replicated, may hold values from 0.5 to 1.5
- ffn_gain: float32 [2048], replicated, may hold values from 0.5 to 1.5
- head_gain: float32 [512], replicated, may hold values from 0.5 to 1.5
- rank_down: bfloat16 [2048, 16], replicated, may hold values from -0.125 to 0.125
- rank_up: float32 [16, 1024], replicated, may hold values from -2.4 to 2.4
- gate_bias: float32 [1024], replicated, may hold values from -0.5 to 7
Outputs:
- output: bfloat16 [3, 2048, 2048], P(None, ('seq', 'head'))
- input_grad: float32 [3, 2048, 2048], P(None, ('seq', 'head'))
- grad_mix_in: float32 [2048, 6144], P(('seq', 'head'))
- grad_mix_out: float32 [2048, 2048], P(('seq', 'head'))
- grad_gate_up: float32 [2048, 2, 5632], P('seq', None, 'head')
- grad_down: float32 [2048, 5632], P('seq', 'head')
- grad_norm_gain: float32 [2048], replicated
- grad_ffn_gain: float32 [2048], replicated
- grad_head_gain: float32 [512], replicated
- grad_rank_down: float32 [2048, 16], replicated
- grad_rank_up: float32 [16, 1024], replicated
- grad_gate_bias: float32 [1024], replicated
Inputs may be any that keep to these rules, and one draw needn't show every extreme that they name: starts[b, 0] is 1 for every micro-batch b; two ones of a row lie at least 32 blocks apart, and the last one of a row lies at least 32 blocks before the row's end.
All inputs are finite; a program needn't handle non-finite values.
Results may differ from a plain program's by a relative error of at most 0.015.
The roundings to bfloat16 on the way count: a program that leaves them out, or rounds other values in their place, can miss the bound.
Values may be sent and summed in bfloat16 or wider, within the bound.
A program may use at most 248 MiB of HBM per device.

v0:
```python
import jax
import jax.numpy as jnp
from jax import lax
from jax.sharding import PartitionSpec as P

highest_precision = lax.Precision.HIGHEST
gate_norm = 16.0


def entering(part, axis, combine, identity):
    place = lax.axis_index(axis)
    gathered = jax.tree.map(lambda a: lax.all_gather(a, axis), part)
    state = jax.tree.map(lambda a, e: jnp.zeros_like(a) + jnp.asarray(e, a.dtype), part, identity)

    def one(hop, state):
        return combine(
            state, jax.tree.map(lambda a: lax.dynamic_index_in_dim(a, hop, 0, False), gathered)
        )

    return lax.fori_loop(0, place, one, state)


def carried_in(x, axis, combine, identity):
    length, place = (lax.axis_size(axis), lax.axis_index(axis))
    everything = jax.tree.map(
        lambda part, kind: lax.all_gather(part.astype(kind), axis),
        x,
        jax.tree.map(lambda a: jnp.bfloat16 if a.dtype == jnp.float32 else a.dtype, x),
    )
    start = jax.tree.map(
        lambda part, zero: jnp.broadcast_to(jnp.asarray(zero, part.dtype), part.shape), x, identity
    )

    def hop(k, before):
        at = length - 1 - k
        reached = at > place
        new = combine(
            before, jax.tree.map(lambda part, own: part[at].astype(own.dtype), everything, x)
        )
        return jax.tree.map(lambda a, b: jnp.where(reached, a, b), new, before)

    return lax.fori_loop(0, length, hop, start)


def norm_forward(incoming_values, gain_vec, epsilon):
    inv_rms = lax.rsqrt(
        jnp.mean(incoming_values * incoming_values, axis=-1, keepdims=True) + epsilon
    )
    normed = incoming_values * inv_rms
    return (normed * gain_vec, normed, inv_rms)


def norm_backward(grad_in, gain_vec, normed, inv_rms):
    scaled = grad_in * gain_vec
    inner_mean = jnp.mean(scaled * normed, axis=-1, keepdims=True)
    return (inv_rms * (scaled - normed * inner_mean), jnp.sum(grad_in * normed, axis=0))


def compose(earlier, later_part):
    return (earlier[0] * later_part[0], later_part[0][:, None] * earlier[1] + later_part[1])


def block_step(carry_state, inputs):
    queries, keys_in, incoming_values, decays, reset_flag = inputs
    incoming_state = carry_state * (1.0 - reset_flag)
    decay_sum = jnp.cumsum(decays, axis=0)
    decay_total = decay_sum[-1]
    queried_state = queries * jnp.exp(decay_sum) * queries.shape[1] ** (-0.5)
    keyed = keys_in * jnp.exp(-decay_sum)
    scores = jnp.dot(queried_state, keyed.T, precision=highest_precision)
    row_ids = lax.broadcasted_iota(jnp.int32, scores.shape, 0)
    col_ids = lax.broadcasted_iota(jnp.int32, scores.shape, 1)
    scores = jnp.where(row_ids >= col_ids, scores, 0.0)
    output = jnp.dot(scores, incoming_values, precision=highest_precision) + jnp.dot(
        queried_state, incoming_state, precision=highest_precision
    )
    carried_state_value = keys_in * jnp.exp(decay_total[None, :] - decay_sum)
    updated_state = jnp.exp(decay_total)[:, None] * incoming_state + jnp.dot(
        carried_state_value.T, incoming_values, precision=highest_precision
    )
    return (updated_state, output)


def local_mixer(queries, keys_in, incoming_values, decays, flags, incoming):
    block_count = flags.shape[0]

    def to_blocks(tensor):
        return tensor.reshape(block_count, tensor.shape[0] // block_count, tensor.shape[1])

    final_state, outputs = lax.scan(
        jax.checkpoint(block_step),
        incoming,
        (
            to_blocks(queries),
            to_blocks(keys_in),
            to_blocks(incoming_values),
            to_blocks(decays),
            flags,
        ),
    )
    return (outputs.reshape(queries.shape[0], incoming_values.shape[1]), final_state)


def contract_rows(left_side, right_side):
    return lax.dot_general(
        left_side, right_side, (((0,), (0,)), ((), ())), preferred_element_type=jnp.float32
    )


def reduce_weight_grads(
    all_in, all_proj, all_mixgrad, all_gated, all_group, all_gugrad, all_cotan, all_product
):
    mixer_piece = lax.psum_scatter(
        jnp.concatenate(
            [contract_rows(all_in, all_proj), contract_rows(all_mixgrad, all_gated)], axis=1
        ),
        ("seq", "head"),
        scatter_dimension=0,
        tiled=True,
    )
    ffn_piece = lax.psum_scatter(
        jnp.concatenate(
            [contract_rows(all_group, all_gugrad), contract_rows(all_cotan, all_product)], axis=1
        ).astype(jnp.bfloat16),
        "seq",
        scatter_dimension=0,
        tiled=True,
    ).astype(jnp.float32)
    return (mixer_piece, ffn_piece)


def on_device(
    tokens,
    starts,
    cotangent,
    mix_in,
    mix_out,
    gate_up,
    down_proj,
    norm_gain,
    ffn_gain,
    head_gain,
    rank_down,
    rank_up,
    gate_bias,
):
    micro_count = tokens.shape[0]
    row_count = tokens.shape[1]
    head_count = lax.axis_size("head")
    key_total = rank_up.shape[1]
    key_width = key_total // head_count
    value_width = head_gain.shape[0]
    value_total = value_width * head_count
    rank_full = rank_down.astype(jnp.float32)
    zero_state = jnp.zeros((key_width, value_width), jnp.float32)
    norm_gain_grad = jnp.zeros_like(norm_gain)
    ffn_gain_grad = jnp.zeros_like(ffn_gain)
    head_gain_grad = jnp.zeros_like(head_gain)
    rank_down_grad = jnp.zeros(rank_down.shape, jnp.float32)
    rank_up_grad = jnp.zeros_like(rank_up)
    bias_grad = jnp.zeros_like(gate_bias)
    outputs_list = []
    input_gradient_list = []
    saved_in = []
    saved_proj = []
    saved_gated = []
    saved_mixgrad = []
    saved_group = []
    saved_gugrad = []
    saved_product = []
    saved_cotan = []
    mixer_total = None
    ffn_total = None
    for micro_index in range(micro_count):
        fetched = (
            lax.all_gather(mix_in, "seq", axis=0, tiled=True),
            lax.all_gather(mix_out, "seq", axis=0, tiled=True),
            lax.all_gather(gate_up, "seq", axis=0, tiled=True),
            lax.all_gather(down_proj, "seq", axis=0, tiled=True),
        )
        full_in, full_out, full_gu, full_down = fetched
        source = tokens[micro_index].astype(jnp.float32)
        normed_in, plain_in, scale_in = norm_forward(source, norm_gain, 1e-06)
        low_in = normed_in.astype(jnp.bfloat16)
        projected = jnp.dot(low_in, full_in, preferred_element_type=jnp.float32)
        queries = projected[:, :key_total].astype(jnp.bfloat16)
        keys_low = projected[:, key_total : 2 * key_total].astype(jnp.bfloat16)
        values_low = projected[:, 2 * key_total : 2 * key_total + value_total].astype(jnp.bfloat16)
        out_gate = projected[:, 2 * key_total + value_total :]
        ranked = jnp.dot(low_in, rank_down, preferred_element_type=jnp.float32)
        logits = jnp.dot(ranked, rank_up, precision=highest_precision) + gate_bias
        decays = (jax.nn.log_sigmoid(logits) / gate_norm).astype(jnp.bfloat16)
        received = (
            lax.all_to_all(
                queries.reshape(row_count, head_count, key_width),
                "head",
                split_axis=1,
                concat_axis=0,
                tiled=True,
            ),
            lax.all_to_all(
                keys_low.reshape(row_count, head_count, key_width),
                "head",
                split_axis=1,
                concat_axis=0,
                tiled=True,
            ),
            lax.all_to_all(
                values_low.reshape(row_count, head_count, value_width),
                "head",
                split_axis=1,
                concat_axis=0,
                tiled=True,
            ),
            lax.all_to_all(
                decays.reshape(row_count, head_count, key_width),
                "head",
                split_axis=1,
                concat_axis=0,
                tiled=True,
            ),
        )
        head_query = received[0][:, 0, :].astype(jnp.float32)
        head_key = received[1][:, 0, :].astype(jnp.float32)
        head_value = received[2][:, 0, :].astype(jnp.float32)
        head_decay = received[3][:, 0, :].astype(jnp.float32)
        flags = starts[micro_index].astype(jnp.float32)
        local_part, own_state = local_mixer(
            head_query, head_key, head_value, head_decay, flags, zero_state
        )
        group_count = head_query.shape[0]
        block_len = group_count // flags.shape[0]
        alive_block = (jnp.cumsum(flags) == 0.0).astype(jnp.float32)
        alive_rows = jnp.broadcast_to(alive_block[:, None], (flags.shape[0], block_len)).reshape(
            group_count, 1
        )
        decay_run = jnp.cumsum(head_decay, axis=0)
        reach_rows = head_query * jnp.exp(decay_run) * alive_rows * key_width ** (-0.5)
        through = alive_block[-1] * jnp.exp(decay_run[-1])
        identity = (jnp.ones_like(through), jnp.zeros_like(zero_state))
        before = entering((through, own_state), "seq", compose, identity)[1]
        mixed_head = local_part + jnp.dot(reach_rows, before, precision=highest_precision)
        head_out, head_plain, head_scale = norm_forward(mixed_head, head_gain, 1e-05)
        returned = lax.all_to_all(
            head_out.astype(jnp.bfloat16)[:, None, :],
            "head",
            split_axis=0,
            concat_axis=1,
            tiled=True,
        )
        normed_out = returned.reshape(row_count, value_total).astype(jnp.float32)
        gate_sig = jax.nn.sigmoid(out_gate)
        swish = out_gate * gate_sig
        gated = (normed_out * swish).astype(jnp.bfloat16)
        mixed = jnp.dot(gated, full_out.T, preferred_element_type=jnp.float32)
        hidden = source + mixed
        normed_ffn, plain_ffn, scale_ffn = norm_forward(hidden, ffn_gain, 1e-06)
        low_ffn = normed_ffn.astype(jnp.bfloat16)
        group_rows, group_grad = (
            lax.all_gather(low_ffn, "head", axis=0, tiled=True),
            lax.all_gather(cotangent[micro_index], "head", axis=0, tiled=True),
        )
        gate_both = jnp.einsum(
            "td,dsf->tsf", group_rows, full_gu, preferred_element_type=jnp.float32
        )
        gate_lin = gate_both[:, 0]
        up_lin = gate_both[:, 1]
        gate_sigma = jax.nn.sigmoid(gate_lin)
        gate_act = gate_lin * gate_sigma
        product = (gate_act * up_lin).astype(jnp.bfloat16)
        ffn_part = jnp.dot(product, full_down.T, preferred_element_type=jnp.float32)
        ffn_out = lax.psum_scatter(
            ffn_part.astype(jnp.bfloat16), "head", scatter_dimension=0, tiled=True
        ).astype(jnp.float32)
        outputs_list.append((hidden + ffn_out).astype(jnp.bfloat16))
        product_grad = jnp.dot(group_grad, full_down, preferred_element_type=jnp.float32)
        grad_gate = (
            product_grad * up_lin * gate_sigma * (1.0 + gate_lin * (1.0 - gate_sigma))
        ).astype(jnp.bfloat16)
        grad_upper = (product_grad * gate_act).astype(jnp.bfloat16)
        grad_both = jnp.stack([grad_gate, grad_upper], axis=1)
        ffn_in_part = jnp.einsum(
            "tsf,dsf->td", grad_both, full_gu, preferred_element_type=jnp.float32
        )
        ffn_in_grad = lax.psum_scatter(ffn_in_part, "head", scatter_dimension=0, tiled=True)
        back_ffn, ffn_piece_gain = norm_backward(ffn_in_grad, ffn_gain, plain_ffn, scale_ffn)
        ffn_gain_grad = ffn_gain_grad + ffn_piece_gain
        hidden_grad = cotangent[micro_index].astype(jnp.float32) + back_ffn
        mixed_grad = hidden_grad.astype(jnp.bfloat16)
        gated_grad = jnp.dot(mixed_grad, full_out, preferred_element_type=jnp.float32)
        normed_grad = (gated_grad * swish).astype(jnp.bfloat16)
        outgate_grad = (
            gated_grad * normed_out * gate_sig * (1.0 + out_gate * (1.0 - gate_sig))
        ).astype(jnp.bfloat16)
        head_grad = lax.all_to_all(
            normed_grad.reshape(row_count, head_count, value_width),
            "head",
            split_axis=1,
            concat_axis=0,
            tiled=True,
        )
        head_grad = head_grad[:, 0, :].astype(jnp.float32)
        mixed_head_grad, head_piece = norm_backward(head_grad, head_gain, head_plain, head_scale)
        head_gain_grad = head_gain_grad + head_piece
        pulled_state = jnp.dot(reach_rows.T, mixed_head_grad, precision=highest_precision)
        state_grad = carried_in((through, pulled_state), "seq", compose, identity)[1]

        def run_local(queries_in, keys_in, incoming_values, decays_in):
            return local_mixer(queries_in, keys_in, incoming_values, decays_in, flags, before)

        pullback = jax.vjp(run_local, head_query, head_key, head_value, head_decay)[1]
        query_grad, key_grad, value_grad, decay_grad = pullback((mixed_head_grad, state_grad))
        sent_back = (
            lax.all_to_all(
                query_grad.astype(jnp.bfloat16)[:, None, :],
                "head",
                split_axis=0,
                concat_axis=1,
                tiled=True,
            ),
            lax.all_to_all(
                key_grad.astype(jnp.bfloat16)[:, None, :],
                "head",
                split_axis=0,
                concat_axis=1,
                tiled=True,
            ),
            lax.all_to_all(
                value_grad.astype(jnp.bfloat16)[:, None, :],
                "head",
                split_axis=0,
                concat_axis=1,
                tiled=True,
            ),
            lax.all_to_all(
                decay_grad.astype(jnp.bfloat16)[:, None, :],
                "head",
                split_axis=0,
                concat_axis=1,
                tiled=True,
            ),
        )
        decay_back = sent_back[3].reshape(row_count, key_total).astype(jnp.float32)
        logit_grad = decay_back * jax.nn.sigmoid(-logits) / gate_norm
        ranked_grad = jnp.dot(logit_grad, rank_up.T, precision=highest_precision)
        proj_grad = jnp.concatenate(
            [
                sent_back[0].reshape(row_count, key_total),
                sent_back[1].reshape(row_count, key_total),
                sent_back[2].reshape(row_count, value_total),
                outgate_grad,
            ],
            axis=1,
        )
        in_grad = jnp.dot(proj_grad, full_in.T, preferred_element_type=jnp.float32)
        in_grad = in_grad + jnp.dot(ranked_grad, rank_full.T, precision=highest_precision)
        back_in, norm_piece = norm_backward(in_grad, norm_gain, plain_in, scale_in)
        norm_gain_grad = norm_gain_grad + norm_piece
        input_gradient_list.append(hidden_grad + back_in)
        rank_down_grad = rank_down_grad + jnp.dot(
            low_in.astype(jnp.float32).T, ranked_grad, precision=highest_precision
        )
        rank_up_grad = rank_up_grad + jnp.dot(ranked.T, logit_grad, precision=highest_precision)
        bias_grad = bias_grad + jnp.sum(logit_grad, axis=0)
        flat_gugrad = grad_both.reshape(grad_both.shape[0], -1)
        saved_in.append(low_in)
        saved_proj.append(proj_grad)
        saved_gated.append(gated)
        saved_mixgrad.append(mixed_grad)
        saved_group.append(group_rows)
        saved_gugrad.append(flat_gugrad)
        saved_product.append(product)
        saved_cotan.append(group_grad)
    mixer_total, ffn_total = reduce_weight_grads(
        jnp.concatenate(saved_in, axis=0),
        jnp.concatenate(saved_proj, axis=0),
        jnp.concatenate(saved_mixgrad, axis=0),
        jnp.concatenate(saved_gated, axis=0),
        jnp.concatenate(saved_group, axis=0),
        jnp.concatenate(saved_gugrad, axis=0),
        jnp.concatenate(saved_cotan, axis=0),
        jnp.concatenate(saved_product, axis=0),
    )
    proj_width = 2 * key_total + 2 * value_total
    hidden_width = down_proj.shape[1]
    ffn_rows_dev = ffn_total.shape[0]
    small = lax.psum(
        (norm_gain_grad, ffn_gain_grad, head_gain_grad, rank_down_grad, rank_up_grad, bias_grad),
        ("seq", "head"),
    )
    return (
        jnp.stack(outputs_list),
        jnp.stack(input_gradient_list),
        mixer_total[:, :proj_width],
        mixer_total[:, proj_width:],
        ffn_total[:, : 2 * hidden_width].reshape(ffn_rows_dev, 2, hidden_width),
        ffn_total[:, 2 * hidden_width :],
        small[0],
        small[1],
        small[2],
        small[3],
        small[4],
        small[5],
    )


def solution(mesh):
    return jax.shard_map(
        on_device,
        mesh=mesh,
        in_specs=(
            P(None, ("seq", "head"), None),
            P(None, "seq"),
            P(None, ("seq", "head"), None),
            P("seq", None),
            P("seq", None),
            P("seq", None, "head"),
            P("seq", "head"),
            P(),
            P(),
            P(),
            P(),
            P(),
            P(),
        ),
        out_specs=(
            P(None, ("seq", "head"), None),
            P(None, ("seq", "head"), None),
            P(("seq", "head"), None),
            P(("seq", "head"), None),
            P("seq", None, "head"),
            P("seq", "head"),
            P(),
            P(),
            P(),
            P(),
            P(),
            P(),
        ),
        check_vma=False,
    )
```

profile of v0, /device:TPU:0, one launch (start us, length us, event | category | flops | bytes accessed | tf_op | source)
XLA Modules:
  0.0 3053.7 jit_solution(15395980412652879313)
XLA Ops:
  19.8 118.3 %all-gather.32.cloned.1.call-done = bf16[2048,6144]{1,0:T(8,128)(2,1)} async-done(((bf16[256,6144]{1,0:T(8,128)(2,1)}), bf16[2048,6144]{1,0:T(8,128)(2,1)}) %all-gather.32.cloned.1.call-update) | async-done | bytes 25165840 | tf_op jit(solution)/shard_map/all_gather | solution.py:176
  188.1 25.0 while.234
  264.2 32.7 %while.236 = (s32[]{:T(128)}, f32[256,512]{1,0:T(8,128)S(1)}, f32[4,64,512]{2,1,0:T(8,128)S(1)}, f32[4,64,256]{2,1,0:T(8,128)}, f32[4]{0:T(128)}, /*index=5*/f32...) while((s32[]{:T(128)}, f32[256,512]{1,0:T(8,128)S(1)}, ...), condition=%wide.region_27.28_spmd.clone, body=%wide.region_25.27_spmd.clone.sunk | while | flops 241065984 | bytes 3058858 | solution.py:90
  341.0 12.4 while.235
  415.1 31.0 %all-gather.34.cloned.1.call-done = bf16[2048,2048]{1,0:T(8,128)(2,1)} async-done(((bf16[256,2048]{1,0:T(8,128)(2,1)}), bf16[2048,2048]{1,0:T(8,128)(2,1)}) %all-gather.34.cloned.1.call-update) | async-done | bytes 8388624 | tf_op jit(solution)/shard_map/all_gather | solution.py:177
  456.1 60.0 %all-gather.38.cloned.1.call-done = bf16[2048,2,1408]{2,0,1:T(8,128)(2,1)} async-done(((bf16[256,2,1408]{2,0,1:T(8,128)(2,1)}), bf16[2048,2,1408]{2,0,1:T(8,128)(2,1)}) %all-gather.38.cloned.1.call-update) | async-done | bytes 11534352 | tf_op jit(solution)/shard_map/all_gather | solution.py:178
  516.1 30.1 all-gather.36.cloned.1.call-done
  555.5 20.3 all-gather.52.cloned.1.call-done
  575.8 44.7 %all-gather.40.cloned.1.call-done = bf16[2048,1408]{1,0:T(8,128)(2,1)} async-done(((bf16[256,1408]{1,0:T(8,128)(2,1)}), bf16[2048,1408]{1,0:T(8,128)(2,1)}) %all-gather.40.cloned.1.call-update) | async-done | bytes 5767184 | tf_op jit(solution)/shard_map/all_gather | solution.py:179
  648.4 13.6 all-to-all-done.9
  703.9 26.2 all-gather.44.cloned.1.call-done
  739.4 19.6 all-gather.60.cloned.1.call-done
  798.1 19.6 all-gather.56.cloned.1.call-done
  846.0 17.3 reduce-scatter.19.cloned.1.call-done
  863.3 45.9 %reduce-scatter.17.cloned.1.call-done = f32[64,2048]{1,0:T(8,128)} async-done(((f32[256,2048]{1,0:T(8,128)}), f32[64,2048]{1,0:T(8,128)}) %reduce-scatter.17.cloned.1.call-update) | async-done | bytes 524304 | tf_op jit(solution)/shard_map/reduce_scatter | solution.py:285
  911.4 26.6 reduce-scatter.13.cloned.1.call-done
  938.0 28.6 reduce-scatter.11.cloned.1.call-done
  1049.9 24.5 while.228
  1078.5 27.4 while.232
  1107.6 21.0 while.230
  1148.9 14.7 convolution_convert_fusion
  1188.5 47.2 %while.233 = (s32[]{:T(128)}, f32[256,512]{1,0:T(8,128)S(1)}, bf16[4,64,256]{2,1,0:T(8,128)(2,1)}, bf16[4,64,256]{2,1,0:T(8,128)(2,1)}, bf16[4,64,512]{2,1,0:T(8...) while((s32[]{:T(128)}, f32[256,512]{1,0:T(8,128)S(1)}, ...), condition=%wide.region_79.80_spmd, body=%wide.region_74.79_spmd.sunk | while | flops 494370816 | bytes 13386137 | solution.py:90
  1259.3 43.8 %while.231 = (s32[]{:T(128)}, f32[256,512]{1,0:T(8,128)S(1)}, bf16[4,64,256]{2,1,0:T(8,128)(2,1)}, bf16[4,64,256]{2,1,0:T(8,128)(2,1)}, bf16[4,64,512]{2,1,0:T(8...) while((s32[]{:T(128)}, f32[256,512]{1,0:T(8,128)S(1)}, ...), condition=%wide.region_64.65_spmd, body=%wide.region_59.64_spmd.sunk | while | flops 494370816 | bytes 11288929 | solution.py:90
  1326.3 38.6 %while.229 = (s32[]{:T(128)}, f32[256,512]{1,0:T(8,128)S(1)}, bf16[4,64,256]{2,1,0:T(8,128)(2,1)S(1)}, bf16[4,64,256]{2,1,0:T(8,128)(2,1)S(1)}, bf16[4,64,512]{2...) while((s32[]{:T(128)}, f32[256,512]{1,0:T(8,128)S(1)}, ...), condition=%wide.region_49.50_spmd, body=%wide.region_44.49_spmd.sunk | while | flops 494370816 | bytes 9191665 | solution.py:90
  1425.3 25.3 fusion.204
  1450.7 43.3 %pad_maximum_fusion = f32[2048,8192]{1,0:T(8,128)} fusion(f32[2048,2048]{1,0:T(8,128)} %fusion.271, f32[2048,6144]{1,0:T(8,128)} %fusion.204), kind=kLoop, calls=%fused_computation.288 | loop fusion | flops 16777216 | bytes 134217728 | tf_op jit(solution)/shard_map/concatenate | solution.py:114
  1544.5 12.7 fusion.242
  1557.7 12.5 fusion.250
  1571.4 13.4 fusion.258
  1594.4 44.7 %all-reduce.3 = (f32[2048]{0:T(1024)}, f32[2048]{0:T(1024)}, f32[512]{0:T(512)}, f32[1024]{0:T(1024)}) all-reduce(f32[2048]{0:T(1024)S(1)} %add_add_fusion.1, f32[2048]{0:T(1024)S(1)} %add_add_fusion, f32[512]{0:T(512)S(1)} %add_add_fusion.3, f32[1024]{0:T(1024)S(1)} %add_add_fusion.2), channel_id=1, replica_groups=mesh['seq'=8,'head'=4] {'seq','head'}, use_global_device_ids=true, to_apply=%region_86.87 | all-reduce | flops 5632 | bytes 45056 | tf_op jit(solution)/shard_map/psum | solution.py:387
  1645.8 1267.7 %reduce-scatter.21.cloned.1.call-done = f32[64,8192]{1,0:T(8,128)} async-done(((f32[2048,8192]{1,0:T(8,128)}), f32[64,8192]{1,0:T(8,128)}) %reduce-scatter.21.cloned.1.call-update) | async-done | bytes 2097168 | tf_op jit(solution)/shard_map/reduce_scatter | solution.py:113
  2918.0 125.9 %all-reduce.7.cloned.1.call-done = (f32[2048,16]{0,1:T(8,128)}, f32[16,1024]{1,0:T(8,128)}) async-done(((f32[2048,16]{0,1:T(8,128)}, f32[16,1024]{1,0:T(8,128)}), (f32[2048,16]{0,1:T(8,128)}, f32[16,1024]{1,0:T(8,128)})) %all-reduce.7.cloned.1.call-update) | async-done | bytes 196624 | tf_op jit(solution)/shard_map/psum | solution.py:387
  (1338 shorter events, 975.1 us)
Async XLA Ops:
  7.2 130.8 %all-gather.32.cloned.1.call-start = ((), (), s32[]{:S(2)}) async-start(), calls=%async_computation.38 | async-start | bytes 28311552 | tf_op jit(solution)/shard_map/all_gather | solution.py:176
  11.1 140.2 %all-to-all-start = ((bf16[64,4,256]{2,0,1:T(8,128)(2,1)}), bf16[64,4,256]{2,0,1:T(8,128)(2,1)S(1)}, u32[]{:S(2)}, u32[]{:S(2)}) async-start(bf16[64,4,256]{2,0,1:T(8,128)(2,1)} %bitcast.1055), calls=%async_computation | async-start | bytes 262144 | tf_op jit(solution)/shard_map/all_to_all | solution.py:215
  182.3 45.3 %all-to-all-start.10 = ((bf16[64,4,256]{2,0,1:T(8,128)(2,1)}), bf16[64,4,256]{2,0,1:T(8,128)(2,1)}, u32[]{:S(2)}, u32[]{:S(2)}) async-start(bf16[64,4,256]{2,0,1:T(8,128)(2,1)} %bitcast.1454), calls=%async_computation.12 | async-start | bytes 262144 | tf_op jit(solution)/shard_map/all_to_all | solution.py:215
  186.2 205.9 %all-gather.46.cloned.1.call-start = ((), (), s32[]{:S(2)}) async-start(), calls=%async_computation.53 | async-start | bytes 4718592 | tf_op jit(solution)/shard_map/all_gather | solution.py:12
  259.3 51.2 %all-to-all-start.5 = ((bf16[64,4,256]{2,0,1:T(8,128)(2,1)}), bf16[64,4,256]{2,0,1:T(8,128)(2,1)S(1)}, u32[]{:S(2)}, u32[]{:S(2)}) async-start(bf16[64,4,256]{2,0,1:T(8,128)(2,1)} %bitcast.1052), calls=%async_computation.6 | async-start | bytes 262144 | tf_op jit(solution)/shard_map/all_to_all | solution.py:215
  262.8 131.1 %all-gather.50.cloned.1.call-start = ((), (), s32[]{:S(2)}) async-start(), calls=%async_computation.55 | async-start | bytes 4718592 | tf_op jit(solution)/shard_map/all_gather | solution.py:12
  334.2 61.7 %all-gather.48.cloned.1.call-start = ((), (), s32[]{:S(2)}) async-start(), calls=%async_computation.54 | async-start | bytes 4718592 | tf_op jit(solution)/shard_map/all_gather | solution.py:12
  354.3 91.7 %all-gather.34.cloned.1.call-start = ((), (), s32[]{:S(2)}) async-start(), calls=%async_computation.39 | async-start | bytes 9437184 | tf_op jit(solution)/shard_map/all_gather | solution.py:177
  354.9 161.2 %all-gather.38.cloned.1.call-start = ((), (), s32[]{:S(2)}) async-start(), calls=%async_computation.41 | async-start | bytes 12976128 | tf_op jit(solution)/shard_map/all_gather | solution.py:178
  357.7 188.5 %all-gather.36.cloned.1.call-start = ((), (), s32[]{:S(2)}) async-start(), calls=%async_computation.40 | async-start | bytes 1310720 | tf_op jit(solution)/shard_map/all_gather | solution.py:260
  453.2 122.6 %all-gather.52.cloned.1.call-start = ((), (), s32[]{:S(2)}) async-start(), calls=%async_computation.56 | async-start | bytes 1310720 | tf_op jit(solution)/shard_map/all_gather | solution.py:261
  455.3 165.3 %all-gather.40.cloned.1.call-start = ((), (), s32[]{:S(2)}) async-start(), calls=%async_computation.42 | async-start | bytes 6488064 | tf_op jit(solution)/shard_map/all_gather | solution.py:179
  456.0 243.0 %reduce-scatter.15.cloned.1.call-start = ((), (), s32[]{:S(2)}) async-start(), calls=%async_computation.48 | async-start | bytes 2621440 | tf_op jit(solution)/shard_map/reduce_scatter | solution.py:285
  640.5 21.5 all-to-all-start.9
  662.1 19.2 all-to-all-start.14
  666.1 64.0 %all-gather.44.cloned.1.call-start = ((), (), s32[]{:S(2)}) async-start(), calls=%async_computation.46 | async-start | bytes 1310720 | tf_op jit(solution)/shard_map/all_gather | solution.py:260
  701.9 57.2 %all-gather.60.cloned.1.call-start = ((), (), s32[]{:S(2)}) async-start(), calls=%async_computation.60 | async-start | bytes 1310720 | tf_op jit(solution)/shard_map/all_gather | solution.py:261
  702.5 86.3 %all-gather.42.cloned.1.call-start = ((), (), s32[]{:S(2)}) async-start(), calls=%async_computation.44 | async-start | bytes 1310720 | tf_op jit(solution)/shard_map/all_gather | solution.py:260
  703.2 114.5 %all-gather.56.cloned.1.call-start = ((), (), s32[]{:S(2)}) async-start(), calls=%async_computation.58 | async-start | bytes 1310720 | tf_op jit(solution)/shard_map/all_gather | solution.py:261
  703.8 159.5 %reduce-scatter.19.cloned.1.call-start = ((), (), s32[]{:S(2)}) async-start(), calls=%async_computation.50 | async-start | bytes 2621440 | tf_op jit(solution)/shard_map/reduce_scatter | solution.py:285
  776.0 133.3 %reduce-scatter.17.cloned.1.call-start = ((), (), s32[]{:S(2)}) async-start(), calls=%async_computation.49 | async-start | bytes 2621440 | tf_op jit(solution)/shard_map/reduce_scatter | solution.py:285
  834.4 103.6 %reduce-scatter.13.cloned.1.call-start = ((), (), s32[]{:S(2)}) async-start(), calls=%async_computation.47 | async-start | bytes 1310720 | tf_op jit(solution)/shard_map/reduce_scatter | solution.py:272
  840.2 126.4 %reduce-scatter.11.cloned.1.call-start = ((), (), s32[]{:S(2)}) async-start(), calls=%async_computation.45 | async-start | bytes 1310720 | tf_op jit(solution)/shard_map/reduce_scatter | solution.py:272
  1004.9 172.3 %all-gather.62.cloned.1.call-start = ((), (), s32[]{:S(2)}) async-start(), calls=%async_computation.61 | async-start | bytes 2359296 | tf_op jit(solution)/shard_map/all_gather | solution.py:26
  1019.3 222.2 %all-gather.58.cloned.1.call-start = ((), (), s32[]{:S(2)}) async-start(), calls=%async_computation.59 | async-start | bytes 2359296 | tf_op jit(solution)/shard_map/all_gather | solution.py:26
  1021.8 288.8 %all-gather.54.cloned.1.call-start = ((), (), s32[]{:S(2)}) async-start(), calls=%async_computation.57 | async-start | bytes 2359296 | tf_op jit(solution)/shard_map/all_gather | solution.py:26
  1076.8 513.8 %reduce-scatter.9.cloned.1.call-start = ((), (), s32[]{:S(2)}) async-start(), calls=%async_computation.43 | async-start | bytes 1310720 | tf_op jit(solution)/shard_map/reduce_scatter | solution.py:272
  1139.5 499.7 %reduce-scatter.23.cloned.1.call-start = ((), (), s32[]{:S(2)}) async-start(), calls=%async_computation.52 | async-start | bytes 19464192 | tf_op jit(solution)/shard_map/reduce_scatter | solution.py:121
  1252.2 53.2 %all-to-all-start.27 = ((bf16[4,2,8192]{2,1,0:T(2,128)(2,1)}), bf16[4,2,8192]{2,1,0:T(2,128)(2,1)}, u32[]{:S(2)}, u32[]{:S(2)}) async-start(bf16[4,2,8192]{2,1,0:T(2,128)(2,1)} %reshape.1321), calls=%async_computation.33 | async-start | bytes 262144 | tf_op jit(solution)/shard_map/all_to_all | solution.py:321
  1321.2 45.1 %all-to-all-start.22 = ((bf16[4,2,8192]{2,1,0:T(2,128)(2,1)}), bf16[4,2,8192]{2,1,0:T(2,128)(2,1)S(1)}, u32[]{:S(2)}, u32[]{:S(2)}) async-start(bf16[4,2,8192]{2,1,0:T(2,128)(2,1)} %reshape.1329), calls=%async_computation.27 | async-start | bytes 262144 | tf_op jit(solution)/shard_map/all_to_all | solution.py:321
  1411.0 1502.5 %reduce-scatter.21.cloned.1.call-start = ((), (), s32[]{:S(2)}) async-start(), calls=%async_computation.51 | async-start | bytes 69206016 | tf_op jit(solution)/shard_map/reduce_scatter | solution.py:113
  1529.7 1514.3 %all-reduce.7.cloned.1.call-start = ((), (), s32[]{:S(2)}) async-start(), calls=%async_computation.62 | async-start | bytes 393216 | tf_op jit(solution)/shard_map/psum | solution.py:387
  (222 other events, 4982.3 us)
Sparse Core Ops, SparseCore 0:
  9.9 128.0 all-gather.31
  214.1 37.0 all-gather.45
  298.0 37.0 all-gather.49
  354.4 35.4 all-gather.47
  391.6 54.3 all-gather.33
  448.4 67.6 all-gather.37
  518.2 27.9 all-gather.35
  548.3 27.4 all-gather.51
  577.7 42.8 all-gather.39
  637.3 52.1 reduce-scatter.14
  702.0 28.0 all-gather.43
  731.6 27.4 all-gather.59
  761.3 27.4 all-gather.41
  790.2 27.4 all-gather.55
  819.9 43.3 reduce-scatter.18
  866.1 43.1 reduce-scatter.16
  911.5 26.4 reduce-scatter.12
  940.7 25.7 reduce-scatter.10
  1019.4 27.6 all-gather.61
  1049.0 27.8 all-gather.57
  1079.0 27.9 all-gather.53
  1139.6 26.0 reduce-scatter.8
  1177.3 117.4 reduce-scatter.22
  1494.2 1419.1 reduce-scatter.20
  2920.5 123.3 all-reduce.6
where the time goes:
time: 3070 us; the launch traced here: 3050 us
  waiting for transfers between devices  2010 us (65%)
  matrix products  388 us (13%)
  local copies, waits for them, and re-layouts  213 us (7%)
  other arithmetic  166 us (5%)
  starting transfers between devices  123 us (4%)
  blocking collectives  106 us (3%)
    reduce_scatter x1, waiting for transfers between devices, reduce_weight_grads(): lax.psum_scatter(jnp.concatenate([contract_rows(all_in, all_proj), contra...  1270 us
    psum x1, waiting for transfers between devices, on_device(): lax.psum((norm_gain_grad, ffn_gain_grad, head_gain_grad, rank_down_grad,...  126 us
    all_gather x1, waiting for transfers between devices, on_device(): lax.all_gather(mix_in, 'seq', axis=0, tiled=True)  118 us
    all_gather x3, waiting for transfers between devices, on_device(): lax.all_gather(low_ffn, 'head', axis=0, tiled=True)  68.6 us
    squeeze x72, local copies, waits for them, and re-layouts, local_mixer(): lax.scan(jax.checkpoint(block_step), incoming, (to_blocks(queries), to_bl...  67.6 us
    reduce_scatter x3, waiting for transfers between devices, on_device(): lax.psum_scatter(ffn_in_part, 'head', scatter_dimension=0, tiled=True)  63.3 us
  transfers between devices with their start and end apart: 54, of which 37 were waited for; matrix products, arithmetic and copies ran while one was open for 23% of the time, Pallas kernels for 0%

commit v1 on v0

v1 whole, which is shorter than its diff:
```python
import functools

import jax
import jax.numpy as jnp
from jax import lax
from jax.experimental import pallas as pl
from jax.experimental.pallas import tpu as pltpu
from jax.sharding import PartitionSpec as P

HIGHEST = lax.Precision.HIGHEST
GATE_NORM = 16.0
BF16 = jnp.bfloat16
F32 = jnp.float32


def mm(a, b, contract, precision=HIGHEST):
    return lax.dot_general(
        a, b, ((contract[:1], contract[1:]), ((), ())),
        precision=precision, preferred_element_type=F32,
    )


def lower_ones(size):
    rows = lax.broadcasted_iota(jnp.int32, (size, size), 0)
    cols = lax.broadcasted_iota(jnp.int32, (size, size), 1)
    return rows >= cols


def running(decay_low):
    ones = lower_ones(decay_low.shape[0]).astype(F32).astype(BF16)
    return mm(ones, decay_low, (1, 0), None)


def sigmoid(x):
    return 1.0 / (1.0 + jnp.exp(-x))


def state_kernel(flags, qkv, decay, out, state, total_run):
    m, b = pl.program_id(0), pl.program_id(1)
    last = pl.num_programs(1) - 1
    dk = decay.shape[-1]
    keys, values = qkv[0, 0, :, dk : 2 * dk].astype(F32), qkv[0, 0, :, 2 * dk :].astype(F32)
    keep = 1.0 - flags[m, b].astype(F32)

    @pl.when(b == 0)
    def _():
        state[...] = jnp.zeros_like(state)
        total_run[0:1, :] = jnp.zeros((1, dk), F32)
        total_run[1:2, :] = jnp.ones((1, dk), F32)

    run = running(decay[0, 0])
    total = run[-1:, :]
    carried = keys * jnp.exp(total - run)
    state[...] = jnp.exp(total) * (state[...] * keep) + mm(values, carried, (0, 0))
    total_run[0:1, :] += total
    total_run[1:2, :] *= keep

    @pl.when(b == last)
    def _():
        through = jnp.exp(total_run[0:1, :]) * total_run[1:2, :]
        high = through.astype(BF16)
        low = (through - high.astype(F32)).astype(BF16)
        slices, part = out.shape[0], state.shape[0] // out.shape[0]
        tail = out.shape[2] - part
        at = lax.broadcasted_iota(jnp.int32, (tail, dk), 0)
        extra = jnp.where(
            at == 0, high.astype(F32), jnp.where(at == 1, low.astype(F32), 0.0)
        ).astype(BF16)
        for i in range(slices):
            out[i, 0, :part, :] = state[i * part : (i + 1) * part, :].astype(BF16)
            out[i, 0, part:, :] = extra


def prefix_kernel(reverse, own, through, out):
    count = own.shape[0]
    part = out.shape[2]

    def step(k, state):
        j = count - 1 - k if reverse else k
        out[j] = state.astype(BF16)
        decay = through[j, :, 0:1, :].astype(F32) + through[j, :, 1:2, :].astype(F32)
        return decay * state + own[j, :, :part, :].astype(F32)

    lax.fori_loop(0, count, step, jnp.zeros(out.shape[1:], F32))


def mix_kernel(flags, qkv, decay, og, before, gain, o_out, gated, kept, state):
    m, b = pl.program_id(0), pl.program_id(1)
    dk, dv = decay.shape[-1], og.shape[-1]
    q = qkv[0, 0, :, :dk].astype(F32)
    k = qkv[0, 0, :, dk : 2 * dk].astype(F32)
    v = qkv[0, 0, :, 2 * dk :].astype(F32)
    keep = 1.0 - flags[m, b].astype(F32)

    @pl.when(b == 0)
    def _():
        state[...] = before[:, 0].astype(F32).reshape(dv, dk)

    entry = state[...] * keep
    kept[0, 0] = entry
    run = running(decay[0, 0])
    total = run[-1:, :]
    queried = q * jnp.exp(run) * dk ** (-0.5)
    scores = mm(queried, k * jnp.exp(-run), (1, 1))
    scores = jnp.where(lower_ones(scores.shape[0]), scores, 0.0)
    o = mm(scores, v, (1, 0)) + mm(queried, entry, (1, 1))
    state[...] = jnp.exp(total) * entry + mm(v, k * jnp.exp(total - run), (0, 0))
    o_out[0, 0] = o
    scale = lax.rsqrt(jnp.mean(o * o, axis=-1, keepdims=True) + 1e-5)
    normed = (o * scale * gain[...]).astype(BF16).astype(F32)
    gate = og[0, 0]
    gated[0, 0] = (normed * gate * sigmoid(gate)).astype(BF16)


def gate_back_kernel(flags, g_gated, og, o_in, qkv, decay, gain, g_og, g_o, pulled, g_gain,
                     state, total_run):
    m, b = pl.program_id(0), pl.program_id(1)
    last = pl.num_programs(1) - 1
    dk, dv = decay.shape[-1], og.shape[-1]

    @pl.when((m == 0) & (b == 0))
    def _():
        g_gain[...] = jnp.zeros_like(g_gain)

    @pl.when(b == 0)
    def _():
        state[...] = jnp.zeros_like(state)
        total_run[0:1, :] = jnp.zeros((1, dk), F32)
        total_run[1:2, :] = jnp.ones((1, dk), F32)

    gate = og[0, 0]
    grad = g_gated[0, 0].astype(F32)
    sig = sigmoid(gate)
    o = o_in[0, 0]
    scale = lax.rsqrt(jnp.mean(o * o, axis=-1, keepdims=True) + 1e-5)
    plain = o * scale
    normed = (plain * gain[...]).astype(BF16).astype(F32)
    g_on = (grad * gate * sig).astype(BF16).astype(F32)
    g_og[0, 0] = (grad * normed * sig * (1.0 + gate * (1.0 - sig))).astype(BF16)
    scaled = g_on * gain[...]
    inner = jnp.mean(scaled * plain, axis=-1, keepdims=True)
    go = scale * (scaled - plain * inner)
    g_o[0, 0] = go
    g_gain[0:1, :] += jnp.sum(g_on * plain, axis=0, keepdims=True)

    total_run[1:2, :] *= 1.0 - flags[m, b].astype(F32)
    run = running(decay[0, 0])
    reach = (
        qkv[0, 0, :, :dk].astype(F32)
        * jnp.exp(run + total_run[0:1, :])
        * total_run[1:2, :]
        * dk ** (-0.5)
    )
    state[...] += mm(go, reach, (0, 0))
    total_run[0:1, :] += run[-1:, :]

    @pl.when(b == last)
    def _():
        slices, part = pulled.shape[0], dv // pulled.shape[0]
        for i in range(slices):
            pulled[i, 0] = state[i * part : (i + 1) * part, :].astype(BF16)


def mix_back_kernel(flags, qkv, decay, g_o, g_og, kept, after, logits, g_proj, g_logits, g_state):
    m, step = pl.program_id(0), pl.program_id(1)
    b = pl.num_programs(1) - 1 - step
    dk, dv = decay.shape[-1], g_o.shape[-1]
    q = qkv[0, 0, :, :dk].astype(F32)
    k = qkv[0, 0, :, dk : 2 * dk].astype(F32)
    v = qkv[0, 0, :, 2 * dk :].astype(F32)
    keep = 1.0 - flags[m, b].astype(F32)

    @pl.when(step == 0)
    def _():
        g_state[...] = after[:, 0].astype(F32).reshape(dv, dk)

    go, gs, entry = g_o[0, 0], g_state[...], kept[0, 0]
    run = running(decay[0, 0])
    total = run[-1:, :]
    up, down, rest = jnp.exp(run) * dk ** (-0.5), jnp.exp(-run), jnp.exp(total - run)
    decayed = jnp.exp(total)
    queried, keyed, carried = q * up, k * down, k * rest
    causal = lower_ones(q.shape[0])
    scores = jnp.where(causal, mm(queried, keyed, (1, 1)), 0.0)
    g_scores = jnp.where(causal, mm(go, v, (1, 1)), 0.0)
    g_queried = mm(g_scores, keyed, (1, 0)) + mm(go, entry, (1, 0))
    g_keyed = mm(g_scores, queried, (0, 0))
    g_v = mm(scores, go, (0, 0)) + mm(carried, gs, (1, 1))
    g_carried = mm(v, gs, (1, 0))
    g_state[...] = (decayed * gs + mm(go, queried, (0, 0))) * keep
    from_carried = g_carried * carried
    g_total = (
        jnp.sum(decayed * entry * gs, axis=0, keepdims=True)
        + jnp.sum(from_carried, axis=0, keepdims=True)
    )
    g_run = g_queried * queried - g_keyed * keyed - from_carried
    later = mm(causal.astype(F32), g_run, (0, 0)) + g_total
    proj = jnp.concatenate([g_queried * up, g_keyed * down + g_carried * rest, g_v], axis=1)
    width = proj.shape[1]
    g_proj[0, 0, :, :width] = proj.astype(BF16)
    g_proj[0, 0, :, width:] = g_og[0, 0]
    low = later.astype(BF16).astype(F32)
    g_logits[0, 0] = low * sigmoid(-logits[0, 0]) * (1.0 / GATE_NORM)


def params(limit=48):
    return pltpu.CompilerParams(
        dimension_semantics=("arbitrary", "arbitrary"), vmem_limit_bytes=limit << 20
    )


def per_block(rows, width):
    return pl.BlockSpec((1, 1, rows, width), lambda m, b, *_: (b, m, 0, 0))


def backwards(rows, width, count):
    return pl.BlockSpec((1, 1, rows, width), lambda m, b, *_: (count - 1 - b, m, 0, 0))


def per_batch(slices, rows, width):
    return pl.BlockSpec((slices, 1, rows, width), lambda m, b, *_: (0, m, 0, 0))


def states_of(flags, qkv, decays, dv, slices, pad):
    blocks, micro, rows, width = qkv.shape
    dk = decays.shape[-1]
    part = dv // slices
    return pl.pallas_call(
        state_kernel,
        out_shape=jax.ShapeDtypeStruct((slices, micro, part + pad, dk), BF16),
        grid_spec=pltpu.PrefetchScalarGridSpec(
            num_scalar_prefetch=1,
            grid=(micro, blocks),
            in_specs=[per_block(rows, width), per_block(rows, dk)],
            out_specs=per_batch(slices, part + pad, dk),
            scratch_shapes=[pltpu.VMEM((dv, dk), F32), pltpu.VMEM((8, dk), F32)],
        ),
        compiler_params=params(),
        name="states",
    )(flags, qkv, decays)


def prefix_of(own, through, part, reverse):
    return pl.pallas_call(
        functools.partial(prefix_kernel, reverse),
        out_shape=jax.ShapeDtypeStruct(own.shape[:2] + (part, own.shape[3]), BF16),
        in_specs=[pl.BlockSpec(memory_space=pltpu.VMEM)] * 2,
        out_specs=pl.BlockSpec(memory_space=pltpu.VMEM),
        compiler_params=pltpu.CompilerParams(vmem_limit_bytes=48 << 20),
        name="suffix" if reverse else "prefix",
    )(own, through)


def mix_of(flags, qkv, decays, og, before, gain):
    blocks, micro, rows, width = qkv.shape
    dk, dv = decays.shape[-1], og.shape[-1]
    slices, _, part, _ = before.shape
    return pl.pallas_call(
        mix_kernel,
        out_shape=(
            jax.ShapeDtypeStruct((blocks, micro, rows, dv), F32),
            jax.ShapeDtypeStruct((blocks, micro, rows, dv), BF16),
            jax.ShapeDtypeStruct((blocks, micro, dv, dk), F32),
        ),
        grid_spec=pltpu.PrefetchScalarGridSpec(
            num_scalar_prefetch=1,
            grid=(micro, blocks),
            in_specs=[
                per_block(rows, width),
                per_block(rows, dk),
                per_block(rows, dv),
                per_batch(slices, part, dk),
                pl.BlockSpec((1, dv), lambda m, b, *_: (0, 0)),
            ],
            out_specs=(per_block(rows, dv), per_block(rows, dv), per_block(dv, dk)),
            scratch_shapes=[pltpu.VMEM((dv, dk), F32)],
        ),
        compiler_params=params(),
        name="mix",
    )(flags, qkv, decays, og, before, gain)


def gate_back_of(flags, g_gated, og, o, qkv, decays, gain, slices):
    blocks, micro, rows, width = qkv.shape
    dk, dv = decays.shape[-1], og.shape[-1]
    part = dv // slices
    return pl.pallas_call(
        gate_back_kernel,
        out_shape=(
            jax.ShapeDtypeStruct((blocks, micro, rows, dv), BF16),
            jax.ShapeDtypeStruct((blocks, micro, rows, dv), F32),
            jax.ShapeDtypeStruct((slices, micro, part, dk), BF16),
            jax.ShapeDtypeStruct((8, dv), F32),
        ),
        grid_spec=pltpu.PrefetchScalarGridSpec(
            num_scalar_prefetch=1,
            grid=(micro, blocks),
            in_specs=[
                per_block(rows, dv),
                per_block(rows, dv),
                per_block(rows, dv),
                per_block(rows, width),
                per_block(rows, dk),
                pl.BlockSpec((1, dv), lambda m, b, *_: (0, 0)),
            ],
            out_specs=(
                per_block(rows, dv),
                per_block(rows, dv),
                per_batch(slices, part, dk),
                pl.BlockSpec((8, dv), lambda m, b, *_: (0, 0)),
            ),
            scratch_shapes=[pltpu.VMEM((dv, dk), F32), pltpu.VMEM((8, dk), F32)],
        ),
        compiler_params=params(),
        name="gate_back",
    )(flags, g_gated, og, o, qkv, decays, gain)


def mix_back_of(flags, qkv, decays, g_o, g_og, kept, after, logits):
    blocks, micro, rows, width = qkv.shape
    dk, dv = decays.shape[-1], g_o.shape[-1]
    slices, _, part, _ = after.shape
    back = functools.partial(backwards, count=blocks)
    return pl.pallas_call(
        mix_back_kernel,
        out_shape=(
            jax.ShapeDtypeStruct((blocks, micro, rows, width + dv), BF16),
            jax.ShapeDtypeStruct((blocks, micro, rows, dk), F32),
        ),
        grid_spec=pltpu.PrefetchScalarGridSpec(
            num_scalar_prefetch=1,
            grid=(micro, blocks),
            in_specs=[
                back(rows, width),
                back(rows, dk),
                back(rows, dv),
                back(rows, dv),
                back(dv, dk),
                per_batch(slices, part, dk),
                back(rows, dk),
            ],
            out_specs=(back(rows, width + dv), back(rows, dk)),
            scratch_shapes=[pltpu.VMEM((dv, dk), F32)],
        ),
        compiler_params=params(),
        name="mix_back",
    )(flags, qkv, decays, g_o, g_og, kept, after, logits)


def exchange(x, axis):
    return lax.all_to_all(x, axis, split_axis=0, concat_axis=0, tiled=True)


def gather_rows(x, axis):
    return exchange(jnp.broadcast_to(x[None], (lax.axis_size(axis),) + x.shape), axis)


def gather_weight(w):
    return lax.all_gather(w, "seq", axis=0, tiled=True)


def scatter_grad(g):
    return lax.psum_scatter(g.astype(BF16), "seq", scatter_dimension=0, tiled=True)


def dot(a, b, contract, precision=None):
    return lax.dot_general(
        a, b, (((contract[0],), (contract[1],)), ((), ())),
        precision=precision, preferred_element_type=F32,
    )


def rms(x, epsilon):
    return lax.rsqrt(jnp.mean(x * x, axis=-1, keepdims=True) + epsilon)


def norm_back(grad, gain, normed, inv):
    scaled = grad * gain
    inner = jnp.mean(scaled * normed, axis=-1, keepdims=True)
    return inv * (scaled - normed * inner), jnp.sum(grad * normed, axis=0)


def total_of(parts, seq, head):
    flat = jnp.concatenate([p.reshape(-1) for p in parts])
    unit = seq * head * 1024
    length = -(-flat.shape[0] // unit) * unit
    flat = jnp.pad(flat, (0, length - flat.shape[0]))
    piece = exchange(flat.reshape(seq, -1, 128), "seq").sum(0)
    piece = exchange(piece.reshape(head, -1, 128), "head").sum(0)
    piece = lax.all_gather(piece, "head", axis=0, tiled=True)
    whole = lax.all_gather(piece, "seq", axis=0, tiled=True).reshape(-1)
    result, at = [], 0
    for p in parts:
        result.append(whole[at : at + p.size].reshape(p.shape))
        at += p.size
    return result


def on_device(
    tokens, starts, cotangent, mix_in, mix_out, gate_up, down_proj,
    norm_gain, ffn_gain, head_gain, rank_down, rank_up, gate_bias,
):
    micro, rows, width = tokens.shape
    heads, seq = lax.axis_size("head"), lax.axis_size("seq")
    head = lax.axis_index("head")
    keys, dv = rank_up.shape[1], head_gain.shape[0]
    dk, vals = keys // heads, dv * heads
    hidden_units = down_proj.shape[1]
    group = heads * micro * rows
    proj_width = 2 * dk + 2 * dv

    def own_columns(w, start, size):
        return lax.dynamic_slice_in_dim(w, start + head * size, size, 1)

    w_in = gather_weight(
        jnp.concatenate(
            [
                own_columns(mix_in, 0, dk),
                own_columns(mix_in, keys, dk),
                own_columns(mix_in, 2 * keys, dv),
                own_columns(mix_in, 2 * keys + vals, dv),
            ],
            axis=1,
        )
    )
    w_out = gather_weight(mix_out)
    w_gu = gather_weight(gate_up.reshape(gate_up.shape[0], 2 * hidden_units))
    w_down = gather_weight(down_proj)
    up_own = own_columns(rank_up, 0, dk)
    bias_own = lax.dynamic_slice_in_dim(gate_bias, head * dk, dk, 0)

    all_tokens = gather_rows(tokens, "head").reshape(group, width)
    all_cot = gather_rows(cotangent, "head").reshape(group, width)

    source_all = all_tokens.astype(F32)
    xn = (source_all * rms(source_all, 1e-6) * norm_gain).astype(BF16)
    qkv = dot(xn, w_in[:, : 2 * dk + dv], (1, 0)).astype(BF16)
    og = dot(xn, w_in[:, 2 * dk + dv :], (1, 0))
    ranked = dot(xn, rank_down, (1, 0))
    logits = dot(ranked, up_own, (1, 0), HIGHEST) + bias_own
    decays = (jax.nn.log_sigmoid(logits) / GATE_NORM).astype(BF16)

    def blocks(x):
        return x.reshape(heads, micro, rows, x.shape[-1])

    qkv_b, og_b, decays_b = blocks(qkv), blocks(og), blocks(decays)
    gain_row = head_gain.reshape(1, dv)
    part = dv // seq
    own_states = exchange(states_of(starts, qkv_b, decays_b, dv, seq, 16), "seq")
    through = own_states[:, :, part:, :]
    before = exchange(prefix_of(own_states, through, part, False), "seq")
    o_b, gated_b, kept = mix_of(starts, qkv_b, decays_b, og_b, before, gain_row)

    gated = exchange(gated_b, "head")
    gated = gated.transpose(1, 2, 0, 3).reshape(micro * rows, vals)
    source = tokens.astype(F32).reshape(micro * rows, width)
    hidden = source + dot(gated, w_out, (1, 1))
    inv_ffn = rms(hidden, 1e-6)
    plain_ffn = hidden * inv_ffn
    h2 = (plain_ffn * ffn_gain).astype(BF16)

    all_h2 = gather_rows(h2, "head").reshape(group, width)
    gu = dot(all_h2, w_gu, (1, 0))
    gate_lin, up_lin = gu[:, :hidden_units], gu[:, hidden_units:]
    sig = jax.nn.sigmoid(gate_lin)
    act = gate_lin * sig
    product = (act * up_lin).astype(BF16)
    g_product = dot(all_cot, w_down, (1, 0))
    g_gate = (g_product * up_lin * sig * (1.0 + gate_lin * (1.0 - sig))).astype(BF16)
    g_up = (g_product * act).astype(BF16)
    g_gu = jnp.concatenate([g_gate, g_up], axis=1)
    g_h2_part = dot(g_gu, w_gu, (1, 1)).astype(BF16).reshape(heads, micro * rows, width)
    g_h2 = exchange(g_h2_part, "head").astype(F32).sum(0)
    ffn_part = dot(product, w_down, (1, 1)).astype(BF16).reshape(heads, micro * rows, width)
    ffn_out = exchange(ffn_part, "head").astype(F32).sum(0)
    output = (hidden + ffn_out).astype(BF16)
    grad_gu = scatter_grad(dot(all_h2, g_gu, (0, 0))).astype(F32)
    grad_down = scatter_grad(dot(all_cot, product, (0, 0))).astype(F32)

    back_ffn, g_ffn_gain = norm_back(g_h2, ffn_gain, plain_ffn, inv_ffn)
    g_hidden = cotangent.astype(F32).reshape(micro * rows, width) + back_ffn
    g_mixed = g_hidden.astype(BF16)
    g_gated = dot(g_mixed, w_out, (1, 0)).astype(BF16)
    g_gated = g_gated.reshape(micro, rows, heads, dv).transpose(2, 0, 1, 3)
    g_gated_b = exchange(g_gated, "head")
    g_og_b, g_o_b, pulled, g_head_gain = gate_back_of(
        starts, g_gated_b, og_b, o_b, qkv_b, decays_b, gain_row, seq
    )
    own_pulled = exchange(pulled, "seq")
    after = exchange(prefix_of(own_pulled, through, part, True), "seq")
    g_proj_b, g_logits_b = mix_back_of(
        starts, qkv_b, decays_b, g_o_b, g_og_b, kept, after, blocks(logits)
    )
    g_proj, g_logits = g_proj_b.reshape(group, proj_width), g_logits_b.reshape(group, dk)
    g_ranked = dot(g_logits, up_own, (1, 1), HIGHEST)
    g_xn_part = dot(g_proj, w_in, (1, 1)) + dot(
        g_ranked, rank_down.astype(F32), (1, 1), HIGHEST
    )
    g_xn_part = g_xn_part.astype(BF16).reshape(heads, micro * rows, width)
    g_xn = exchange(g_xn_part, "head").astype(F32).sum(0)
    inv_in = rms(source, 1e-6)
    back_in, g_norm_gain = norm_back(g_xn, norm_gain, source * inv_in, inv_in)
    input_grad = g_hidden + back_in

    slab = width // (seq * heads)
    grad_out = scatter_grad(dot(g_mixed, gated, (0, 0)))
    grad_out = exchange(grad_out.reshape(heads, slab, vals), "head").astype(F32).sum(0)
    grad_in = scatter_grad(dot(xn, g_proj, (0, 0)))
    grad_in = exchange(grad_in.reshape(heads, slab, proj_width), "head").astype(F32)
    cuts = ((0, dk), (dk, 2 * dk), (2 * dk, 2 * dk + dv), (2 * dk + dv, proj_width))
    grad_in = jnp.concatenate(
        [grad_in[:, :, a:b].transpose(1, 0, 2).reshape(slab, -1) for a, b in cuts], axis=1
    )
    g_rank_down = dot(xn.astype(F32), g_ranked, (0, 0), HIGHEST)
    g_rank_up = dot(ranked, g_logits, (0, 0), HIGHEST)
    g_rank_up = lax.dynamic_update_slice_in_dim(
        jnp.zeros(rank_up.shape, F32), g_rank_up, head * dk, 1
    )
    g_bias = lax.dynamic_update_slice_in_dim(
        jnp.zeros(gate_bias.shape, F32), g_logits.sum(0), head * dk, 0
    )
    small = total_of(
        [g_norm_gain, g_ffn_gain, g_head_gain[0], g_rank_down, g_rank_up, g_bias], seq, heads
    )
    return (
        output.reshape(tokens.shape),
        input_grad.reshape(tokens.shape),
        grad_in,
        grad_out,
        grad_gu.reshape(grad_gu.shape[0], 2, hidden_units),
        grad_down,
        *small,
    )


def solution(mesh):
    rows = P(None, ("seq", "head"), None)
    return jax.shard_map(
        on_device,
        mesh=mesh,
        in_specs=(
            rows, P(None, "seq"), rows, P("seq", None), P("seq", None),
            P("seq", None, "head"), P("seq", "head"), P(), P(), P(), P(), P(), P(),
        ),
        out_specs=(
            rows, rows, P(("seq", "head"), None), P(("seq", "head"), None),
            P("seq", None, "head"), P("seq", "head"), P(), P(), P(), P(), P(), P(),
        ),
        check_vma=False,
    )
```

time: 3070 us -> 965 us (0.31)
  waiting for transfers between devices: 2010 us -> 433 us
  matrix products: 388 us -> 141 us
  local copies, waits for them, and re-layouts: 213 us -> 36.4 us
  other arithmetic: 166 us -> 22.5 us
  blocking collectives: 106 us -> 195 us
  starting transfers between devices: 123 us -> 42.7 us
  Pallas kernels: 0 us -> 69.3 us
    reduce_scatter x8 -> x4, waiting for transfers between devices: 1390 us -> 95.5 us  [scatter_grad(): lax.psum_scatter(g.astype(BF16), 'seq', scatter_dimension=0, tiled=True)]
    all_gather x16 -> x4, waiting for transfers between devices: 382 us -> 0.03 us  [gather_weight(): return lax.all_gather(w, 'seq', axis=0, tiled=True)]
    dot_general x220 -> x19, matrix products: 388 us -> 141 us  [dot(): lax.dot_general(a, b, (((contract[0],), (contract[1],)), ((), ())), preci...]
    all_to_all x29 -> x9, waiting for transfers between devices: 115 us -> 337 us  [exchange(): return lax.all_to_all(x, axis, split_axis=0, concat_axis=0, tiled=True)]
    all_to_all x1 -> x7, blocking collectives: 10.6 us -> 168 us  [exchange(): return lax.all_to_all(x, axis, split_axis=0, concat_axis=0, tiled=True)]
    psum x1 -> x0, waiting for transfers between devices: 126 us -> none  [on_device(): lax.psum((norm_gain_grad, ffn_gain_grad, head_gain_grad, rank_down_grad,...]
    all_to_all x29 -> x9, starting transfers between devices: 121 us -> 41.1 us  [exchange(): return lax.all_to_all(x, axis, split_axis=0, concat_axis=0, tiled=True)]
    pallas_call x0 -> x6, Pallas kernels: none -> 69.3 us  [the longest x1 28.3 us: mix_back_of(): pl.pallas_call(mix_back_kernel, out_shape=(jax.ShapeDtypeStruct((blocks,...]
  transfers between devices with their start and end apart: 54 -> 17, of which waited for: 37 -> 9; matrix products, arithmetic and copies ran while one was open for 23% -> 14% of each run, Pallas kernels for 0% -> 3%
where the time goes in v1:
time: 965 us; the launch traced here: 955 us
  waiting for transfers between devices  433 us (45%)
  blocking collectives  195 us (20%)
  matrix products  141 us (15%)
  Pallas kernels  69.3 us (7%)
  starting transfers between devices  42.7 us (4%)
  local copies, waits for them, and re-layouts  36.4 us (4%)
  other arithmetic  22.5 us (2%)
  between operations  14.8 us (2%)
    all_to_all x9, waiting for transfers between devices, exchange(): return lax.all_to_all(x, axis, split_axis=0, concat_axis=0, tiled=True)  337 us
    all_to_all x7, blocking collectives, exchange(): return lax.all_to_all(x, axis, split_axis=0, concat_axis=0, tiled=True)  168 us
    dot_general x19, matrix products, dot(): lax.dot_general(a, b, (((contract[0],), (contract[1],)), ((), ())), preci...  141 us
    reduce_scatter x4, waiting for transfers between devices, scatter_grad(): lax.psum_scatter(g.astype(BF16), 'seq', scatter_dimension=0, tiled=True)  95.5 us
    all_to_all x9, starting transfers between devices, exchange(): return lax.all_to_all(x, axis, split_axis=0, concat_axis=0, tiled=True)  41.1 us
    pallas_call x1, Pallas kernels, mix_back_of(): pl.pallas_call(mix_back_kernel, out_shape=(jax.ShapeDtypeStruct((blocks,...  28.3 us
  transfers between devices with their start and end apart: 17, of which 9 were waited for; matrix products, arithmetic and copies ran while one was open for 14% of the time, Pallas kernels for 3%

profile of v1, /device:TPU:0, one launch (start us, length us, event | category | flops | bytes accessed | tf_op | source)
XLA Modules:
  0.0 955.0 jit_solution(8927174594792130514)
XLA Ops:
  21.7 69.9 %all-to-all-done = bf16[4,3,64,2048]{3,2,1,0:T(8,128)(2,1)S(1)} async-done(((bf16[4,3,64,2048]{3,2,1,0:T(8,128)(2,1)}), bf16[4,3,64,2048]{3,2,1,0:T(8,128)(2,1)S(1)}, u32[]{:S(2)}, u32[]{:S(2)}) %all-to-all-start) | async-done | bytes 3145760 | tf_op jit(solution)/shard_map/all_to_all | solution.py:351
  104.9 9.7 %states.1 = bf16[8,3,80,256]{3,2,1,0:T(8,128)(2,1)S(1)} custom-call(s32[3,4]{1,0:T(4,128)S(1)} %copy-done.9, bf16[4,3,64,1024]{3,2,1,0:T(8,128)(2,1)S(1)} %bitcast.113, bf16[4,3,64,256]{3,2,1,0:T(8,128)(2,1)S(1)} %bitcast.119), custom_call_target="tpu_custom_call" | custom-call | tf_op jit(solution)/shard_map/states/pallas_call | solution.py:228
  114.5 21.7 %all_to_all.80.own = bf16[8,3,80,256]{3,2,1,0:T(8,128)(2,1)S(1)} all-to-all(bf16[8,3,80,256]{3,2,1,0:T(8,128)(2,1)S(1)} %states.1), channel_id=1, replica_groups=mesh['seq'=8,'head'=4] {'seq'}, dimensions={0} | all-to-all | bytes 1966080 | tf_op jit(solution)/shard_map/all_to_all | solution.py:351
  146.5 10.1 %all-to-all-done.2.before = bf16[8,3,64,256]{3,2,1,0:T(8,128)(2,1)S(1)} async-done(((bf16[8,3,64,256]{3,2,1,0:T(8,128)(2,1)}), bf16[8,3,64,256]{3,2,1,0:T(8,128)(2,1)S(1)}, u32[]{:S(2)}, u32[]{:S(2)}) %all-to-all-start.2) | async-done | bytes 786464 | tf_op jit(solution)/shard_map/all_to_all | solution.py:351
  156.6 18.1 %mix.1 = (f32[4,3,64,512]{3,2,1,0:T(8,128)S(1)}, bf16[4,3,64,512]{3,2,1,0:T(8,128)(2,1)S(1)}, f32[4,3,512,256]{3,2,1,0:T(8,128)}) custom-call(s32[3,4]{1,0:T(4,128)S(1)} %copy-done.9, bf16[4,3,64,1024]{3,2,1,0:T(8,128)(2,1)S(1)} %bitcast.114, bf16[4,3,64,256]{3,2,1,0:T(8,128)(2,1)S(1)} %bitcast.120, f32[4,3,64,512]{3,2,1,0:T(8,128)} %fusion.6.og, ...), custom_call_target="tpu_custom_call" | custom-call | tf_op jit(solution)/shard_map/mix/pallas_call | solution.py:258
  181.0 17.1 %all-to-all-done.3 = bf16[4,3,64,512]{3,2,1,0:T(8,128)(2,1)S(1)} async-done(((bf16[4,3,64,512]{3,2,1,0:T(8,128)(2,1)}), bf16[4,3,64,512]{3,2,1,0:T(8,128)(2,1)S(1)}, u32[]{:S(2)}, u32[]{:S(2)}) %all-to-all-start.3) | async-done | bytes 786464 | tf_op jit(solution)/shard_map/all_to_all | solution.py:351
  199.8 6.9 multiply_reduce_fusion.6
  207.3 72.7 %all_to_all.81 = bf16[4,192,2048]{2,1,0:T(8,128)(2,1)} all-to-all(bf16[4,192,2048]{2,1,0:T(8,128)(2,1)S(1)} %broadcast_in_dim.11), channel_id=1, replica_groups=mesh['seq'=8,'head'=4] {'head'}, dimensions={0} | all-to-all | bytes 6291456 | tf_op jit(solution)/shard_map/all_to_all | solution.py:351
  286.8 15.7 %fusion.27 = f32[768,2816]{1,0:T(8,128)} fusion(bf16[768,2048]{1,0:T(8,128)(2,1)} %bitcast.132, bf16[2048,2816]{1,0:T(8,128)(2,1)} %all-gather.9.cloned.1.call-done), kind=kOutput, calls=%fused_computation.86 | convolution fusion | flops 8858370048 | bytes 23330816 | tf_op jit(solution)/shard_map/dot_general | solution.py:367
  302.5 53.8 %all-to-all-done.6 = bf16[4,3,64,2048]{3,2,1,0:T(8,128)(2,1)} async-done(((bf16[4,3,64,2048]{3,2,1,0:T(8,128)(2,1)}), bf16[4,3,64,2048]{3,2,1,0:T(8,128)(2,1)}, u32[]{:S(2)}, u32[]{:S(2)}) %all-to-all-start.6) | async-done | bytes 3145760 | tf_op jit(solution)/shard_map/all_to_all | solution.py:351
  356.4 13.1 %multiply_convert_fusion.2 = (bf16[768,1408]{1,0:T(8,128)(2,1)}, bf16[768,1408]{1,0:T(8,128)(2,1)}, bf16[768,1408]{1,0:T(8,128)(2,1)}) fusion(f32[768,2816]{1,0:T(8,128)} %fusion.27, bf16[768,2048]{1,0:T(8,128)(2,1)} %bitcast.12, bf16[2048,1408]{1,0:T(8,128)(2,1)} %all-gather.11.cloned.1.call-done), kind=kOutput, calls=%fused_computation.16 | convolution fusion | flops 4445405184 | bytes 24051712 | tf_op jit(solution)/shard_map/dot_general | solution.py:367
  369.5 12.2 %convolution_convert_fusion.3 = bf16[768,2048]{1,0:T(8,128)(2,1)} fusion(bf16[2048,2816]{1,0:T(8,128)(2,1)S(1)} %copy-done.28, bf16[768,1408]{1,0:T(8,128)(2,1)} %get-tuple-element.71, bf16[768,1408]{1,0:T(8,128)(2,1)} %get-tuple-element.70), kind=kOutput, calls=%fused_computation.22 | convolution fusion | flops 8868593664 | bytes 19005440 | tf_op jit(solution)/shard_map/dot_general | solution.py:367
  386.3 9.0 convolution_convert_fusion.4
  395.3 61.2 %all-to-all-done.7 = bf16[4,192,2048]{2,1,0:T(8,128)(2,1)} async-done(((bf16[4,192,2048]{2,1,0:T(8,128)(2,1)}), bf16[4,192,2048]{2,1,0:T(8,128)(2,1)}, u32[]{:S(2)}, u32[]{:S(2)}) %all-to-all-start.7) | async-done | bytes 3145760 | tf_op jit(solution)/shard_map/all_to_all | solution.py:351
  465.9 65.6 %all-to-all-done.5 = bf16[4,192,2048]{2,1,0:T(8,128)(2,1)} async-done(((bf16[4,192,2048]{2,1,0:T(8,128)(2,1)}), bf16[4,192,2048]{2,1,0:T(8,128)(2,1)}, u32[]{:S(2)}, u32[]{:S(2)}) %all-to-all-start.5) | async-done | bytes 3145760 | tf_op jit(solution)/shard_map/all_to_all | solution.py:351
  545.4 22.1 %all_to_all.82.g_gated = bf16[4,3,64,512]{3,2,1,0:T(8,128)(2,1)S(1)} all-to-all(bf16[4,3,64,512]{3,2,1,0:T(8,128)(2,1)S(1)} %bitcast.138), channel_id=1, replica_groups=mesh['seq'=8,'head'=4] {'head'}, dimensions={0} | all-to-all | bytes 1572864 | tf_op jit(solution)/shard_map/all_to_all | solution.py:351
  567.5 12.6 %gate_back.1 = (bf16[4,3,64,512]{3,2,1,0:T(8,128)(2,1)S(1)}, f32[4,3,64,512]{3,2,1,0:T(8,128)S(1)}, bf16[8,3,64,256]{3,2,1,0:T(8,128)(2,1)S(1)}, f32[8,512]{1,0:T(8,128)S(1)}) custom-call(s32[3,4]{1,0:T(4,128)S(1)} %copy-done.9, bf16[4,3,64,512]{3,2,1,0:T(8,128)(2,1)S(1)} %all_to_all.82.g_gated, f32[4,3,64,512]{3,2,1,0:T(8,128)S(1)} %copy-done.3, ...), custom_call_target="tpu_custom_call" | custom-call | tf_op jit(solution)/shard_map/gate_back/pallas_call | solution.py:287
  581.3 18.6 %all_to_all.83.own = bf16[8,3,64,256]{3,2,1,0:T(8,128)(2,1)S(1)} all-to-all(bf16[8,3,64,256]{3,2,1,0:T(8,128)(2,1)S(1)} %get-tuple-element.26), channel_id=1, replica_groups=mesh['seq'=8,'head'=4] {'seq'}, dimensions={0} | all-to-all | bytes 1572864 | tf_op jit(solution)/shard_map/all_to_all | solution.py:351
  600.1 15.0 %all_to_all.84.after = bf16[8,3,64,256]{3,2,1,0:T(8,128)(2,1)S(1)} all-to-all(bf16[8,3,64,256]{3,2,1,0:T(8,128)(2,1)S(1)} %suffix.1), channel_id=1, replica_groups=mesh['seq'=8,'head'=4] {'seq'}, dimensions={0} | all-to-all | bytes 1572864 | tf_op jit(solution)/shard_map/all_to_all | solution.py:351
  615.1 28.3 %mix_back.1 = (bf16[4,3,64,1536]{3,2,1,0:T(8,128)(2,1)}, f32[4,3,64,256]{3,2,1,0:T(8,128)S(1)}) custom-call(s32[3,4]{1,0:T(4,128)S(1)} %copy-done.9, bf16[4,3,64,1024]{3,2,1,0:T(8,128)(2,1)S(1)} %bitcast.116, bf16[4,3,64,256]{3,2,1,0:T(8,128)(2,1)S(1)} %bitcast.122, f32[4,3,64,512]{3,2,1,0:T(8,128)} %copy-done.5, ...), custom_call_target="tpu_custom_call" | custom-call | tf_op jit(solution)/shard_map/mix_back/pallas_call | solution.py:324
  643.5 9.1 bitcast_convert_fusion
  652.8 10.2 %fusion = bf16[2048,1408]{0,1:T(8,128)(2,1)} fusion(bf16[768,1408]{1,0:T(8,128)(2,1)} %get-tuple-element.72, bf16[768,2048]{1,0:T(8,128)(2,1)} %bitcast.12), kind=kOutput, calls=%fused_computation.4 | convolution fusion | flops 4432068608 | bytes 11075584 | tf_op jit(solution)/shard_map/dot_general | solution.py:367
  664.6 6.8 convolution_convert_fusion.2
  671.9 15.6 %convolution_convert_fusion = bf16[2048,2816]{1,0:T(8,128)(2,1)} fusion(bf16[768,2048]{1,0:T(8,128)(2,1)} %bitcast.133, bf16[768,1408]{1,0:T(8,128)(2,1)} %get-tuple-element.71, bf16[768,1408]{1,0:T(8,128)(2,1)} %get-tuple-element.70), kind=kOutput, calls=%fused_computation.1 | convolution fusion | flops 8872787968 | bytes 19005440 | tf_op jit(solution)/shard_map/dot_general | solution.py:367
  689.0 8.1 fusion.28
  716.4 59.3 %all-to-all-done.11 = bf16[4,192,2048]{2,1,0:T(8,128)(2,1)} async-done(((bf16[4,192,2048]{2,1,0:T(8,128)(2,1)}), bf16[4,192,2048]{2,1,0:T(8,128)(2,1)}, u32[]{:S(2)}, u32[]{:S(2)}) %all-to-all-start.11) | async-done | bytes 3145760 | tf_op jit(solution)/shard_map/all_to_all | solution.py:351
  781.3 9.5 all_to_all.85
  790.8 8.2 all_to_all.86
  808.9 18.1 %all_gather.22 = f32[64,128]{1,0:T(8,128)S(1)} all-gather(f32[16,128]{1,0:T(8,128)S(1)} %reduce_sum.142), channel_id=1, replica_groups=mesh['seq'=8,'head'=4] {'head'}, dimensions={0}, use_global_device_ids=true | all-gather | bytes 40960 | tf_op jit(solution)/shard_map/all_gather | solution.py:390
  827.0 9.1 all_gather.23
  838.6 10.5 %reduce-scatter.7.cloned.1.call-done = bf16[256,2048]{1,0:T(8,128)(2,1)} async-done(((bf16[2048,2048]{1,0:T(8,128)(2,1)}), bf16[256,2048]{1,0:T(8,128)(2,1)}) %reduce-scatter.7.cloned.1.call-update) | async-done | bytes 1048592 | tf_op jit(solution)/shard_map/reduce_scatter | solution.py:363
  855.0 84.9 %reduce-scatter.9.cloned.1.call-done = bf16[256,2816]{1,0:T(8,128)(2,1)} async-done(((bf16[2048,2816]{1,0:T(8,128)(2,1)}), bf16[256,2816]{1,0:T(8,128)(2,1)}) %reduce-scatter.9.cloned.1.call-update) | async-done | bytes 1441808 | tf_op jit(solution)/shard_map/reduce_scatter | solution.py:363
  (169 shorter events, 137.4 us)
Async XLA Ops:
  7.2 86.0 %copy-start = (bf16[2048,16]{0,1:T(8,128)(2,1)S(1)}, bf16[2048,16]{0,1:T(8,128)(2,1)}, u32[]{:S(2)}) copy-start(bf16[2048,16]{0,1:T(8,128)(2,1)} %param.23) | copy-start | bytes 196612
  7.2 91.0 %all-gather.5.cloned.1.call-start = ((), (), s32[]{:S(2)}) async-start(), calls=%async_computation.20 | async-start | bytes 7077888 | tf_op jit(solution)/shard_map/all_gather | solution.py:359
  10.4 189.4 %all-gather.7.cloned.1.call-start = ((), (), s32[]{:S(2)}) async-start(), calls=%async_computation.21 | async-start | bytes 9437184 | tf_op jit(solution)/shard_map/all_gather | solution.py:359
  11.1 275.6 %all-gather.9.cloned.1.call-start = ((), (), s32[]{:S(2)}) async-start(), calls=%async_computation.22 | async-start | bytes 12976128 | tf_op jit(solution)/shard_map/all_gather | solution.py:359
  14.6 77.0 %all-to-all-start = ((bf16[4,3,64,2048]{3,2,1,0:T(8,128)(2,1)}), bf16[4,3,64,2048]{3,2,1,0:T(8,128)(2,1)S(1)}, u32[]{:S(2)}, u32[]{:S(2)}) async-start(bf16[4,3,64,2048]{3,2,1,0:T(8,128)(2,1)} %broadcast_in_dim.10), calls=%async_computation | async-start | bytes 6291456 | tf_op jit(solution)/shard_map/all_to_all | solution.py:351
  20.9 71.5 %copy-start.27 = (f32[2048]{0:T(1024)S(1)}, f32[2048]{0:T(1024)}, u32[]{:S(2)}) copy-start(f32[2048]{0:T(1024)} %param.20) | copy-start | bytes 24580
  98.2 6.6 copy-start.9
  104.9 51.7 %copy-start.1 = (bf16[768,1024]{1,0:T(8,128)(2,1)}, bf16[768,1024]{1,0:T(8,128)(2,1)S(1)}, u32[]{:S(2)}) copy-start(bf16[768,1024]{1,0:T(8,128)(2,1)S(1)} %fusion.7) | copy-start | bytes 4718596
  137.5 19.1 %all-to-all-start.2 = ((bf16[8,3,64,256]{3,2,1,0:T(8,128)(2,1)}), bf16[8,3,64,256]{3,2,1,0:T(8,128)(2,1)S(1)}, u32[]{:S(2)}, u32[]{:S(2)}) async-start(bf16[8,3,64,256]{3,2,1,0:T(8,128)(2,1)} %copy-done.4), calls=%async_computation.2 | async-start | bytes 1572864 | tf_op jit(solution)/shard_map/all_to_all | solution.py:351
  141.0 15.6 %copy-start.10 = (f32[512]{0:T(512)S(1)}, f32[512]{0:T(512)}, u32[]{:S(2)}) copy-start(f32[512]{0:T(512)} %param.22) | copy-start | bytes 6148
  176.8 23.0 %copy-start.20 = (bf16[3,64,2048]{2,1,0:T(8,128)(2,1)S(1)}, bf16[3,64,2048]{2,1,0:T(8,128)(2,1)}, u32[]{:S(2)}) copy-start(bf16[3,64,2048]{2,1,0:T(8,128)(2,1)} %param.13) | copy-start | bytes 2359300
  176.8 21.3 %all-to-all-start.3 = ((bf16[4,3,64,512]{3,2,1,0:T(8,128)(2,1)}), bf16[4,3,64,512]{3,2,1,0:T(8,128)(2,1)S(1)}, u32[]{:S(2)}, u32[]{:S(2)}) async-start(bf16[4,3,64,512]{3,2,1,0:T(8,128)(2,1)} %copy-done.8), calls=%async_computation.3 | async-start | bytes 1572864 | tf_op jit(solution)/shard_map/all_to_all | solution.py:351
  180.4 176.0 %all-gather.11.cloned.1.call-start = ((), (), s32[]{:S(2)}) async-start(), calls=%async_computation.23 | async-start | bytes 6488064 | tf_op jit(solution)/shard_map/all_gather | solution.py:359
  199.8 6.9 copy-start.26
  207.3 72.7 %copy-start.22 = (bf16[3,64,2048]{2,1,0:T(8,128)(2,1)S(1)}, bf16[3,64,2048]{2,1,0:T(8,128)(2,1)}, u32[]{:S(2)}) copy-start(bf16[3,64,2048]{2,1,0:T(8,128)(2,1)} %param.15) | copy-start | bytes 2359300
  282.1 74.3 %all-to-all-start.6 = ((bf16[4,3,64,2048]{3,2,1,0:T(8,128)(2,1)}), bf16[4,3,64,2048]{3,2,1,0:T(8,128)(2,1)}, u32[]{:S(2)}, u32[]{:S(2)}) async-start(bf16[4,3,64,2048]{3,2,1,0:T(8,128)(2,1)} %broadcast_in_dim.12), calls=%async_computation.6 | async-start | bytes 6291456 | tf_op jit(solution)/shard_map/all_to_all | solution.py:351
  356.3 13.1 %copy-start.28 = (bf16[2048,2816]{1,0:T(8,128)(2,1)S(1)}, bf16[2048,2816]{1,0:T(8,128)(2,1)}, u32[]{:S(2)}) copy-start(bf16[2048,2816]{1,0:T(8,128)(2,1)} %all-gather.9.cloned.1.call-done) | copy-start | bytes 34603012
  381.7 74.9 %all-to-all-start.7 = ((bf16[4,192,2048]{2,1,0:T(8,128)(2,1)}), bf16[4,192,2048]{2,1,0:T(8,128)(2,1)}, u32[]{:S(2)}, u32[]{:S(2)}) async-start(bf16[4,192,2048]{2,1,0:T(8,128)(2,1)} %bitcast.135), calls=%async_computation.7 | async-start | bytes 6291456 | tf_op jit(solution)/shard_map/all_to_all | solution.py:351
  456.5 74.9 %all-to-all-start.5 = ((bf16[4,192,2048]{2,1,0:T(8,128)(2,1)}), bf16[4,192,2048]{2,1,0:T(8,128)(2,1)}, u32[]{:S(2)}, u32[]{:S(2)}) async-start(bf16[4,192,2048]{2,1,0:T(8,128)(2,1)} %bitcast.134), calls=%async_computation.5 | async-start | bytes 6291456 | tf_op jit(solution)/shard_map/all_to_all | solution.py:351
  461.2 337.8 %reduce-scatter.5.cloned.1.call-start = ((), (), s32[]{:S(2)}) async-start(), calls=%async_computation.24 | async-start | bytes 7077888 | tf_op jit(solution)/shard_map/reduce_scatter | solution.py:363
  542.9 24.6 %copy-start.3 = (f32[4,3,64,512]{3,2,1,0:T(8,128)S(1)}, f32[4,3,64,512]{3,2,1,0:T(8,128)}, u32[]{:S(2)}) copy-start(f32[4,3,64,512]{3,2,1,0:T(8,128)} %fusion.6.og) | copy-start | bytes 4718596
  581.3 33.8 %copy-start.2 = (bf16[768,1024]{1,0:T(8,128)(2,1)S(1)}, bf16[768,1024]{1,0:T(8,128)(2,1)}, u32[]{:S(2)}) copy-start(bf16[768,1024]{1,0:T(8,128)(2,1)} %copy-done.1) | copy-start | bytes 4718596
  581.3 33.8 %copy-start.7 = (f32[768,256]{1,0:T(8,128)S(1)}, f32[768,256]{1,0:T(8,128)}, u32[]{:S(2)}) copy-start(f32[768,256]{1,0:T(8,128)} %get-tuple-element.86) | copy-start | bytes 2359300
  615.1 28.3 %copy-start.13 = (bf16[4,3,64,2048]{3,2,1,0:T(8,128)(2,1)S(1)}, bf16[4,3,64,2048]{3,2,1,0:T(8,128)(2,1)}, u32[]{:S(2)}) copy-start(bf16[4,3,64,2048]{3,2,1,0:T(8,128)(2,1)} %copy-done.12) | copy-start | bytes 9437188
  652.6 150.7 %reduce-scatter.11.cloned.1.call-start = ((), (), s32[]{:S(2)}) async-start(), calls=%async_computation.27 | async-start | bytes 6488064 | tf_op jit(solution)/shard_map/reduce_scatter | solution.py:363
  663.0 186.2 %reduce-scatter.7.cloned.1.call-start = ((), (), s32[]{:S(2)}) async-start(), calls=%async_computation.25 | async-start | bytes 9437184 | tf_op jit(solution)/shard_map/reduce_scatter | solution.py:363
  671.4 268.5 %reduce-scatter.9.cloned.1.call-start = ((), (), s32[]{:S(2)}) async-start(), calls=%async_computation.26 | async-start | bytes 12976128 | tf_op jit(solution)/shard_map/reduce_scatter | solution.py:363
  701.5 74.1 %all-to-all-start.11 = ((bf16[4,192,2048]{2,1,0:T(8,128)(2,1)}), bf16[4,192,2048]{2,1,0:T(8,128)(2,1)}, u32[]{:S(2)}, u32[]{:S(2)}) async-start(bf16[4,192,2048]{2,1,0:T(8,128)(2,1)} %bitcast.127), calls=%async_computation.11 | async-start | bytes 6291456 | tf_op jit(solution)/shard_map/all_to_all | solution.py:351
  707.8 7.9 copy-start.25
  781.2 24.7 %copy-start.21 = (bf16[3,64,2048]{2,1,0:T(8,128)(2,1)S(1)}, bf16[3,64,2048]{2,1,0:T(8,128)(2,1)}, u32[]{:S(2)}) copy-start(bf16[3,64,2048]{2,1,0:T(8,128)(2,1)} %param.13) | copy-start | bytes 2359300
  799.0 50.2 %all-to-all-start.12 = ((bf16[4,64,1536]{2,1,0:T(8,128)(2,1)}), bf16[4,64,1536]{2,1,0:T(8,128)(2,1)}, u32[]{:S(2)}, u32[]{:S(2)}) async-start(bf16[4,64,1536]{2,1,0:T(8,128)(2,1)} %bitcast.148), calls=%async_computation.13 | async-start | bytes 1572864 | tf_op jit(solution)/shard_map/all_to_all | solution.py:351
  849.2 97.9 %all-to-all-start.13 = ((bf16[4,64,2048]{2,1,0:T(8,128)(2,1)}), bf16[4,64,2048]{2,1,0:T(8,128)(2,1)S(1)}, u32[]{:S(2)}, u32[]{:S(2)}) async-start(bf16[4,64,2048]{2,1,0:T(8,128)(2,1)} %bitcast.145), calls=%async_computation.15 | async-start | bytes 2097152 | tf_op jit(solution)/shard_map/all_to_all | solution.py:351
  (14 other events, 21.8 us)
Sparse Core Ops, SparseCore 0:
  10.5 48.2 all-gather.4
  60.7 54.3 all-gather.6
  117.6 76.9 all-gather.8
  196.3 43.3 all-gather.10
  652.7 58.9 reduce-scatter.4
  715.3 59.0 reduce-scatter.10
  777.9 71.2 reduce-scatter.6
  853.1 86.7 reduce-scatter.8

commit v2 on v1

--- a/solution.py
+++ b/solution.py
@@ -209,6 +209,10 @@
     )
 
 
+def cost(micros):
+    return pl.CostEstimate(flops=0, bytes_accessed=int(micros * 3.0e6), transcendentals=0)
+
+
 def per_block(rows, width):
     return pl.BlockSpec((1, 1, rows, width), lambda m, b, *_: (b, m, 0, 0))
 
@@ -236,6 +240,7 @@
             scratch_shapes=[pltpu.VMEM((dv, dk), F32), pltpu.VMEM((8, dk), F32)],
         ),
         compiler_params=params(),
+        cost_estimate=cost(10),
         name="states",
     )(flags, qkv, decays)
 
@@ -276,6 +281,7 @@
             scratch_shapes=[pltpu.VMEM((dv, dk), F32)],
         ),
         compiler_params=params(),
+        cost_estimate=cost(18),
         name="mix",
     )(flags, qkv, decays, og, before, gain)
 
@@ -312,6 +318,7 @@
             scratch_shapes=[pltpu.VMEM((dv, dk), F32), pltpu.VMEM((8, dk), F32)],
         ),
         compiler_params=params(),
+        cost_estimate=cost(12),
         name="gate_back",
     )(flags, g_gated, og, o, qkv, decays, gain)
 
@@ -343,8 +350,46 @@
             scratch_shapes=[pltpu.VMEM((dv, dk), F32)],
         ),
         compiler_params=params(),
+        cost_estimate=cost(28),
         name="mix_back",
     )(flags, qkv, decays, g_o, g_og, kept, after, logits)
+
+
+def weight_grad_kernel(left, right, *rest):
+    out, turned = rest[-2:]
+
+    @pl.when(pl.program_id(1) == 0)
+    def _():
+        turned[...] = left[...].T
+
+    out[...] = jnp.dot(turned[...], right[...], preferred_element_type=F32).astype(BF16)
+
+
+def weight_grad(left, right, into, columns, start, tile):
+    depth, rows = left.shape
+    high = min(rows, 512)
+    first = start // tile
+    given = () if into is None else (into,)
+    return pl.pallas_call(
+        weight_grad_kernel,
+        out_shape=jax.ShapeDtypeStruct((rows, columns), BF16),
+        grid=(rows // high, right.shape[1] // tile),
+        in_specs=[
+            pl.BlockSpec((depth, high), lambda i, j: (0, i)),
+            pl.BlockSpec((depth, tile), lambda i, j: (0, j)),
+        ]
+        + [pl.BlockSpec(memory_space=pl.ANY) for _ in given],
+        out_specs=pl.BlockSpec((high, tile), lambda i, j: (i, first + j)),
+        scratch_shapes=[pltpu.VMEM((high, depth), BF16)],
+        input_output_aliases={2: 0} if given else {},
+        compiler_params=params(),
+        cost_estimate=pl.CostEstimate(
+            flops=2 * depth * rows * right.shape[1],
+            bytes_accessed=2 * (depth * rows + (depth + rows) * right.shape[1]),
+            transcendentals=0,
+        ),
+        name="weight_grad",
+    )(left, right, *given)
 
 
 def exchange(x, axis):
@@ -412,25 +457,28 @@
     def own_columns(w, start, size):
         return lax.dynamic_slice_in_dim(w, start + head * size, size, 1)
 
-    w_in = gather_weight(
+    mixer = gather_weight(
         jnp.concatenate(
             [
                 own_columns(mix_in, 0, dk),
                 own_columns(mix_in, keys, dk),
                 own_columns(mix_in, 2 * keys, dv),
                 own_columns(mix_in, 2 * keys + vals, dv),
+                mix_out,
             ],
             axis=1,
         )
     )
-    w_out = gather_weight(mix_out)
-    w_gu = gather_weight(gate_up.reshape(gate_up.shape[0], 2 * hidden_units))
-    w_down = gather_weight(down_proj)
+    w_in, w_out = mixer[:, :proj_width], mixer[:, proj_width:]
+    ffn_weights = gather_weight(
+        jnp.concatenate([gate_up.reshape(gate_up.shape[0], 2 * hidden_units), down_proj], axis=1)
+    )
+    w_gu, w_down = ffn_weights[:, : 2 * hidden_units], ffn_weights[:, 2 * hidden_units :]
     up_own = own_columns(rank_up, 0, dk)
     bias_own = lax.dynamic_slice_in_dim(gate_bias, head * dk, dk, 0)
 
     all_tokens = gather_rows(tokens, "head").reshape(group, width)
-    all_cot = gather_rows(cotangent, "head").reshape(group, width)
+    all_cot = lax.all_gather(cotangent, "head").reshape(group, width)
 
     source_all = all_tokens.astype(F32)
     xn = (source_all * rms(source_all, 1e-6) * norm_gain).astype(BF16)
@@ -470,17 +518,22 @@
     g_up = (g_product * act).astype(BF16)
     g_gu = jnp.concatenate([g_gate, g_up], axis=1)
     g_h2_part = dot(g_gu, w_gu, (1, 1)).astype(BF16).reshape(heads, micro * rows, width)
-    g_h2 = exchange(g_h2_part, "head").astype(F32).sum(0)
+    g_h2 = exchange(g_h2_part, "head")
+    grad_ffn = weight_grad(all_h2, g_gu, None, 3 * hidden_units, 0, hidden_units)
+    grad_ffn = weight_grad(
+        all_cot, product, grad_ffn, 3 * hidden_units, 2 * hidden_units, hidden_units
+    )
     ffn_part = dot(product, w_down, (1, 1)).astype(BF16).reshape(heads, micro * rows, width)
-    ffn_out = exchange(ffn_part, "head").astype(F32).sum(0)
-    output = (hidden + ffn_out).astype(BF16)
-    grad_gu = scatter_grad(dot(all_h2, g_gu, (0, 0))).astype(F32)
-    grad_down = scatter_grad(dot(all_cot, product, (0, 0))).astype(F32)
-
+    g_h2, grad_ffn, ffn_part = lax.optimization_barrier((g_h2, grad_ffn, ffn_part))
+    ffn_out = exchange(ffn_part, "head")
+    grad_ffn = scatter_grad(grad_ffn)
+
+    g_h2 = g_h2.astype(F32).sum(0)
     back_ffn, g_ffn_gain = norm_back(g_h2, ffn_gain, plain_ffn, inv_ffn)
     g_hidden = cotangent.astype(F32).reshape(micro * rows, width) + back_ffn
     g_mixed = g_hidden.astype(BF16)
     g_gated = dot(g_mixed, w_out, (1, 0)).astype(BF16)
+    grad_mix = weight_grad(g_mixed, gated, None, proj_width + vals, proj_width, dv)
     g_gated = g_gated.reshape(micro, rows, heads, dv).transpose(2, 0, 1, 3)
     g_gated_b = exchange(g_gated, "head")
     g_og_b, g_o_b, pulled, g_head_gain = gate_back_of(
@@ -491,6 +544,7 @@
     g_proj_b, g_logits_b = mix_back_of(
         starts, qkv_b, decays_b, g_o_b, g_og_b, kept, after, blocks(logits)
     )
+    g_proj_b, g_logits_b, ffn_out = lax.optimization_barrier((g_proj_b, g_logits_b, ffn_out))
     g_proj, g_logits = g_proj_b.reshape(group, proj_width), g_logits_b.reshape(group, dk)
     g_ranked = dot(g_logits, up_own, (1, 1), HIGHEST)
     g_xn_part = dot(g_proj, w_in, (1, 1)) + dot(
@@ -498,15 +552,17 @@
     )
     g_xn_part = g_xn_part.astype(BF16).reshape(heads, micro * rows, width)
     g_xn = exchange(g_xn_part, "head").astype(F32).sum(0)
+    output = (hidden + ffn_out.astype(F32).sum(0)).astype(BF16)
     inv_in = rms(source, 1e-6)
     back_in, g_norm_gain = norm_back(g_xn, norm_gain, source * inv_in, inv_in)
     input_grad = g_hidden + back_in
 
     slab = width // (seq * heads)
-    grad_out = scatter_grad(dot(g_mixed, gated, (0, 0)))
-    grad_out = exchange(grad_out.reshape(heads, slab, vals), "head").astype(F32).sum(0)
-    grad_in = scatter_grad(dot(xn, g_proj, (0, 0)))
-    grad_in = exchange(grad_in.reshape(heads, slab, proj_width), "head").astype(F32)
+    grad_mix = weight_grad(xn, g_proj, grad_mix, proj_width + vals, 0, dv)
+    grad_mix, grad_ffn = lax.optimization_barrier((grad_mix, grad_ffn))
+    grad_mix = scatter_grad(grad_mix).reshape(heads, slab, proj_width + vals)
+    grad_mix = exchange(grad_mix, "head").astype(F32)
+    grad_in, grad_out = grad_mix[:, :, :proj_width], grad_mix[:, :, proj_width:].sum(0)
     cuts = ((0, dk), (dk, 2 * dk), (2 * dk, 2 * dk + dv), (2 * dk + dv, proj_width))
     grad_in = jnp.concatenate(
         [grad_in[:, :, a:b].transpose(1, 0, 2).reshape(slab, -1) for a, b in cuts], axis=1
@@ -527,8 +583,8 @@
         input_grad.reshape(tokens.shape),
         grad_in,
         grad_out,
-        grad_gu.reshape(grad_gu.shape[0], 2, hidden_units),
-        grad_down,
+        grad_ffn[:, : 2 * hidden_units].astype(F32).reshape(-1, 2, hidden_units),
+        grad_ffn[:, 2 * hidden_units :].astype(F32),
         *small,
     )
 

time: 965 us -> 864 us (0.90)
  waiting for transfers between devices: 433 us -> 317 us
  Pallas kernels: 69.3 us -> 115 us
  matrix products: 141 us -> 105 us
  blocking collectives: 195 us -> 170 us
  other arithmetic: 22.5 us -> 36.4 us
  starting transfers between devices: 42.7 us -> 52.7 us
    reduce_scatter x4 -> x2, waiting for transfers between devices: 95.5 us -> 0.01 us  [scatter_grad(): lax.psum_scatter(g.astype(BF16), 'seq', scatter_dimension=0, tiled=True)]
    all_to_all x7 -> x5, blocking collectives: 168 us -> 119 us  [exchange(): return lax.all_to_all(x, axis, split_axis=0, concat_axis=0, tiled=True)]
    pallas_call x0 -> x4, Pallas kernels: none -> 46.1 us  [weight_grad(): pl.pallas_call(weight_grad_kernel, out_shape=jax.ShapeDtypeStruct((rows,...]
    dot_general x19 -> x15, matrix products: 141 us -> 105 us  [dot(): lax.dot_general(a, b, (((contract[0],), (contract[1],)), ((), ())), preci...]
    all_gather x1, blocking collectives: 18.1 us -> 41.8 us  [total_of(): piece = lax.all_gather(piece, 'head', axis=0, tiled=True)]
    all_to_all x9, waiting for transfers between devices: 337 us -> 316 us  [exchange(): return lax.all_to_all(x, axis, split_axis=0, concat_axis=0, tiled=True)]
    reduce_scatter x4 -> x2, starting transfers between devices: 0.96 us -> 11.7 us  [scatter_grad(): lax.psum_scatter(g.astype(BF16), 'seq', scatter_dimension=0, tiled=True)]
    unnamed x70 -> x109, local copies, waits for them, and re-layouts: 16.5 us -> 22.5 us
  transfers between devices with their start and end apart: 17 -> 14, of which waited for: 9 -> 8; matrix products, arithmetic and copies ran while one was open for 14% -> 15% of each run, Pallas kernels for 3% -> 14%
where the time goes in v2:
time: 864 us; the launch traced here: 853 us
  waiting for transfers between devices  317 us (37%)
  blocking collectives  170 us (20%)
  Pallas kernels  115 us (13%)
  matrix products  105 us (12%)
  starting transfers between devices  52.7 us (6%)
  local copies, waits for them, and re-layouts  42.7 us (5%)
  other arithmetic  36.4 us (4%)
  between operations  14.8 us (2%)
    all_to_all x9, waiting for transfers between devices, exchange(): return lax.all_to_all(x, axis, split_axis=0, concat_axis=0, tiled=True)  316 us
    all_to_all x5, blocking collectives, exchange(): return lax.all_to_all(x, axis, split_axis=0, concat_axis=0, tiled=True)  119 us
    dot_general x15, matrix products, dot(): lax.dot_general(a, b, (((contract[0],), (contract[1],)), ((), ())), preci...  105 us
    pallas_call x4, Pallas kernels, weight_grad(): pl.pallas_call(weight_grad_kernel, out_shape=jax.ShapeDtypeStruct((rows,...  46.1 us
    all_gather x1, blocking collectives, total_of(): piece = lax.all_gather(piece, 'head', axis=0, tiled=True)  41.8 us
    all_to_all x9, starting transfers between devices, exchange(): return lax.all_to_all(x, axis, split_axis=0, concat_axis=0, tiled=True)  40.8 us
    pallas_call x1, Pallas kernels, mix_back_of(): pl.pallas_call(mix_back_kernel, out_shape=(jax.ShapeDtypeStruct((blocks,...  28.1 us
    unnamed x109, local copies, waits for them, and re-layouts  22.5 us
  transfers between devices with their start and end apart: 14, of which 8 were waited for; matrix products, arithmetic and copies ran while one was open for 15% of the time, Pallas kernels for 14%

profile of v2, /device:TPU:0, one launch (start us, length us, event | category | flops | bytes accessed | tf_op | source)
XLA Modules:
  0.0 853.5 jit_solution(4004804133486797281)
XLA Ops:
  18.4 6.3 all-to-all-start
  25.5 69.9 %all-to-all-done = bf16[4,3,64,2048]{3,2,1,0:T(8,128)(2,1)S(1)} async-done(((bf16[4,3,64,2048]{3,2,1,0:T(8,128)(2,1)}), bf16[4,3,64,2048]{3,2,1,0:T(8,128)(2,1)S(1)}, u32[]{:S(2)}, u32[]{:S(2)}) %all-to-all-start) | async-done | bytes 3145760 | tf_op jit(solution)/shard_map/all_to_all | solution.py:396
  104.3 5.7 fusion.39
  110.0 9.6 %states.1 = bf16[8,3,80,256]{3,2,1,0:T(8,128)(2,1)S(1)} custom-call(s32[3,4]{1,0:T(4,128)S(1)} %copy-done.24, bf16[4,3,64,1024]{3,2,1,0:T(8,128)(2,1)S(1)} %bitcast.110, bf16[4,3,64,256]{3,2,1,0:T(8,128)(2,1)S(1)} %bitcast.116), custom_call_target="tpu_custom_call" | custom-call | bytes 30000000 | tf_op jit(solution)/shard_map/states/pallas_call | solution.py:232
  120.8 25.7 %all_to_all.70.own = bf16[8,3,80,256]{3,2,1,0:T(8,128)(2,1)S(1)} all-to-all(bf16[8,3,80,256]{3,2,1,0:T(8,128)(2,1)S(1)} %states.1), channel_id=1, replica_groups=mesh['seq'=8,'head'=4] {'seq'}, dimensions={0} | all-to-all | bytes 1966080 | tf_op jit(solution)/shard_map/all_to_all | solution.py:396
  151.9 7.1 fusion.29.og
  159.0 14.0 %all-to-all-done.2.before = bf16[8,3,64,256]{3,2,1,0:T(8,128)(2,1)} async-done(((bf16[8,3,64,256]{3,2,1,0:T(8,128)(2,1)}), bf16[8,3,64,256]{3,2,1,0:T(8,128)(2,1)}, u32[]{:S(2)}, u32[]{:S(2)}) %all-to-all-start.2) | async-done | bytes 786464 | tf_op jit(solution)/shard_map/all_to_all | solution.py:396
  175.6 18.3 %mix.1 = (f32[4,3,64,512]{3,2,1,0:T(8,128)S(1)}, bf16[4,3,64,512]{3,2,1,0:T(8,128)(2,1)S(1)}, f32[4,3,512,256]{3,2,1,0:T(8,128)}) custom-call(s32[3,4]{1,0:T(4,128)S(1)} %copy-done.24, bf16[4,3,64,1024]{3,2,1,0:T(8,128)(2,1)S(1)} %bitcast.112, bf16[4,3,64,256]{3,2,1,0:T(8,128)(2,1)S(1)} %bitcast.117, f32[4,3,64,512]{3,2,1,0:T(8,128)} %fusion.29.og, ...), custom_call_target="tpu_custom_call" | custom-call | bytes 54000000 | tf_op jit(solution)/shard_map/mix/pallas_call | solution.py:263
  193.8 21.6 %all_to_all.71 = bf16[4,3,64,512]{3,2,1,0:T(8,128)(2,1)S(1)} all-to-all(bf16[4,3,64,512]{3,2,1,0:T(8,128)(2,1)S(1)} %get-tuple-element.29), channel_id=1, replica_groups=mesh['seq'=8,'head'=4] {'head'}, dimensions={0} | all-to-all | bytes 1572864 | tf_op jit(solution)/shard_map/all_to_all | solution.py:396
  216.2 6.7 multiply_reduce_fusion.6
  231.7 118.7 %all-to-all-done.4 = bf16[4,192,2048]{2,1,0:T(8,128)(2,1)} async-done(((bf16[4,192,2048]{2,1,0:T(8,128)(2,1)}), bf16[4,192,2048]{2,1,0:T(8,128)(2,1)}, u32[]{:S(2)}, u32[]{:S(2)}) %all-to-all-start.4) | async-done | bytes 3145760 | tf_op jit(solution)/shard_map/all_to_all | solution.py:396
  350.4 15.8 %fusion.2 = f32[768,2816]{1,0:T(8,128)} fusion(bf16[768,2048]{1,0:T(8,128)(2,1)} %bitcast.11.left, bf16[2048,4224]{1,0:T(8,128)(2,1)} %all-gather.7.cloned.1.call-done), kind=kOutput, calls=%fused_computation.2 | convolution fusion | flops 8858370048 | bytes 23330816 | tf_op jit(solution)/shard_map/dot_general | solution.py:412
  366.2 13.8 %fusion.18 = (bf16[768,1408]{1,0:T(8,128)(2,1)S(1)}, bf16[768,1408]{1,0:T(8,128)(2,1)S(1)}, bf16[768,1408]{1,0:T(8,128)(2,1)}) fusion(f32[768,2816]{1,0:T(8,128)} %fusion.2, bf16[768,2048]{1,0:T(8,128)(2,1)} %bitcast.122, bf16[2048,4224]{1,0:T(8,128)(2,1)} %all-gather.7.cloned.1.call-done), kind=kOutput, calls=%fused_computation.28 | convolution fusion | flops 4445405184 | bytes 24051712 | tf_op jit(solution)/shard_map/dot_general | solution.py:412
  380.1 14.8 %fusion.26 = bf16[768,2048]{1,0:T(8,128)(2,1)} fusion(bf16[2048,4224]{1,0:T(8,128)(2,1)} %all-gather.7.cloned.1.call-done, bf16[768,1408]{1,0:T(8,128)(2,1)S(1)} %get-tuple-element.87, bf16[768,1408]{1,0:T(8,128)(2,1)S(1)} %get-tuple-element.86), kind=kOutput, calls=%fused_computation.36 | convolution fusion | flops 8868593664 | bytes 19005440 | tf_op jit(solution)/shard_map/dot_general | solution.py:412
  399.5 11.7 %reduce-scatter.3.cloned.1.call-start = ((), (), s32[]{:S(2)}) async-start(), calls=%async_computation.18 | async-start | bytes 19464192 | tf_op jit(solution)/shard_map/reduce_scatter | solution.py:408
  415.8 18.3 %weight_grad.4.rest_0_ = bf16[2048,4224]{1,0:T(8,128)(2,1)} custom-call(bf16[768,2048]{1,0:T(8,128)(2,1)} %bitcast.11.left, bf16[768,2816]{1,0:T(8,128)(2,1)} %pad_maximum_fusion.right), custom_call_target="tpu_custom_call" | custom-call | flops 8858370048 | bytes 19005440 | tf_op jit(solution)/shard_map/weight_grad/pallas_call | solution.py:373
  434.1 7.2 weight_grad.5
  441.3 9.0 %fusion.23 = bf16[768,2048]{1,0:T(8,128)(2,1)} fusion(bf16[768,1408]{1,0:T(8,128)(2,1)} %get-tuple-element.88.right, bf16[2048,4224]{1,0:T(8,128)(2,1)} %all-gather.7.cloned.1.call-done), kind=kOutput, calls=%fused_computation.35 | convolution fusion | flops 4430757888 | bytes 11075584 | tf_op jit(solution)/shard_map/dot_general | solution.py:412
  450.3 19.4 %all-to-all-done.5 = bf16[4,192,2048]{2,1,0:T(8,128)(2,1)} async-done(((bf16[4,192,2048]{2,1,0:T(8,128)(2,1)}), bf16[4,192,2048]{2,1,0:T(8,128)(2,1)}, u32[]{:S(2)}, u32[]{:S(2)}) %all-to-all-start.5) | async-done | bytes 3145760 | tf_op jit(solution)/shard_map/all_to_all | solution.py:396
  474.3 7.3 fusion.36
  487.2 21.5 %all_to_all.72.g_gated = bf16[4,3,64,512]{3,2,1,0:T(8,128)(2,1)S(1)} all-to-all(bf16[4,3,64,512]{3,2,1,0:T(8,128)(2,1)S(1)} %bitcast.137), channel_id=1, replica_groups=mesh['seq'=8,'head'=4] {'head'}, dimensions={0} | all-to-all | bytes 1572864 | tf_op jit(solution)/shard_map/all_to_all | solution.py:396
  508.7 12.7 %gate_back.1 = (bf16[4,3,64,512]{3,2,1,0:T(8,128)(2,1)S(1)}, f32[4,3,64,512]{3,2,1,0:T(8,128)S(1)}, bf16[8,3,64,256]{3,2,1,0:T(8,128)(2,1)S(1)}, f32[8,512]{1,0:T(8,128)S(1)}) custom-call(s32[3,4]{1,0:T(4,128)S(1)} %copy-done.24, bf16[4,3,64,512]{3,2,1,0:T(8,128)(2,1)S(1)} %all_to_all.72.g_gated, f32[4,3,64,512]{3,2,1,0:T(8,128)S(1)} %copy-done.9, ...), custom_call_target="tpu_custom_call" | custom-call | bytes 36000000 | tf_op jit(solution)/shard_map/gate_back/pallas_call | solution.py:293
  521.4 25.7 %all_to_all.73.own = bf16[8,3,64,256]{3,2,1,0:T(8,128)(2,1)S(1)} all-to-all(bf16[8,3,64,256]{3,2,1,0:T(8,128)(2,1)S(1)} %get-tuple-element.35), channel_id=1, replica_groups=mesh['seq'=8,'head'=4] {'seq'}, dimensions={0} | all-to-all | bytes 1572864 | tf_op jit(solution)/shard_map/all_to_all | solution.py:396
  547.4 24.4 %all_to_all.74.after = bf16[8,3,64,256]{3,2,1,0:T(8,128)(2,1)} all-to-all(bf16[8,3,64,256]{3,2,1,0:T(8,128)(2,1)S(1)} %suffix.1), channel_id=1, replica_groups=mesh['seq'=8,'head'=4] {'seq'}, dimensions={0} | all-to-all | bytes 1572864 | tf_op jit(solution)/shard_map/all_to_all | solution.py:396
  579.1 9.9 %weight_grad.6.rest_0_ = bf16[2048,3584]{1,0:T(8,128)(2,1)} custom-call(bf16[192,2048]{1,0:T(8,128)(2,1)S(1)} %copy-done.13, bf16[192,2048]{1,0:T(8,128)(2,1)S(1)} %bitcast.121), custom_call_target="tpu_custom_call" | custom-call | flops 1610612736 | bytes 9961472 | tf_op jit(solution)/shard_map/weight_grad/pallas_call | solution.py:373
  589.0 28.1 %mix_back.1 = (bf16[4,3,64,1536]{3,2,1,0:T(8,128)(2,1)}, f32[4,3,64,256]{3,2,1,0:T(8,128)S(1)}) custom-call(s32[3,4]{1,0:T(4,128)S(1)} %copy-done.24, bf16[4,3,64,1024]{3,2,1,0:T(8,128)(2,1)S(1)} %bitcast.113, bf16[4,3,64,256]{3,2,1,0:T(8,128)(2,1)S(1)} %bitcast.119, f32[4,3,64,512]{3,2,1,0:T(8,128)} %copy-done.19, bf16[4,3,64,512]{3,2,1,0:T(8,128)(2,1)S(1)} %copy-done.23, ...), custom_call_target="tpu_custom_call" | custom-call | bytes 84000000 | tf_op jit(solution)/shard_map/mix_back/pallas_call | solution.py:331
  618.0 26.8 %all-to-all-done.9 = bf16[4,192,2048]{2,1,0:T(8,128)(2,1)} async-done(((bf16[4,192,2048]{2,1,0:T(8,128)(2,1)}), bf16[4,192,2048]{2,1,0:T(8,128)(2,1)}, u32[]{:S(2)}, u32[]{:S(2)}) %all-to-all-start.9) | async-done | bytes 3145760 | tf_op jit(solution)/shard_map/all_to_all | solution.py:396
  646.5 10.7 %weight_grad.7 = bf16[2048,3584]{1,0:T(8,128)(2,1)} custom-call(bf16[768,2048]{1,0:T(8,128)(2,1)S(1)} %fusion.11.left, bf16[768,1536]{1,0:T(8,128)(2,1)S(1)} %bitcast.125, bf16[2048,3584]{1,0:T(8,128)(2,1)} %weight_grad.6.rest_0_), custom_call_target="tpu_custom_call", output_to_operand_aliasing={{}: (2, {})} | custom-call | flops 4831838208 | bytes 11796480 | tf_op jit(solution)/shard_map/weight_grad/pallas_call | solution.py:373
  659.1 8.5 fusion.8
  688.0 58.8 %all-to-all-done.10 = bf16[4,192,2048]{2,1,0:T(8,128)(2,1)} async-done(((bf16[4,192,2048]{2,1,0:T(8,128)(2,1)}), bf16[4,192,2048]{2,1,0:T(8,128)(2,1)}, u32[]{:S(2)}, u32[]{:S(2)}) %all-to-all-start.10) | async-done | bytes 3145760 | tf_op jit(solution)/shard_map/all_to_all | solution.py:396
  781.0 41.8 %all_gather.22 = f32[64,128]{1,0:T(8,128)S(1)} all-gather(f32[16,128]{1,0:T(8,128)S(1)} %reduce_sum.142), channel_id=1, replica_groups=mesh['seq'=8,'head'=4] {'head'}, dimensions={0}, use_global_device_ids=true | all-gather | bytes 40960 | tf_op jit(solution)/shard_map/all_gather | solution.py:435
  822.8 9.1 %all_gather.23 = f32[512,128]{1,0:T(8,128)S(1)} all-gather(f32[64,128]{1,0:T(8,128)S(1)} %all_gather.22), channel_id=1, replica_groups=mesh['seq'=8,'head'=4] {'seq'}, dimensions={0}, use_global_device_ids=true | all-gather | bytes 294912 | tf_op jit(solution)/shard_map/all_gather | solution.py:436
  (198 shorter events, 139.7 us)
Async XLA Ops:
  7.2 92.6 %copy-start = (bf16[2048,16]{0,1:T(8,128)(2,1)S(1)}, bf16[2048,16]{0,1:T(8,128)(2,1)}, u32[]{:S(2)}) copy-start(bf16[2048,16]{0,1:T(8,128)(2,1)} %param.23) | copy-start | bytes 196612
  7.2 97.1 %all-gather.5.cloned.1.call-start = ((), (), s32[]{:S(2)}) async-start(), calls=%async_computation.16 | async-start | bytes 16515072 | tf_op jit(solution)/shard_map/all_gather | solution.py:404
  13.7 218.0 %all-gather.7.cloned.1.call-start = ((), (), s32[]{:S(2)}) async-start(), calls=%async_computation.17 | async-start | bytes 19464192 | tf_op jit(solution)/shard_map/all_gather | solution.py:404
  18.4 77.0 %all-to-all-start = ((bf16[4,3,64,2048]{3,2,1,0:T(8,128)(2,1)}), bf16[4,3,64,2048]{3,2,1,0:T(8,128)(2,1)S(1)}, u32[]{:S(2)}, u32[]{:S(2)}) async-start(bf16[4,3,64,2048]{3,2,1,0:T(8,128)(2,1)} %broadcast_in_dim.8), calls=%async_computation | async-start | bytes 6291456 | tf_op jit(solution)/shard_map/all_to_all | solution.py:396
  24.7 72.4 %copy-start.45 = (f32[2048]{0:T(1024)S(1)}, f32[2048]{0:T(1024)}, u32[]{:S(2)}) copy-start(f32[2048]{0:T(1024)} %param.20) | copy-start | bytes 24580
  147.6 25.4 %all-to-all-start.2 = ((bf16[8,3,64,256]{3,2,1,0:T(8,128)(2,1)}), bf16[8,3,64,256]{3,2,1,0:T(8,128)(2,1)}, u32[]{:S(2)}, u32[]{:S(2)}) async-start(bf16[8,3,64,256]{3,2,1,0:T(8,128)(2,1)} %copy-done.16), calls=%async_computation.2 | async-start | bytes 1572864 | tf_op jit(solution)/shard_map/all_to_all | solution.py:396
  151.9 21.2 %copy-start.25 = (f32[512]{0:T(512)S(1)}, f32[512]{0:T(512)}, u32[]{:S(2)}) copy-start(f32[512]{0:T(512)} %param.22) | copy-start | bytes 6148
  193.8 29.1 %copy-start.20 = (f32[4,3,64,512]{3,2,1,0:T(8,128)}, f32[4,3,64,512]{3,2,1,0:T(8,128)S(1)}, u32[]{:S(2)}) copy-start(f32[4,3,64,512]{3,2,1,0:T(8,128)S(1)} %get-tuple-element.31.o_in) | copy-start | bytes 4718596
  193.8 22.4 %copy-start.34 = (bf16[3,64,2048]{2,1,0:T(8,128)(2,1)S(1)}, bf16[3,64,2048]{2,1,0:T(8,128)(2,1)}, u32[]{:S(2)}) copy-start(bf16[3,64,2048]{2,1,0:T(8,128)(2,1)} %param.13) | copy-start | bytes 2359300
  226.3 124.1 %all-to-all-start.4 = ((bf16[4,192,2048]{2,1,0:T(8,128)(2,1)}), bf16[4,192,2048]{2,1,0:T(8,128)(2,1)}, u32[]{:S(2)}, u32[]{:S(2)}) async-start(bf16[4,192,2048]{2,1,0:T(8,128)(2,1)} %broadcast_in_dim.9), calls=%async_computation.4 | async-start | bytes 6291456 | tf_op jit(solution)/shard_map/all_to_all | solution.py:396
  230.9 135.3 %all-gather.9.cloned.1.call-start = ((), (), s32[]{:S(2)}) async-start(), calls=%async_computation.20 | async-start | bytes 3932160 | tf_op jit(solution)/shard_map/all_gather | solution.py:481
  380.1 14.8 %copy-start.37 = (bf16[768,1408]{1,0:T(8,128)(2,1)}, bf16[768,1408]{1,0:T(8,128)(2,1)S(1)}, u32[]{:S(2)}) copy-start(bf16[768,1408]{1,0:T(8,128)(2,1)S(1)} %get-tuple-element.86) | copy-start | bytes 6488068
  380.1 14.8 %copy-start.38 = (bf16[768,1408]{1,0:T(8,128)(2,1)}, bf16[768,1408]{1,0:T(8,128)(2,1)S(1)}, u32[]{:S(2)}) copy-start(bf16[768,1408]{1,0:T(8,128)(2,1)S(1)} %get-tuple-element.87) | copy-start | bytes 6488068
  394.8 74.9 %all-to-all-start.5 = ((bf16[4,192,2048]{2,1,0:T(8,128)(2,1)}), bf16[4,192,2048]{2,1,0:T(8,128)(2,1)}, u32[]{:S(2)}, u32[]{:S(2)}) async-start(bf16[4,192,2048]{2,1,0:T(8,128)(2,1)} %bitcast.134), calls=%async_computation.5 | async-start | bytes 6291456 | tf_op jit(solution)/shard_map/all_to_all | solution.py:396
  399.5 257.7 %reduce-scatter.3.cloned.1.call-start = ((), (), s32[]{:S(2)}) async-start(), calls=%async_computation.18 | async-start | bytes 19464192 | tf_op jit(solution)/shard_map/reduce_scatter | solution.py:408
  415.8 18.3 %copy-start.14 = (bf16[12,64,2048]{2,1,0:T(8,128)(2,1)S(1)}, bf16[12,64,2048]{2,1,0:T(8,128)(2,1)}, u32[]{:S(2)}) copy-start(bf16[12,64,2048]{2,1,0:T(8,128)(2,1)} %all-gather.9.cloned.1.call-done) | copy-start | bytes 9437188
  415.8 18.3 %copy-start.18 = (bf16[768,1408]{1,0:T(8,128)(2,1)S(1)}, bf16[768,1408]{1,0:T(8,128)(2,1)}, u32[]{:S(2)}) copy-start(bf16[768,1408]{1,0:T(8,128)(2,1)} %get-tuple-element.88.right) | copy-start | bytes 6488068
  485.6 23.2 %copy-start.7 = (bf16[768,256]{1,0:T(8,128)(2,1)S(1)}, bf16[768,256]{1,0:T(8,128)(2,1)}, u32[]{:S(2)}) copy-start(bf16[768,256]{1,0:T(8,128)(2,1)} %get-tuple-element.97) | copy-start | bytes 1179652
  485.6 23.2 %copy-start.9 = (f32[4,3,64,512]{3,2,1,0:T(8,128)S(1)}, f32[4,3,64,512]{3,2,1,0:T(8,128)}, u32[]{:S(2)}) copy-start(f32[4,3,64,512]{3,2,1,0:T(8,128)} %fusion.29.og) | copy-start | bytes 4718596
  521.4 26.0 %copy-start.19 = (f32[4,3,64,512]{3,2,1,0:T(8,128)}, f32[4,3,64,512]{3,2,1,0:T(8,128)S(1)}, u32[]{:S(2)}) copy-start(f32[4,3,64,512]{3,2,1,0:T(8,128)S(1)} %get-tuple-element.32.g_o) | copy-start | bytes 4718596
  521.4 26.0 %copy-start.22 = (bf16[4,3,64,512]{3,2,1,0:T(8,128)(2,1)}, bf16[4,3,64,512]{3,2,1,0:T(8,128)(2,1)S(1)}, u32[]{:S(2)}) copy-start(bf16[4,3,64,512]{3,2,1,0:T(8,128)(2,1)S(1)} %get-tuple-element.33.g_og) | copy-start | bytes 2359300
  571.8 73.0 %all-to-all-start.9 = ((bf16[4,192,2048]{2,1,0:T(8,128)(2,1)}), bf16[4,192,2048]{2,1,0:T(8,128)(2,1)}, u32[]{:S(2)}, u32[]{:S(2)}) async-start(bf16[4,192,2048]{2,1,0:T(8,128)(2,1)} %bitcast.133), calls=%async_computation.9 | async-start | bytes 6291456 | tf_op jit(solution)/shard_map/all_to_all | solution.py:396
  576.5 195.5 %reduce-scatter.5.cloned.1.call-start = ((), (), s32[]{:S(2)}) async-start(), calls=%async_computation.19 | async-start | bytes 16515072 | tf_op jit(solution)/shard_map/reduce_scatter | solution.py:408
  579.0 10.0 %copy-start.23 = (bf16[4,3,64,512]{3,2,1,0:T(8,128)(2,1)S(1)}, bf16[4,3,64,512]{3,2,1,0:T(8,128)(2,1)}, u32[]{:S(2)}) copy-start(bf16[4,3,64,512]{3,2,1,0:T(8,128)(2,1)} %copy-done.22) | copy-start | bytes 2359300
  672.0 74.8 %all-to-all-start.10 = ((bf16[4,192,2048]{2,1,0:T(8,128)(2,1)}), bf16[4,192,2048]{2,1,0:T(8,128)(2,1)}, u32[]{:S(2)}, u32[]{:S(2)}) async-start(bf16[4,192,2048]{2,1,0:T(8,128)(2,1)} %bitcast.130), calls=%async_computation.10 | async-start | bytes 6291456 | tf_op jit(solution)/shard_map/all_to_all | solution.py:396
  685.9 64.8 %copy-start.35 = (bf16[3,64,2048]{2,1,0:T(8,128)(2,1)S(1)}, bf16[3,64,2048]{2,1,0:T(8,128)(2,1)}, u32[]{:S(2)}) copy-start(bf16[3,64,2048]{2,1,0:T(8,128)(2,1)} %param.13) | copy-start | bytes 2359300
  685.9 64.8 %copy-start.46 = (f32[2048]{0:T(1024)S(1)}, f32[2048]{0:T(1024)}, u32[]{:S(2)}) copy-start(f32[2048]{0:T(1024)} %param.20) | copy-start | bytes 24580
  752.0 10.3 %all-to-all-start.12 = ((f32[8,64,128]{2,1,0:T(8,128)}), f32[8,64,128]{2,1,0:T(8,128)S(1)}, u32[]{:S(2)}, u32[]{:S(2)}) async-start(f32[8,64,128]{2,1,0:T(8,128)} %bitcast.28), calls=%async_computation.14 | async-start | bytes 524288 | tf_op jit(solution)/shard_map/all_to_all | solution.py:396
  759.2 17.2 %copy-start.29 = (f32[192,2048]{1,0:T(8,128)S(1)}, f32[192,2048]{1,0:T(8,128)}, u32[]{:S(2)}) copy-start(f32[192,2048]{1,0:T(8,128)} %copy-done.27) | copy-start | bytes 4718596
  759.2 17.2 %copy-start.31 = (f32[192,2048]{1,0:T(8,128)S(1)}, f32[192,2048]{1,0:T(8,128)}, u32[]{:S(2)}) copy-start(f32[192,2048]{1,0:T(8,128)} %copy-done.30) | copy-start | bytes 4718596
  763.0 9.0 %all-to-all-start.13 = ((f32[4,16,128]{2,1,0:T(8,128)}), f32[4,16,128]{2,1,0:T(8,128)S(1)}, u32[]{:S(2)}, u32[]{:S(2)}) async-start(f32[4,16,128]{2,1,0:T(8,128)} %bitcast.29), calls=%async_computation.15 | async-start | bytes 65536 | tf_op jit(solution)/shard_map/all_to_all | solution.py:396
  772.0 70.2 %all-to-all-start.11 = ((bf16[4,64,3584]{2,1,0:T(8,128)(2,1)}), bf16[4,64,3584]{2,1,0:T(8,128)(2,1)}, u32[]{:S(2)}, u32[]{:S(2)}) async-start(bf16[4,64,3584]{2,1,0:T(8,128)(2,1)} %bitcast.140), calls=%async_computation.13 | async-start | bytes 3670016 | tf_op jit(solution)/shard_map/all_to_all | solution.py:396
  (29 other events, 107.5 us)
Sparse Core Ops, SparseCore 0:
  13.9 83.6 all-gather.4
  100.0 111.0 all-gather.6
  233.4 109.9 all-gather.8
  469.9 135.3 reduce-scatter.2
  657.3 102.0 reduce-scatter.4

commit v3 on v2

--- a/solution.py
+++ b/solution.py
@@ -69,19 +69,6 @@
         for i in range(slices):
             out[i, 0, :part, :] = state[i * part : (i + 1) * part, :].astype(BF16)
             out[i, 0, part:, :] = extra
-
-
-def prefix_kernel(reverse, own, through, out):
-    count = own.shape[0]
-    part = out.shape[2]
-
-    def step(k, state):
-        j = count - 1 - k if reverse else k
-        out[j] = state.astype(BF16)
-        decay = through[j, :, 0:1, :].astype(F32) + through[j, :, 1:2, :].astype(F32)
-        return decay * state + own[j, :, :part, :].astype(F32)
-
-    lax.fori_loop(0, count, step, jnp.zeros(out.shape[1:], F32))
 
 
 def mix_kernel(flags, qkv, decay, og, before, gain, o_out, gated, kept, state):
@@ -243,17 +230,6 @@
         cost_estimate=cost(10),
         name="states",
     )(flags, qkv, decays)
-
-
-def prefix_of(own, through, part, reverse):
-    return pl.pallas_call(
-        functools.partial(prefix_kernel, reverse),
-        out_shape=jax.ShapeDtypeStruct(own.shape[:2] + (part, own.shape[3]), BF16),
-        in_specs=[pl.BlockSpec(memory_space=pltpu.VMEM)] * 2,
-        out_specs=pl.BlockSpec(memory_space=pltpu.VMEM),
-        compiler_params=pltpu.CompilerParams(vmem_limit_bytes=48 << 20),
-        name="suffix" if reverse else "prefix",
-    )(own, through)
 
 
 def mix_of(flags, qkv, decays, og, before, gain):
@@ -392,53 +368,552 @@
     )(left, right, *given)
 
 
-def exchange(x, axis):
-    return lax.all_to_all(x, axis, split_axis=0, concat_axis=0, tiled=True)
-
-
-def gather_rows(x, axis):
-    return exchange(jnp.broadcast_to(x[None], (lax.axis_size(axis),) + x.shape), axis)
-
-
-def gather_weight(w):
-    return lax.all_gather(w, "seq", axis=0, tiled=True)
-
-
-def scatter_grad(g):
-    return lax.psum_scatter(g.astype(BF16), "seq", scatter_dimension=0, tiled=True)
-
-
-def dot(a, b, contract, precision=None):
-    return lax.dot_general(
-        a, b, (((contract[0],), (contract[1],)), ((), ())),
-        precision=precision, preferred_element_type=F32,
-    )
-
-
-def rms(x, epsilon):
-    return lax.rsqrt(jnp.mean(x * x, axis=-1, keepdims=True) + epsilon)
-
-
-def norm_back(grad, gain, normed, inv):
-    scaled = grad * gain
-    inner = jnp.mean(scaled * normed, axis=-1, keepdims=True)
-    return inv * (scaled - normed * inner), jnp.sum(grad * normed, axis=0)
-
-
-def total_of(parts, seq, head):
+def greet(axes):
+    barrier = pltpu.get_barrier_semaphore()
+    met = 0
+    for axis in axes:
+        me, count = lax.axis_index(axis), lax.axis_size(axis)
+        for hop in range(1, count):
+            pl.semaphore_signal(
+                barrier, inc=1, device_id={axis: lax.rem(me + hop, count)},
+                device_id_type=pl.DeviceIdType.MESH,
+            )
+        met += count - 1
+    pl.semaphore_wait(barrier, met)
+
+
+def push(src, dst, send, recv, to, axis="head"):
+    return pltpu.make_async_remote_copy(
+        src_ref=src, dst_ref=dst, send_sem=send, recv_sem=recv,
+        device_id={axis: to}, device_id_type=pl.DeviceIdType.MESH,
+    )
+
+
+def near_order(z, count, i):
+    both = jnp.minimum(z, count - 1 - z)
+    left = z > count - 1 - z
+    paired = jnp.where(i % 2 == 1, z - (i + 1) // 2, z + i // 2)
+    single = jnp.where(left, z - (i - both), z + (i - both))
+    return jnp.where(i <= 2 * both, paired, single)
+
+
+class Line:
+    def __init__(self, own, all_rows, send, recv):
+        self.own, self.all, self.send, self.recv = own, all_rows, send, recv
+        self.z, self.count, self.rows = lax.axis_index("head"), lax.axis_size("head"), own.shape[0]
+        z, count = self.z, self.count
+        self.right = push(own, self.at(z), send.at[0], recv.at[z], lax.rem(z + 1, count))
+        self.left = push(own, self.at(z), send.at[1], recv.at[z], lax.rem(z + count - 1, count))
+
+    def chunk(self, b):
+        return pl.ds(pl.multiple_of(b * self.rows, self.rows), self.rows)
+
+    def at(self, b):
+        return self.all.at[self.chunk(b)]
+
+    def start(self):
+        pl.when(self.z < self.count - 1)(self.right.start)
+        pl.when(self.z > 0)(self.left.start)
+
+    def passing(self, i, b):
+        z, count = self.z, self.count
+        to = jnp.where(b < z, z + 1, z - 1)
+        going = ((b < z) & (z < count - 1)) | ((b > z) & (z > 0))
+        copy = push(
+            self.at(b), self.at(b), self.send.at[i + 1], self.recv.at[b], lax.rem(to + count, count)
+        )
+        return copy, going
+
+    def receive(self, i, b):
+        copy, going = self.passing(i, b)
+        copy.wait_recv()
+        pl.when(going)(copy.start)
+
+    def finish(self):
+        def sent(i, _):
+            copy, going = self.passing(i, near_order(self.z, self.count, i))
+            pl.when(going)(copy.wait_send)
+            return 0
+
+        lax.fori_loop(1, self.count, sent, 0)
+        pl.when(self.z < self.count - 1)(self.right.wait_send)
+        pl.when(self.z > 0)(self.left.wait_send)
+
+
+def gather_norm_kernel(own, gain, normed, rows_all, here_sem, send, recv):
+    z, count, rows = lax.axis_index("head"), lax.axis_size("head"), own.shape[0]
+    greet(("head",))
+    line = Line(own, rows_all, send, recv)
+    line.start()
+    here = pltpu.make_async_copy(own, line.at(z), here_sem)
+    here.start()
+    here.wait()
+    band = 16
+
+    def step(i, _):
+        b = near_order(z, count, i)
+        pl.when(i > 0)(lambda: line.receive(i, b))
+
+        def norm(r, _):
+            at = pl.ds(pl.multiple_of(b * rows + r * band, band), band)
+            x = rows_all[at, :].astype(F32)
+            inv = lax.rsqrt(jnp.mean(x * x, axis=-1, keepdims=True) + 1e-6)
+            normed[at, :] = (x * inv * gain[...]).astype(BF16)
+            return 0
+
+        lax.fori_loop(0, rows // band, norm, 0)
+        return 0
+
+    lax.fori_loop(0, count, step, 0)
+    line.finish()
+
+
+def gather_norm(x, gain):
+    rows, width = x.shape
+    count = lax.axis_size("head")
+    vmem = pl.BlockSpec(memory_space=pltpu.VMEM)
+    dma = pltpu.SemaphoreType.DMA
+    return pl.pallas_call(
+        gather_norm_kernel,
+        out_shape=jax.ShapeDtypeStruct((count * rows, width), BF16),
+        in_specs=[vmem, vmem],
+        out_specs=vmem,
+        scratch_shapes=[
+            pltpu.VMEM((count * rows, width), BF16), dma(()), dma((count + 1,)), dma((count,)),
+        ],
+        compiler_params=pltpu.CompilerParams(
+            collective_id=1, has_side_effects=True, vmem_limit_bytes=32 << 20
+        ),
+        cost_estimate=cost(50),
+        name="gather_norm",
+    )(x, gain)
+
+
+def swap_slices(own, got, send, recv):
+    me, count = lax.axis_index("seq"), lax.axis_size("seq")
+
+    def copy(hop, index):
+        to = lax.rem(me + hop, count)
+        return push(own.at[to], got.at[index], send.at[hop], recv.at[index], to, "seq")
+
+    def start(hop, _):
+        copy(hop, me).start()
+        return 0
+
+    def wait_recv(hop, _):
+        copy(hop, lax.rem(me + hop, count)).wait_recv()
+        return 0
+
+    def wait_send(hop, _):
+        copy(hop, me).wait_send()
+        return 0
+
+    def begin():
+        lax.fori_loop(1, count, start, 0)
+        got[me] = own[me]
+
+    def end():
+        lax.fori_loop(1, count, wait_recv, 0)
+
+    def drain():
+        lax.fori_loop(1, count, wait_send, 0)
+
+    return begin, end, drain
+
+
+def scan_states(reverse, own, through, out):
+    count, part = out.shape[0], out.shape[2]
+
+    def step(k, state):
+        j = count - 1 - k if reverse else k
+        out[j] = state.astype(BF16)
+        decay = through[j, :, 0:1, :].astype(F32) + through[j, :, 1:2, :].astype(F32)
+        return decay * state + own[j, :, :part, :].astype(F32)
+
+    lax.fori_loop(0, count, step, jnp.zeros(out.shape[1:], F32))
+
+
+def enter_kernel(own, rows_own, before, through, rows_all,
+                 got, scanned, send, recv, send_back, recv_back, here_sem, go, come):
+    z, count = lax.axis_index("head"), lax.axis_size("head")
+    part = scanned.shape[2]
+    greet(("seq", "head"))
+    begin, end, drain = swap_slices(own, got, send, recv)
+    begin()
+    line = Line(rows_own, rows_all, go, come)
+    line.start()
+    here = pltpu.make_async_copy(rows_own, line.at(z), here_sem)
+    here.start()
+    end()
+    through[...] = got[:, :, part:, :]
+    scan_states(False, got, through, scanned)
+    begin_back, end_back, drain_back = swap_slices(scanned, before, send_back, recv_back)
+    begin_back()
+
+    def step(i, _):
+        line.receive(i, near_order(z, count, i))
+        return 0
+
+    lax.fori_loop(1, count, step, 0)
+    end_back()
+    here.wait()
+    line.finish()
+    drain()
+    drain_back()
+
+
+def enter(own, rows_own, part):
+    slices, micro, deep, dk = own.shape
+    rows, width = rows_own.shape
+    count = lax.axis_size("head")
+    vmem, anywhere = pl.BlockSpec(memory_space=pltpu.VMEM), pl.BlockSpec(memory_space=pl.ANY)
+    dma = pltpu.SemaphoreType.DMA
+    return pl.pallas_call(
+        enter_kernel,
+        out_shape=(
+            jax.ShapeDtypeStruct((slices, micro, part, dk), BF16),
+            jax.ShapeDtypeStruct((slices, micro, deep - part, dk), BF16),
+            jax.ShapeDtypeStruct((count * rows, width), BF16),
+        ),
+        in_specs=[vmem, anywhere],
+        out_specs=(vmem, vmem, anywhere),
+        scratch_shapes=[
+            pltpu.VMEM(own.shape, BF16), pltpu.VMEM((slices, micro, part, dk), BF16),
+            dma((slices,)), dma((slices,)), dma((slices,)), dma((slices,)),
+            dma(()), dma((count + 1,)), dma((count,)),
+        ],
+        compiler_params=pltpu.CompilerParams(
+            collective_id=2, has_side_effects=True, vmem_limit_bytes=32 << 20
+        ),
+        cost_estimate=cost(50),
+        name="enter",
+    )(own, rows_own)
+
+
+def leave_kernel(own, through, after, got, scanned, send, recv, send_back, recv_back):
+    greet(("seq",))
+    begin, end, drain = swap_slices(own, got, send, recv)
+    begin()
+    end()
+    scan_states(True, got, through, scanned)
+    begin_back, end_back, drain_back = swap_slices(scanned, after, send_back, recv_back)
+    begin_back()
+    end_back()
+    drain()
+    drain_back()
+
+
+def leave(own, through):
+    vmem = pl.BlockSpec(memory_space=pltpu.VMEM)
+    dma = pltpu.SemaphoreType.DMA
+    slices = own.shape[0]
+    return pl.pallas_call(
+        leave_kernel,
+        out_shape=jax.ShapeDtypeStruct(own.shape, BF16),
+        in_specs=[vmem, vmem],
+        out_specs=vmem,
+        scratch_shapes=[
+            pltpu.VMEM(own.shape, BF16), pltpu.VMEM(own.shape, BF16),
+            dma((slices,)), dma((slices,)), dma((slices,)), dma((slices,)),
+        ],
+        compiler_params=pltpu.CompilerParams(
+            collective_id=3, has_side_effects=True, vmem_limit_bytes=32 << 20
+        ),
+        cost_estimate=cost(25),
+        name="leave",
+    )(own, through)
+
+
+def total_kernel(own, out, from_seq, part, from_head, send_a, recv_a, send_b, recv_b,
+                 send_c, recv_c, send_d, recv_d):
+    seq, head = lax.axis_size("seq"), lax.axis_size("head")
+    s, h = lax.axis_index("seq"), lax.axis_index("head")
+    greet(("seq", "head"))
+
+    def each(axis, me, count, src, dst, send, recv):
+        def copy(hop, index):
+            to = lax.rem(me + hop, count)
+            return push(src(to), dst(index), send.at[hop], recv.at[index], to, axis)
+
+        for hop in range(1, count):
+            copy(hop, me).start()
+        for hop in range(1, count):
+            copy(hop, lax.rem(me + hop, count)).wait_recv()
+        return [copy(hop, me).wait_send for hop in range(1, count)]
+
+    from_seq[s] = own[s]
+    sent = each("seq", s, seq, lambda to: own.at[to], lambda i: from_seq.at[i], send_a, recv_a)
+    part[...] = jnp.sum(from_seq[...], axis=0)
+    from_head[h] = part[h]
+    sent += each("head", h, head, lambda to: part.at[to], lambda i: from_head.at[i], send_b, recv_b)
+    out[s, h] = jnp.sum(from_head[...], axis=0)
+    sent += each("head", h, head, lambda _: out.at[s, h], lambda i: out.at[s, i], send_c, recv_c)
+    sent += each("seq", s, seq, lambda _: out.at[s], lambda i: out.at[i], send_d, recv_d)
+    for wait in sent:
+        wait()
+
+
+def total_of(parts):
+    seq, head = lax.axis_size("seq"), lax.axis_size("head")
     flat = jnp.concatenate([p.reshape(-1) for p in parts])
-    unit = seq * head * 1024
-    length = -(-flat.shape[0] // unit) * unit
-    flat = jnp.pad(flat, (0, length - flat.shape[0]))
-    piece = exchange(flat.reshape(seq, -1, 128), "seq").sum(0)
-    piece = exchange(piece.reshape(head, -1, 128), "head").sum(0)
-    piece = lax.all_gather(piece, "head", axis=0, tiled=True)
-    whole = lax.all_gather(piece, "seq", axis=0, tiled=True).reshape(-1)
+    deep = -(-flat.shape[0] // (seq * head * 1024)) * 8
+    flat = jnp.pad(flat, (0, seq * head * deep * 128 - flat.shape[0]))
+    vmem = pl.BlockSpec(memory_space=pltpu.VMEM)
+    dma = pltpu.SemaphoreType.DMA
+    shape = (seq, head, deep, 128)
+    whole = pl.pallas_call(
+        total_kernel,
+        out_shape=jax.ShapeDtypeStruct(shape, F32),
+        in_specs=[vmem],
+        out_specs=vmem,
+        scratch_shapes=[
+            pltpu.VMEM(shape, F32), pltpu.VMEM(shape[1:], F32), pltpu.VMEM(shape[1:], F32),
+        ]
+        + [dma((n,)) for n in (seq, seq, head, head, head, head, seq, seq)],
+        compiler_params=pltpu.CompilerParams(collective_id=4, has_side_effects=True),
+        cost_estimate=cost(15),
+        name="total",
+    )(flat.reshape(shape)).reshape(-1)
     result, at = [], 0
     for p in parts:
         result.append(whole[at : at + p.size].reshape(p.shape))
         at += p.size
     return result
+
+
+def ffn_kernel(count, x_own, c_all, w, g_x, f_parts, grad,
+               wv, xs, cs, act, lin, parts, landed, turned, turned_c, tiles,
+               w_sem, own_sem, go_sem, x_sem, p_sem, q_sem, o_sem):
+    z = lax.axis_index("head")
+    rows, width = x_own.shape
+    hidden = act.shape[1] // 3
+    chunk = lambda b: pl.ds(pl.multiple_of(b * rows, rows), rows)
+
+    weights = [
+        pltpu.make_async_copy(
+            w.at[:, pl.ds(k * hidden, hidden)], wv.at[:, pl.ds(k * hidden, hidden)], w_sem.at[k]
+        )
+        for k in range(3)
+    ]
+    own = [
+        pltpu.make_async_copy(x_own, xs.at[chunk(z)], own_sem.at[0]),
+        pltpu.make_async_copy(c_all, cs, own_sem.at[1]),
+    ]
+    for copy in own + weights:
+        copy.start()
+    greet(("head",))
+    line = Line(x_own, xs, go_sem, x_sem)
+    line.start()
+    for copy in own + weights:
+        copy.wait()
+
+    pieces = p_sem.shape[1]
+    piece_rows = rows // pieces
+
+    def piece(b, p):
+        start = b * rows + p * piece_rows
+        return pl.ds(pl.multiple_of(start, piece_rows), piece_rows)
+
+    def onward(b, p):
+        to = jnp.where(b > z, z + 1, z - 1)
+        slot = jnp.where((to == b) & (z > b), count, b)
+        return push(
+            parts.at[piece(b, p)], landed.at[piece(slot, p)],
+            p_sem.at[b, p], q_sem.at[slot, p], lax.rem(to + count, count),
+        )
+
+    def arrived(slot, p):
+        at = piece(slot, p)
+        push(landed.at[at], landed.at[at], p_sem.at[0, p], q_sem.at[slot, p], z).wait_recv()
+        return landed[at, :].astype(F32)
+
+    inner = (z > 0) & (z < count - 1)
+
+    def relay(b, p):
+        at = piece(b, p)
+        parts[at, :] = (parts[at, :].astype(F32) + arrived(b, p)).astype(BF16)
+        onward(b, p).start()
+
+    def step(i, _):
+        b = near_order(z, count, i)
+
+        pl.when(i > 0)(lambda: line.receive(i, b))
+
+        at = chunk(b)
+        x = xs[at, :]
+        lin[0] = jnp.dot(x, wv[:, :hidden], preferred_element_type=F32)
+        lin[1] = jnp.dot(x, wv[:, hidden : 2 * hidden], preferred_element_type=F32)
+        lin[2] = jnp.dot(cs[at, :], wv[:, 2 * hidden :], preferred_element_type=F32)
+        band = 16
+
+        def act_rows(r, _):
+            here = pl.ds(pl.multiple_of(r * band, band), band)
+            there = pl.ds(pl.multiple_of(b * rows + r * band, band), band)
+            gate, up, g_product = lin[0, here, :], lin[1, here, :], lin[2, here, :]
+            sig = sigmoid(gate)
+            gated = gate * sig
+            act[there, :hidden] = (g_product * up * sig * (1.0 + gate * (1.0 - sig))).astype(BF16)
+            act[there, hidden : 2 * hidden] = (g_product * gated).astype(BF16)
+            act[there, 2 * hidden :] = (gated * up).astype(BF16)
+            return 0
+
+        lax.fori_loop(0, rows // band, act_rows, 0)
+        parts[at, :] = mm(act[at, : 2 * hidden], wv[:, : 2 * hidden], (1, 1), None).astype(BF16)
+
+        @pl.when((i > 0) & jnp.logical_not(inner))
+        def _():
+            for p in range(pieces):
+                onward(b, p).start()
+
+        return 0
+
+    lax.fori_loop(0, count, step, 0)
+
+    @pl.when(inner)
+    def _():
+        for p in range(pieces):
+            relay(count - 1 - z, p)
+
+    high = tiles.shape[1]
+    steps = width // high
+
+    def store(t, r, k):
+        return pltpu.make_async_copy(
+            tiles.at[lax.rem(t, 2)],
+            grad.at[pl.ds(pl.multiple_of(r * high, high), high), pl.ds(k * hidden, hidden)],
+            o_sem.at[lax.rem(t, 2)],
+        )
+
+    turned[...] = xs[...].T
+    turned_c[...] = cs[...].T
+    far_end = jnp.where(z < count - 1 - z, count - 1, 0)
+
+    def slab(r, _):
+        for k in range(3):
+            t = 3 * r + k
+
+            @pl.when(t >= 2)
+            def _():
+                store(t, r, k).wait()
+
+            left_rows = (turned_c if k == 2 else turned)[
+                pl.ds(pl.multiple_of(r * high, high), high), :
+            ]
+            tiles[lax.rem(t, 2)] = jnp.dot(
+                left_rows, act[:, k * hidden : (k + 1) * hidden], preferred_element_type=F32
+            ).astype(BF16)
+            store(t, r, k).start()
+
+        @pl.when(inner)
+        def _():
+            relay(far_end, r)
+            relay(count - 1 - far_end, r)
+
+        return 0
+
+    lax.fori_loop(0, steps, slab, 0)
+
+    def part(b, _):
+        at = chunk(b)
+        f_parts[b] = mm(act[at, 2 * hidden :], wv[:, 2 * hidden :], (1, 1), None).astype(BF16)
+        return 0
+
+    lax.fori_loop(0, count, part, 0)
+
+    for p in range(pieces):
+        here = pl.ds(p * piece_rows, piece_rows)
+        g_x[here, :] = parts[piece(z, p), :].astype(F32)
+
+        @pl.when(z > 0)
+        def _():
+            g_x[here, :] += arrived(z, p)
+
+        @pl.when(z < count - 1)
+        def _():
+            g_x[here, :] += arrived(count, p)
+
+    def finish(i, _):
+        b = near_order(z, count, i)
+        for p in range(pieces):
+            onward(b, p).wait_send()
+        return 0
+
+    lax.fori_loop(1, count, finish, 0)
+    line.finish()
+    store(3 * steps - 2, 0, 0).wait()
+    store(3 * steps - 1, 0, 0).wait()
+
+
+def feed_forward(x_own, c_all, w, hidden, count):
+    rows, width = x_own.shape
+    group = rows * count
+    assert count == 4 and width % 4 == 0 and rows % 64 == 0
+    anywhere = pl.BlockSpec(memory_space=pl.ANY)
+    vmem = pl.BlockSpec(memory_space=pltpu.VMEM)
+    dma = pltpu.SemaphoreType.DMA
+    return pl.pallas_call(
+        functools.partial(ffn_kernel, count),
+        out_shape=(
+            jax.ShapeDtypeStruct((rows, width), F32),
+            jax.ShapeDtypeStruct((count, rows, width), BF16),
+            jax.ShapeDtypeStruct((width, 3 * hidden), BF16),
+        ),
+        in_specs=[anywhere] * 3,
+        out_specs=(vmem, vmem, anywhere),
+        scratch_shapes=[
+            pltpu.VMEM((width, 3 * hidden), BF16),
+            pltpu.VMEM((group, width), BF16),
+            pltpu.VMEM((group, width), BF16),
+            pltpu.VMEM((group, 3 * hidden), BF16),
+            pltpu.VMEM((3, rows, hidden), F32),
+            pltpu.VMEM((group, width), BF16),
+            pltpu.VMEM((group + rows, width), BF16),
+            pltpu.VMEM((width, group), BF16),
+            pltpu.VMEM((width, group), BF16),
+            pltpu.VMEM((2, width // 4, hidden), BF16),
+            dma((3,)), dma((2,)), dma((count + 1,)), dma((count,)),
+            dma((count, 4)), dma((count + 1, 4)), dma((2,)),
+        ],
+        compiler_params=pltpu.CompilerParams(
+            collective_id=0, has_side_effects=True, vmem_limit_bytes=60 << 20
+        ),
+        cost_estimate=cost(100),
+        name="feed_forward",
+    )(x_own, c_all, w)
+
+
+def exchange(x, axis):
+    return lax.all_to_all(x, axis, split_axis=0, concat_axis=0, tiled=True)
+
+
+def ring(x, axis, hop):
+    count = lax.axis_size(axis)
+    return lax.ppermute(x, axis, [((i + hop) % count, i) for i in range(count)])
+
+
+def gather_weight(w):
+    return lax.all_gather(w, "seq", axis=0, tiled=True)
+
+
+def scatter_grad(g):
+    return lax.psum_scatter(g.astype(BF16), "seq", scatter_dimension=0, tiled=True)
+
+
+def dot(a, b, contract, precision=None):
+    return lax.dot_general(
+        a, b, (((contract[0],), (contract[1],)), ((), ())),
+        precision=precision, preferred_element_type=F32,
+    )
+
+
+def rms(x, epsilon):
+    return lax.rsqrt(jnp.mean(x * x, axis=-1, keepdims=True) + epsilon)
+
+
+def norm_back(grad, gain, normed, inv):
+    scaled = grad * gain
+    inner = jnp.mean(scaled * normed, axis=-1, keepdims=True)
+    return inv * (scaled - normed * inner), jnp.sum(grad * normed, axis=0)
 
 
 def on_device(
@@ -457,31 +932,27 @@
     def own_columns(w, start, size):
         return lax.dynamic_slice_in_dim(w, start + head * size, size, 1)
 
-    mixer = gather_weight(
+    w_in = gather_weight(
         jnp.concatenate(
             [
                 own_columns(mix_in, 0, dk),
                 own_columns(mix_in, keys, dk),
                 own_columns(mix_in, 2 * keys, dv),
                 own_columns(mix_in, 2 * keys + vals, dv),
-                mix_out,
             ],
             axis=1,
         )
     )
-    w_in, w_out = mixer[:, :proj_width], mixer[:, proj_width:]
-    ffn_weights = gather_weight(
-        jnp.concatenate([gate_up.reshape(gate_up.shape[0], 2 * hidden_units), down_proj], axis=1)
-    )
-    w_gu, w_down = ffn_weights[:, : 2 * hidden_units], ffn_weights[:, 2 * hidden_units :]
+    later = gather_weight(
+        jnp.concatenate(
+            [gate_up.reshape(gate_up.shape[0], 2 * hidden_units), down_proj, mix_out], axis=1
+        )
+    )
+    w_out = later[:, 3 * hidden_units :]
     up_own = own_columns(rank_up, 0, dk)
     bias_own = lax.dynamic_slice_in_dim(gate_bias, head * dk, dk, 0)
 
-    all_tokens = gather_rows(tokens, "head").reshape(group, width)
-    all_cot = lax.all_gather(cotangent, "head").reshape(group, width)
-
-    source_all = all_tokens.astype(F32)
-    xn = (source_all * rms(source_all, 1e-6) * norm_gain).astype(BF16)
+    xn = gather_norm(tokens.reshape(micro * rows, width), norm_gain.reshape(1, width))
     qkv = dot(xn, w_in[:, : 2 * dk + dv], (1, 0)).astype(BF16)
     og = dot(xn, w_in[:, 2 * dk + dv :], (1, 0))
     ranked = dot(xn, rank_down, (1, 0))
@@ -494,9 +965,8 @@
     qkv_b, og_b, decays_b = blocks(qkv), blocks(og), blocks(decays)
     gain_row = head_gain.reshape(1, dv)
     part = dv // seq
-    own_states = exchange(states_of(starts, qkv_b, decays_b, dv, seq, 16), "seq")
-    through = own_states[:, :, part:, :]
-    before = exchange(prefix_of(own_states, through, part, False), "seq")
+    own_states = states_of(starts, qkv_b, decays_b, dv, seq, 16)
+    before, through, all_cot = enter(own_states, cotangent.reshape(micro * rows, width), part)
     o_b, gated_b, kept = mix_of(starts, qkv_b, decays_b, og_b, before, gain_row)
 
     gated = exchange(gated_b, "head")
@@ -507,28 +977,9 @@
     plain_ffn = hidden * inv_ffn
     h2 = (plain_ffn * ffn_gain).astype(BF16)
 
-    all_h2 = gather_rows(h2, "head").reshape(group, width)
-    gu = dot(all_h2, w_gu, (1, 0))
-    gate_lin, up_lin = gu[:, :hidden_units], gu[:, hidden_units:]
-    sig = jax.nn.sigmoid(gate_lin)
-    act = gate_lin * sig
-    product = (act * up_lin).astype(BF16)
-    g_product = dot(all_cot, w_down, (1, 0))
-    g_gate = (g_product * up_lin * sig * (1.0 + gate_lin * (1.0 - sig))).astype(BF16)
-    g_up = (g_product * act).astype(BF16)
-    g_gu = jnp.concatenate([g_gate, g_up], axis=1)
-    g_h2_part = dot(g_gu, w_gu, (1, 1)).astype(BF16).reshape(heads, micro * rows, width)
-    g_h2 = exchange(g_h2_part, "head")
-    grad_ffn = weight_grad(all_h2, g_gu, None, 3 * hidden_units, 0, hidden_units)
-    grad_ffn = weight_grad(
-        all_cot, product, grad_ffn, 3 * hidden_units, 2 * hidden_units, hidden_units
-    )
-    ffn_part = dot(product, w_down, (1, 1)).astype(BF16).reshape(heads, micro * rows, width)
-    g_h2, grad_ffn, ffn_part = lax.optimization_barrier((g_h2, grad_ffn, ffn_part))
-    ffn_out = exchange(ffn_part, "head")
+    g_h2, ffn_part, grad_ffn = feed_forward(h2, all_cot, later, hidden_units, heads)
     grad_ffn = scatter_grad(grad_ffn)
 
-    g_h2 = g_h2.astype(F32).sum(0)
     back_ffn, g_ffn_gain = norm_back(g_h2, ffn_gain, plain_ffn, inv_ffn)
     g_hidden = cotangent.astype(F32).reshape(micro * rows, width) + back_ffn
     g_mixed = g_hidden.astype(BF16)
@@ -536,15 +987,17 @@
     grad_mix = weight_grad(g_mixed, gated, None, proj_width + vals, proj_width, dv)
     g_gated = g_gated.reshape(micro, rows, heads, dv).transpose(2, 0, 1, 3)
     g_gated_b = exchange(g_gated, "head")
+    g_gated_b, ffn_part = lax.optimization_barrier((g_gated_b, ffn_part))
+    ffn_out = ffn_part[head].astype(F32)
+    for hop in range(1, heads):
+        ffn_out += ring(ffn_part[lax.rem(head + heads - hop, heads)], "head", hop).astype(F32)
     g_og_b, g_o_b, pulled, g_head_gain = gate_back_of(
         starts, g_gated_b, og_b, o_b, qkv_b, decays_b, gain_row, seq
     )
-    own_pulled = exchange(pulled, "seq")
-    after = exchange(prefix_of(own_pulled, through, part, True), "seq")
+    after = leave(pulled, through)
     g_proj_b, g_logits_b = mix_back_of(
         starts, qkv_b, decays_b, g_o_b, g_og_b, kept, after, blocks(logits)
     )
-    g_proj_b, g_logits_b, ffn_out = lax.optimization_barrier((g_proj_b, g_logits_b, ffn_out))
     g_proj, g_logits = g_proj_b.reshape(group, proj_width), g_logits_b.reshape(group, dk)
     g_ranked = dot(g_logits, up_own, (1, 1), HIGHEST)
     g_xn_part = dot(g_proj, w_in, (1, 1)) + dot(
@@ -552,7 +1005,7 @@
     )
     g_xn_part = g_xn_part.astype(BF16).reshape(heads, micro * rows, width)
     g_xn = exchange(g_xn_part, "head").astype(F32).sum(0)
-    output = (hidden + ffn_out.astype(F32).sum(0)).astype(BF16)
+    output = (hidden + ffn_out).astype(BF16)
     inv_in = rms(source, 1e-6)
     back_in, g_norm_gain = norm_back(g_xn, norm_gain, source * inv_in, inv_in)
     input_grad = g_hidden + back_in
@@ -576,7 +1029,7 @@
         jnp.zeros(gate_bias.shape, F32), g_logits.sum(0), head * dk, 0
     )
     small = total_of(
-        [g_norm_gain, g_ffn_gain, g_head_gain[0], g_rank_down, g_rank_up, g_bias], seq, heads
+        [g_norm_gain, g_ffn_gain, g_head_gain[0], g_rank_down, g_rank_up, g_bias]
     )
     return (
         output.reshape(tokens.shape),

time: 864 us -> 722 us (0.84)
  Pallas kernels: 115 us -> 438 us
  waiting for transfers between devices: 317 us -> 73.1 us
  blocking collectives: 170 us -> 26.2 us
  matrix products: 105 us -> 48 us
  other arithmetic: 36.4 us -> 25.4 us
  starting transfers between devices: 52.7 us -> 42.5 us
    pallas_call x2 -> x5, Pallas kernels: 0.52 us -> 349 us  [the longest x1 122 us: feed_forward(): pl.pallas_call(functools.partial(ffn_kernel, count), out_shape=(jax.Shape...]
    all_to_all x9 -> x3, waiting for transfers between devices: 316 us -> 56.7 us  [exchange(): return lax.all_to_all(x, axis, split_axis=0, concat_axis=0, tiled=True)]
    all_to_all x5 -> x1, blocking collectives: 119 us -> 26.2 us  [exchange(): return lax.all_to_all(x, axis, split_axis=0, concat_axis=0, tiled=True)]
    dot_general x15 -> x11, matrix products: 105 us -> 48 us  [dot(): lax.dot_general(a, b, (((contract[0],), (contract[1],)), ((), ())), preci...]
    all_gather x2 -> x0, blocking collectives: 50.9 us -> none  [the longest x1 41.8 us: total_of(): piece = lax.all_gather(piece, 'head', axis=0, tiled=True)]
    pallas_call x4 -> x2, Pallas kernels: 46.1 us -> 20.7 us  [weight_grad(): pl.pallas_call(weight_grad_kernel, out_shape=jax.ShapeDtypeStruct((rows,...]
    reduce_scatter x2, waiting for transfers between devices: 0.01 us -> 16.3 us  [scatter_grad(): lax.psum_scatter(g.astype(BF16), 'seq', scatter_dimension=0, tiled=True)]
    reduce_scatter x2, starting transfers between devices: 11.7 us -> 0.5 us  [scatter_grad(): lax.psum_scatter(g.astype(BF16), 'seq', scatter_dimension=0, tiled=True)]
  transfers between devices with their start and end apart: 14 -> 10, of which waited for: 8 -> 4; matrix products, arithmetic and copies ran while one was open for 15% -> 13% of each run, Pallas kernels for 14% -> 44%
where the time goes in v3:
time: 722 us; the launch traced here: 713 us
  Pallas kernels  438 us (61%)
  waiting for transfers between devices  73.1 us (10%)
  matrix products  48 us (7%)
  local copies, waits for them, and re-layouts  45.5 us (6%)
  starting transfers between devices  42.5 us (6%)
  blocking collectives  26.2 us (4%)
  other arithmetic  25.4 us (4%)
  between operations  14.5 us (2%)
    pallas_call x1, Pallas kernels, feed_forward(): pl.pallas_call(functools.partial(ffn_kernel, count), out_shape=(jax.Shape...  122 us
    pallas_call x1, Pallas kernels, total_of(): pl.pallas_call(total_kernel, out_shape=jax.ShapeDtypeStruct(shape, F32),...  73.8 us
    pallas_call x1, Pallas kernels, gather_norm(): pl.pallas_call(gather_norm_kernel, out_shape=jax.ShapeDtypeStruct((count...  60.8 us
    all_to_all x3, waiting for transfers between devices, exchange(): return lax.all_to_all(x, axis, split_axis=0, concat_axis=0, tiled=True)  56.7 us
    pallas_call x1, Pallas kernels, enter(): pl.pallas_call(enter_kernel, out_shape=(jax.ShapeDtypeStruct((slices, mic...  56.5 us
    dot_general x11, matrix products, dot(): lax.dot_general(a, b, (((contract[0],), (contract[1],)), ((), ())), preci...  48 us
    all_to_all x3, starting transfers between devices, exchange(): return lax.all_to_all(x, axis, split_axis=0, concat_axis=0, tiled=True)  36.9 us
    pallas_call x1, Pallas kernels, leave(): pl.pallas_call(leave_kernel, out_shape=jax.ShapeDtypeStruct(own.shape, BF...  35.6 us
  transfers between devices with their start and end apart: 10, of which 4 were waited for; matrix products, arithmetic and copies ran while one was open for 13% of the time, Pallas kernels for 44%

profile of v3, /device:TPU:0, one launch (start us, length us, event | category | flops | bytes accessed | tf_op | source)
XLA Modules:
  0.0 713.3 jit_solution(15298823220370246386)
XLA Ops:
  15.5 60.8 %gather_norm.1.left = bf16[768,2048]{1,0:T(8,128)(2,1)S(1)} custom-call(bf16[192,2048]{1,0:T(8,128)(2,1)S(1)} %bitcast.93, f32[1,2048]{1,0:T(1,128)S(1)} %bitcast.108), custom_call_target="tpu_custom_call" | custom-call | bytes 150000000 | tf_op jit(solution)/shard_map/gather_norm/pallas_call | solution.py:476
  77.9 3.0 fusion.27
  80.9 5.6 fusion.14
  86.6 9.6 %states.1.own = bf16[8,3,80,256]{3,2,1,0:T(8,128)(2,1)S(1)} custom-call(s32[3,4]{1,0:T(4,128)S(1)} %copy-done.22, bf16[4,3,64,1024]{3,2,1,0:T(8,128)(2,1)S(1)} %bitcast.88, bf16[4,3,64,256]{3,2,1,0:T(8,128)(2,1)S(1)} %bitcast.97), custom_call_target="tpu_custom_call" | custom-call | bytes 30000000 | tf_op jit(solution)/shard_map/states/pallas_call | solution.py:219
  96.2 56.5 %enter.1 = (bf16[8,3,64,256]{3,2,1,0:T(8,128)(2,1)S(1)}, bf16[8,3,16,256]{3,2,1,0:T(8,128)(2,1)S(1)}, bf16[768,2048]{1,0:T(8,128)(2,1)S(1)}) custom-call(bf16[8,3,80,256]{3,2,1,0:T(8,128)(2,1)S(1)} %states.1.own, bf16[192,2048]{1,0:T(8,128)(2,1)S(1)} %bitcast.96), custom_call_target="tpu_custom_call" | custom-call | bytes 150000000 | tf_op jit(solution)/shard_map/enter/pallas_call | solution.py:571
  152.8 5.7 fusion.12
  158.5 18.1 %mix.1 = (f32[4,3,64,512]{3,2,1,0:T(8,128)S(1)}, bf16[4,3,64,512]{3,2,1,0:T(8,128)(2,1)S(1)}, f32[4,3,512,256]{3,2,1,0:T(8,128)}) custom-call(s32[3,4]{1,0:T(4,128)S(1)} %copy-done.22, bf16[4,3,64,1024]{3,2,1,0:T(8,128)(2,1)S(1)} %bitcast.89, bf16[4,3,64,256]{3,2,1,0:T(8,128)(2,1)S(1)} %bitcast.98, f32[4,3,64,512]{3,2,1,0:T(8,128)} %bitcast.101, ...), custom_call_target="tpu_custom_call" | custom-call | bytes 54000000 | tf_op jit(solution)/shard_map/mix/pallas_call | solution.py:239
  176.6 26.2 %all_to_all.20 = bf16[4,3,64,512]{3,2,1,0:T(8,128)(2,1)S(1)} all-to-all(bf16[4,3,64,512]{3,2,1,0:T(8,128)(2,1)S(1)} %get-tuple-element.32), channel_id=1, replica_groups=mesh['seq'=8,'head'=4] {'head'}, dimensions={0} | all-to-all | bytes 1572864 | tf_op jit(solution)/shard_map/all_to_all | solution.py:886
  204.5 6.9 multiply_reduce_fusion.5
  213.7 121.8 %feed_forward.1 = (f32[192,2048]{1,0:T(8,128)}, bf16[4,192,2048]{2,1,0:T(8,128)(2,1)}, bf16[2048,4224]{1,0:T(8,128)(2,1)}) custom-call(bf16[192,2048]{1,0:T(8,128)(2,1)} %multiply_convert_fusion.x_own, bf16[768,2048]{1,0:T(8,128)(2,1)} %copy-done.16, bf16[2048,6272]{1,0:T(8,128)(2,1)} %all-gather.5.cloned.1.call-done.w), custom_call_target="tpu_custom_call" | custom-call | bytes 300000000 | tf_op jit(solution)/shard_map/feed_forward/pallas_call | solution.py:854
  340.0 6.8 fusion.9
  347.7 3.1 reshape.189
  353.1 7.7 %all-to-all-start.1 = ((bf16[4,3,64,512]{3,2,1,0:T(8,128)(2,1)}), bf16[4,3,64,512]{3,2,1,0:T(8,128)(2,1)}, u32[]{:S(2)}, u32[]{:S(2)}) async-start(bf16[4,3,64,512]{3,2,1,0:T(8,128)(2,1)} %bitcast.114), calls=%async_computation.1 | async-start | bytes 1572864 | tf_op jit(solution)/shard_map/all_to_all | solution.py:886
  363.7 10.1 %weight_grad.2.rest_0_ = bf16[2048,3584]{1,0:T(8,128)(2,1)} custom-call(bf16[192,2048]{1,0:T(8,128)(2,1)S(1)} %copy-done.15, bf16[192,2048]{1,0:T(8,128)(2,1)S(1)} %bitcast.104), custom_call_target="tpu_custom_call" | custom-call | flops 1610612736 | bytes 9961472 | tf_op jit(solution)/shard_map/weight_grad/pallas_call | solution.py:349
  376.4 13.0 %gate_back.1 = (bf16[4,3,64,512]{3,2,1,0:T(8,128)(2,1)S(1)}, f32[4,3,64,512]{3,2,1,0:T(8,128)S(1)}, bf16[8,3,64,256]{3,2,1,0:T(8,128)(2,1)S(1)}, f32[8,512]{1,0:T(8,128)S(1)}) custom-call(s32[3,4]{1,0:T(4,128)S(1)} %copy-done.22, bf16[4,3,64,512]{3,2,1,0:T(8,128)(2,1)} %all-to-all-done.1.g_gated, f32[4,3,64,512]{3,2,1,0:T(8,128)S(1)} %bitcast.102, ...), custom_call_target="tpu_custom_call" | custom-call | bytes 36000000 | tf_op jit(solution)/shard_map/gate_back/pallas_call | solution.py:269
  390.5 35.6 %leave.1.after = bf16[8,3,64,256]{3,2,1,0:T(8,128)(2,1)S(1)} custom-call(bf16[8,3,64,256]{3,2,1,0:T(8,128)(2,1)S(1)} %get-tuple-element.42.own, bf16[8,3,16,256]{3,2,1,0:T(8,128)(2,1)S(1)} %get-tuple-element.43.through), custom_call_target="tpu_custom_call" | custom-call | bytes 75000000 | tf_op jit(solution)/shard_map/leave/pallas_call | solution.py:610
  426.2 28.1 %mix_back.1 = (bf16[4,3,64,1536]{3,2,1,0:T(8,128)(2,1)}, f32[4,3,64,256]{3,2,1,0:T(8,128)S(1)}) custom-call(s32[3,4]{1,0:T(4,128)S(1)} %copy-done.22, bf16[4,3,64,1024]{3,2,1,0:T(8,128)(2,1)S(1)} %bitcast.91, bf16[4,3,64,256]{3,2,1,0:T(8,128)(2,1)S(1)} %bitcast.100, f32[4,3,64,512]{3,2,1,0:T(8,128)} %copy-done.18, ...), custom_call_target="tpu_custom_call" | custom-call | bytes 84000000 | tf_op jit(solution)/shard_map/mix_back/pallas_call | solution.py:307
  456.8 10.6 %weight_grad.3 = bf16[2048,3584]{1,0:T(8,128)(2,1)} custom-call(bf16[768,2048]{1,0:T(8,128)(2,1)S(1)} %gather_norm.1.left, bf16[768,1536]{1,0:T(8,128)(2,1)S(1)} %bitcast.106, bf16[2048,3584]{1,0:T(8,128)(2,1)} %weight_grad.2.rest_0_), custom_call_target="tpu_custom_call", output_to_operand_aliasing={{}: (2, {})} | custom-call | flops 4831838208 | bytes 11796480 | tf_op jit(solution)/shard_map/weight_grad/pallas_call | solution.py:349
  467.4 4.6 reduce-scatter.3.cloned.1.call-done
  473.8 7.9 %fusion.36 = f32[768,2048]{1,0:T(8,128)S(1)} fusion(bf16[768,1536]{1,0:T(8,128)(2,1)} %bitcast.105, bf16[2048,1536]{1,0:T(8,128)(2,1)} %all-gather.3.cloned.1.call-done), kind=kOutput, calls=%fused_computation.73 | convolution fusion | flops 4831838208 | bytes 14942208 | tf_op jit(solution)/shard_map/dot_general | solution.py:903
  481.8 4.4 add_convert_fusion
  486.2 5.0 all-to-all-start.2
  492.8 4.3 fusion.37
  499.4 3.1 dynamic-slice_bitcast_fusion.2
  502.6 3.9 collective-permute-start
  507.8 56.6 %all-to-all-done.2 = bf16[4,192,2048]{2,1,0:T(8,128)(2,1)} async-done(((bf16[4,192,2048]{2,1,0:T(8,128)(2,1)}), bf16[4,192,2048]{2,1,0:T(8,128)(2,1)}, u32[]{:S(2)}, u32[]{:S(2)}) %all-to-all-start.2) | async-done | bytes 3145760 | tf_op jit(solution)/shard_map/all_to_all | solution.py:886
  567.5 11.8 %reduce-scatter.5.cloned.1.call-done = bf16[256,3584]{1,0:T(8,128)(2,1)} async-done(((bf16[2048,3584]{1,0:T(8,128)(2,1)}), bf16[256,3584]{1,0:T(8,128)(2,1)}) %reduce-scatter.5.cloned.1.call-update) | async-done | bytes 1835024 | tf_op jit(solution)/shard_map/reduce_scatter | solution.py:899
  579.3 24.2 %all-to-all-start.3 = ((bf16[4,64,3584]{2,1,0:T(8,128)(2,1)}), bf16[4,64,3584]{2,1,0:T(8,128)(2,1)}, u32[]{:S(2)}, u32[]{:S(2)}) async-start(bf16[4,64,3584]{2,1,0:T(8,128)(2,1)} %bitcast.119), calls=%async_computation.5 | async-start | bytes 3670016 | tf_op jit(solution)/shard_map/all_to_all | solution.py:886
  604.3 73.8 %total.1 = f32[8,4,16,128]{3,2,1,0:T(8,128)} custom-call(f32[8,4,16,128]{3,2,1,0:T(8,128)} %bitcast.128), custom_call_target="tpu_custom_call" | custom-call | bytes 45000000 | tf_op jit(solution)/shard_map/total/pallas_call | solution.py:664
  678.2 2.8 slice.73
  691.1 5.8 fusion.24
  697.1 2.8 reshape.210
  (139 shorter events, 58.5 us)
Async XLA Ops:
  7.2 69.8 %copy-start = (bf16[2048,16]{0,1:T(8,128)(2,1)S(1)}, bf16[2048,16]{0,1:T(8,128)(2,1)}, u32[]{:S(2)}) copy-start(bf16[2048,16]{0,1:T(8,128)(2,1)} %param.23) | copy-start | bytes 196612
  7.2 73.7 %all-gather.3.cloned.1.call-start = ((), (), s32[]{:S(2)}) async-start(), calls=%async_computation.6 | async-start | bytes 7077888 | tf_op jit(solution)/shard_map/all_gather | solution.py:895
  8.2 2.2 copy-start.29
  10.4 1.4 copy-start.31
  10.4 194.1 %all-gather.5.cloned.1.call-start = ((), (), s32[]{:S(2)}) async-start(), calls=%async_computation.7 | async-start | bytes 28901376 | tf_op jit(solution)/shard_map/all_gather | solution.py:895
  13.7 458.3 %reduce-scatter.3.cloned.1.call-start = ((), (), s32[]{:S(2)}) async-start(), calls=%async_computation.8 | async-start | bytes 19464192 | tf_op jit(solution)/shard_map/reduce_scatter | solution.py:899
  80.9 5.7 copy-start.22
  80.9 5.7 copy-start.10
  86.5 72.0 %copy-start.1 = (bf16[768,1024]{1,0:T(8,128)(2,1)}, bf16[768,1024]{1,0:T(8,128)(2,1)S(1)}, u32[]{:S(2)}) copy-start(bf16[768,1024]{1,0:T(8,128)(2,1)S(1)} %fusion.14) | copy-start | bytes 4718596
  86.5 9.7 %copy-start.7 = (bf16[3,64,2048]{2,1,0:T(8,128)(2,1)S(1)}, bf16[3,64,2048]{2,1,0:T(8,128)(2,1)}, u32[]{:S(2)}) copy-start(bf16[3,64,2048]{2,1,0:T(8,128)(2,1)} %param.15) | copy-start | bytes 2359300
  152.8 5.7 copy-start.16
  152.8 5.7 copy-start.23
  176.6 26.8 %copy-start.19 = (f32[4,3,64,512]{3,2,1,0:T(8,128)}, f32[4,3,64,512]{3,2,1,0:T(8,128)S(1)}, u32[]{:S(2)}) copy-start(f32[4,3,64,512]{3,2,1,0:T(8,128)S(1)} %get-tuple-element.38.o_in) | copy-start | bytes 4718596
  204.5 8.1 %copy-start.32 = (f32[2048]{0:T(1024)S(1)}, f32[2048]{0:T(1024)}, u32[]{:S(2)}) copy-start(f32[2048]{0:T(1024)} %param.21) | copy-start | bytes 24580
  335.5 2.6 copy-start.8
  335.5 2.6 copy-start.25
  353.1 20.9 %all-to-all-start.1 = ((bf16[4,3,64,512]{3,2,1,0:T(8,128)(2,1)}), bf16[4,3,64,512]{3,2,1,0:T(8,128)(2,1)}, u32[]{:S(2)}, u32[]{:S(2)}) async-start(bf16[4,3,64,512]{3,2,1,0:T(8,128)(2,1)} %bitcast.114), calls=%async_computation.1 | async-start | bytes 1572864 | tf_op jit(solution)/shard_map/all_to_all | solution.py:886
  360.8 218.5 %reduce-scatter.5.cloned.1.call-start = ((), (), s32[]{:S(2)}) async-start(), calls=%async_computation.9 | async-start | bytes 16515072 | tf_op jit(solution)/shard_map/reduce_scatter | solution.py:899
  376.4 49.7 %copy-start.20 = (f32[768,256]{1,0:T(8,128)S(1)}, f32[768,256]{1,0:T(8,128)}, u32[]{:S(2)}) copy-start(f32[768,256]{1,0:T(8,128)} %get-tuple-element.82) | copy-start | bytes 2359300
  390.5 35.6 %copy-start.2 = (bf16[768,1024]{1,0:T(8,128)(2,1)S(1)}, bf16[768,1024]{1,0:T(8,128)(2,1)}, u32[]{:S(2)}) copy-start(bf16[768,1024]{1,0:T(8,128)(2,1)} %copy-done.1) | copy-start | bytes 4718596
  455.1 1.7 copy-start.17
  486.2 78.1 %all-to-all-start.2 = ((bf16[4,192,2048]{2,1,0:T(8,128)(2,1)}), bf16[4,192,2048]{2,1,0:T(8,128)(2,1)}, u32[]{:S(2)}, u32[]{:S(2)}) async-start(bf16[4,192,2048]{2,1,0:T(8,128)(2,1)} %bitcast.112), calls=%async_computation.2 | async-start | bytes 6291456 | tf_op jit(solution)/shard_map/all_to_all | solution.py:886
  497.2 1.7 copy-start.6
  502.6 188.5 %collective-permute-start = (bf16[192,2048]{1,0:T(8,128)(2,1)}, bf16[192,2048]{1,0:T(8,128)(2,1)}, u32[]{:S(2)}, u32[]{:S(2)}) collective-permute-start(bf16[192,2048]{1,0:T(8,128)(2,1)} %get-tuple-element.70), channel_id=1, source_target_pairs={{1,0},{2,1},{3,2},{0,3},{5,4},{6,5},{7,6},{4,7},{9,8},{10,9},{11,1... | collective-permute-start | bytes 2359304 | tf_op jit(solution)/shard_map/ppermute | solution.py:891
  506.4 184.6 %collective-permute-start.1 = (bf16[192,2048]{1,0:T(8,128)(2,1)}, bf16[192,2048]{1,0:T(8,128)(2,1)}, u32[]{:S(2)}, u32[]{:S(2)}) collective-permute-start(bf16[192,2048]{1,0:T(8,128)(2,1)} %get-tuple-element.72), channel_id=1, source_target_pairs={{2,0},{3,1},{0,2},{1,3},{6,4},{7,5},{4,6},{5,7},{10,8},{11,9},{8,1... | collective-permute-start | bytes 2359304 | tf_op jit(solution)/shard_map/ppermute | solution.py:891
  506.4 184.6 %collective-permute-start.2 = (bf16[192,2048]{1,0:T(8,128)(2,1)}, bf16[192,2048]{1,0:T(8,128)(2,1)}, u32[]{:S(2)}, u32[]{:S(2)}) collective-permute-start(bf16[192,2048]{1,0:T(8,128)(2,1)} %get-tuple-element.71), channel_id=1, source_target_pairs={{3,0},{0,1},{1,2},{2,3},{7,4},{4,5},{5,6},{6,7},{11,8},{8,9},{9,10... | collective-permute-start | bytes 2359304 | tf_op jit(solution)/shard_map/ppermute | solution.py:891
  507.7 59.2 %copy-start.4 = (bf16[3,64,2048]{2,1,0:T(8,128)(2,1)S(1)}, bf16[3,64,2048]{2,1,0:T(8,128)(2,1)}, u32[]{:S(2)}) copy-start(bf16[3,64,2048]{2,1,0:T(8,128)(2,1)} %param.13) | copy-start | bytes 2359300
  567.0 12.3 %copy-start.27 = (f32[192,2048]{1,0:T(8,128)}, f32[192,2048]{1,0:T(8,128)S(1)}, u32[]{:S(2)}) copy-start(f32[192,2048]{1,0:T(8,128)S(1)} %convert_reduce_fusion) | copy-start | bytes 4718596
  579.3 122.9 %all-to-all-start.3 = ((bf16[4,64,3584]{2,1,0:T(8,128)(2,1)}), bf16[4,64,3584]{2,1,0:T(8,128)(2,1)}, u32[]{:S(2)}, u32[]{:S(2)}) async-start(bf16[4,64,3584]{2,1,0:T(8,128)(2,1)} %bitcast.119), calls=%async_computation.5 | async-start | bytes 3670016 | tf_op jit(solution)/shard_map/all_to_all | solution.py:886
  684.4 6.7 copy-start.9
  684.4 6.7 copy-start.26
  691.1 5.9 copy-start.28
  (11 other events, 12.0 us)
Sparse Core Ops, SparseCore 0:
  10.5 48.2 all-gather.2
  60.7 138.9 all-gather.4
  335.6 136.2 reduce-scatter.2
  475.7 103.5 reduce-scatter.4

commit v4 on v3

--- a/solution.py
+++ b/solution.py
@@ -99,97 +99,6 @@
     gated[0, 0] = (normed * gate * sigmoid(gate)).astype(BF16)
 
 
-def gate_back_kernel(flags, g_gated, og, o_in, qkv, decay, gain, g_og, g_o, pulled, g_gain,
-                     state, total_run):
-    m, b = pl.program_id(0), pl.program_id(1)
-    last = pl.num_programs(1) - 1
-    dk, dv = decay.shape[-1], og.shape[-1]
-
-    @pl.when((m == 0) & (b == 0))
-    def _():
-        g_gain[...] = jnp.zeros_like(g_gain)
-
-    @pl.when(b == 0)
-    def _():
-        state[...] = jnp.zeros_like(state)
-        total_run[0:1, :] = jnp.zeros((1, dk), F32)
-        total_run[1:2, :] = jnp.ones((1, dk), F32)
-
-    gate = og[0, 0]
-    grad = g_gated[0, 0].astype(F32)
-    sig = sigmoid(gate)
-    o = o_in[0, 0]
-    scale = lax.rsqrt(jnp.mean(o * o, axis=-1, keepdims=True) + 1e-5)
-    plain = o * scale
-    normed = (plain * gain[...]).astype(BF16).astype(F32)
-    g_on = (grad * gate * sig).astype(BF16).astype(F32)
-    g_og[0, 0] = (grad * normed * sig * (1.0 + gate * (1.0 - sig))).astype(BF16)
-    scaled = g_on * gain[...]
-    inner = jnp.mean(scaled * plain, axis=-1, keepdims=True)
-    go = scale * (scaled - plain * inner)
-    g_o[0, 0] = go
-    g_gain[0:1, :] += jnp.sum(g_on * plain, axis=0, keepdims=True)
-
-    total_run[1:2, :] *= 1.0 - flags[m, b].astype(F32)
-    run = running(decay[0, 0])
-    reach = (
-        qkv[0, 0, :, :dk].astype(F32)
-        * jnp.exp(run + total_run[0:1, :])
-        * total_run[1:2, :]
-        * dk ** (-0.5)
-    )
-    state[...] += mm(go, reach, (0, 0))
-    total_run[0:1, :] += run[-1:, :]
-
-    @pl.when(b == last)
-    def _():
-        slices, part = pulled.shape[0], dv // pulled.shape[0]
-        for i in range(slices):
-            pulled[i, 0] = state[i * part : (i + 1) * part, :].astype(BF16)
-
-
-def mix_back_kernel(flags, qkv, decay, g_o, g_og, kept, after, logits, g_proj, g_logits, g_state):
-    m, step = pl.program_id(0), pl.program_id(1)
-    b = pl.num_programs(1) - 1 - step
-    dk, dv = decay.shape[-1], g_o.shape[-1]
-    q = qkv[0, 0, :, :dk].astype(F32)
-    k = qkv[0, 0, :, dk : 2 * dk].astype(F32)
-    v = qkv[0, 0, :, 2 * dk :].astype(F32)
-    keep = 1.0 - flags[m, b].astype(F32)
-
-    @pl.when(step == 0)
-    def _():
-        g_state[...] = after[:, 0].astype(F32).reshape(dv, dk)
-
-    go, gs, entry = g_o[0, 0], g_state[...], kept[0, 0]
-    run = running(decay[0, 0])
-    total = run[-1:, :]
-    up, down, rest = jnp.exp(run) * dk ** (-0.5), jnp.exp(-run), jnp.exp(total - run)
-    decayed = jnp.exp(total)
-    queried, keyed, carried = q * up, k * down, k * rest
-    causal = lower_ones(q.shape[0])
-    scores = jnp.where(causal, mm(queried, keyed, (1, 1)), 0.0)
-    g_scores = jnp.where(causal, mm(go, v, (1, 1)), 0.0)
-    g_queried = mm(g_scores, keyed, (1, 0)) + mm(go, entry, (1, 0))
-    g_keyed = mm(g_scores, queried, (0, 0))
-    g_v = mm(scores, go, (0, 0)) + mm(carried, gs, (1, 1))
-    g_carried = mm(v, gs, (1, 0))
-    g_state[...] = (decayed * gs + mm(go, queried, (0, 0))) * keep
-    from_carried = g_carried * carried
-    g_total = (
-        jnp.sum(decayed * entry * gs, axis=0, keepdims=True)
-        + jnp.sum(from_carried, axis=0, keepdims=True)
-    )
-    g_run = g_queried * queried - g_keyed * keyed - from_carried
-    later = mm(causal.astype(F32), g_run, (0, 0)) + g_total
-    proj = jnp.concatenate([g_queried * up, g_keyed * down + g_carried * rest, g_v], axis=1)
-    width = proj.shape[1]
-    g_proj[0, 0, :, :width] = proj.astype(BF16)
-    g_proj[0, 0, :, width:] = g_og[0, 0]
-    low = later.astype(BF16).astype(F32)
-    g_logits[0, 0] = low * sigmoid(-logits[0, 0]) * (1.0 / GATE_NORM)
-
-
 def params(limit=48):
     return pltpu.CompilerParams(
         dimension_semantics=("arbitrary", "arbitrary"), vmem_limit_bytes=limit << 20
@@ -202,10 +111,6 @@
 
 def per_block(rows, width):
     return pl.BlockSpec((1, 1, rows, width), lambda m, b, *_: (b, m, 0, 0))
-
-
-def backwards(rows, width, count):
-    return pl.BlockSpec((1, 1, rows, width), lambda m, b, *_: (count - 1 - b, m, 0, 0))
 
 
 def per_batch(slices, rows, width):
@@ -262,112 +167,6 @@
     )(flags, qkv, decays, og, before, gain)
 
 
-def gate_back_of(flags, g_gated, og, o, qkv, decays, gain, slices):
-    blocks, micro, rows, width = qkv.shape
-    dk, dv = decays.shape[-1], og.shape[-1]
-    part = dv // slices
-    return pl.pallas_call(
-        gate_back_kernel,
-        out_shape=(
-            jax.ShapeDtypeStruct((blocks, micro, rows, dv), BF16),
-            jax.ShapeDtypeStruct((blocks, micro, rows, dv), F32),
-            jax.ShapeDtypeStruct((slices, micro, part, dk), BF16),
-            jax.ShapeDtypeStruct((8, dv), F32),
-        ),
-        grid_spec=pltpu.PrefetchScalarGridSpec(
-            num_scalar_prefetch=1,
-            grid=(micro, blocks),
-            in_specs=[
-                per_block(rows, dv),
-                per_block(rows, dv),
-                per_block(rows, dv),
-                per_block(rows, width),
-                per_block(rows, dk),
-                pl.BlockSpec((1, dv), lambda m, b, *_: (0, 0)),
-            ],
-            out_specs=(
-                per_block(rows, dv),
-                per_block(rows, dv),
-                per_batch(slices, part, dk),
-                pl.BlockSpec((8, dv), lambda m, b, *_: (0, 0)),
-            ),
-            scratch_shapes=[pltpu.VMEM((dv, dk), F32), pltpu.VMEM((8, dk), F32)],
-        ),
-        compiler_params=params(),
-        cost_estimate=cost(12),
-        name="gate_back",
-    )(flags, g_gated, og, o, qkv, decays, gain)
-
-
-def mix_back_of(flags, qkv, decays, g_o, g_og, kept, after, logits):
-    blocks, micro, rows, width = qkv.shape
-    dk, dv = decays.shape[-1], g_o.shape[-1]
-    slices, _, part, _ = after.shape
-    back = functools.partial(backwards, count=blocks)
-    return pl.pallas_call(
-        mix_back_kernel,
-        out_shape=(
-            jax.ShapeDtypeStruct((blocks, micro, rows, width + dv), BF16),
-            jax.ShapeDtypeStruct((blocks, micro, rows, dk), F32),
-        ),
-        grid_spec=pltpu.PrefetchScalarGridSpec(
-            num_scalar_prefetch=1,
-            grid=(micro, blocks),
-            in_specs=[
-                back(rows, width),
-                back(rows, dk),
-                back(rows, dv),
-                back(rows, dv),
-                back(dv, dk),
-                per_batch(slices, part, dk),
-                back(rows, dk),
-            ],
-            out_specs=(back(rows, width + dv), back(rows, dk)),
-            scratch_shapes=[pltpu.VMEM((dv, dk), F32)],
-        ),
-        compiler_params=params(),
-        cost_estimate=cost(28),
-        name="mix_back",
-    )(flags, qkv, decays, g_o, g_og, kept, after, logits)
-
-
-def weight_grad_kernel(left, right, *rest):
-    out, turned = rest[-2:]
-
-    @pl.when(pl.program_id(1) == 0)
-    def _():
-        turned[...] = left[...].T
-
-    out[...] = jnp.dot(turned[...], right[...], preferred_element_type=F32).astype(BF16)
-
-
-def weight_grad(left, right, into, columns, start, tile):
-    depth, rows = left.shape
-    high = min(rows, 512)
-    first = start // tile
-    given = () if into is None else (into,)
-    return pl.pallas_call(
-        weight_grad_kernel,
-        out_shape=jax.ShapeDtypeStruct((rows, columns), BF16),
-        grid=(rows // high, right.shape[1] // tile),
-        in_specs=[
-            pl.BlockSpec((depth, high), lambda i, j: (0, i)),
-            pl.BlockSpec((depth, tile), lambda i, j: (0, j)),
-        ]
-        + [pl.BlockSpec(memory_space=pl.ANY) for _ in given],
-        out_specs=pl.BlockSpec((high, tile), lambda i, j: (i, first + j)),
-        scratch_shapes=[pltpu.VMEM((high, depth), BF16)],
-        input_output_aliases={2: 0} if given else {},
-        compiler_params=params(),
-        cost_estimate=pl.CostEstimate(
-            flops=2 * depth * rows * right.shape[1],
-            bytes_accessed=2 * (depth * rows + (depth + rows) * right.shape[1]),
-            transcendentals=0,
-        ),
-        name="weight_grad",
-    )(left, right, *given)
-
-
 def greet(axes):
     barrier = pltpu.get_barrier_semaphore()
     met = 0
@@ -438,6 +237,72 @@
         lax.fori_loop(1, self.count, sent, 0)
         pl.when(self.z < self.count - 1)(self.right.wait_send)
         pl.when(self.z > 0)(self.left.wait_send)
+
+
+class LineSum:
+    def __init__(self, parts, landed, send, recv, rows):
+        self.parts, self.landed, self.send, self.recv = parts, landed, send, recv
+        self.z, self.count = lax.axis_index("head"), lax.axis_size("head")
+        self.rows, self.pieces = rows, send.shape[1]
+        self.deep = rows // self.pieces
+        self.inner = (self.z > 0) & (self.z < self.count - 1)
+        self.far_end = jnp.where(self.z < self.count - 1 - self.z, self.count - 1, 0)
+
+    def piece(self, b, p):
+        return pl.ds(pl.multiple_of(b * self.rows + p * self.deep, self.deep), self.deep)
+
+    def onward(self, b, p):
+        z, count = self.z, self.count
+        to = jnp.where(b > z, z + 1, z - 1)
+        slot = jnp.where((to == b) & (z > b), count, b)
+        return push(
+            self.parts.at[self.piece(b, p)], self.landed.at[self.piece(slot, p)],
+            self.send.at[b, p], self.recv.at[slot, p], lax.rem(to + count, count),
+        )
+
+    def send_all(self):
+        @pl.when(jnp.logical_not(self.inner))
+        def _():
+            for i in range(1, self.count):
+                b = jnp.where(self.z == 0, self.count - i, i - 1)
+                for p in range(self.pieces):
+                    self.onward(b, p).start()
+
+    def arrived(self, slot, p):
+        at = self.piece(slot, p)
+        push(
+            self.landed.at[at], self.landed.at[at], self.send.at[0, p], self.recv.at[slot, p],
+            lax.rem(self.z + 1, self.count),
+        ).wait_recv()
+        return self.landed[at, :].astype(F32)
+
+    def relay(self, b, p):
+        at = self.piece(b, p)
+        self.parts[at, :] = (self.parts[at, :].astype(F32) + self.arrived(b, p)).astype(BF16)
+        self.onward(b, p).start()
+
+    def result(self, out):
+        z, count = self.z, self.count
+        for p in range(self.pieces):
+            here = pl.ds(p * self.deep, self.deep)
+            out[here, :] = self.parts[self.piece(z, p), :].astype(F32)
+
+            @pl.when(z > 0)
+            def _():
+                out[here, :] += self.arrived(z, p)
+
+            @pl.when(z < count - 1)
+            def _():
+                out[here, :] += self.arrived(count, p)
+
+    def finish(self):
+        def sent(i, _):
+            b = near_order(self.z, self.count, i)
+            for p in range(self.pieces):
+                self.onward(b, p).wait_send()
+            return 0
+
+        lax.fori_loop(1, self.count, sent, 0)
 
 
 def gather_norm_kernel(own, gain, normed, rows_all, here_sem, send, recv):
@@ -588,40 +453,6 @@
         cost_estimate=cost(50),
         name="enter",
     )(own, rows_own)
-
-
-def leave_kernel(own, through, after, got, scanned, send, recv, send_back, recv_back):
-    greet(("seq",))
-    begin, end, drain = swap_slices(own, got, send, recv)
-    begin()
-    end()
-    scan_states(True, got, through, scanned)
-    begin_back, end_back, drain_back = swap_slices(scanned, after, send_back, recv_back)
-    begin_back()
-    end_back()
-    drain()
-    drain_back()
-
-
-def leave(own, through):
-    vmem = pl.BlockSpec(memory_space=pltpu.VMEM)
-    dma = pltpu.SemaphoreType.DMA
-    slices = own.shape[0]
-    return pl.pallas_call(
-        leave_kernel,
-        out_shape=jax.ShapeDtypeStruct(own.shape, BF16),
-        in_specs=[vmem, vmem],
-        out_specs=vmem,
-        scratch_shapes=[
-            pltpu.VMEM(own.shape, BF16), pltpu.VMEM(own.shape, BF16),
-            dma((slices,)), dma((slices,)), dma((slices,)), dma((slices,)),
-        ],
-        compiler_params=pltpu.CompilerParams(
-            collective_id=3, has_side_effects=True, vmem_limit_bytes=32 << 20
-        ),
-        cost_estimate=cost(25),
-        name="leave",
-    )(own, through)
 
 
 def total_kernel(own, out, from_seq, part, from_head, send_a, recv_a, send_b, recv_b,
@@ -707,32 +538,7 @@
     for copy in own + weights:
         copy.wait()
 
-    pieces = p_sem.shape[1]
-    piece_rows = rows // pieces
-
-    def piece(b, p):
-        start = b * rows + p * piece_rows
-        return pl.ds(pl.multiple_of(start, piece_rows), piece_rows)
-
-    def onward(b, p):
-        to = jnp.where(b > z, z + 1, z - 1)
-        slot = jnp.where((to == b) & (z > b), count, b)
-        return push(
-            parts.at[piece(b, p)], landed.at[piece(slot, p)],
-            p_sem.at[b, p], q_sem.at[slot, p], lax.rem(to + count, count),
-        )
-
-    def arrived(slot, p):
-        at = piece(slot, p)
-        push(landed.at[at], landed.at[at], p_sem.at[0, p], q_sem.at[slot, p], z).wait_recv()
-        return landed[at, :].astype(F32)
-
-    inner = (z > 0) & (z < count - 1)
-
-    def relay(b, p):
-        at = piece(b, p)
-        parts[at, :] = (parts[at, :].astype(F32) + arrived(b, p)).astype(BF16)
-        onward(b, p).start()
+    total = LineSum(parts, landed, p_sem, q_sem, rows)
 
     def step(i, _):
         b = near_order(z, count, i)
@@ -760,33 +566,35 @@
         lax.fori_loop(0, rows // band, act_rows, 0)
         parts[at, :] = mm(act[at, : 2 * hidden], wv[:, : 2 * hidden], (1, 1), None).astype(BF16)
 
-        @pl.when((i > 0) & jnp.logical_not(inner))
+        @pl.when((i > 0) & jnp.logical_not(total.inner))
         def _():
-            for p in range(pieces):
-                onward(b, p).start()
+            for p in range(total.pieces):
+                total.onward(b, p).start()
 
         return 0
 
     lax.fori_loop(0, count, step, 0)
 
-    @pl.when(inner)
+    @pl.when(total.inner)
     def _():
-        for p in range(pieces):
-            relay(count - 1 - z, p)
+        for p in range(total.pieces):
+            total.relay(count - 1 - z, p)
 
     high = tiles.shape[1]
     steps = width // high
+    first = grad.shape[1] - 3 * hidden
 
     def store(t, r, k):
         return pltpu.make_async_copy(
             tiles.at[lax.rem(t, 2)],
-            grad.at[pl.ds(pl.multiple_of(r * high, high), high), pl.ds(k * hidden, hidden)],
+            grad.at[
+                pl.ds(pl.multiple_of(r * high, high), high), pl.ds(first + k * hidden, hidden)
+            ],
             o_sem.at[lax.rem(t, 2)],
         )
 
     turned[...] = xs[...].T
     turned_c[...] = cs[...].T
-    far_end = jnp.where(z < count - 1 - z, count - 1, 0)
 
     def slab(r, _):
         for k in range(3):
@@ -804,10 +612,10 @@
             ).astype(BF16)
             store(t, r, k).start()
 
-        @pl.when(inner)
+        @pl.when(total.inner)
         def _():
-            relay(far_end, r)
-            relay(count - 1 - far_end, r)
+            total.relay(total.far_end, r)
+            total.relay(count - 1 - total.far_end, r)
 
         return 0
 
@@ -820,25 +628,8 @@
 
     lax.fori_loop(0, count, part, 0)
 
-    for p in range(pieces):
-        here = pl.ds(p * piece_rows, piece_rows)
-        g_x[here, :] = parts[piece(z, p), :].astype(F32)
-
-        @pl.when(z > 0)
-        def _():
-            g_x[here, :] += arrived(z, p)
-
-        @pl.when(z < count - 1)
-        def _():
-            g_x[here, :] += arrived(count, p)
-
-    def finish(i, _):
-        b = near_order(z, count, i)
-        for p in range(pieces):
-            onward(b, p).wait_send()
-        return 0
-
-    lax.fori_loop(1, count, finish, 0)
+    total.result(g_x)
+    total.finish()
     line.finish()
     store(3 * steps - 2, 0, 0).wait()
     store(3 * steps - 1, 0, 0).wait()
@@ -882,13 +673,424 @@
     )(x_own, c_all, w)
 
 
+def split(x):
+    high = x.astype(BF16)
+    return high, (x - high.astype(F32)).astype(BF16)
+
+
+def mms(left, right, contract):
+    total = mm(left[0], right[0], contract, None)
+    if len(right) > 1:
+        total += mm(left[0], right[1], contract, None)
+    if len(left) > 1:
+        total += mm(left[1], right[0], contract, None)
+    return total
+
+
+def back_kernel(keep, gated_own, og, o_in, qkv, decay, logits, through, gain, left, right,
+                kept_in, parts_in, g_proj, g_logits, g_gain, f_out, g_out,
+                gated_all, go, runs, g_queried, g_keyed, g_values, pulls, weights, kept,
+                parts, landed, state, sending, got, scanned, after, turned, tiles, in_sem, t_sem,
+                z_send, z_recv, s_send, s_recv, b_send, b_recv, p_sem, q_sem):
+    h, head = lax.axis_index("head"), lax.axis_size("head")
+    count, micro, rows, dk = decay.shape
+    dv = og.shape[-1]
+    width = qkv.shape[-1]
+    slices, part = sending.shape[0], sending.shape[2]
+    scale = dk ** (-0.5)
+    loads = [
+        pltpu.make_async_copy(parts_in, parts, in_sem.at[0]),
+        pltpu.make_async_copy(kept_in, kept, in_sem.at[1]),
+    ]
+    for load in loads:
+        load.start()
+    greet(("seq", "head"))
+
+    def to_head(hop, slot):
+        to = lax.rem(h + hop, head)
+        return push(gated_own.at[to], gated_all.at[slot], z_send.at[hop], z_recv.at[slot], to)
+
+    for hop in range(1, head):
+        to_head(hop, h).start()
+    gated_all[h] = gated_own[h]
+
+    causal = lower_ones(rows)
+    before = [jnp.zeros((1, dk), F32)] * micro
+    alive = [jnp.ones((1, dk), F32)] * micro
+    for b in range(count):
+        for m in range(micro):
+            run = running(decay[b, m])
+            runs[b, m] = run
+            alive[m] = alive[m] * keep[b, m]
+            weights[b, m] = jnp.exp(before[m]) * alive[m]
+            before[m] = before[m] + run[rows - 1 : rows, :]
+    g_gain[...] = jnp.zeros_like(g_gain)
+    state[...] = jnp.zeros_like(state)
+
+    turned[...] = left[...].T
+    high, wide = tiles.shape[1:]
+    across_tiles = g_out.shape[1] // wide
+
+    def store(t):
+        at = pl.ds(pl.multiple_of((t // across_tiles) * high, high), high)
+        columns = pl.ds(pl.multiple_of(lax.rem(t, across_tiles) * wide, wide), wide)
+        return pltpu.make_async_copy(
+            tiles.at[lax.rem(t, 2)], g_out.at[at, columns], t_sem.at[lax.rem(t, 2)]
+        )
+
+    def tile(t, _):
+        @pl.when(t >= 2)
+        def _():
+            store(t - 2).wait()
+
+        at = pl.ds(pl.multiple_of((t // across_tiles) * high, high), high)
+        columns = pl.ds(pl.multiple_of(lax.rem(t, across_tiles) * wide, wide), wide)
+        tiles[lax.rem(t, 2)] = jnp.dot(
+            turned[at, :], right[:, columns], preferred_element_type=F32
+        ).astype(BF16)
+        store(t).start()
+        return 0
+
+    tile_count = (g_out.shape[0] // high) * across_tiles
+    lax.fori_loop(0, tile_count, tile, 0)
+
+    def gates(i, _):
+        b = near_order(h, head, i)
+        pl.when(i > 0)(lambda: to_head(lax.rem(b - h + head, head), b).wait_recv())
+        for m in range(micro):
+            gate, o = og[b, m], o_in[b, m]
+            grad = gated_all[b, m].astype(F32)
+            sig = sigmoid(gate)
+            inv = lax.rsqrt(jnp.mean(o * o, axis=-1, keepdims=True) + 1e-5)
+            plain = o * inv
+            normed = (plain * gain[...]).astype(BF16).astype(F32)
+            g_on = (grad * gate * sig).astype(BF16).astype(F32)
+            g_proj[b, m, :, width:] = (
+                grad * normed * sig * (1.0 + gate * (1.0 - sig))
+            ).astype(BF16)
+            scaled = g_on * gain[...]
+            g_o = inv * (scaled - plain * jnp.mean(scaled * plain, axis=-1, keepdims=True))
+            go[b, m] = g_o
+            g_gain[0:1, :] += jnp.sum(g_on * plain, axis=0, keepdims=True)
+            queried = qkv[b, m, :, :dk].astype(F32) * (jnp.exp(runs[b, m]) * scale)
+            pull = mms(split(g_o), split(queried), (0, 0))
+            pulls[b, m] = pull
+            state[m] += pull * weights[b, m]
+        return 0
+
+    lax.fori_loop(0, head, gates, 0)
+    for i in range(slices):
+        sending[i] = state[:, i * part : (i + 1) * part, :].astype(BF16)
+    begin, end, drain = swap_slices(sending, got, s_send, s_recv)
+    begin()
+    for load in loads:
+        load.wait()
+    total = LineSum(parts, landed, p_sem, q_sem, f_out.shape[0])
+    total.send_all()
+
+    def inside(b, _):
+        for m in range(micro):
+            q = qkv[b, m, :, :dk].astype(F32)
+            k = qkv[b, m, :, dk : 2 * dk].astype(F32)
+            v = (qkv[b, m, :, 2 * dk :],)
+            run = runs[b, m]
+            queried, keyed = split(q * (jnp.exp(run) * scale)), split(k * jnp.exp(-run))
+            g_o, entry = split(go[b, m]), split(kept[b, m])
+            scores = split(jnp.where(causal, mms(queried, keyed, (1, 1)), 0.0))
+            g_scores = split(jnp.where(causal, mms(g_o, v, (1, 1)), 0.0))
+            g_queried[b, m] = mms(g_scores, keyed, (1, 0)) + mms(g_o, entry, (1, 0))
+            g_keyed[b, m] = mms(g_scores, queried, (0, 0))
+            g_values[b, m] = mms(scores, g_o, (0, 0))
+        pl.when(total.inner)(lambda: total.relay(total.far_end, b))
+        return 0
+
+    lax.fori_loop(0, count, inside, 0)
+    end()
+    scan_states(True, got, through, scanned)
+    begin_back, end_back, drain_back = swap_slices(scanned, after, b_send, b_recv)
+    begin_back()
+
+    @pl.when(total.inner)
+    def _():
+        for p in range(total.pieces):
+            total.relay(head - 1 - total.far_end, p)
+        for p in range(total.pieces):
+            total.relay(head - 1 - h, p)
+
+    end_back()
+    for i in range(slices):
+        state[:, i * part : (i + 1) * part, :] = after[i].astype(F32)
+
+    def across(step, _):
+        b = count - 1 - step
+        for m in range(micro):
+            q = qkv[b, m, :, :dk].astype(F32)
+            k = qkv[b, m, :, dk : 2 * dk].astype(F32)
+            v = (qkv[b, m, :, 2 * dk :],)
+            run = runs[b, m]
+            last = run[rows - 1 : rows, :]
+            up, down, rest = jnp.exp(run) * scale, jnp.exp(-run), jnp.exp(last - run)
+            decayed = jnp.exp(last)
+            gs = state[m]
+            gs_parts = split(gs)
+            carried = k * rest
+            g_v = g_values[b, m] + mms(split(carried), gs_parts, (1, 1))
+            g_carried = mms(v, gs_parts, (1, 0))
+            from_carried = g_carried * carried
+            g_total = jnp.sum(decayed * kept[b, m] * gs, axis=0, keepdims=True) + jnp.sum(
+                from_carried, axis=0, keepdims=True
+            )
+            state[m] = (decayed * gs + pulls[b, m]) * keep[b, m]
+            gq, gk = g_queried[b, m], g_keyed[b, m]
+            g_run = gq * (q * up) - gk * (k * down) - from_carried
+            later = mms((causal.astype(F32).astype(BF16),), split(g_run), (0, 0)) + g_total
+            g_proj[b, m, :, :dk] = (gq * up).astype(BF16)
+            g_proj[b, m, :, dk : 2 * dk] = (gk * down + g_carried * rest).astype(BF16)
+            g_proj[b, m, :, 2 * dk : width] = g_v.astype(BF16)
+            g_logits[b, m] = (
+                later.astype(BF16).astype(F32) * sigmoid(-logits[b, m]) * (1.0 / GATE_NORM)
+            )
+        return 0
+
+    lax.fori_loop(0, count, across, 0)
+    total.result(f_out)
+    total.finish()
+    store(tile_count - 2).wait()
+    store(tile_count - 1).wait()
+    drain()
+    drain_back()
+    for hop in range(1, head):
+        to_head(hop, h).wait_send()
+
+
+def attention_back(
+    keep, gated_own, og, o, qkv, decays, logits, through, gain, left, right, kept, parts
+):
+    blocks, micro, rows, width = qkv.shape
+    dk, dv = decays.shape[-1], og.shape[-1]
+    head, seq = lax.axis_size("head"), lax.axis_size("seq")
+    own_rows = parts.shape[0] // head
+    vmem, anywhere = pl.BlockSpec(memory_space=pltpu.VMEM), pl.BlockSpec(memory_space=pl.ANY)
+    dma = pltpu.SemaphoreType.DMA
+    blocked = lambda w, kind: pltpu.VMEM((blocks, micro, rows, w), kind)
+    states = (seq, micro, dv // seq, dk)
+    return pl.pallas_call(
+        back_kernel,
+        out_shape=(
+            jax.ShapeDtypeStruct((blocks, micro, rows, width + dv), BF16),
+            jax.ShapeDtypeStruct((blocks, micro, rows, dk), F32),
+            jax.ShapeDtypeStruct((8, dv), F32),
+            jax.ShapeDtypeStruct((own_rows, parts.shape[1]), F32),
+            jax.ShapeDtypeStruct((left.shape[1], right.shape[1]), BF16),
+        ),
+        in_specs=[vmem] * 11 + [anywhere] * 2,
+        out_specs=(vmem,) * 4 + (anywhere,),
+        scratch_shapes=[
+            blocked(dv, BF16), blocked(dv, F32), blocked(dk, F32),
+            blocked(dk, F32), blocked(dk, F32), blocked(dv, F32),
+            pltpu.VMEM((blocks, micro, dv, dk), F32), pltpu.VMEM((blocks, micro, 1, dk), F32),
+            pltpu.VMEM((blocks, micro, dv, dk), F32),
+            pltpu.VMEM(parts.shape, BF16),
+            pltpu.VMEM((parts.shape[0] + own_rows, parts.shape[1]), BF16),
+            pltpu.VMEM((micro, dv, dk), F32),
+            pltpu.VMEM(states, BF16), pltpu.VMEM(states, BF16), pltpu.VMEM(states, BF16),
+            pltpu.VMEM(states, BF16),
+            pltpu.VMEM(left.shape[::-1], BF16),
+            pltpu.VMEM((2, left.shape[1] // 4, right.shape[1] // 2), BF16),
+            dma((2,)), dma((2,)), dma((head,)), dma((head,)), dma((seq,)), dma((seq,)), dma((seq,)),
+            dma((seq,)), dma((head, 4)), dma((head + 1, 4)),
+        ],
+        compiler_params=pltpu.CompilerParams(
+            collective_id=3, has_side_effects=True, vmem_limit_bytes=60 << 20
+        ),
+        cost_estimate=cost(80),
+        name="attention_back",
+    )(keep, gated_own, og, o, qkv, decays, logits, through, gain, left, right, kept, parts)
+
+
+def finish_kernel(xn_in, proj_in, w_in, g_logits, ranked, up_own, rank_down,
+                  g_x, grad, g_down, g_up, g_bias,
+                  turned, proj, w, outgoing, mine, paired, peers, slab, heads_in, parts, landed, slim_high,
+                  slim_low, in_sem, pair_send, pair_recv, peer_send, peer_recv, x_send, x_recv,
+                  p_sem, q_sem):
+    s, seq = lax.axis_index("seq"), lax.axis_size("seq")
+    h, head = lax.axis_index("head"), lax.axis_size("head")
+    rows, width = g_x.shape
+    deep = grad.shape[0] * head
+    side = lax.rem(s, 2)
+    pairs = seq // 2
+    own_pair = s // 2
+
+    loads = [
+        pltpu.make_async_copy(proj_in, proj, in_sem.at[0]),
+        pltpu.make_async_copy(w_in, w, in_sem.at[1]),
+        pltpu.make_async_copy(xn_in, landed.at[pl.ds(0, xn_in.shape[0])], in_sem.at[2]),
+    ]
+    for load in loads:
+        load.start()
+    for load in loads:
+        load.wait()
+    turned[...] = landed[: xn_in.shape[0], :].T
+    greet(("seq", "head"))
+    total = LineSum(parts, landed, p_sem, q_sem, rows)
+    logit_parts = split(g_logits[...])
+    g_ranked = mms(logit_parts, split(up_own[...]), (1, 1))
+    slim = split(g_ranked)
+    slim_high[...], slim_low[...] = slim
+
+    def chunk(i, _):
+        b = near_order(h, head, head - 1 - i)
+        at = pl.ds(pl.multiple_of(b * rows, rows), rows)
+        rank_part = mms((slim_high[at, :], slim_low[at, :]), (rank_down[...],), (1, 1))
+        parts[at, :] = (mm(proj[at, :], w[...], (1, 1), None) + rank_part).astype(BF16)
+
+        @pl.when((b != h) & jnp.logical_not(total.inner))
+        def _():
+            for p in range(total.pieces):
+                total.onward(b, p).start()
+
+        return 0
+
+    lax.fori_loop(0, head, chunk, 0)
+
+    def block(i):
+        return pl.ds(pl.multiple_of(i * deep, deep), deep)
+
+    def to_partner(k):
+        return push(
+            outgoing.at[k], paired.at[k], pair_send.at[k], pair_recv.at[k], s + 1 - 2 * side, "seq"
+        )
+
+    def to_peer(k):
+        return push(
+            mine.at[k], peers.at[own_pair], peer_send.at[k], peer_recv.at[own_pair],
+            2 * k + side, "seq",
+        )
+
+    def gone(k, _):
+        outgoing[k] = jnp.dot(
+            turned[block(2 * k + 1 - side), :], proj[...], preferred_element_type=F32
+        ).astype(BF16)
+        to_partner(k).start()
+        return 0
+
+    lax.fori_loop(0, pairs, gone, 0)
+
+    def kept(k, _):
+        here = jnp.dot(turned[block(2 * k + side), :], proj[...], preferred_element_type=F32)
+        to_partner(k).wait_recv()
+        mine[k] = (here + paired[k].astype(F32)).astype(BF16)
+        pl.when(own_pair != k)(to_peer(k).start)
+
+        @pl.when(total.inner & (k < total.pieces))
+        def _():
+            total.relay(total.far_end, k)
+            total.relay(head - 1 - total.far_end, k)
+
+        return 0
+
+    lax.fori_loop(0, pairs, kept, 0)
+
+    @pl.when(total.inner)
+    def _():
+        for p in range(pairs, total.pieces):
+            total.relay(total.far_end, p)
+            total.relay(head - 1 - total.far_end, p)
+        for p in range(total.pieces):
+            total.relay(head - 1 - h, p)
+
+    g_down[...] = mms((turned[...],), slim, (1, 0))
+    g_up[...] = mms(split(ranked[...]), logit_parts, (0, 0))
+    g_bias[...] = jnp.broadcast_to(jnp.sum(g_logits[...], axis=0, keepdims=True), g_bias.shape)
+
+    def arrived(k):
+        return push(
+            mine.at[k], peers.at[k], peer_send.at[k], peer_recv.at[k],
+            lax.rem(s + 1, seq), "seq",
+        )
+
+    peers[own_pair] = mine[own_pair]
+    for k in range(pairs):
+        pl.when(own_pair != k)(arrived(k).wait_recv)
+    band = 16
+
+    def add_rows(r, _):
+        at = pl.ds(pl.multiple_of(r * band, band), band)
+        slab[at, :] = jnp.sum(peers[:, at, :].astype(F32), axis=0).astype(BF16)
+        return 0
+
+    lax.fori_loop(0, deep // band, add_rows, 0)
+    thin = grad.shape[0]
+
+    def to_head(hop, slot):
+        to = lax.rem(h + hop, head)
+        return push(
+            slab.at[pl.ds(pl.multiple_of(to * thin, thin), thin)], heads_in.at[slot],
+            x_send.at[hop], x_recv.at[slot], to,
+        )
+
+    for hop in range(1, head):
+        to_head(hop, h).start()
+    heads_in[h] = slab[pl.ds(pl.multiple_of(h * thin, thin), thin), :]
+    total.result(g_x)
+    for hop in range(1, head):
+        to_head(hop, lax.rem(h + hop, head)).wait_recv()
+    dk = g_up.shape[1]
+    dv = slab.shape[1] // 2 - dk
+    for j in range(head):
+        at, start = 0, 0
+        for size in (dk, dk, dv, dv):
+            grad[:, start + j * size : start + (j + 1) * size] = heads_in[
+                j, :, at : at + size
+            ].astype(F32)
+            at, start = at + size, start + head * size
+    for k in range(pairs):
+        to_partner(k).wait_send()
+        pl.when(own_pair != k)(to_peer(k).wait_send)
+    for hop in range(1, head):
+        to_head(hop, h).wait_send()
+    total.finish()
+
+
+def finish(xn, g_proj, w_in, g_logits, ranked, up_own, rank_down):
+    seq, head = lax.axis_size("seq"), lax.axis_size("head")
+    group, width = xn.shape
+    columns, rank = w_in.shape[1], ranked.shape[1]
+    deep, rows, pairs = width // seq, group // head, seq // 2
+    dk = up_own.shape[1]
+    vmem, anywhere = pl.BlockSpec(memory_space=pltpu.VMEM), pl.BlockSpec(memory_space=pl.ANY)
+    dma = pltpu.SemaphoreType.DMA
+    blocks = pltpu.VMEM((pairs, deep, columns), BF16)
+    return pl.pallas_call(
+        finish_kernel,
+        out_shape=(
+            jax.ShapeDtypeStruct((rows, width), F32),
+            jax.ShapeDtypeStruct((deep // head, columns * head), F32),
+            jax.ShapeDtypeStruct((width, rank), F32),
+            jax.ShapeDtypeStruct((rank, dk), F32),
+            jax.ShapeDtypeStruct((8, dk), F32),
+        ),
+        in_specs=[anywhere] * 3 + [vmem] * 4,
+        out_specs=(vmem,) * 5,
+        scratch_shapes=[
+            pltpu.VMEM((width, group), BF16), pltpu.VMEM(g_proj.shape, BF16),
+            pltpu.VMEM(w_in.shape, BF16), blocks, blocks, blocks, blocks,
+            pltpu.VMEM((deep, columns), BF16), pltpu.VMEM((head, deep // head, columns), BF16),
+            pltpu.VMEM((group, width), BF16), pltpu.VMEM((group + rows, width), BF16),
+            pltpu.VMEM(ranked.shape, BF16), pltpu.VMEM(ranked.shape, BF16),
+            dma((3,)), dma((pairs,)), dma((pairs,)), dma((pairs,)), dma((pairs,)),
+            dma((head,)), dma((head,)), dma((head, 4)), dma((head + 1, 4)),
+        ],
+        compiler_params=pltpu.CompilerParams(
+            collective_id=5, has_side_effects=True, vmem_limit_bytes=56 << 20
+        ),
+        cost_estimate=cost(60),
+        name="finish",
+    )(xn, g_proj, w_in, g_logits, ranked, up_own, rank_down)
+
+
 def exchange(x, axis):
     return lax.all_to_all(x, axis, split_axis=0, concat_axis=0, tiled=True)
-
-
-def ring(x, axis, hop):
-    count = lax.axis_size(axis)
-    return lax.ppermute(x, axis, [((i + hop) % count, i) for i in range(count)])
 
 
 def gather_weight(w):
@@ -984,53 +1186,35 @@
     g_hidden = cotangent.astype(F32).reshape(micro * rows, width) + back_ffn
     g_mixed = g_hidden.astype(BF16)
     g_gated = dot(g_mixed, w_out, (1, 0)).astype(BF16)
-    grad_mix = weight_grad(g_mixed, gated, None, proj_width + vals, proj_width, dv)
     g_gated = g_gated.reshape(micro, rows, heads, dv).transpose(2, 0, 1, 3)
-    g_gated_b = exchange(g_gated, "head")
-    g_gated_b, ffn_part = lax.optimization_barrier((g_gated_b, ffn_part))
-    ffn_out = ffn_part[head].astype(F32)
-    for hop in range(1, heads):
-        ffn_out += ring(ffn_part[lax.rem(head + heads - hop, heads)], "head", hop).astype(F32)
-    g_og_b, g_o_b, pulled, g_head_gain = gate_back_of(
-        starts, g_gated_b, og_b, o_b, qkv_b, decays_b, gain_row, seq
+    keep = 1.0 - jnp.broadcast_to(starts.T[:, :, None, None], (heads, micro, 1, dk)).astype(F32)
+    g_proj_b, g_logits_b, g_head_gain, ffn_out, grad_out = attention_back(
+        keep, g_gated, og_b, o_b, qkv_b, decays_b, blocks(logits), through, gain_row,
+        g_mixed, gated, kept, ffn_part.reshape(group, width),
     )
-    after = leave(pulled, through)
-    g_proj_b, g_logits_b = mix_back_of(
-        starts, qkv_b, decays_b, g_o_b, g_og_b, kept, after, blocks(logits)
+    grad_out = scatter_grad(grad_out)
+    output = (hidden + ffn_out).astype(BF16)
+    g_proj, g_logits = g_proj_b.reshape(group, proj_width), g_logits_b.reshape(group, dk)
+    g_xn, grad_in, g_rank_down, g_rank_up, g_bias = finish(
+        xn, g_proj, w_in, g_logits, ranked, up_own, rank_down
     )
-    g_proj, g_logits = g_proj_b.reshape(group, proj_width), g_logits_b.reshape(group, dk)
-    g_ranked = dot(g_logits, up_own, (1, 1), HIGHEST)
-    g_xn_part = dot(g_proj, w_in, (1, 1)) + dot(
-        g_ranked, rank_down.astype(F32), (1, 1), HIGHEST
-    )
-    g_xn_part = g_xn_part.astype(BF16).reshape(heads, micro * rows, width)
-    g_xn = exchange(g_xn_part, "head").astype(F32).sum(0)
-    output = (hidden + ffn_out).astype(BF16)
+    g_xn, grad_ffn = lax.optimization_barrier((g_xn, grad_ffn))
     inv_in = rms(source, 1e-6)
     back_in, g_norm_gain = norm_back(g_xn, norm_gain, source * inv_in, inv_in)
     input_grad = g_hidden + back_in
 
-    slab = width // (seq * heads)
-    grad_mix = weight_grad(xn, g_proj, grad_mix, proj_width + vals, 0, dv)
-    grad_mix, grad_ffn = lax.optimization_barrier((grad_mix, grad_ffn))
-    grad_mix = scatter_grad(grad_mix).reshape(heads, slab, proj_width + vals)
-    grad_mix = exchange(grad_mix, "head").astype(F32)
-    grad_in, grad_out = grad_mix[:, :, :proj_width], grad_mix[:, :, proj_width:].sum(0)
-    cuts = ((0, dk), (dk, 2 * dk), (2 * dk, 2 * dk + dv), (2 * dk + dv, proj_width))
-    grad_in = jnp.concatenate(
-        [grad_in[:, :, a:b].transpose(1, 0, 2).reshape(slab, -1) for a, b in cuts], axis=1
-    )
-    g_rank_down = dot(xn.astype(F32), g_ranked, (0, 0), HIGHEST)
-    g_rank_up = dot(ranked, g_logits, (0, 0), HIGHEST)
     g_rank_up = lax.dynamic_update_slice_in_dim(
         jnp.zeros(rank_up.shape, F32), g_rank_up, head * dk, 1
     )
     g_bias = lax.dynamic_update_slice_in_dim(
-        jnp.zeros(gate_bias.shape, F32), g_logits.sum(0), head * dk, 0
+        jnp.zeros(gate_bias.shape, F32), g_bias[0], head * dk, 0
     )
     small = total_of(
         [g_norm_gain, g_ffn_gain, g_head_gain[0], g_rank_down, g_rank_up, g_bias]
     )
+    slab = width // (seq * heads)
+    small, grad_out = lax.optimization_barrier((small, grad_out))
+    grad_out = exchange(grad_out.reshape(heads, slab, vals), "head").astype(F32).sum(0)
     return (
         output.reshape(tokens.shape),
         input_grad.reshape(tokens.shape),

time: 722 us -> 619 us (0.86)
  waiting for transfers between devices: 73.1 us -> 10.4 us
  starting transfers between devices: 42.5 us -> 4.41 us
  Pallas kernels: 438 us -> 468 us
  matrix products: 48 us -> 27.9 us
    pallas_call x5 -> x2, Pallas kernels: 97.4 us -> 169 us  [the longest x1 92.3 us: finish(): pl.pallas_call(finish_kernel, out_shape=(jax.ShapeDtypeStruct((rows, widt...]
    all_to_all x3 -> x1, waiting for transfers between devices: 56.7 us -> 10.3 us  [exchange(): return lax.all_to_all(x, axis, split_axis=0, concat_axis=0, tiled=True)]
    pallas_call x1, Pallas kernels: 73.8 us -> 30.3 us  [total_of(): pl.pallas_call(total_kernel, out_shape=jax.ShapeDtypeStruct(shape, F32),...]
    all_to_all x3 -> x1, starting transfers between devices: 36.9 us -> 4.24 us  [exchange(): return lax.all_to_all(x, axis, split_axis=0, concat_axis=0, tiled=True)]
    dot_general x11 -> x6, matrix products: 48 us -> 27.9 us  [dot(): lax.dot_general(a, b, (((contract[0],), (contract[1],)), ((), ())), preci...]
    reduce_scatter x2, waiting for transfers between devices: 16.3 us -> 0.01 us  [scatter_grad(): lax.psum_scatter(g.astype(BF16), 'seq', scatter_dimension=0, tiled=True)]
    unnamed x77 -> x63, local copies, waits for them, and re-layouts: 17.2 us -> 8.99 us
  transfers between devices with their start and end apart: 10 -> 5, of which waited for: 4 -> 1; matrix products, arithmetic and copies ran while one was open for 13% -> 12% of each run, Pallas kernels for 44% -> 56%
where the time goes in v4:
time: 619 us; the launch traced here: 611 us
  Pallas kernels  468 us (76%)
  local copies, waits for them, and re-layouts  39.6 us (6%)
  matrix products  27.9 us (5%)
  blocking collectives  24.1 us (4%)
  other arithmetic  22.4 us (4%)
  between operations  14.4 us (2%)
  waiting for transfers between devices  10.4 us (2%)
    pallas_call x1, Pallas kernels, feed_forward(): pl.pallas_call(functools.partial(ffn_kernel, count), out_shape=(jax.Shape...  123 us
    pallas_call x1, Pallas kernels, finish(): pl.pallas_call(finish_kernel, out_shape=(jax.ShapeDtypeStruct((rows, widt...  92.3 us
    pallas_call x1, Pallas kernels, attention_back(): pl.pallas_call(back_kernel, out_shape=(jax.ShapeDtypeStruct((blocks, micr...  76.7 us
    pallas_call x1, Pallas kernels, gather_norm(): pl.pallas_call(gather_norm_kernel, out_shape=jax.ShapeDtypeStruct((count...  60.8 us
    pallas_call x1, Pallas kernels, enter(): pl.pallas_call(enter_kernel, out_shape=(jax.ShapeDtypeStruct((slices, mic...  56.5 us
    pallas_call x1, Pallas kernels, total_of(): pl.pallas_call(total_kernel, out_shape=jax.ShapeDtypeStruct(shape, F32),...  30.3 us
    dot_general x6, matrix products, dot(): lax.dot_general(a, b, (((contract[0],), (contract[1],)), ((), ())), preci...  27.9 us
    all_to_all x1, blocking collectives, exchange(): return lax.all_to_all(x, axis, split_axis=0, concat_axis=0, tiled=True)  24.1 us
  transfers between devices with their start and end apart: 5, of which 1 were waited for; matrix products, arithmetic and copies ran while one was open for 12% of the time, Pallas kernels for 56%

profile of v4, /device:TPU:0, one launch (start us, length us, event | category | flops | bytes accessed | tf_op | source)
XLA Modules:
  0.0 610.8 jit_solution(6681284793967177138)
XLA Ops:
  11.8 1.8 pad_maximum_fusion
  15.4 60.8 %gather_norm.1.xn_in = bf16[768,2048]{1,0:T(8,128)(2,1)S(1)} custom-call(bf16[192,2048]{1,0:T(8,128)(2,1)S(1)} %bitcast.53, f32[1,2048]{1,0:T(1,128)S(1)} %bitcast.62), custom_call_target="tpu_custom_call" | custom-call | bytes 150000000 | tf_op jit(solution)/shard_map/gather_norm/pallas_call | solution.py:341
  78.0 2.2 fusion.19
  80.2 5.7 fusion.14
  85.9 9.6 %states.1.own = bf16[8,3,80,256]{3,2,1,0:T(8,128)(2,1)S(1)} custom-call(s32[3,4]{1,0:T(4,128)S(1)} %copy-done.13, bf16[4,3,64,1024]{3,2,1,0:T(8,128)(2,1)S(1)} %bitcast.55, bf16[4,3,64,256]{3,2,1,0:T(8,128)(2,1)S(1)} %bitcast.60), custom_call_target="tpu_custom_call" | custom-call | bytes 30000000 | tf_op jit(solution)/shard_map/states/pallas_call | solution.py:124
  95.6 56.5 %enter.1 = (bf16[8,3,64,256]{3,2,1,0:T(8,128)(2,1)S(1)}, bf16[8,3,16,256]{3,2,1,0:T(8,128)(2,1)S(1)}, bf16[768,2048]{1,0:T(8,128)(2,1)S(1)}) custom-call(bf16[8,3,80,256]{3,2,1,0:T(8,128)(2,1)S(1)} %states.1.own, bf16[192,2048]{1,0:T(8,128)(2,1)S(1)} %bitcast.58), custom_call_target="tpu_custom_call" | custom-call | bytes 150000000 | tf_op jit(solution)/shard_map/enter/pallas_call | solution.py:436
  152.2 5.8 fusion.12
  158.0 18.1 %mix.1 = (f32[4,3,64,512]{3,2,1,0:T(8,128)S(1)}, bf16[4,3,64,512]{3,2,1,0:T(8,128)(2,1)S(1)}, f32[4,3,512,256]{3,2,1,0:T(8,128)}) custom-call(s32[3,4]{1,0:T(4,128)S(1)} %copy-done.13, bf16[4,3,64,1024]{3,2,1,0:T(8,128)(2,1)S(1)} %bitcast.56, bf16[4,3,64,256]{3,2,1,0:T(8,128)(2,1)S(1)} %bitcast.61, f32[4,3,64,512]{3,2,1,0:T(8,128)} %bitcast.65, ...), custom_call_target="tpu_custom_call" | custom-call | bytes 54000000 | tf_op jit(solution)/shard_map/mix/pallas_call | solution.py:144
  176.1 24.1 %all_to_all.10 = bf16[4,3,64,512]{3,2,1,0:T(8,128)(2,1)S(1)} all-to-all(bf16[4,3,64,512]{3,2,1,0:T(8,128)(2,1)S(1)} %get-tuple-element.41), channel_id=1, replica_groups=mesh['seq'=8,'head'=4] {'head'}, dimensions={0} | all-to-all | bytes 1572864 | tf_op jit(solution)/shard_map/all_to_all | solution.py:1093
  201.3 6.5 %multiply_reduce_fusion.5 = (f32[192]{0:T(256)S(1)}, f32[192,2048]{1,0:T(8,128)S(1)}) fusion(bf16[192,2048]{1,0:T(8,128)(2,1)S(1)} %bitcast.68, bf16[2048,6272]{1,0:T(8,128)(2,1)} %all-gather.5.cloned.1.call-done.w, bf16[192,2048]{1,0:T(8,128)(2,1)S(1)} %bitcast.54), kind=kOutput, calls=%fused_computation.24 | convolution fusion | flops 1612185344 | bytes 11535104 | tf_op jit(solution)/shard_map/dot_general | solution.py:1105
  208.9 123.3 %feed_forward.1 = (f32[192,2048]{1,0:T(8,128)}, bf16[4,192,2048]{2,1,0:T(8,128)(2,1)}, bf16[2048,4224]{1,0:T(8,128)(2,1)}) custom-call(bf16[192,2048]{1,0:T(8,128)(2,1)} %multiply_convert_fusion.x_own, bf16[768,2048]{1,0:T(8,128)(2,1)} %copy-done.9, bf16[2048,6272]{1,0:T(8,128)(2,1)} %all-gather.5.cloned.1.call-done.w), custom_call_target="tpu_custom_call" | custom-call | bytes 300000000 | tf_op jit(solution)/shard_map/feed_forward/pallas_call | solution.py:645
  332.4 2.1 multiply_reduce_fusion
  335.9 6.8 %fusion.9 = bf16[192,2048]{1,0:T(8,128)(2,1)} fusion(bf16[192,2048]{1,0:T(8,128)(2,1)S(1)} %fusion.20.left, bf16[2048,6272]{1,0:T(8,128)(2,1)} %all-gather.5.cloned.1.call-done.w), kind=kOutput, calls=%fused_computation.8 | convolution fusion | flops 1611005952 | bytes 9961472 | tf_op jit(solution)/shard_map/dot_general | solution.py:1105
  342.7 3.0 reshape.160
  345.7 2.4 copy.40
  348.8 76.7 %attention_back.1 = (bf16[4,3,64,1536]{3,2,1,0:T(8,128)(2,1)}, f32[4,3,64,256]{3,2,1,0:T(8,128)}, f32[8,512]{1,0:T(8,128)}, f32[192,2048]{1,0:T(8,128)}, bf16[2048,2048]{1,0:T(8,128)(2,1)}) custom-call(f32[4,3,1,256]{3,2,1,0:T(1,128)} %broadcast_in_dim.6.keep, bf16[4,3,64,512]{3,2,1,0:T(8,128)(2,1)} %bitcast.70, f32[4,3,64,512]{3,2,1,0:T(8,128)} %bitcast.66, ...), custom_call_target="tpu_custom_call" | custom-call | bytes 240000000 | tf_op jit(solution)/shard_map/attention_back/pallas_call | solution.py:877
  427.8 1.3 bitcast_multiply_fusion
  429.9 92.3 %finish.1 = (f32[192,2048]{1,0:T(8,128)}, f32[64,6144]{1,0:T(8,128)}, f32[2048,16]{1,0:T(8,128)}, f32[16,256]{1,0:T(8,128)}, f32[8,256]{1,0:T(8,128)}) custom-call(bf16[768,2048]{1,0:T(8,128)(2,1)} %copy-done.2, bf16[768,1536]{1,0:T(8,128)(2,1)} %bitcast.74, bf16[2048,1536]{1,0:T(8,128)(2,1)} %all-gather.3.cloned.1.call-done.w_in, f32[768,256]{1,0:T(8,128)} %bitcast.84, ...), custom_call_target="tpu_custom_call" | custom-call | bytes 180000000 | tf_op jit(solution)/shard_map/finish/pallas_call | solution.py:1064
  522.2 1.5 reshape.167
  525.3 2.4 multiply_reduce_fusion.1
  528.6 30.3 %total.1 = f32[8,4,16,128]{3,2,1,0:T(8,128)} custom-call(f32[8,4,16,128]{3,2,1,0:T(8,128)} %bitcast.82), custom_call_target="tpu_custom_call" | custom-call | bytes 45000000 | tf_op jit(solution)/shard_map/total/pallas_call | solution.py:495
  558.9 2.8 slice.50
  565.2 2.3 slice.62
  568.1 1.3 fusion.21
  569.4 4.2 all-to-all-start.1
  573.7 3.1 slice_convert_fusion
  576.8 2.2 copy.35
  579.0 4.7 reshape.176
  583.7 2.4 slice_convert_fusion.1
  586.1 4.3 multiply_add_fusion
  590.3 10.3 %all-to-all-done.1 = bf16[4,64,2048]{2,1,0:T(8,128)(2,1)} async-done(((bf16[4,64,2048]{2,1,0:T(8,128)(2,1)}), bf16[4,64,2048]{2,1,0:T(8,128)(2,1)}, u32[]{:S(2)}, u32[]{:S(2)}) %all-to-all-start.1) | async-done | bytes 1048608 | tf_op jit(solution)/shard_map/all_to_all | solution.py:1093
  600.6 2.2 convert_reduce_fusion
  (105 shorter events, 23.2 us)
Async XLA Ops:
  7.2 69.8 %copy-start = (f32[16,1024]{1,0:T(8,128)S(1)}, f32[16,1024]{1,0:T(8,128)}, u32[]{:S(2)}) copy-start(f32[16,1024]{1,0:T(8,128)} %param.24) | copy-start | bytes 196612
  7.2 73.0 %all-gather.3.cloned.1.call-start = ((), (), s32[]{:S(2)}) async-start(), calls=%async_computation.4 | async-start | bytes 7077888 | tf_op jit(solution)/shard_map/all_gather | solution.py:1097
  8.2 2.2 copy-start.20
  10.4 1.2 copy-start.21
  10.4 1.4 copy-start.22
  10.4 190.6 %all-gather.5.cloned.1.call-start = ((), (), s32[]{:S(2)}) async-start(), calls=%async_computation.5 | async-start | bytes 28901376 | tf_op jit(solution)/shard_map/all_gather | solution.py:1097
  13.6 0.7 copy-start.12
  13.6 511.7 %reduce-scatter.3.cloned.1.call-start = ((), (), s32[]{:S(2)}) async-start(), calls=%async_computation.6 | async-start | bytes 19464192 | tf_op jit(solution)/shard_map/reduce_scatter | solution.py:1101
  14.3 1.1 copy-start.3
  15.4 61.6 %copy-start.23 = (bf16[2048,16]{0,1:T(8,128)(2,1)S(1)}, bf16[2048,16]{0,1:T(8,128)(2,1)}, u32[]{:S(2)}) copy-start(bf16[2048,16]{0,1:T(8,128)(2,1)} %param.23) | copy-start | bytes 196612
  76.2 75.9 %copy-start.2 = (bf16[768,2048]{1,0:T(8,128)(2,1)}, bf16[768,2048]{1,0:T(8,128)(2,1)S(1)}, u32[]{:S(2)}) copy-start(bf16[768,2048]{1,0:T(8,128)(2,1)S(1)} %gather_norm.1.xn_in) | copy-start | bytes 9437188
  77.0 0.9 copy-start.25
  80.2 5.7 copy-start.13
  80.2 5.7 copy-start.8
  85.9 72.1 %copy-start.5 = (bf16[768,1024]{1,0:T(8,128)(2,1)}, bf16[768,1024]{1,0:T(8,128)(2,1)S(1)}, u32[]{:S(2)}) copy-start(bf16[768,1024]{1,0:T(8,128)(2,1)S(1)} %fusion.14) | copy-start | bytes 4718596
  85.9 9.7 %copy-start.6 = (bf16[3,64,2048]{2,1,0:T(8,128)(2,1)S(1)}, bf16[3,64,2048]{2,1,0:T(8,128)(2,1)}, u32[]{:S(2)}) copy-start(bf16[3,64,2048]{2,1,0:T(8,128)(2,1)} %param.15) | copy-start | bytes 2359300
  152.1 5.8 copy-start.9
  152.1 5.8 copy-start.11
  152.1 5.8 copy-start.14
  176.1 24.7 %copy-start.10 = (f32[4,3,64,512]{3,2,1,0:T(8,128)}, f32[4,3,64,512]{3,2,1,0:T(8,128)S(1)}, u32[]{:S(2)}) copy-start(f32[4,3,64,512]{3,2,1,0:T(8,128)S(1)} %get-tuple-element.44.o_in) | copy-start | bytes 4718596
  200.2 1.1 copy-start.4
  201.0 6.8 %copy-start.17 = (bf16[24,8,4,512]{3,1,2,0:T(8,128)(2,1)}, bf16[24,8,4,512]{3,1,2,0:T(8,128)(2,1)S(1)}, u32[]{:S(2)}) copy-start(bf16[24,8,4,512]{3,1,2,0:T(8,128)(2,1)S(1)} %copy.36) | copy-start | bytes 2359300
  201.3 6.5 %copy-start.24 = (f32[2048]{0:T(1024)S(1)}, f32[2048]{0:T(1024)}, u32[]{:S(2)}) copy-start(f32[2048]{0:T(1024)} %param.21) | copy-start | bytes 24580
  332.3 237.2 %reduce-scatter.5.cloned.1.call-start = ((), (), s32[]{:S(2)}) async-start(), calls=%async_computation.7 | async-start | bytes 9437184 | tf_op jit(solution)/shard_map/reduce_scatter | solution.py:1101
  332.4 2.1 copy-start.7
  332.4 2.1 copy-start.15
  335.0 0.9 copy-start.18
  569.4 31.2 %all-to-all-start.1 = ((bf16[4,64,2048]{2,1,0:T(8,128)(2,1)}), bf16[4,64,2048]{2,1,0:T(8,128)(2,1)}, u32[]{:S(2)}, u32[]{:S(2)}) async-start(bf16[4,64,2048]{2,1,0:T(8,128)(2,1)} %bitcast.81), calls=%async_computation.3 | async-start | bytes 2097152 | tf_op jit(solution)/shard_map/all_to_all | solution.py:1093
  583.7 2.4 copy-start.16
  590.3 12.5 %copy-start.19 = (f32[64,6144]{1,0:T(8,128)S(1)}, f32[64,6144]{1,0:T(8,128)}, u32[]{:S(2)}) copy-start(f32[64,6144]{1,0:T(8,128)} %get-tuple-element.110) | copy-start | bytes 4718596
  602.8 1.1 copy-start.1
Sparse Core Ops, SparseCore 0:
  10.5 48.2 all-gather.2
  60.7 138.8 all-gather.4
  332.4 155.6 reduce-scatter.2
  491.7 76.6 reduce-scatter.4

commit v5 on v4

--- a/solution.py
+++ b/solution.py
@@ -281,6 +281,26 @@
         self.parts[at, :] = (self.parts[at, :].astype(F32) + self.arrived(b, p)).astype(BF16)
         self.onward(b, p).start()
 
+    def relay_in_turn(self, j):
+        pieces = self.pieces
+
+        @pl.when(self.inner & (j < pieces))
+        def _():
+            self.relay(self.count - 1 - self.z, j)
+
+        @pl.when(self.inner & (j >= pieces))
+        def _():
+            self.relay(self.far_end, j - pieces)
+
+        @pl.when(self.inner & (j > pieces))
+        def _():
+            self.relay(self.count - 1 - self.far_end, j - pieces - 1)
+
+    def relay_last(self):
+        @pl.when(self.inner)
+        def _():
+            self.relay(self.count - 1 - self.far_end, self.pieces - 1)
+
     def result(self, out):
         z, count = self.z, self.count
         for p in range(self.pieces):
@@ -303,6 +323,56 @@
             return 0
 
         lax.fori_loop(1, self.count, sent, 0)
+
+
+class PairSum:
+    def __init__(self, mine, paired, peers, pair_send, pair_recv, peer_send, peer_recv):
+        self.mine, self.paired, self.peers = mine, paired, peers
+        self.sems = pair_send, pair_recv, peer_send, peer_recv
+        self.s, self.seq = lax.axis_index("seq"), lax.axis_size("seq")
+        self.side, self.pairs, self.own = lax.rem(self.s, 2), self.seq // 2, self.s // 2
+        self.deep = mine.shape[1]
+
+    def block(self, k, other=False):
+        i = 2 * k + (1 - self.side if other else self.side)
+        return pl.ds(pl.multiple_of(i * self.deep, self.deep), self.deep)
+
+    def to_partner(self, src, k):
+        return push(
+            src, self.paired.at[k], self.sems[0].at[k], self.sems[1].at[k],
+            self.s + 1 - 2 * self.side, "seq",
+        )
+
+    def to_peer(self, k):
+        return push(
+            self.mine.at[k], self.peers.at[self.own], self.sems[2].at[k], self.sems[3].at[self.own],
+            2 * k + self.side, "seq",
+        )
+
+    def pass_on(self, k):
+        pl.when(self.own != k)(self.to_peer(k).start)
+
+    def collect(self, out):
+        self.peers[self.own] = self.mine[self.own]
+        for k in range(self.pairs):
+            copy = push(
+                self.mine.at[k], self.peers.at[k], self.sems[2].at[k], self.sems[3].at[k],
+                lax.rem(self.s + 1, self.seq), "seq",
+            )
+            pl.when(self.own != k)(copy.wait_recv)
+        band = 16
+
+        def add_rows(r, _):
+            at = pl.ds(pl.multiple_of(r * band, band), band)
+            out[at, :] = jnp.sum(self.peers[:, at, :].astype(F32), axis=0).astype(out.dtype)
+            return 0
+
+        lax.fori_loop(0, self.deep // band, add_rows, 0)
+
+    def finish(self, src):
+        for k in range(self.pairs):
+            self.to_partner(src(k), k).wait_send()
+            pl.when(self.own != k)(self.to_peer(k).wait_send)
 
 
 def gather_norm_kernel(own, gain, normed, rows_all, here_sem, send, recv):
@@ -575,59 +645,44 @@
 
     lax.fori_loop(0, count, step, 0)
 
-    @pl.when(total.inner)
-    def _():
-        for p in range(total.pieces):
-            total.relay(count - 1 - z, p)
-
     high = tiles.shape[1]
     steps = width // high
-    first = grad.shape[1] - 3 * hidden
 
     def store(t, r, k):
-        return pltpu.make_async_copy(
-            tiles.at[lax.rem(t, 2)],
-            grad.at[
-                pl.ds(pl.multiple_of(r * high, high), high), pl.ds(first + k * hidden, hidden)
-            ],
-            o_sem.at[lax.rem(t, 2)],
-        )
+        down = pl.ds(pl.multiple_of(r * high, high), high)
+        into = grad.at[down, pl.ds(k * hidden, hidden)]
+        return pltpu.make_async_copy(tiles.at[lax.rem(t, 2)], into, o_sem.at[lax.rem(t, 2)])
 
     turned[...] = xs[...].T
     turned_c[...] = cs[...].T
 
+    def tile(r, k):
+        t = 3 * r + k
+
+        @pl.when(t >= 2)
+        def _():
+            store(t, r, k).wait()
+
+        left_rows = (turned_c if k == 2 else turned)[
+            pl.ds(pl.multiple_of(r * high, high), high), :
+        ]
+        tiles[lax.rem(t, 2)] = jnp.dot(
+            left_rows, act[:, k * hidden : (k + 1) * hidden], preferred_element_type=F32
+        ).astype(BF16)
+        store(t, r, k).start()
+
     def slab(r, _):
-        for k in range(3):
-            t = 3 * r + k
-
-            @pl.when(t >= 2)
-            def _():
-                store(t, r, k).wait()
-
-            left_rows = (turned_c if k == 2 else turned)[
-                pl.ds(pl.multiple_of(r * high, high), high), :
-            ]
-            tiles[lax.rem(t, 2)] = jnp.dot(
-                left_rows, act[:, k * hidden : (k + 1) * hidden], preferred_element_type=F32
-            ).astype(BF16)
-            store(t, r, k).start()
-
-        @pl.when(total.inner)
-        def _():
-            total.relay(total.far_end, r)
-            total.relay(count - 1 - total.far_end, r)
-
+        tile(r, 0)
+        tile(r, 1)
+        total.relay_in_turn(2 * r)
+        tile(r, 2)
+        at = chunk(r)
+        f_parts[r] = mm(act[at, 2 * hidden :], wv[:, 2 * hidden :], (1, 1), None).astype(BF16)
+        total.relay_in_turn(2 * r + 1)
         return 0
 
     lax.fori_loop(0, steps, slab, 0)
-
-    def part(b, _):
-        at = chunk(b)
-        f_parts[b] = mm(act[at, 2 * hidden :], wv[:, 2 * hidden :], (1, 1), None).astype(BF16)
-        return 0
-
-    lax.fori_loop(0, count, part, 0)
-
+    total.relay_last()
     total.result(g_x)
     total.finish()
     line.finish()
@@ -708,11 +763,12 @@
 
     def to_head(hop, slot):
         to = lax.rem(h + hop, head)
-        return push(gated_own.at[to], gated_all.at[slot], z_send.at[hop], z_recv.at[slot], to)
+        columns = gated_own.at[:, pl.ds(pl.multiple_of(to * dv, dv), dv)]
+        return push(columns, gated_all.at[slot], z_send.at[hop], z_recv.at[slot], to)
 
     for hop in range(1, head):
         to_head(hop, h).start()
-    gated_all[h] = gated_own[h]
+    gated_all[h] = gated_own[:, pl.ds(pl.multiple_of(h * dv, dv), dv)]
 
     causal = lower_ones(rows)
     before = [jnp.zeros((1, dk), F32)] * micro
@@ -759,7 +815,7 @@
         pl.when(i > 0)(lambda: to_head(lax.rem(b - h + head, head), b).wait_recv())
         for m in range(micro):
             gate, o = og[b, m], o_in[b, m]
-            grad = gated_all[b, m].astype(F32)
+            grad = gated_all[b, m * rows : (m + 1) * rows, :].astype(F32)
             sig = sigmoid(gate)
             inv = lax.rsqrt(jnp.mean(o * o, axis=-1, keepdims=True) + 1e-5)
             plain = o * inv
@@ -886,7 +942,7 @@
         in_specs=[vmem] * 11 + [anywhere] * 2,
         out_specs=(vmem,) * 4 + (anywhere,),
         scratch_shapes=[
-            blocked(dv, BF16), blocked(dv, F32), blocked(dk, F32),
+            pltpu.VMEM((blocks, micro * rows, dv), BF16), blocked(dv, F32), blocked(dk, F32),
             blocked(dk, F32), blocked(dk, F32), blocked(dv, F32),
             pltpu.VMEM((blocks, micro, dv, dk), F32), pltpu.VMEM((blocks, micro, 1, dk), F32),
             pltpu.VMEM((blocks, micro, dv, dk), F32),
@@ -913,13 +969,10 @@
                   turned, proj, w, outgoing, mine, paired, peers, slab, heads_in, parts, landed, slim_high,
                   slim_low, in_sem, pair_send, pair_recv, peer_send, peer_recv, x_send, x_recv,
                   p_sem, q_sem):
-    s, seq = lax.axis_index("seq"), lax.axis_size("seq")
     h, head = lax.axis_index("head"), lax.axis_size("head")
     rows, width = g_x.shape
     deep = grad.shape[0] * head
-    side = lax.rem(s, 2)
-    pairs = seq // 2
-    own_pair = s // 2
+    pairs = lax.axis_size("seq") // 2
 
     loads = [
         pltpu.make_async_copy(proj_in, proj, in_sem.at[0]),
@@ -953,39 +1006,30 @@
 
     lax.fori_loop(0, head, chunk, 0)
 
-    def block(i):
-        return pl.ds(pl.multiple_of(i * deep, deep), deep)
-
-    def to_partner(k):
-        return push(
-            outgoing.at[k], paired.at[k], pair_send.at[k], pair_recv.at[k], s + 1 - 2 * side, "seq"
-        )
-
-    def to_peer(k):
-        return push(
-            mine.at[k], peers.at[own_pair], peer_send.at[k], peer_recv.at[own_pair],
-            2 * k + side, "seq",
-        )
+    sums = PairSum(mine, paired, peers, pair_send, pair_recv, peer_send, peer_recv)
 
     def gone(k, _):
         outgoing[k] = jnp.dot(
-            turned[block(2 * k + 1 - side), :], proj[...], preferred_element_type=F32
+            turned[sums.block(k, True), :], proj[...], preferred_element_type=F32
         ).astype(BF16)
-        to_partner(k).start()
+        sums.to_partner(outgoing.at[k], k).start()
         return 0
 
     lax.fori_loop(0, pairs, gone, 0)
 
     def kept(k, _):
-        here = jnp.dot(turned[block(2 * k + side), :], proj[...], preferred_element_type=F32)
-        to_partner(k).wait_recv()
+        here = jnp.dot(turned[sums.block(k), :], proj[...], preferred_element_type=F32)
+        sums.to_partner(outgoing.at[k], k).wait_recv()
         mine[k] = (here + paired[k].astype(F32)).astype(BF16)
-        pl.when(own_pair != k)(to_peer(k).start)
+        sums.pass_on(k)
 
         @pl.when(total.inner & (k < total.pieces))
         def _():
             total.relay(total.far_end, k)
-            total.relay(head - 1 - total.far_end, k)
+
+        @pl.when(total.inner & (k > 0) & (k <= total.pieces))
+        def _():
+            total.relay(head - 1 - total.far_end, k - 1)
 
         return 0
 
@@ -993,9 +1037,10 @@
 
     @pl.when(total.inner)
     def _():
-        for p in range(pairs, total.pieces):
-            total.relay(total.far_end, p)
-            total.relay(head - 1 - total.far_end, p)
+        for p in range(pairs, total.pieces + 1):
+            if p < total.pieces:
+                total.relay(total.far_end, p)
+            total.relay(head - 1 - total.far_end, p - 1)
         for p in range(total.pieces):
             total.relay(head - 1 - h, p)
 
@@ -1003,23 +1048,7 @@
     g_up[...] = mms(split(ranked[...]), logit_parts, (0, 0))
     g_bias[...] = jnp.broadcast_to(jnp.sum(g_logits[...], axis=0, keepdims=True), g_bias.shape)
 
-    def arrived(k):
-        return push(
-            mine.at[k], peers.at[k], peer_send.at[k], peer_recv.at[k],
-            lax.rem(s + 1, seq), "seq",
-        )
-
-    peers[own_pair] = mine[own_pair]
-    for k in range(pairs):
-        pl.when(own_pair != k)(arrived(k).wait_recv)
-    band = 16
-
-    def add_rows(r, _):
-        at = pl.ds(pl.multiple_of(r * band, band), band)
-        slab[at, :] = jnp.sum(peers[:, at, :].astype(F32), axis=0).astype(BF16)
-        return 0
-
-    lax.fori_loop(0, deep // band, add_rows, 0)
+    sums.collect(slab)
     thin = grad.shape[0]
 
     def to_head(hop, slot):
@@ -1044,9 +1073,7 @@
                 j, :, at : at + size
             ].astype(F32)
             at, start = at + size, start + head * size
-    for k in range(pairs):
-        to_partner(k).wait_send()
-        pl.when(own_pair != k)(to_peer(k).wait_send)
+    sums.finish(lambda k: outgoing.at[k])
     for hop in range(1, head):
         to_head(hop, h).wait_send()
     total.finish()
@@ -1186,7 +1213,6 @@
     g_hidden = cotangent.astype(F32).reshape(micro * rows, width) + back_ffn
     g_mixed = g_hidden.astype(BF16)
     g_gated = dot(g_mixed, w_out, (1, 0)).astype(BF16)
-    g_gated = g_gated.reshape(micro, rows, heads, dv).transpose(2, 0, 1, 3)
     keep = 1.0 - jnp.broadcast_to(starts.T[:, :, None, None], (heads, micro, 1, dk)).astype(F32)
     g_proj_b, g_logits_b, g_head_gain, ffn_out, grad_out = attention_back(
         keep, g_gated, og_b, o_b, qkv_b, decays_b, blocks(logits), through, gain_row,

time: 619 us -> 606 us (0.979)
  Pallas kernels: 468 us -> 449 us
  waiting for transfers between devices: 10.4 us -> 21.8 us
  local copies, waits for them, and re-layouts: 39.6 us -> 33.2 us
    pallas_call x1, Pallas kernels: 123 us -> 106 us  [feed_forward(): pl.pallas_call(functools.partial(ffn_kernel, count), out_shape=(jax.Shape...]
    reduce_scatter x2, waiting for transfers between devices: 0.01 us -> 12.5 us  [scatter_grad(): lax.psum_scatter(g.astype(BF16), 'seq', scatter_dimension=0, tiled=True)]
  transfers between devices with their start and end apart: 5 -> 5, of which waited for: 1 -> 2; matrix products, arithmetic and copies ran while one was open for 12% -> 11% of each run, Pallas kernels for 56% -> 57%
where the time goes in v5:
time: 606 us; the launch traced here: 598 us
  Pallas kernels  449 us (74%)
  local copies, waits for them, and re-layouts  33.2 us (5%)
  matrix products  28.1 us (5%)
  blocking collectives  23.9 us (4%)
  other arithmetic  22.2 us (4%)
  waiting for transfers between devices  21.8 us (4%)
  between operations  14.3 us (2%)
    pallas_call x1, Pallas kernels, feed_forward(): pl.pallas_call(functools.partial(ffn_kernel, count), out_shape=(jax.Shape...  106 us
    pallas_call x1, Pallas kernels, finish(): pl.pallas_call(finish_kernel, out_shape=(jax.ShapeDtypeStruct((rows, widt...  95.8 us
    pallas_call x1, Pallas kernels, attention_back(): pl.pallas_call(back_kernel, out_shape=(jax.ShapeDtypeStruct((blocks, micr...  74.1 us
    pallas_call x1, Pallas kernels, gather_norm(): pl.pallas_call(gather_norm_kernel, out_shape=jax.ShapeDtypeStruct((count...  60.8 us
    pallas_call x1, Pallas kernels, enter(): pl.pallas_call(enter_kernel, out_shape=(jax.ShapeDtypeStruct((slices, mic...  56.5 us
    pallas_call x1, Pallas kernels, total_of(): pl.pallas_call(total_kernel, out_shape=jax.ShapeDtypeStruct(shape, F32),...  28.4 us
    dot_general x6, matrix products, dot(): lax.dot_general(a, b, (((contract[0],), (contract[1],)), ((), ())), preci...  28.1 us
    all_to_all x1, blocking collectives, exchange(): return lax.all_to_all(x, axis, split_axis=0, concat_axis=0, tiled=True)  23.9 us
  transfers between devices with their start and end apart: 5, of which 2 were waited for; matrix products, arithmetic and copies ran while one was open for 11% of the time, Pallas kernels for 57%

profile of v5, /device:TPU:0, one launch (start us, length us, event | category | flops | bytes accessed | tf_op | source)
XLA Modules:
  0.0 597.6 jit_solution(14788687197071208878)
XLA Ops:
  11.8 1.8 pad_maximum_fusion
  15.4 60.8 %gather_norm.1.xn_in = bf16[768,2048]{1,0:T(8,128)(2,1)S(1)} custom-call(bf16[192,2048]{1,0:T(8,128)(2,1)S(1)} %bitcast.50, f32[1,2048]{1,0:T(1,128)S(1)} %bitcast.59), custom_call_target="tpu_custom_call" | custom-call | bytes 150000000 | tf_op jit(solution)/shard_map/gather_norm/pallas_call | solution.py:411
  78.0 2.2 fusion.19
  80.2 5.6 fusion.14
  85.9 9.7 %states.1.own = bf16[8,3,80,256]{3,2,1,0:T(8,128)(2,1)S(1)} custom-call(s32[3,4]{1,0:T(4,128)S(1)} %copy-done.13, bf16[4,3,64,1024]{3,2,1,0:T(8,128)(2,1)S(1)} %bitcast.52, bf16[4,3,64,256]{3,2,1,0:T(8,128)(2,1)S(1)} %bitcast.57), custom_call_target="tpu_custom_call" | custom-call | bytes 30000000 | tf_op jit(solution)/shard_map/states/pallas_call | solution.py:124
  95.6 56.5 %enter.1 = (bf16[8,3,64,256]{3,2,1,0:T(8,128)(2,1)S(1)}, bf16[8,3,16,256]{3,2,1,0:T(8,128)(2,1)S(1)}, bf16[768,2048]{1,0:T(8,128)(2,1)S(1)}) custom-call(bf16[8,3,80,256]{3,2,1,0:T(8,128)(2,1)S(1)} %states.1.own, bf16[192,2048]{1,0:T(8,128)(2,1)S(1)} %bitcast.55), custom_call_target="tpu_custom_call" | custom-call | bytes 150000000 | tf_op jit(solution)/shard_map/enter/pallas_call | solution.py:506
  152.1 5.8 fusion.12
  157.9 18.1 %mix.1 = (f32[4,3,64,512]{3,2,1,0:T(8,128)S(1)}, bf16[4,3,64,512]{3,2,1,0:T(8,128)(2,1)S(1)}, f32[4,3,512,256]{3,2,1,0:T(8,128)}) custom-call(s32[3,4]{1,0:T(4,128)S(1)} %copy-done.13, bf16[4,3,64,1024]{3,2,1,0:T(8,128)(2,1)S(1)} %bitcast.53, bf16[4,3,64,256]{3,2,1,0:T(8,128)(2,1)S(1)} %bitcast.58, f32[4,3,64,512]{3,2,1,0:T(8,128)} %bitcast.62, ...), custom_call_target="tpu_custom_call" | custom-call | bytes 54000000 | tf_op jit(solution)/shard_map/mix/pallas_call | solution.py:144
  176.1 23.9 %all_to_all.10 = bf16[4,3,64,512]{3,2,1,0:T(8,128)(2,1)S(1)} all-to-all(bf16[4,3,64,512]{3,2,1,0:T(8,128)(2,1)S(1)} %get-tuple-element.41), channel_id=1, replica_groups=mesh['seq'=8,'head'=4] {'head'}, dimensions={0} | all-to-all | bytes 1572864 | tf_op jit(solution)/shard_map/all_to_all | solution.py:1120
  201.1 6.4 %multiply_reduce_fusion.5 = (f32[192]{0:T(256)S(1)}, f32[192,2048]{1,0:T(8,128)S(1)}) fusion(bf16[192,2048]{1,0:T(8,128)(2,1)S(1)} %bitcast.65, bf16[2048,6272]{1,0:T(8,128)(2,1)} %all-gather.5.cloned.1.call-done.w, bf16[192,2048]{1,0:T(8,128)(2,1)S(1)} %bitcast.51), kind=kOutput, calls=%fused_computation.24 | convolution fusion | flops 1612185344 | bytes 11535104 | tf_op jit(solution)/shard_map/dot_general | solution.py:1132
  208.6 105.8 %feed_forward.1 = (f32[192,2048]{1,0:T(8,128)}, bf16[4,192,2048]{2,1,0:T(8,128)(2,1)}, bf16[2048,4224]{1,0:T(8,128)(2,1)}) custom-call(bf16[192,2048]{1,0:T(8,128)(2,1)} %multiply_convert_fusion.x_own, bf16[768,2048]{1,0:T(8,128)(2,1)} %copy-done.9, bf16[2048,6272]{1,0:T(8,128)(2,1)} %all-gather.5.cloned.1.call-done.w), custom_call_target="tpu_custom_call" | custom-call | bytes 300000000 | tf_op jit(solution)/shard_map/feed_forward/pallas_call | solution.py:700
  314.6 2.1 multiply_reduce_fusion
  317.3 7.2 %fusion.9.gated_own = bf16[192,2048]{1,0:T(8,128)(2,1)} fusion(bf16[192,2048]{1,0:T(8,128)(2,1)S(1)} %fusion.20.left, bf16[2048,6272]{1,0:T(8,128)(2,1)} %all-gather.5.cloned.1.call-done.w), kind=kOutput, calls=%fused_computation.8 | convolution fusion | flops 1611005952 | bytes 9961472 | tf_op jit(solution)/shard_map/dot_general | solution.py:1132
  325.1 74.1 %attention_back.1 = (bf16[4,3,64,1536]{3,2,1,0:T(8,128)(2,1)}, f32[4,3,64,256]{3,2,1,0:T(8,128)}, f32[8,512]{1,0:T(8,128)}, f32[192,2048]{1,0:T(8,128)}, bf16[2048,2048]{1,0:T(8,128)(2,1)}) custom-call(f32[4,3,1,256]{3,2,1,0:T(1,128)} %broadcast_in_dim.6.keep, bf16[192,2048]{1,0:T(8,128)(2,1)} %fusion.9.gated_own, f32[4,3,64,512]{3,2,1,0:T(8,128)} %bitcast.63, ...), custom_call_target="tpu_custom_call" | custom-call | bytes 240000000 | tf_op jit(solution)/shard_map/attention_back/pallas_call | solution.py:933
  401.5 1.3 bitcast_multiply_fusion
  403.6 95.8 %finish.1 = (f32[192,2048]{1,0:T(8,128)}, f32[64,6144]{1,0:T(8,128)}, f32[2048,16]{1,0:T(8,128)}, f32[16,256]{1,0:T(8,128)}, f32[8,256]{1,0:T(8,128)}) custom-call(bf16[768,2048]{1,0:T(8,128)(2,1)} %copy-done.2, bf16[768,1536]{1,0:T(8,128)(2,1)} %bitcast.70, bf16[2048,1536]{1,0:T(8,128)(2,1)} %all-gather.3.cloned.1.call-done.w_in, f32[768,256]{1,0:T(8,128)} %bitcast.80, ...), custom_call_target="tpu_custom_call" | custom-call | bytes 180000000 | tf_op jit(solution)/shard_map/finish/pallas_call | solution.py:1091
  499.4 1.5 reshape.163
  502.5 2.4 multiply_reduce_fusion.1
  505.7 28.4 %total.1 = f32[8,4,16,128]{3,2,1,0:T(8,128)} custom-call(f32[8,4,16,128]{3,2,1,0:T(8,128)} %bitcast.78), custom_call_target="tpu_custom_call" | custom-call | bytes 45000000 | tf_op jit(solution)/shard_map/total/pallas_call | solution.py:565
  534.1 2.8 slice.50
  537.8 1.3 slice.64
  540.4 2.3 slice.62
  543.3 1.3 fusion.21
  544.6 12.5 %reduce-scatter.5.cloned.1.call-done = bf16[256,2048]{1,0:T(8,128)(2,1)} async-done(((bf16[2048,2048]{1,0:T(8,128)(2,1)}), bf16[256,2048]{1,0:T(8,128)(2,1)}) %reduce-scatter.5.cloned.1.call-update) | async-done | bytes 1048592 | tf_op jit(solution)/shard_map/reduce_scatter | solution.py:1128
  557.1 4.6 all-to-all-start.1
  561.7 3.1 slice_convert_fusion
  564.8 2.2 copy.34
  567.0 4.7 reshape.172
  571.6 2.4 slice_convert_fusion.1
  574.1 4.2 multiply_add_fusion
  578.2 9.2 %all-to-all-done.1 = bf16[4,64,2048]{2,1,0:T(8,128)(2,1)} async-done(((bf16[4,64,2048]{2,1,0:T(8,128)(2,1)}), bf16[4,64,2048]{2,1,0:T(8,128)(2,1)}, u32[]{:S(2)}, u32[]{:S(2)}) %all-to-all-start.1) | async-done | bytes 1048608 | tf_op jit(solution)/shard_map/all_to_all | solution.py:1120
  587.5 2.2 convert_reduce_fusion
  (103 shorter events, 21.1 us)
Async XLA Ops:
  7.2 69.8 %copy-start = (f32[16,1024]{1,0:T(8,128)S(1)}, f32[16,1024]{1,0:T(8,128)}, u32[]{:S(2)}) copy-start(f32[16,1024]{1,0:T(8,128)} %param.24) | copy-start | bytes 196612
  7.2 73.0 %all-gather.3.cloned.1.call-start = ((), (), s32[]{:S(2)}) async-start(), calls=%async_computation.4 | async-start | bytes 7077888 | tf_op jit(solution)/shard_map/all_gather | solution.py:1124
  8.2 2.2 copy-start.20
  10.4 1.2 copy-start.21
  10.4 1.4 copy-start.22
  10.4 190.4 %all-gather.5.cloned.1.call-start = ((), (), s32[]{:S(2)}) async-start(), calls=%async_computation.5 | async-start | bytes 28901376 | tf_op jit(solution)/shard_map/all_gather | solution.py:1124
  13.6 0.7 copy-start.12
  13.6 488.9 %reduce-scatter.3.cloned.1.call-start = ((), (), s32[]{:S(2)}) async-start(), calls=%async_computation.6 | async-start | bytes 19464192 | tf_op jit(solution)/shard_map/reduce_scatter | solution.py:1128
  14.3 1.1 copy-start.3
  15.4 61.6 %copy-start.23 = (bf16[2048,16]{0,1:T(8,128)(2,1)S(1)}, bf16[2048,16]{0,1:T(8,128)(2,1)}, u32[]{:S(2)}) copy-start(bf16[2048,16]{0,1:T(8,128)(2,1)} %param.23) | copy-start | bytes 196612
  76.2 75.9 %copy-start.2 = (bf16[768,2048]{1,0:T(8,128)(2,1)}, bf16[768,2048]{1,0:T(8,128)(2,1)S(1)}, u32[]{:S(2)}) copy-start(bf16[768,2048]{1,0:T(8,128)(2,1)S(1)} %gather_norm.1.xn_in) | copy-start | bytes 9437188
  77.0 0.9 copy-start.25
  80.2 5.7 copy-start.13
  80.2 5.7 copy-start.8
  85.8 72.1 %copy-start.5 = (bf16[768,1024]{1,0:T(8,128)(2,1)}, bf16[768,1024]{1,0:T(8,128)(2,1)S(1)}, u32[]{:S(2)}) copy-start(bf16[768,1024]{1,0:T(8,128)(2,1)S(1)} %fusion.14) | copy-start | bytes 4718596
  85.9 9.7 %copy-start.6 = (bf16[3,64,2048]{2,1,0:T(8,128)(2,1)S(1)}, bf16[3,64,2048]{2,1,0:T(8,128)(2,1)}, u32[]{:S(2)}) copy-start(bf16[3,64,2048]{2,1,0:T(8,128)(2,1)} %param.15) | copy-start | bytes 2359300
  152.1 5.8 copy-start.9
  152.1 5.8 copy-start.11
  152.1 5.8 copy-start.14
  176.1 24.5 %copy-start.10 = (f32[4,3,64,512]{3,2,1,0:T(8,128)}, f32[4,3,64,512]{3,2,1,0:T(8,128)S(1)}, u32[]{:S(2)}) copy-start(f32[4,3,64,512]{3,2,1,0:T(8,128)S(1)} %get-tuple-element.44.o_in) | copy-start | bytes 4718596
  200.0 1.1 copy-start.4
  200.8 6.7 %copy-start.17 = (bf16[24,8,4,512]{3,1,2,0:T(8,128)(2,1)}, bf16[24,8,4,512]{3,1,2,0:T(8,128)(2,1)S(1)}, u32[]{:S(2)}) copy-start(bf16[24,8,4,512]{3,1,2,0:T(8,128)(2,1)S(1)} %copy.35) | copy-start | bytes 2359300
  201.1 6.4 %copy-start.24 = (f32[2048]{0:T(1024)S(1)}, f32[2048]{0:T(1024)}, u32[]{:S(2)}) copy-start(f32[2048]{0:T(1024)} %param.21) | copy-start | bytes 24580
  314.5 242.6 %reduce-scatter.5.cloned.1.call-start = ((), (), s32[]{:S(2)}) async-start(), calls=%async_computation.7 | async-start | bytes 9437184 | tf_op jit(solution)/shard_map/reduce_scatter | solution.py:1128
  314.6 2.1 copy-start.7
  314.6 2.1 copy-start.15
  317.3 7.2 %copy-start.18 = (bf16[192,2048]{1,0:T(8,128)(2,1)}, bf16[192,2048]{1,0:T(8,128)(2,1)S(1)}, u32[]{:S(2)}) copy-start(bf16[192,2048]{1,0:T(8,128)(2,1)S(1)} %fusion.20.left) | copy-start | bytes 2359300
  557.1 30.4 %all-to-all-start.1 = ((bf16[4,64,2048]{2,1,0:T(8,128)(2,1)}), bf16[4,64,2048]{2,1,0:T(8,128)(2,1)}, u32[]{:S(2)}, u32[]{:S(2)}) async-start(bf16[4,64,2048]{2,1,0:T(8,128)(2,1)} %bitcast.77), calls=%async_computation.3 | async-start | bytes 2097152 | tf_op jit(solution)/shard_map/all_to_all | solution.py:1120
  571.6 2.4 copy-start.16
  578.2 11.5 %copy-start.19 = (f32[64,6144]{1,0:T(8,128)S(1)}, f32[64,6144]{1,0:T(8,128)}, u32[]{:S(2)}) copy-start(f32[64,6144]{1,0:T(8,128)} %get-tuple-element.110) | copy-start | bytes 4718596
  589.7 1.1 copy-start.1
Sparse Core Ops, SparseCore 0:
  10.5 48.2 all-gather.2
  60.7 138.8 all-gather.4
  314.6 161.2 reduce-scatter.2
  479.6 77.4 reduce-scatter.4

commit v6 on v5

--- a/solution.py
+++ b/solution.py
@@ -582,7 +582,7 @@
     return result
 
 
-def ffn_kernel(count, x_own, c_all, w, g_x, f_parts, grad,
+def ffn_kernel(count, x_own, c_all, w, g_x, f_parts, grad, grad_down,
                wv, xs, cs, act, lin, parts, landed, turned, turned_c, tiles,
                w_sem, own_sem, go_sem, x_sem, p_sem, q_sem, o_sem):
     z = lax.axis_index("head")
@@ -650,7 +650,7 @@
 
     def store(t, r, k):
         down = pl.ds(pl.multiple_of(r * high, high), high)
-        into = grad.at[down, pl.ds(k * hidden, hidden)]
+        into = grad_down.at[down] if k == 2 else grad.at[down, pl.ds(k * hidden, hidden)]
         return pltpu.make_async_copy(tiles.at[lax.rem(t, 2)], into, o_sem.at[lax.rem(t, 2)])
 
     turned[...] = xs[...].T
@@ -702,10 +702,11 @@
         out_shape=(
             jax.ShapeDtypeStruct((rows, width), F32),
             jax.ShapeDtypeStruct((count, rows, width), BF16),
-            jax.ShapeDtypeStruct((width, 3 * hidden), BF16),
+            jax.ShapeDtypeStruct((width, 2 * hidden), BF16),
+            jax.ShapeDtypeStruct((width, hidden), BF16),
         ),
         in_specs=[anywhere] * 3,
-        out_specs=(vmem, vmem, anywhere),
+        out_specs=(vmem, vmem, anywhere, anywhere),
         scratch_shapes=[
             pltpu.VMEM((width, 3 * hidden), BF16),
             pltpu.VMEM((group, width), BF16),
@@ -1206,8 +1207,8 @@
     plain_ffn = hidden * inv_ffn
     h2 = (plain_ffn * ffn_gain).astype(BF16)
 
-    g_h2, ffn_part, grad_ffn = feed_forward(h2, all_cot, later, hidden_units, heads)
-    grad_ffn = scatter_grad(grad_ffn)
+    g_h2, ffn_part, grad_gu, grad_down = feed_forward(h2, all_cot, later, hidden_units, heads)
+    grad_gu, grad_down = scatter_grad(grad_gu), scatter_grad(grad_down)
 
     back_ffn, g_ffn_gain = norm_back(g_h2, ffn_gain, plain_ffn, inv_ffn)
     g_hidden = cotangent.astype(F32).reshape(micro * rows, width) + back_ffn
@@ -1224,10 +1225,13 @@
     g_xn, grad_in, g_rank_down, g_rank_up, g_bias = finish(
         xn, g_proj, w_in, g_logits, ranked, up_own, rank_down
     )
-    g_xn, grad_ffn = lax.optimization_barrier((g_xn, grad_ffn))
+    g_xn, grad_gu = lax.optimization_barrier((g_xn, grad_gu))
     inv_in = rms(source, 1e-6)
     back_in, g_norm_gain = norm_back(g_xn, norm_gain, source * inv_in, inv_in)
     input_grad = g_hidden + back_in
+    slab = width // (seq * heads)
+    g_norm_gain, grad_out = lax.optimization_barrier((g_norm_gain, grad_out))
+    grad_out = exchange(grad_out.reshape(heads, slab, vals), "head").astype(F32).sum(0)
 
     g_rank_up = lax.dynamic_update_slice_in_dim(
         jnp.zeros(rank_up.shape, F32), g_rank_up, head * dk, 1
@@ -1238,16 +1242,14 @@
     small = total_of(
         [g_norm_gain, g_ffn_gain, g_head_gain[0], g_rank_down, g_rank_up, g_bias]
     )
-    slab = width // (seq * heads)
-    small, grad_out = lax.optimization_barrier((small, grad_out))
-    grad_out = exchange(grad_out.reshape(heads, slab, vals), "head").astype(F32).sum(0)
+    small, grad_down = lax.optimization_barrier((small, grad_down))
     return (
         output.reshape(tokens.shape),
         input_grad.reshape(tokens.shape),
         grad_in,
         grad_out,
-        grad_ffn[:, : 2 * hidden_units].astype(F32).reshape(-1, 2, hidden_units),
-        grad_ffn[:, 2 * hidden_units :].astype(F32),
+        grad_gu.astype(F32).reshape(-1, 2, hidden_units),
+        grad_down.astype(F32),
         *small,
     )
 

time: 606 us -> 620 us (1.023)
  waiting for transfers between devices: 21.8 us -> 30.5 us
  Pallas kernels: 449 us -> 457 us
    reduce_scatter x2 -> x3, waiting for transfers between devices: 12.5 us -> 29.8 us  [scatter_grad(): lax.psum_scatter(g.astype(BF16), 'seq', scatter_dimension=0, tiled=True)]
    all_to_all x1, waiting for transfers between devices: 9.24 us -> 0.01 us  [exchange(): return lax.all_to_all(x, axis, split_axis=0, concat_axis=0, tiled=True)]
    pallas_call x1, Pallas kernels: 28.4 us -> 36.3 us  [total_of(): pl.pallas_call(total_kernel, out_shape=jax.ShapeDtypeStruct(shape, F32),...]
  transfers between devices with their start and end apart: 5 -> 6, of which waited for: 2 -> 2; matrix products, arithmetic and copies ran while one was open for 11% -> 10% of each run, Pallas kernels for 57% -> 57%
where the time goes in v6:
time: 620 us; the launch traced here: 612 us
  Pallas kernels  457 us (74%)
  local copies, waits for them, and re-layouts  33 us (5%)
  waiting for transfers between devices  30.5 us (5%)
  matrix products  28.4 us (5%)
  blocking collectives  23.9 us (4%)
  other arithmetic  19.5 us (3%)
  between operations  14.4 us (2%)
    pallas_call x1, Pallas kernels, feed_forward(): pl.pallas_call(functools.partial(ffn_kernel, count), out_shape=(jax.Shape...  106 us
    pallas_call x1, Pallas kernels, finish(): pl.pallas_call(finish_kernel, out_shape=(jax.ShapeDtypeStruct((rows, widt...  95.8 us
    pallas_call x1, Pallas kernels, attention_back(): pl.pallas_call(back_kernel, out_shape=(jax.ShapeDtypeStruct((blocks, micr...  74.4 us
    pallas_call x1, Pallas kernels, gather_norm(): pl.pallas_call(gather_norm_kernel, out_shape=jax.ShapeDtypeStruct((count...  60.8 us
    pallas_call x1, Pallas kernels, enter(): pl.pallas_call(enter_kernel, out_shape=(jax.ShapeDtypeStruct((slices, mic...  56.5 us
    pallas_call x1, Pallas kernels, total_of(): pl.pallas_call(total_kernel, out_shape=jax.ShapeDtypeStruct(shape, F32),...  36.3 us
    reduce_scatter x3, waiting for transfers between devices, scatter_grad(): lax.psum_scatter(g.astype(BF16), 'seq', scatter_dimension=0, tiled=True)  29.8 us
    dot_general x6, matrix products, dot(): lax.dot_general(a, b, (((contract[0],), (contract[1],)), ((), ())), preci...  28.4 us
  transfers between devices with their start and end apart: 6, of which 2 were waited for; matrix products, arithmetic and copies ran while one was open for 10% of the time, Pallas kernels for 57%

profile of v6, /device:TPU:0, one launch (start us, length us, event | category | flops | bytes accessed | tf_op | source)
XLA Modules:
  0.0 612.0 jit_solution(3881416099021581397)
XLA Ops:
  11.8 1.8 pad_maximum_fusion
  15.4 60.8 %gather_norm.1.xn_in = bf16[768,2048]{1,0:T(8,128)(2,1)S(1)} custom-call(bf16[192,2048]{1,0:T(8,128)(2,1)S(1)} %bitcast.50, f32[1,2048]{1,0:T(1,128)S(1)} %bitcast.59), custom_call_target="tpu_custom_call" | custom-call | bytes 150000000 | tf_op jit(solution)/shard_map/gather_norm/pallas_call | solution.py:411
  78.0 2.2 fusion.19
  80.2 5.6 fusion.14
  85.9 9.7 %states.1.own = bf16[8,3,80,256]{3,2,1,0:T(8,128)(2,1)S(1)} custom-call(s32[3,4]{1,0:T(4,128)S(1)} %copy-done.13, bf16[4,3,64,1024]{3,2,1,0:T(8,128)(2,1)S(1)} %bitcast.52, bf16[4,3,64,256]{3,2,1,0:T(8,128)(2,1)S(1)} %bitcast.57), custom_call_target="tpu_custom_call" | custom-call | bytes 30000000 | tf_op jit(solution)/shard_map/states/pallas_call | solution.py:124
  95.6 56.5 %enter.1 = (bf16[8,3,64,256]{3,2,1,0:T(8,128)(2,1)S(1)}, bf16[8,3,16,256]{3,2,1,0:T(8,128)(2,1)S(1)}, bf16[768,2048]{1,0:T(8,128)(2,1)S(1)}) custom-call(bf16[8,3,80,256]{3,2,1,0:T(8,128)(2,1)S(1)} %states.1.own, bf16[192,2048]{1,0:T(8,128)(2,1)S(1)} %bitcast.55), custom_call_target="tpu_custom_call" | custom-call | bytes 150000000 | tf_op jit(solution)/shard_map/enter/pallas_call | solution.py:506
  152.1 5.8 fusion.12
  157.9 18.2 %mix.1 = (f32[4,3,64,512]{3,2,1,0:T(8,128)S(1)}, bf16[4,3,64,512]{3,2,1,0:T(8,128)(2,1)S(1)}, f32[4,3,512,256]{3,2,1,0:T(8,128)}) custom-call(s32[3,4]{1,0:T(4,128)S(1)} %copy-done.13, bf16[4,3,64,1024]{3,2,1,0:T(8,128)(2,1)S(1)} %bitcast.53, bf16[4,3,64,256]{3,2,1,0:T(8,128)(2,1)S(1)} %bitcast.58, f32[4,3,64,512]{3,2,1,0:T(8,128)} %bitcast.62, ...), custom_call_target="tpu_custom_call" | custom-call | bytes 54000000 | tf_op jit(solution)/shard_map/mix/pallas_call | solution.py:144
  176.1 23.9 %all_to_all.10 = bf16[4,3,64,512]{3,2,1,0:T(8,128)(2,1)S(1)} all-to-all(bf16[4,3,64,512]{3,2,1,0:T(8,128)(2,1)S(1)} %get-tuple-element.44), channel_id=1, replica_groups=mesh['seq'=8,'head'=4] {'head'}, dimensions={0} | all-to-all | bytes 1572864 | tf_op jit(solution)/shard_map/all_to_all | solution.py:1121
  201.1 6.4 %multiply_reduce_fusion.5 = (f32[192]{0:T(256)S(1)}, f32[192,2048]{1,0:T(8,128)S(1)}) fusion(bf16[192,2048]{1,0:T(8,128)(2,1)S(1)} %bitcast.65, bf16[2048,6272]{1,0:T(8,128)(2,1)} %all-gather.5.cloned.1.call-done.w, bf16[192,2048]{1,0:T(8,128)(2,1)S(1)} %bitcast.51), kind=kOutput, calls=%fused_computation.24 | convolution fusion | flops 1612185344 | bytes 11535104 | tf_op jit(solution)/shard_map/dot_general | solution.py:1133
  208.7 105.8 %feed_forward.1 = (f32[192,2048]{1,0:T(8,128)}, bf16[4,192,2048]{2,1,0:T(8,128)(2,1)}, bf16[2048,2816]{1,0:T(8,128)(2,1)}, bf16[2048,1408]{1,0:T(8,128)(2,1)}) custom-call(bf16[192,2048]{1,0:T(8,128)(2,1)} %multiply_convert_fusion.x_own, bf16[768,2048]{1,0:T(8,128)(2,1)} %copy-done.9, bf16[2048,6272]{1,0:T(8,128)(2,1)} %all-gather.5.cloned.1.call-done.w), custom_call_target="tpu_custom_call" | custom-call | bytes 300000000 | tf_op jit(solution)/shard_map/feed_forward/pallas_call | solution.py:700
  314.7 2.1 multiply_reduce_fusion
  317.3 7.4 %fusion.9.gated_own = bf16[192,2048]{1,0:T(8,128)(2,1)} fusion(bf16[192,2048]{1,0:T(8,128)(2,1)S(1)} %fusion.20.left, bf16[2048,6272]{1,0:T(8,128)(2,1)} %all-gather.5.cloned.1.call-done.w), kind=kOutput, calls=%fused_computation.8 | convolution fusion | flops 1611005952 | bytes 9961472 | tf_op jit(solution)/shard_map/dot_general | solution.py:1133
  325.4 74.4 %attention_back.1 = (bf16[4,3,64,1536]{3,2,1,0:T(8,128)(2,1)}, f32[4,3,64,256]{3,2,1,0:T(8,128)}, f32[8,512]{1,0:T(8,128)}, f32[192,2048]{1,0:T(8,128)}, bf16[2048,2048]{1,0:T(8,128)(2,1)}) custom-call(f32[4,3,1,256]{3,2,1,0:T(1,128)} %broadcast_in_dim.6.keep, bf16[192,2048]{1,0:T(8,128)(2,1)} %fusion.9.gated_own, f32[4,3,64,512]{3,2,1,0:T(8,128)} %bitcast.63, ...), custom_call_target="tpu_custom_call" | custom-call | bytes 240000000 | tf_op jit(solution)/shard_map/attention_back/pallas_call | solution.py:934
  402.6 1.3 bitcast_multiply_fusion
  404.7 95.8 %finish.1 = (f32[192,2048]{1,0:T(8,128)}, f32[64,6144]{1,0:T(8,128)}, f32[2048,16]{1,0:T(8,128)}, f32[16,256]{1,0:T(8,128)}, f32[8,256]{1,0:T(8,128)}) custom-call(bf16[768,2048]{1,0:T(8,128)(2,1)} %copy-done.2, bf16[768,1536]{1,0:T(8,128)(2,1)} %bitcast.70, bf16[2048,1536]{1,0:T(8,128)(2,1)} %all-gather.3.cloned.1.call-done.w_in, f32[768,256]{1,0:T(8,128)} %bitcast.80, ...), custom_call_target="tpu_custom_call" | custom-call | bytes 180000000 | tf_op jit(solution)/shard_map/finish/pallas_call | solution.py:1092
  500.5 1.5 reshape.166
  503.7 2.4 multiply_reduce_fusion.1
  506.0 16.7 %reduce-scatter.6.cloned.1.call-done = bf16[256,2048]{1,0:T(8,128)(2,1)} async-done(((bf16[2048,2048]{1,0:T(8,128)(2,1)}), bf16[256,2048]{1,0:T(8,128)(2,1)}) %reduce-scatter.6.cloned.1.call-update) | async-done | bytes 1048592 | tf_op jit(solution)/shard_map/reduce_scatter | solution.py:1129
  522.8 4.8 all-to-all-start.1
  528.4 36.3 %total.1 = f32[8,4,16,128]{3,2,1,0:T(8,128)} custom-call(f32[8,4,16,128]{3,2,1,0:T(8,128)} %bitcast.78), custom_call_target="tpu_custom_call" | custom-call | bytes 45000000 | tf_op jit(solution)/shard_map/total/pallas_call | solution.py:565
  564.7 2.8 slice.44
  568.4 1.3 slice.56
  569.7 1.3 slice.53
  570.9 2.3 slice.54
  573.9 1.3 fusion.21
  575.2 13.1 %reduce-scatter.8.cloned.1.call-done = bf16[256,1408]{1,0:T(8,128)(2,1)} async-done(((bf16[2048,1408]{1,0:T(8,128)(2,1)}), bf16[256,1408]{1,0:T(8,128)(2,1)}) %reduce-scatter.8.cloned.1.call-update) | async-done | bytes 720912 | tf_op jit(solution)/shard_map/reduce_scatter | solution.py:1129
  588.3 2.3 convert_element_type.48
  590.6 2.2 copy.34
  592.8 4.3 reshape.172
  597.2 4.6 multiply_add_fusion
  601.7 2.3 convert_reduce_fusion
  (103 shorter events, 20.4 us)
Async XLA Ops:
  7.2 69.8 %copy-start = (f32[16,1024]{1,0:T(8,128)S(1)}, f32[16,1024]{1,0:T(8,128)}, u32[]{:S(2)}) copy-start(f32[16,1024]{1,0:T(8,128)} %param.24) | copy-start | bytes 196612
  7.2 73.0 %all-gather.3.cloned.1.call-start = ((), (), s32[]{:S(2)}) async-start(), calls=%async_computation.5 | async-start | bytes 7077888 | tf_op jit(solution)/shard_map/all_gather | solution.py:1125
  8.2 2.2 copy-start.19
  10.4 1.2 copy-start.20
  10.4 1.4 copy-start.21
  10.4 190.4 %all-gather.5.cloned.1.call-start = ((), (), s32[]{:S(2)}) async-start(), calls=%async_computation.6 | async-start | bytes 28901376 | tf_op jit(solution)/shard_map/all_gather | solution.py:1125
  13.6 0.7 copy-start.12
  13.6 490.0 %reduce-scatter.4.cloned.1.call-start = ((), (), s32[]{:S(2)}) async-start(), calls=%async_computation.7 | async-start | bytes 12976128 | tf_op jit(solution)/shard_map/reduce_scatter | solution.py:1129
  14.3 1.1 copy-start.3
  15.4 61.6 %copy-start.22 = (bf16[2048,16]{0,1:T(8,128)(2,1)S(1)}, bf16[2048,16]{0,1:T(8,128)(2,1)}, u32[]{:S(2)}) copy-start(bf16[2048,16]{0,1:T(8,128)(2,1)} %param.23) | copy-start | bytes 196612
  76.2 75.9 %copy-start.2 = (bf16[768,2048]{1,0:T(8,128)(2,1)}, bf16[768,2048]{1,0:T(8,128)(2,1)S(1)}, u32[]{:S(2)}) copy-start(bf16[768,2048]{1,0:T(8,128)(2,1)S(1)} %gather_norm.1.xn_in) | copy-start | bytes 9437188
  77.0 0.9 copy-start.24
  80.2 5.7 copy-start.13
  80.2 5.7 copy-start.8
  85.8 72.1 %copy-start.5 = (bf16[768,1024]{1,0:T(8,128)(2,1)}, bf16[768,1024]{1,0:T(8,128)(2,1)S(1)}, u32[]{:S(2)}) copy-start(bf16[768,1024]{1,0:T(8,128)(2,1)S(1)} %fusion.14) | copy-start | bytes 4718596
  85.9 9.7 %copy-start.6 = (bf16[3,64,2048]{2,1,0:T(8,128)(2,1)S(1)}, bf16[3,64,2048]{2,1,0:T(8,128)(2,1)}, u32[]{:S(2)}) copy-start(bf16[3,64,2048]{2,1,0:T(8,128)(2,1)} %param.15) | copy-start | bytes 2359300
  152.1 5.8 copy-start.9
  152.1 5.8 copy-start.11
  152.1 5.8 copy-start.14
  176.1 24.5 %copy-start.10 = (f32[4,3,64,512]{3,2,1,0:T(8,128)}, f32[4,3,64,512]{3,2,1,0:T(8,128)S(1)}, u32[]{:S(2)}) copy-start(f32[4,3,64,512]{3,2,1,0:T(8,128)S(1)} %get-tuple-element.47.o_in) | copy-start | bytes 4718596
  200.0 1.1 copy-start.4
  200.8 6.7 %copy-start.16 = (bf16[24,8,4,512]{3,1,2,0:T(8,128)(2,1)}, bf16[24,8,4,512]{3,1,2,0:T(8,128)(2,1)S(1)}, u32[]{:S(2)}) copy-start(bf16[24,8,4,512]{3,1,2,0:T(8,128)(2,1)S(1)} %copy.35) | copy-start | bytes 2359300
  201.1 6.4 %copy-start.23 = (f32[2048]{0:T(1024)S(1)}, f32[2048]{0:T(1024)}, u32[]{:S(2)}) copy-start(f32[2048]{0:T(1024)} %param.21) | copy-start | bytes 24580
  314.5 208.2 %reduce-scatter.6.cloned.1.call-start = ((), (), s32[]{:S(2)}) async-start(), calls=%async_computation.8 | async-start | bytes 9437184 | tf_op jit(solution)/shard_map/reduce_scatter | solution.py:1129
  314.7 2.1 copy-start.7
  314.7 2.1 copy-start.15
  317.3 7.4 %copy-start.17 = (bf16[192,2048]{1,0:T(8,128)(2,1)}, bf16[192,2048]{1,0:T(8,128)(2,1)S(1)}, u32[]{:S(2)}) copy-start(bf16[192,2048]{1,0:T(8,128)(2,1)S(1)} %fusion.20.left) | copy-start | bytes 2359300
  399.8 188.5 %reduce-scatter.8.cloned.1.call-start = ((), (), s32[]{:S(2)}) async-start(), calls=%async_computation.9 | async-start | bytes 6488064 | tf_op jit(solution)/shard_map/reduce_scatter | solution.py:1129
  522.8 79.0 %all-to-all-start.1 = ((bf16[4,64,2048]{2,1,0:T(8,128)(2,1)}), bf16[4,64,2048]{2,1,0:T(8,128)(2,1)}, u32[]{:S(2)}, u32[]{:S(2)}) async-start(bf16[4,64,2048]{2,1,0:T(8,128)(2,1)} %bitcast.77), calls=%async_computation.3 | async-start | bytes 2097152 | tf_op jit(solution)/shard_map/all_to_all | solution.py:1121
  601.7 2.3 copy-start.18
  604.1 1.1 copy-start.1
Sparse Core Ops, SparseCore 0:
  10.5 48.2 all-gather.2
  60.7 138.8 all-gather.4
  314.7 101.3 reduce-scatter.3
  419.4 103.3 reduce-scatter.5
  526.4 61.8 reduce-scatter.7

commit v7 on v5

--- a/solution.py
+++ b/solution.py
@@ -20,6 +20,20 @@
     )
 
 
+def split(x):
+    high = x.astype(BF16)
+    return high, (x - high.astype(F32)).astype(BF16)
+
+
+def mms(left, right, contract):
+    total = mm(left[0], right[0], contract, None)
+    if len(right) > 1:
+        total += mm(left[0], right[1], contract, None)
+    if len(left) > 1:
+        total += mm(left[1], right[0], contract, None)
+    return total
+
+
 def lower_ones(size):
     rows = lax.broadcasted_iota(jnp.int32, (size, size), 0)
     cols = lax.broadcasted_iota(jnp.int32, (size, size), 1)
@@ -35,136 +49,8 @@
     return 1.0 / (1.0 + jnp.exp(-x))
 
 
-def state_kernel(flags, qkv, decay, out, state, total_run):
-    m, b = pl.program_id(0), pl.program_id(1)
-    last = pl.num_programs(1) - 1
-    dk = decay.shape[-1]
-    keys, values = qkv[0, 0, :, dk : 2 * dk].astype(F32), qkv[0, 0, :, 2 * dk :].astype(F32)
-    keep = 1.0 - flags[m, b].astype(F32)
-
-    @pl.when(b == 0)
-    def _():
-        state[...] = jnp.zeros_like(state)
-        total_run[0:1, :] = jnp.zeros((1, dk), F32)
-        total_run[1:2, :] = jnp.ones((1, dk), F32)
-
-    run = running(decay[0, 0])
-    total = run[-1:, :]
-    carried = keys * jnp.exp(total - run)
-    state[...] = jnp.exp(total) * (state[...] * keep) + mm(values, carried, (0, 0))
-    total_run[0:1, :] += total
-    total_run[1:2, :] *= keep
-
-    @pl.when(b == last)
-    def _():
-        through = jnp.exp(total_run[0:1, :]) * total_run[1:2, :]
-        high = through.astype(BF16)
-        low = (through - high.astype(F32)).astype(BF16)
-        slices, part = out.shape[0], state.shape[0] // out.shape[0]
-        tail = out.shape[2] - part
-        at = lax.broadcasted_iota(jnp.int32, (tail, dk), 0)
-        extra = jnp.where(
-            at == 0, high.astype(F32), jnp.where(at == 1, low.astype(F32), 0.0)
-        ).astype(BF16)
-        for i in range(slices):
-            out[i, 0, :part, :] = state[i * part : (i + 1) * part, :].astype(BF16)
-            out[i, 0, part:, :] = extra
-
-
-def mix_kernel(flags, qkv, decay, og, before, gain, o_out, gated, kept, state):
-    m, b = pl.program_id(0), pl.program_id(1)
-    dk, dv = decay.shape[-1], og.shape[-1]
-    q = qkv[0, 0, :, :dk].astype(F32)
-    k = qkv[0, 0, :, dk : 2 * dk].astype(F32)
-    v = qkv[0, 0, :, 2 * dk :].astype(F32)
-    keep = 1.0 - flags[m, b].astype(F32)
-
-    @pl.when(b == 0)
-    def _():
-        state[...] = before[:, 0].astype(F32).reshape(dv, dk)
-
-    entry = state[...] * keep
-    kept[0, 0] = entry
-    run = running(decay[0, 0])
-    total = run[-1:, :]
-    queried = q * jnp.exp(run) * dk ** (-0.5)
-    scores = mm(queried, k * jnp.exp(-run), (1, 1))
-    scores = jnp.where(lower_ones(scores.shape[0]), scores, 0.0)
-    o = mm(scores, v, (1, 0)) + mm(queried, entry, (1, 1))
-    state[...] = jnp.exp(total) * entry + mm(v, k * jnp.exp(total - run), (0, 0))
-    o_out[0, 0] = o
-    scale = lax.rsqrt(jnp.mean(o * o, axis=-1, keepdims=True) + 1e-5)
-    normed = (o * scale * gain[...]).astype(BF16).astype(F32)
-    gate = og[0, 0]
-    gated[0, 0] = (normed * gate * sigmoid(gate)).astype(BF16)
-
-
-def params(limit=48):
-    return pltpu.CompilerParams(
-        dimension_semantics=("arbitrary", "arbitrary"), vmem_limit_bytes=limit << 20
-    )
-
-
 def cost(micros):
     return pl.CostEstimate(flops=0, bytes_accessed=int(micros * 3.0e6), transcendentals=0)
-
-
-def per_block(rows, width):
-    return pl.BlockSpec((1, 1, rows, width), lambda m, b, *_: (b, m, 0, 0))
-
-
-def per_batch(slices, rows, width):
-    return pl.BlockSpec((slices, 1, rows, width), lambda m, b, *_: (0, m, 0, 0))
-
-
-def states_of(flags, qkv, decays, dv, slices, pad):
-    blocks, micro, rows, width = qkv.shape
-    dk = decays.shape[-1]
-    part = dv // slices
-    return pl.pallas_call(
-        state_kernel,
-        out_shape=jax.ShapeDtypeStruct((slices, micro, part + pad, dk), BF16),
-        grid_spec=pltpu.PrefetchScalarGridSpec(
-            num_scalar_prefetch=1,
-            grid=(micro, blocks),
-            in_specs=[per_block(rows, width), per_block(rows, dk)],
-            out_specs=per_batch(slices, part + pad, dk),
-            scratch_shapes=[pltpu.VMEM((dv, dk), F32), pltpu.VMEM((8, dk), F32)],
-        ),
-        compiler_params=params(),
-        cost_estimate=cost(10),
-        name="states",
-    )(flags, qkv, decays)
-
-
-def mix_of(flags, qkv, decays, og, before, gain):
-    blocks, micro, rows, width = qkv.shape
-    dk, dv = decays.shape[-1], og.shape[-1]
-    slices, _, part, _ = before.shape
-    return pl.pallas_call(
-        mix_kernel,
-        out_shape=(
-            jax.ShapeDtypeStruct((blocks, micro, rows, dv), F32),
-            jax.ShapeDtypeStruct((blocks, micro, rows, dv), BF16),
-            jax.ShapeDtypeStruct((blocks, micro, dv, dk), F32),
-        ),
-        grid_spec=pltpu.PrefetchScalarGridSpec(
-            num_scalar_prefetch=1,
-            grid=(micro, blocks),
-            in_specs=[
-                per_block(rows, width),
-                per_block(rows, dk),
-                per_block(rows, dv),
-                per_batch(slices, part, dk),
-                pl.BlockSpec((1, dv), lambda m, b, *_: (0, 0)),
-            ],
-            out_specs=(per_block(rows, dv), per_block(rows, dv), per_block(dv, dk)),
-            scratch_shapes=[pltpu.VMEM((dv, dk), F32)],
-        ),
-        compiler_params=params(),
-        cost_estimate=cost(18),
-        name="mix",
-    )(flags, qkv, decays, og, before, gain)
 
 
 def greet(axes):
@@ -326,12 +212,14 @@
 
 
 class PairSum:
-    def __init__(self, mine, paired, peers, pair_send, pair_recv, peer_send, peer_recv):
-        self.mine, self.paired, self.peers = mine, paired, peers
-        self.sems = pair_send, pair_recv, peer_send, peer_recv
-        self.s, self.seq = lax.axis_index("seq"), lax.axis_size("seq")
-        self.side, self.pairs, self.own = lax.rem(self.s, 2), self.seq // 2, self.s // 2
-        self.deep = mine.shape[1]
+    def __init__(self, mine, paired, inbox, pair_send, pair_recv, send, recv):
+        self.mine, self.paired, self.inbox = mine, paired, inbox
+        self.pair_send, self.pair_recv, self.send, self.recv = pair_send, pair_recv, send, recv
+        self.s, self.pairs = lax.axis_index("seq"), lax.axis_size("seq") // 2
+        self.side, self.own = lax.rem(self.s, 2), self.s // 2
+        self.deep, self.half = mine.shape[1], mine.shape[2] // 2
+        self.levels = self.pairs.bit_length() - 1
+        assert self.pairs == 1 << self.levels
 
     def block(self, k, other=False):
         i = 2 * k + (1 - self.side if other else self.side)
@@ -339,49 +227,99 @@
 
     def to_partner(self, src, k):
         return push(
-            src, self.paired.at[k], self.sems[0].at[k], self.sems[1].at[k],
+            src, self.paired.at[k], self.pair_send.at[k], self.pair_recv.at[k],
             self.s + 1 - 2 * self.side, "seq",
         )
 
-    def to_peer(self, k):
+    def bit(self, i, level):
+        return lax.rem(i // (1 << level), 2)
+
+    def move(self, side, slot, k, level):
+        columns = pl.ds(side * self.half, self.half)
+        to = self.s + (1 - 2 * self.bit(self.own, level)) * (2 << level)
         return push(
-            self.mine.at[k], self.peers.at[self.own], self.sems[2].at[k], self.sems[3].at[self.own],
-            2 * k + self.side, "seq",
+            self.mine.at[k, :, columns], self.inbox.at[slot, :, columns],
+            self.send.at[side, slot], self.recv.at[side, slot], to, "seq",
         )
 
+    def moves(self, side, step):
+        order = list(range(self.levels))
+        if side:
+            order.reverse()
+        level, free = order[step], sorted(order[step + 1 :])
+        fixed = sum((self.bit(self.own, d) * (1 << d) for d in order[:step]), 0)
+        offset = self.pairs - (1 << (self.levels - step))
+        here = self.bit(self.own, level) * (1 << level)
+        for c in range(1 << len(free)):
+            rest = fixed + sum(((c >> j) & 1) << d for j, d in enumerate(free))
+            yield offset + c, rest + here, rest + (1 << level) - here, level
+
     def pass_on(self, k):
-        pl.when(self.own != k)(self.to_peer(k).start)
-
-    def collect(self, out):
-        self.peers[self.own] = self.mine[self.own]
-        for k in range(self.pairs):
-            copy = push(
-                self.mine.at[k], self.peers.at[k], self.sems[2].at[k], self.sems[3].at[k],
-                lax.rem(self.s + 1, self.seq), "seq",
-            )
-            pl.when(self.own != k)(copy.wait_recv)
-        band = 16
-
-        def add_rows(r, _):
-            at = pl.ds(pl.multiple_of(r * band, band), band)
-            out[at, :] = jnp.sum(self.peers[:, at, :].astype(F32), axis=0).astype(out.dtype)
-            return 0
-
-        lax.fori_loop(0, self.deep // band, add_rows, 0)
+        top = 1 << (self.levels - 1)
+        pl.when(self.bit(k, 0) != self.bit(self.own, 0))(self.move(0, k // 2, k, 0).start)
+        pl.when(k // top != self.own // top)(
+            self.move(1, lax.rem(k, top), k, self.levels - 1).start
+        )
+
+    def advance(self, step):
+        for side in range(2):
+            columns = slice(side * self.half, (side + 1) * self.half)
+            for slot, keep, gone, level in self.moves(side, step):
+                self.move(side, slot, gone, level).wait_recv()
+                self.mine[keep, :, columns] = (
+                    self.mine[keep, :, columns].astype(F32)
+                    + self.inbox[slot, :, columns].astype(F32)
+                ).astype(BF16)
+            if step + 1 < self.levels:
+                for slot, keep, gone, level in self.moves(side, step + 1):
+                    self.move(side, slot, gone, level).start()
 
     def finish(self, src):
         for k in range(self.pairs):
             self.to_partner(src(k), k).wait_send()
-            pl.when(self.own != k)(self.to_peer(k).wait_send)
-
-
-def gather_norm_kernel(own, gain, normed, rows_all, here_sem, send, recv):
+        for side in range(2):
+            for step in range(self.levels):
+                for slot, keep, gone, level in self.moves(side, step):
+                    self.move(side, slot, gone, level).wait_send()
+
+
+def gather_norm_kernel(own, gain, shard, normed, rows_of_all, rows_all, here_sem, send, recv,
+                       w_sem, w_peer, w_pair, w_recv):
     z, count, rows = lax.axis_index("head"), lax.axis_size("head"), own.shape[0]
-    greet(("head",))
+    greet(("seq", "head"))
     line = Line(own, rows_all, send, recv)
     line.start()
     here = pltpu.make_async_copy(own, line.at(z), here_sem)
     here.start()
+
+    s, deep = lax.axis_index("seq"), shard.shape[0]
+    side, pairs, own_pair = lax.rem(s, 2), lax.axis_size("seq") // 2, s // 2
+    partner = s + 1 - 2 * side
+
+    def shard_at(i):
+        return rows_of_all.at[pl.ds(pl.multiple_of(i * deep, deep), deep)]
+
+    def to_peer(k):
+        return push(shard, shard_at(s), w_peer.at[k], w_recv.at[s], 2 * k + side, "seq")
+
+    def from_peer(k):
+        i = 2 * k + side
+        return push(shard, shard_at(i), w_peer.at[k], w_recv.at[i], partner, "seq")
+
+    def to_partner(k):
+        i = 2 * k + side
+        return push(shard_at(i), shard_at(i), w_pair.at[k], w_recv.at[i], partner, "seq")
+
+    def from_partner(k):
+        i = 2 * k + 1 - side
+        return push(shard_at(i), shard_at(i), w_pair.at[k], w_recv.at[i], partner, "seq")
+
+    mine = pltpu.make_async_copy(shard, shard_at(s), w_sem)
+    mine.start()
+    for k in range(pairs):
+        pl.when(own_pair != k)(to_peer(k).start)
+    mine.wait()
+    to_partner(own_pair).start()
     here.wait()
     band = 16
 
@@ -400,28 +338,46 @@
         return 0
 
     lax.fori_loop(0, count, step, 0)
+    for k in range(pairs):
+
+        @pl.when(own_pair != k)
+        def _():
+            from_peer(k).wait_recv()
+            to_partner(k).start()
+
+    for k in range(pairs):
+        from_partner(k).wait_recv()
+    for k in range(pairs):
+        to_partner(k).wait_send()
+        pl.when(own_pair != k)(to_peer(k).wait_send)
     line.finish()
 
 
-def gather_norm(x, gain):
+def gather_norm(x, gain, shard):
     rows, width = x.shape
+    seq = lax.axis_size("seq")
+    anywhere = pl.BlockSpec(memory_space=pl.ANY)
     count = lax.axis_size("head")
     vmem = pl.BlockSpec(memory_space=pltpu.VMEM)
     dma = pltpu.SemaphoreType.DMA
     return pl.pallas_call(
         gather_norm_kernel,
-        out_shape=jax.ShapeDtypeStruct((count * rows, width), BF16),
-        in_specs=[vmem, vmem],
-        out_specs=vmem,
+        out_shape=(
+            jax.ShapeDtypeStruct((count * rows, width), BF16),
+            jax.ShapeDtypeStruct((seq * shard.shape[0], shard.shape[1]), BF16),
+        ),
+        in_specs=[vmem, vmem, anywhere],
+        out_specs=(vmem, anywhere),
         scratch_shapes=[
             pltpu.VMEM((count * rows, width), BF16), dma(()), dma((count + 1,)), dma((count,)),
+            dma(()), dma((seq // 2,)), dma((seq // 2,)), dma((seq,)),
         ],
         compiler_params=pltpu.CompilerParams(
             collective_id=1, has_side_effects=True, vmem_limit_bytes=32 << 20
         ),
         cost_estimate=cost(50),
         name="gather_norm",
-    )(x, gain)
+    )(x, gain, shard)
 
 
 def swap_slices(own, got, send, recv):
@@ -466,63 +422,6 @@
         return decay * state + own[j, :, :part, :].astype(F32)
 
     lax.fori_loop(0, count, step, jnp.zeros(out.shape[1:], F32))
-
-
-def enter_kernel(own, rows_own, before, through, rows_all,
-                 got, scanned, send, recv, send_back, recv_back, here_sem, go, come):
-    z, count = lax.axis_index("head"), lax.axis_size("head")
-    part = scanned.shape[2]
-    greet(("seq", "head"))
-    begin, end, drain = swap_slices(own, got, send, recv)
-    begin()
-    line = Line(rows_own, rows_all, go, come)
-    line.start()
-    here = pltpu.make_async_copy(rows_own, line.at(z), here_sem)
-    here.start()
-    end()
-    through[...] = got[:, :, part:, :]
-    scan_states(False, got, through, scanned)
-    begin_back, end_back, drain_back = swap_slices(scanned, before, send_back, recv_back)
-    begin_back()
-
-    def step(i, _):
-        line.receive(i, near_order(z, count, i))
-        return 0
-
-    lax.fori_loop(1, count, step, 0)
-    end_back()
-    here.wait()
-    line.finish()
-    drain()
-    drain_back()
-
-
-def enter(own, rows_own, part):
-    slices, micro, deep, dk = own.shape
-    rows, width = rows_own.shape
-    count = lax.axis_size("head")
-    vmem, anywhere = pl.BlockSpec(memory_space=pltpu.VMEM), pl.BlockSpec(memory_space=pl.ANY)
-    dma = pltpu.SemaphoreType.DMA
-    return pl.pallas_call(
-        enter_kernel,
-        out_shape=(
-            jax.ShapeDtypeStruct((slices, micro, part, dk), BF16),
-            jax.ShapeDtypeStruct((slices, micro, deep - part, dk), BF16),
-            jax.ShapeDtypeStruct((count * rows, width), BF16),
-        ),
-        in_specs=[vmem, anywhere],
-        out_specs=(vmem, vmem, anywhere),
-        scratch_shapes=[
-            pltpu.VMEM(own.shape, BF16), pltpu.VMEM((slices, micro, part, dk), BF16),
-            dma((slices,)), dma((slices,)), dma((slices,)), dma((slices,)),
-            dma(()), dma((count + 1,)), dma((count,)),
-        ],
-        compiler_params=pltpu.CompilerParams(
-            collective_id=2, has_side_effects=True, vmem_limit_bytes=32 << 20
-        ),
-        cost_estimate=cost(50),
-        name="enter",
-    )(own, rows_own)
 
 
 def total_kernel(own, out, from_seq, part, from_head, send_a, recv_a, send_b, recv_b,
@@ -582,6 +481,150 @@
     return result
 
 
+def front_kernel(keep, qkv, decay, og, gain, rows_own, o_out, gated, through, kept_out, rows_all,
+                 kept, runs, state, sending, got, scanned, before, leaving,
+                 here_sem, go, come, s_send, s_recv, b_send, b_recv, z_send, z_recv, k_sem):
+    h, head = lax.axis_index("head"), lax.axis_size("head")
+    count, micro, rows, dk = decay.shape
+    dv = og.shape[-1]
+    slices, part = scanned.shape[0], scanned.shape[2]
+    scale = dk ** (-0.5)
+    greet(("seq", "head"))
+    line = Line(rows_own, rows_all, go, come)
+    line.start()
+    here = pltpu.make_async_copy(rows_own, line.at(h), here_sem)
+    here.start()
+
+    state[...] = jnp.zeros_like(state)
+    passed = [jnp.zeros((1, dk), F32)] * micro
+    alive = [jnp.ones((1, dk), F32)] * micro
+    for b in range(count):
+        for m in range(micro):
+            run = running(decay[b, m])
+            runs[b, m] = run
+            last = run[rows - 1 : rows, :]
+            carried = qkv[b, m, :, dk : 2 * dk].astype(F32) * jnp.exp(last - run)
+            fresh = mms((qkv[b, m, :, 2 * dk :],), split(carried), (0, 0))
+            kept[b, m] = fresh
+            state[m] = jnp.exp(last) * (state[m] * keep[b, m]) + fresh
+            passed[m] = passed[m] + last
+            alive[m] = alive[m] * keep[b, m]
+    tail = sending.shape[2] - part
+    at = lax.broadcasted_iota(jnp.int32, (tail, dk), 0)
+    for m in range(micro):
+        high, low = split(jnp.exp(passed[m]) * alive[m])
+        extra = jnp.where(
+            at == 0, high.astype(F32), jnp.where(at == 1, low.astype(F32), 0.0)
+        ).astype(BF16)
+        for i in range(slices):
+            sending[i, m, :part, :] = state[m, i * part : (i + 1) * part, :].astype(BF16)
+            sending[i, m, part:, :] = extra
+    begin, end, drain = swap_slices(sending, got, s_send, s_recv)
+    begin()
+    causal = lower_ones(rows)
+
+    def inside(b, _):
+        for m in range(micro):
+            run = runs[b, m]
+            queried = split(qkv[b, m, :, :dk].astype(F32) * (jnp.exp(run) * scale))
+            keyed = split(qkv[b, m, :, dk : 2 * dk].astype(F32) * jnp.exp(-run))
+            scores = jnp.where(causal, mms(queried, keyed, (1, 1)), 0.0)
+            o_out[b, m] = mms(split(scores), (qkv[b, m, :, 2 * dk :],), (1, 0))
+        return 0
+
+    lax.fori_loop(0, count, inside, 0)
+    line.receive(1, near_order(h, head, 1))
+    end()
+    through[...] = got[:, :, part:, :]
+    scan_states(False, got, through, scanned)
+    begin_back, end_back, drain_back = swap_slices(scanned, before, b_send, b_recv)
+    begin_back()
+    line.receive(2, near_order(h, head, 2))
+    end_back()
+    for i in range(slices):
+        state[:, i * part : (i + 1) * part, :] = before[i].astype(F32)
+
+    def to_owner(b):
+        columns = gated.at[:, pl.ds(pl.multiple_of(h * dv, dv), dv)]
+        return push(leaving.at[b], columns, z_send.at[b], z_recv.at[h], b)
+
+    def save(b):
+        return pltpu.make_async_copy(kept.at[b], kept_out.at[b], k_sem.at[b])
+
+    def across(b, _):
+        for m in range(micro):
+            run = runs[b, m]
+            queried = split(qkv[b, m, :, :dk].astype(F32) * (jnp.exp(run) * scale))
+            entry = state[m] * keep[b, m]
+            state[m] = jnp.exp(run[rows - 1 : rows, :]) * entry + kept[b, m]
+            kept[b, m] = entry
+            o = o_out[b, m] + mms(queried, split(entry), (1, 1))
+            o_out[b, m] = o
+            inv = lax.rsqrt(jnp.mean(o * o, axis=-1, keepdims=True) + 1e-5)
+            normed = (o * inv * gain[...]).astype(BF16).astype(F32)
+            gate = og[b, m]
+            leaving[b, m * rows : (m + 1) * rows, :] = (normed * gate * sigmoid(gate)).astype(BF16)
+        save(b).start()
+        pl.when(b != h)(to_owner(b).start)
+
+        @pl.when(b == 1)
+        def _():
+            line.receive(3, near_order(h, head, 3))
+
+        return 0
+
+    lax.fori_loop(0, count, across, 0)
+    gated[:, pl.ds(pl.multiple_of(h * dv, dv), dv)] = leaving[h]
+    for hop in range(1, head):
+        other = lax.rem(h + hop, head)
+        columns = gated.at[:, pl.ds(pl.multiple_of(other * dv, dv), dv)]
+        push(leaving.at[other], columns, z_send.at[other], z_recv.at[other], other).wait_recv()
+        to_owner(other).wait_send()
+    for b in range(count):
+        save(b).wait()
+    here.wait()
+    line.finish()
+    drain()
+    drain_back()
+
+
+def attention_forward(keep, qkv, decays, og, gain, rows_own):
+    blocks, micro, rows, width = qkv.shape
+    dk, dv = decays.shape[-1], og.shape[-1]
+    head, seq = lax.axis_size("head"), lax.axis_size("seq")
+    assert blocks == head and head == 4
+    part, tail = dv // seq, 16
+    own_rows = micro * rows
+    vmem, anywhere = pl.BlockSpec(memory_space=pltpu.VMEM), pl.BlockSpec(memory_space=pl.ANY)
+    dma = pltpu.SemaphoreType.DMA
+    states, wider = (seq, micro, part, dk), (seq, micro, part + tail, dk)
+    return pl.pallas_call(
+        front_kernel,
+        out_shape=(
+            jax.ShapeDtypeStruct((blocks, micro, rows, dv), F32),
+            jax.ShapeDtypeStruct((own_rows, head * dv), BF16),
+            jax.ShapeDtypeStruct((seq, micro, tail, dk), BF16),
+            jax.ShapeDtypeStruct((blocks, micro, dv, dk), F32),
+            jax.ShapeDtypeStruct((head * rows_own.shape[0], rows_own.shape[1]), BF16),
+        ),
+        in_specs=[vmem] * 5 + [anywhere],
+        out_specs=(vmem,) * 3 + (anywhere,) * 2,
+        scratch_shapes=[
+            pltpu.VMEM((blocks, micro, dv, dk), F32), pltpu.VMEM((blocks, micro, rows, dk), F32),
+            pltpu.VMEM((micro, dv, dk), F32), pltpu.VMEM(wider, BF16), pltpu.VMEM(wider, BF16),
+            pltpu.VMEM(states, BF16), pltpu.VMEM(states, BF16),
+            pltpu.VMEM((blocks, own_rows, dv), BF16),
+            dma(()), dma((head + 1,)), dma((head,)), dma((seq,)), dma((seq,)), dma((seq,)),
+            dma((seq,)), dma((head,)), dma((head,)), dma((blocks,)),
+        ],
+        compiler_params=pltpu.CompilerParams(
+            collective_id=2, has_side_effects=True, vmem_limit_bytes=40 << 20
+        ),
+        cost_estimate=cost(60),
+        name="attention_forward",
+    )(keep, qkv, decays, og, gain, rows_own)
+
+
 def ffn_kernel(count, x_own, c_all, w, g_x, f_parts, grad,
                wv, xs, cs, act, lin, parts, landed, turned, turned_c, tiles,
                w_sem, own_sem, go_sem, x_sem, p_sem, q_sem, o_sem):
@@ -647,10 +690,11 @@
 
     high = tiles.shape[1]
     steps = width // high
+    first = grad.shape[1] - 3 * hidden
 
     def store(t, r, k):
         down = pl.ds(pl.multiple_of(r * high, high), high)
-        into = grad.at[down, pl.ds(k * hidden, hidden)]
+        into = grad.at[down, pl.ds(first + k * hidden, hidden)]
         return pltpu.make_async_copy(tiles.at[lax.rem(t, 2)], into, o_sem.at[lax.rem(t, 2)])
 
     turned[...] = xs[...].T
@@ -702,7 +746,7 @@
         out_shape=(
             jax.ShapeDtypeStruct((rows, width), F32),
             jax.ShapeDtypeStruct((count, rows, width), BF16),
-            jax.ShapeDtypeStruct((width, 3 * hidden), BF16),
+            jax.ShapeDtypeStruct(w.shape, BF16),
         ),
         in_specs=[anywhere] * 3,
         out_specs=(vmem, vmem, anywhere),
@@ -728,25 +772,10 @@
     )(x_own, c_all, w)
 
 
-def split(x):
-    high = x.astype(BF16)
-    return high, (x - high.astype(F32)).astype(BF16)
-
-
-def mms(left, right, contract):
-    total = mm(left[0], right[0], contract, None)
-    if len(right) > 1:
-        total += mm(left[0], right[1], contract, None)
-    if len(left) > 1:
-        total += mm(left[1], right[0], contract, None)
-    return total
-
-
-def back_kernel(keep, gated_own, og, o_in, qkv, decay, logits, through, gain, left, right,
-                kept_in, parts_in, g_proj, g_logits, g_gain, f_out, g_out,
+def back_kernel(keep, gated_own, og, o_in, qkv, decay, logits, through, gain, kept_in, parts_in,
+                g_proj, g_logits, g_gain, f_out,
                 gated_all, go, runs, g_queried, g_keyed, g_values, pulls, weights, kept,
-                parts, landed, state, sending, got, scanned, after, turned, tiles, in_sem, t_sem,
-                z_send, z_recv, s_send, s_recv, b_send, b_recv, p_sem, q_sem):
+                parts, landed, state, sending, got, scanned, after, in_sem, z_send, z_recv, s_send, s_recv, b_send, b_recv, p_sem, q_sem):
     h, head = lax.axis_index("head"), lax.axis_size("head")
     count, micro, rows, dk = decay.shape
     dv = og.shape[-1]
@@ -782,33 +811,6 @@
             before[m] = before[m] + run[rows - 1 : rows, :]
     g_gain[...] = jnp.zeros_like(g_gain)
     state[...] = jnp.zeros_like(state)
-
-    turned[...] = left[...].T
-    high, wide = tiles.shape[1:]
-    across_tiles = g_out.shape[1] // wide
-
-    def store(t):
-        at = pl.ds(pl.multiple_of((t // across_tiles) * high, high), high)
-        columns = pl.ds(pl.multiple_of(lax.rem(t, across_tiles) * wide, wide), wide)
-        return pltpu.make_async_copy(
-            tiles.at[lax.rem(t, 2)], g_out.at[at, columns], t_sem.at[lax.rem(t, 2)]
-        )
-
-    def tile(t, _):
-        @pl.when(t >= 2)
-        def _():
-            store(t - 2).wait()
-
-        at = pl.ds(pl.multiple_of((t // across_tiles) * high, high), high)
-        columns = pl.ds(pl.multiple_of(lax.rem(t, across_tiles) * wide, wide), wide)
-        tiles[lax.rem(t, 2)] = jnp.dot(
-            turned[at, :], right[:, columns], preferred_element_type=F32
-        ).astype(BF16)
-        store(t).start()
-        return 0
-
-    tile_count = (g_out.shape[0] // high) * across_tiles
-    lax.fori_loop(0, tile_count, tile, 0)
 
     def gates(i, _):
         b = near_order(h, head, i)
@@ -911,8 +913,6 @@
     lax.fori_loop(0, count, across, 0)
     total.result(f_out)
     total.finish()
-    store(tile_count - 2).wait()
-    store(tile_count - 1).wait()
     drain()
     drain_back()
     for hop in range(1, head):
@@ -920,7 +920,7 @@
 
 
 def attention_back(
-    keep, gated_own, og, o, qkv, decays, logits, through, gain, left, right, kept, parts
+    keep, gated_own, og, o, qkv, decays, logits, through, gain, kept, parts
 ):
     blocks, micro, rows, width = qkv.shape
     dk, dv = decays.shape[-1], og.shape[-1]
@@ -937,10 +937,9 @@
             jax.ShapeDtypeStruct((blocks, micro, rows, dk), F32),
             jax.ShapeDtypeStruct((8, dv), F32),
             jax.ShapeDtypeStruct((own_rows, parts.shape[1]), F32),
-            jax.ShapeDtypeStruct((left.shape[1], right.shape[1]), BF16),
-        ),
-        in_specs=[vmem] * 11 + [anywhere] * 2,
-        out_specs=(vmem,) * 4 + (anywhere,),
+        ),
+        in_specs=[vmem] * 9 + [anywhere] * 2,
+        out_specs=(vmem,) * 4,
         scratch_shapes=[
             pltpu.VMEM((blocks, micro * rows, dv), BF16), blocked(dv, F32), blocked(dk, F32),
             blocked(dk, F32), blocked(dk, F32), blocked(dv, F32),
@@ -951,9 +950,7 @@
             pltpu.VMEM((micro, dv, dk), F32),
             pltpu.VMEM(states, BF16), pltpu.VMEM(states, BF16), pltpu.VMEM(states, BF16),
             pltpu.VMEM(states, BF16),
-            pltpu.VMEM(left.shape[::-1], BF16),
-            pltpu.VMEM((2, left.shape[1] // 4, right.shape[1] // 2), BF16),
-            dma((2,)), dma((2,)), dma((head,)), dma((head,)), dma((seq,)), dma((seq,)), dma((seq,)),
+            dma((2,)), dma((head,)), dma((head,)), dma((seq,)), dma((seq,)), dma((seq,)),
             dma((seq,)), dma((head, 4)), dma((head + 1, 4)),
         ],
         compiler_params=pltpu.CompilerParams(
@@ -961,13 +958,13 @@
         ),
         cost_estimate=cost(80),
         name="attention_back",
-    )(keep, gated_own, og, o, qkv, decays, logits, through, gain, left, right, kept, parts)
+    )(keep, gated_own, og, o, qkv, decays, logits, through, gain, kept, parts)
 
 
 def finish_kernel(xn_in, proj_in, w_in, g_logits, ranked, up_own, rank_down,
                   g_x, grad, g_down, g_up, g_bias,
-                  turned, proj, w, outgoing, mine, paired, peers, slab, heads_in, parts, landed, slim_high,
-                  slim_low, in_sem, pair_send, pair_recv, peer_send, peer_recv, x_send, x_recv,
+                  turned, proj, w, outgoing, mine, paired, inbox, heads_in, parts, landed,
+                  slim_high, slim_low, in_sem, pair_send, pair_recv, send, recv, x_send, x_recv,
                   p_sem, q_sem):
     h, head = lax.axis_index("head"), lax.axis_size("head")
     rows, width = g_x.shape
@@ -981,6 +978,7 @@
     ]
     for load in loads:
         load.start()
+    sums = PairSum(mine, paired, inbox, pair_send, pair_recv, send, recv)
     for load in loads:
         load.wait()
     turned[...] = landed[: xn_in.shape[0], :].T
@@ -1006,8 +1004,6 @@
 
     lax.fori_loop(0, head, chunk, 0)
 
-    sums = PairSum(mine, paired, peers, pair_send, pair_recv, peer_send, peer_recv)
-
     def gone(k, _):
         outgoing[k] = jnp.dot(
             turned[sums.block(k, True), :], proj[...], preferred_element_type=F32
@@ -1048,24 +1044,24 @@
     g_up[...] = mms(split(ranked[...]), logit_parts, (0, 0))
     g_bias[...] = jnp.broadcast_to(jnp.sum(g_logits[...], axis=0, keepdims=True), g_bias.shape)
 
-    sums.collect(slab)
     thin = grad.shape[0]
 
     def to_head(hop, slot):
         to = lax.rem(h + hop, head)
-        return push(
-            slab.at[pl.ds(pl.multiple_of(to * thin, thin), thin)], heads_in.at[slot],
-            x_send.at[hop], x_recv.at[slot], to,
-        )
-
+        at = pl.ds(pl.multiple_of(to * thin, thin), thin)
+        return push(mine.at[sums.own, at, :], heads_in.at[slot], x_send.at[hop], x_recv.at[slot], to)
+
+    for step in range(sums.levels):
+        sums.advance(step)
     for hop in range(1, head):
         to_head(hop, h).start()
-    heads_in[h] = slab[pl.ds(pl.multiple_of(h * thin, thin), thin), :]
+    own_rows = pl.ds(pl.multiple_of(h * thin, thin), thin)
+    heads_in[h] = mine[sums.own, own_rows, :]
     total.result(g_x)
     for hop in range(1, head):
         to_head(hop, lax.rem(h + hop, head)).wait_recv()
     dk = g_up.shape[1]
-    dv = slab.shape[1] // 2 - dk
+    dv = mine.shape[2] // 2 - dk
     for j in range(head):
         at, start = 0, 0
         for size in (dk, dk, dv, dv):
@@ -1087,7 +1083,9 @@
     dk = up_own.shape[1]
     vmem, anywhere = pl.BlockSpec(memory_space=pltpu.VMEM), pl.BlockSpec(memory_space=pl.ANY)
     dma = pltpu.SemaphoreType.DMA
-    blocks = pltpu.VMEM((pairs, deep, columns), BF16)
+    blocks = lambda count, w: pltpu.VMEM((count, deep, w), BF16)
+    ends = lambda w: pltpu.VMEM((head, deep // head, w), BF16)
+    moves = dma((2, pairs - 1))
     return pl.pallas_call(
         finish_kernel,
         out_shape=(
@@ -1101,23 +1099,58 @@
         out_specs=(vmem,) * 5,
         scratch_shapes=[
             pltpu.VMEM((width, group), BF16), pltpu.VMEM(g_proj.shape, BF16),
-            pltpu.VMEM(w_in.shape, BF16), blocks, blocks, blocks, blocks,
-            pltpu.VMEM((deep, columns), BF16), pltpu.VMEM((head, deep // head, columns), BF16),
+            pltpu.VMEM(w_in.shape, BF16), blocks(pairs, columns), blocks(pairs, columns),
+            blocks(pairs, columns), blocks(pairs - 1, columns), ends(columns),
             pltpu.VMEM((group, width), BF16), pltpu.VMEM((group + rows, width), BF16),
             pltpu.VMEM(ranked.shape, BF16), pltpu.VMEM(ranked.shape, BF16),
-            dma((3,)), dma((pairs,)), dma((pairs,)), dma((pairs,)), dma((pairs,)),
-            dma((head,)), dma((head,)), dma((head, 4)), dma((head + 1, 4)),
+            dma((3,)), dma((pairs,)), dma((pairs,)), moves, moves, dma((head,)), dma((head,)),
+            dma((head, 4)), dma((head + 1, 4)),
         ],
         compiler_params=pltpu.CompilerParams(
-            collective_id=5, has_side_effects=True, vmem_limit_bytes=56 << 20
+            collective_id=5, has_side_effects=True, vmem_limit_bytes=60 << 20
         ),
         cost_estimate=cost(60),
         name="finish",
     )(xn, g_proj, w_in, g_logits, ranked, up_own, rank_down)
 
 
-def exchange(x, axis):
-    return lax.all_to_all(x, axis, split_axis=0, concat_axis=0, tiled=True)
+def weight_grad_kernel(left, right, *rest):
+    out, turned = rest[-2:]
+
+    @pl.when(pl.program_id(1) == 0)
+    def _():
+        turned[...] = left[...].T
+
+    out[...] = jnp.dot(turned[...], right[...], preferred_element_type=F32).astype(BF16)
+
+
+def weight_grad(left, right, into, columns, start, tile):
+    depth, rows = left.shape
+    high = min(rows, 512)
+    first = start // tile
+    given = () if into is None else (into,)
+    return pl.pallas_call(
+        weight_grad_kernel,
+        out_shape=jax.ShapeDtypeStruct((rows, columns), BF16),
+        grid=(rows // high, right.shape[1] // tile),
+        in_specs=[
+            pl.BlockSpec((depth, high), lambda i, j: (0, i)),
+            pl.BlockSpec((depth, tile), lambda i, j: (0, j)),
+        ]
+        + [pl.BlockSpec(memory_space=pl.ANY) for _ in given],
+        out_specs=pl.BlockSpec((high, tile), lambda i, j: (i, first + j)),
+        scratch_shapes=[pltpu.VMEM((high, depth), BF16)],
+        input_output_aliases={2: 0} if given else {},
+        compiler_params=pltpu.CompilerParams(
+            dimension_semantics=("arbitrary", "arbitrary"), vmem_limit_bytes=48 << 20
+        ),
+        cost_estimate=pl.CostEstimate(
+            flops=2 * depth * rows * right.shape[1],
+            bytes_accessed=2 * (depth * rows + (depth + rows) * right.shape[1]),
+            transcendentals=0,
+        ),
+        name="weight_grad",
+    )(left, right, *given)
 
 
 def gather_weight(w):
@@ -1161,16 +1194,14 @@
     def own_columns(w, start, size):
         return lax.dynamic_slice_in_dim(w, start + head * size, size, 1)
 
-    w_in = gather_weight(
-        jnp.concatenate(
-            [
-                own_columns(mix_in, 0, dk),
-                own_columns(mix_in, keys, dk),
-                own_columns(mix_in, 2 * keys, dv),
-                own_columns(mix_in, 2 * keys + vals, dv),
-            ],
-            axis=1,
-        )
+    w_in_own = jnp.concatenate(
+        [
+            own_columns(mix_in, 0, dk),
+            own_columns(mix_in, keys, dk),
+            own_columns(mix_in, 2 * keys, dv),
+            own_columns(mix_in, 2 * keys + vals, dv),
+        ],
+        axis=1,
     )
     later = gather_weight(
         jnp.concatenate(
@@ -1181,7 +1212,9 @@
     up_own = own_columns(rank_up, 0, dk)
     bias_own = lax.dynamic_slice_in_dim(gate_bias, head * dk, dk, 0)
 
-    xn = gather_norm(tokens.reshape(micro * rows, width), norm_gain.reshape(1, width))
+    xn, w_in = gather_norm(
+        tokens.reshape(micro * rows, width), norm_gain.reshape(1, width), w_in_own
+    )
     qkv = dot(xn, w_in[:, : 2 * dk + dv], (1, 0)).astype(BF16)
     og = dot(xn, w_in[:, 2 * dk + dv :], (1, 0))
     ranked = dot(xn, rank_down, (1, 0))
@@ -1193,38 +1226,32 @@
 
     qkv_b, og_b, decays_b = blocks(qkv), blocks(og), blocks(decays)
     gain_row = head_gain.reshape(1, dv)
-    part = dv // seq
-    own_states = states_of(starts, qkv_b, decays_b, dv, seq, 16)
-    before, through, all_cot = enter(own_states, cotangent.reshape(micro * rows, width), part)
-    o_b, gated_b, kept = mix_of(starts, qkv_b, decays_b, og_b, before, gain_row)
-
-    gated = exchange(gated_b, "head")
-    gated = gated.transpose(1, 2, 0, 3).reshape(micro * rows, vals)
+    keep = 1.0 - jnp.broadcast_to(starts.T[:, :, None, None], (heads, micro, 1, dk)).astype(F32)
+    o_b, gated, through, kept, all_cot = attention_forward(
+        keep, qkv_b, decays_b, og_b, gain_row, cotangent.reshape(micro * rows, width)
+    )
+
     source = tokens.astype(F32).reshape(micro * rows, width)
     hidden = source + dot(gated, w_out, (1, 1))
     inv_ffn = rms(hidden, 1e-6)
     plain_ffn = hidden * inv_ffn
     h2 = (plain_ffn * ffn_gain).astype(BF16)
 
-    g_h2, ffn_part, grad_ffn = feed_forward(h2, all_cot, later, hidden_units, heads)
-    grad_ffn = scatter_grad(grad_ffn)
+    g_h2, ffn_part, grads = feed_forward(h2, all_cot, later, hidden_units, heads)
 
     back_ffn, g_ffn_gain = norm_back(g_h2, ffn_gain, plain_ffn, inv_ffn)
     g_hidden = cotangent.astype(F32).reshape(micro * rows, width) + back_ffn
     g_mixed = g_hidden.astype(BF16)
+    grads = scatter_grad(weight_grad(g_mixed, gated, grads, later.shape[1], 0, dv))
     g_gated = dot(g_mixed, w_out, (1, 0)).astype(BF16)
-    keep = 1.0 - jnp.broadcast_to(starts.T[:, :, None, None], (heads, micro, 1, dk)).astype(F32)
-    g_proj_b, g_logits_b, g_head_gain, ffn_out, grad_out = attention_back(
-        keep, g_gated, og_b, o_b, qkv_b, decays_b, blocks(logits), through, gain_row,
-        g_mixed, gated, kept, ffn_part.reshape(group, width),
-    )
-    grad_out = scatter_grad(grad_out)
+    g_proj_b, g_logits_b, g_head_gain, ffn_out = attention_back(
+        keep, g_gated, og_b, o_b, qkv_b, decays_b, blocks(logits), through, gain_row, kept, ffn_part.reshape(group, width),
+    )
     output = (hidden + ffn_out).astype(BF16)
     g_proj, g_logits = g_proj_b.reshape(group, proj_width), g_logits_b.reshape(group, dk)
     g_xn, grad_in, g_rank_down, g_rank_up, g_bias = finish(
         xn, g_proj, w_in, g_logits, ranked, up_own, rank_down
     )
-    g_xn, grad_ffn = lax.optimization_barrier((g_xn, grad_ffn))
     inv_in = rms(source, 1e-6)
     back_in, g_norm_gain = norm_back(g_xn, norm_gain, source * inv_in, inv_in)
     input_grad = g_hidden + back_in
@@ -1239,8 +1266,11 @@
         [g_norm_gain, g_ffn_gain, g_head_gain[0], g_rank_down, g_rank_up, g_bias]
     )
     slab = width // (seq * heads)
-    small, grad_out = lax.optimization_barrier((small, grad_out))
-    grad_out = exchange(grad_out.reshape(heads, slab, vals), "head").astype(F32).sum(0)
+    grad_ffn = grads[:, vals:]
+    grad_out = lax.all_to_all(
+        grads[:, :vals].reshape(heads, slab, vals), "head", split_axis=0, concat_axis=0, tiled=True
+    )
+    grad_out = grad_out.astype(F32).sum(0)
     return (
         output.reshape(tokens.shape),
         input_grad.reshape(tokens.shape),

time: 606 us -> 584 us (0.964)
  Pallas kernels: 449 us -> 478 us
  blocking collectives: 23.9 us -> 0 us
  waiting for transfers between devices: 21.8 us -> 0.04 us
    pallas_call x4 -> x3, Pallas kernels: 145 us -> 170 us  [the longest x1 90.5 us: attention_forward(): pl.pallas_call(front_kernel, out_shape=(jax.ShapeDtypeStruct((blocks, mic...]
    all_to_all x1 -> x0, blocking collectives: 23.9 us -> none  [exchange(): return lax.all_to_all(x, axis, split_axis=0, concat_axis=0, tiled=True)]
    reduce_scatter x2 -> x1, waiting for transfers between devices: 12.5 us -> 0.01 us  [scatter_grad(): lax.psum_scatter(g.astype(BF16), 'seq', scatter_dimension=0, tiled=True)]
    all_to_all x1, waiting for transfers between devices: 9.24 us -> 0.01 us  [on_device(): lax.all_to_all(grads[:, :vals].reshape(heads, slab, vals), 'head', split_...]
  transfers between devices with their start and end apart: 5 -> 3, of which waited for: 2 -> 0; matrix products, arithmetic and copies ran while one was open for 11% -> 9% of each run, Pallas kernels for 57% -> 62%
where the time goes in v7:
time: 584 us; the launch traced here: 575 us
  Pallas kernels  478 us (82%)
  local copies, waits for them, and re-layouts  32.1 us (5%)
  matrix products  22.6 us (4%)
  other arithmetic  21.7 us (4%)
  between operations  14.8 us (3%)
    pallas_call x1, Pallas kernels, feed_forward(): pl.pallas_call(functools.partial(ffn_kernel, count), out_shape=(jax.Shape...  109 us
    pallas_call x1, Pallas kernels, finish(): pl.pallas_call(finish_kernel, out_shape=(jax.ShapeDtypeStruct((rows, widt...  92.1 us
    pallas_call x1, Pallas kernels, attention_forward(): pl.pallas_call(front_kernel, out_shape=(jax.ShapeDtypeStruct((blocks, mic...  90.5 us
    pallas_call x1, Pallas kernels, attention_back(): pl.pallas_call(back_kernel, out_shape=(jax.ShapeDtypeStruct((blocks, micr...  72.9 us
    pallas_call x1, Pallas kernels, gather_norm(): pl.pallas_call(gather_norm_kernel, out_shape=(jax.ShapeDtypeStruct((count...  69.2 us
    pallas_call x1, Pallas kernels, total_of(): pl.pallas_call(total_kernel, out_shape=jax.ShapeDtypeStruct(shape, F32),...  33.7 us
    dot_general x6, matrix products, dot(): lax.dot_general(a, b, (((contract[0],), (contract[1],)), ((), ())), preci...  22.6 us
  transfers between devices with their start and end apart: 3, of which 0 were waited for; matrix products, arithmetic and copies ran while one was open for 9% of the time, Pallas kernels for 62%

profile of v7, /device:TPU:0, one launch (start us, length us, event | category | flops | bytes accessed | tf_op | source)
XLA Modules:
  0.0 574.6 jit_solution(13023238137101921714)
XLA Ops:
  7.3 1.6 copy.34
  9.1 1.8 pad_maximum_fusion
  14.6 69.2 %gather_norm.1 = (bf16[768,2048]{1,0:T(8,128)(2,1)S(1)}, bf16[2048,1536]{1,0:T(8,128)(2,1)S(1)}) custom-call(bf16[192,2048]{1,0:T(8,128)(2,1)S(1)} %bitcast.46, f32[1,2048]{1,0:T(1,128)S(1)} %bitcast.55, bf16[256,1536]{1,0:T(8,128)(2,1)S(1)} %pad_maximum_fusion.1.shard), custom_call_target="tpu_custom_call" | custom-call | bytes 150000000 | tf_op jit(solution)/shard_map/gather_norm/pallas_call | solution.py:363
  84.8 2.6 fusion.19
  87.4 1.8 fusion.12
  89.3 3.4 fusion.14
  92.8 90.5 %attention_forward.1 = (f32[4,3,64,512]{3,2,1,0:T(8,128)S(1)}, bf16[192,2048]{1,0:T(8,128)(2,1)S(1)}, bf16[8,3,16,256]{3,2,1,0:T(8,128)(2,1)S(1)}, f32[4,3,512,256]{3,2,1,0:T(8,128)}, bf16[768,2048]{1,0:T(8,128)(2,1)S(1)}) custom-call(f32[4,3,1,256]{3,2,1,0:T(1,128)S(1)} %broadcast_in_dim.6.keep, bf16[4,3,64,1024]{3,2,1,0:T(8,128)(2,1)S(1)} %bitcast.51, ...), custom_call_target="tpu_custom_call" | custom-call | bytes 180000000 | tf_op jit(solution)/shard_map/attention_forward/pallas_call | solution.py:601
  184.5 1.6 copy-done.10
  188.0 6.5 %multiply_reduce_fusion.5 = (f32[192]{0:T(256)S(1)}, f32[192,2048]{1,0:T(8,128)S(1)}) fusion(bf16[192,2048]{1,0:T(8,128)(2,1)S(1)} %get-tuple-element.33.right, bf16[2048,6272]{1,0:T(8,128)(2,1)} %all-gather.2.cloned.1.call-done.w, bf16[192,2048]{1,0:T(8,128)(2,1)S(1)} %bitcast.47), kind=kOutput, calls=%fused_computation.24 | convolution fusion | flops 1612185344 | bytes 11535104 | tf_op jit(solution)/shard_map/dot_general | solution.py:1165
  194.5 1.2 multiply_convert_fusion.x_own
  195.7 109.1 %feed_forward.1 = (f32[192,2048]{1,0:T(8,128)}, bf16[4,192,2048]{2,1,0:T(8,128)(2,1)}, bf16[2048,6272]{1,0:T(8,128)(2,1)}) custom-call(bf16[192,2048]{1,0:T(8,128)(2,1)} %multiply_convert_fusion.x_own, bf16[768,2048]{1,0:T(8,128)(2,1)} %copy-done.10, bf16[2048,6272]{1,0:T(8,128)(2,1)} %all-gather.2.cloned.1.call-done.w), custom_call_target="tpu_custom_call" | custom-call | bytes 300000000 | tf_op jit(solution)/shard_map/feed_forward/pallas_call | solution.py:744
  304.9 2.5 multiply_reduce_fusion
  307.5 1.9 fusion.20.left
  309.4 10.2 %weight_grad.1 = bf16[2048,6272]{1,0:T(8,128)(2,1)} custom-call(bf16[192,2048]{1,0:T(8,128)(2,1)S(1)} %fusion.20.left, bf16[192,2048]{1,0:T(8,128)(2,1)S(1)} %get-tuple-element.33.right, bf16[2048,6272]{1,0:T(8,128)(2,1)} %get-tuple-element.45.rest_0_), custom_call_target="tpu_custom_call", output_to_operand_aliasing={{}: (2, {})} | custom-call | flops 1610612736 | bytes 9961472 | tf_op jit(solution)/shard_map/weight_grad/pallas_call | solution.py:1132
  321.8 1.4 bitcast_multiply_fusion
  323.2 7.4 %fusion.9.gated_own = bf16[192,2048]{1,0:T(8,128)(2,1)} fusion(bf16[192,2048]{1,0:T(8,128)(2,1)S(1)} %fusion.20.left, bf16[2048,6272]{1,0:T(8,128)(2,1)} %all-gather.2.cloned.1.call-done.w), kind=kOutput, calls=%fused_computation.8 | convolution fusion | flops 1611005952 | bytes 9961472 | tf_op jit(solution)/shard_map/dot_general | solution.py:1165
  330.6 72.9 %attention_back.1 = (bf16[4,3,64,1536]{3,2,1,0:T(8,128)(2,1)}, f32[4,3,64,256]{3,2,1,0:T(8,128)}, f32[8,512]{1,0:T(8,128)}, f32[192,2048]{1,0:T(8,128)}) custom-call(f32[4,3,1,256]{3,2,1,0:T(1,128)} %copy-done.14, bf16[192,2048]{1,0:T(8,128)(2,1)} %fusion.9.gated_own, f32[4,3,64,512]{3,2,1,0:T(8,128)} %bitcast.50, f32[4,3,64,512]{3,2,1,0:T(8,128)} %copy-done.11, ...), custom_call_target="tpu_custom_call" | custom-call | bytes 240000000 | tf_op jit(solution)/shard_map/attention_back/pallas_call | solution.py:933
  404.3 92.1 %finish.1 = (f32[192,2048]{1,0:T(8,128)}, f32[64,6144]{1,0:T(8,128)}, f32[2048,16]{1,0:T(8,128)}, f32[16,256]{1,0:T(8,128)}, f32[8,256]{1,0:T(8,128)}) custom-call(bf16[768,2048]{1,0:T(8,128)(2,1)} %copy-done.2, bf16[768,1536]{1,0:T(8,128)(2,1)} %bitcast.60, bf16[2048,1536]{1,0:T(8,128)(2,1)} %copy-done.7, f32[768,256]{1,0:T(8,128)} %bitcast.70, ...), custom_call_target="tpu_custom_call" | custom-call | bytes 180000000 | tf_op jit(solution)/shard_map/finish/pallas_call | solution.py:1089
  496.3 1.7 reshape.162
  499.7 2.6 multiply_reduce_fusion.1
  503.0 3.8 multiply_add_fusion
  506.9 2.3 slice.64
  509.2 5.6 all-to-all-start
  515.6 33.7 %total.1 = f32[8,4,16,128]{3,2,1,0:T(8,128)} custom-call(f32[8,4,16,128]{3,2,1,0:T(8,128)} %bitcast.67), custom_call_target="tpu_custom_call" | custom-call | bytes 45000000 | tf_op jit(solution)/shard_map/total/pallas_call | solution.py:464
  549.2 1.7 slice.59
  551.8 1.3 slice.72
  553.1 1.3 slice.69
  556.0 1.3 fusion.21
  557.3 1.5 slice_convert_fusion
  558.9 2.8 reshape.168
  561.7 2.4 slice_convert_fusion.1
  564.1 2.2 convert_reduce_fusion
  (104 shorter events, 17.9 us)
Async XLA Ops:
  7.2 76.6 %copy-start = (f32[16,1024]{1,0:T(8,128)S(1)}, f32[16,1024]{1,0:T(8,128)}, u32[]{:S(2)}) copy-start(f32[16,1024]{1,0:T(8,128)} %param.24) | copy-start | bytes 196612
  7.2 1.7 copy-start.23
  7.2 1.9 copy-start.24
  7.2 180.7 %all-gather.2.cloned.1.call-start = ((), (), s32[]{:S(2)}) async-start(), calls=%async_computation.2 | async-start | bytes 28901376 | tf_op jit(solution)/shard_map/all_gather | solution.py:1157
  10.9 496.0 %reduce-scatter.2.cloned.1.call-start = ((), (), s32[]{:S(2)}) async-start(), calls=%async_computation.3 | async-start | bytes 28901376 | tf_op jit(solution)/shard_map/reduce_scatter | solution.py:1161
  12.4 2.2 copy-start.3
  12.4 2.2 copy-start.15
  14.5 69.3 %copy-start.25 = (bf16[2048,16]{0,1:T(8,128)(2,1)S(1)}, bf16[2048,16]{0,1:T(8,128)(2,1)}, u32[]{:S(2)}) copy-start(bf16[2048,16]{0,1:T(8,128)(2,1)} %param.23) | copy-start | bytes 196612
  83.8 5.4 copy-start.2
  83.8 5.4 copy-start.7
  83.9 5.4 copy-start.29
  87.4 5.4 copy-start.12
  89.3 3.5 copy-start.8
  89.3 3.5 copy-start.5
  89.3 3.5 copy-start.16
  92.8 90.6 %copy-start.14 = (f32[4,3,1,256]{3,2,1,0:T(1,128)}, f32[4,3,1,256]{3,2,1,0:T(1,128)S(1)}, u32[]{:S(2)}) copy-start(f32[4,3,1,256]{3,2,1,0:T(1,128)S(1)} %broadcast_in_dim.6.keep) | copy-start | bytes 36868
  92.8 95.1 %copy-start.4 = (bf16[3,64,2048]{2,1,0:T(8,128)(2,1)S(1)}, bf16[3,64,2048]{2,1,0:T(8,128)(2,1)}, u32[]{:S(2)}) copy-start(bf16[3,64,2048]{2,1,0:T(8,128)(2,1)} %param.13) | copy-start | bytes 2359300
  183.3 1.1 copy-start.9
  184.5 1.6 copy-start.10
  186.1 1.1 copy-start.11
  187.9 6.5 %copy-start.28 = (f32[2048]{0:T(1024)S(1)}, f32[2048]{0:T(1024)}, u32[]{:S(2)}) copy-start(f32[2048]{0:T(1024)} %param.21) | copy-start | bytes 24580
  194.4 110.4 %copy-start.17 = (f32[192,2048]{1,0:T(8,128)}, f32[192,2048]{1,0:T(8,128)S(1)}, u32[]{:S(2)}) copy-start(f32[192,2048]{1,0:T(8,128)S(1)} %get-tuple-element.77) | copy-start | bytes 4718596
  304.9 2.6 copy-start.6
  304.9 2.6 copy-start.18
  496.3 6.7 %copy-start.21 = (f32[192,2048]{1,0:T(8,128)S(1)}, f32[192,2048]{1,0:T(8,128)}, u32[]{:S(2)}) copy-start(f32[192,2048]{1,0:T(8,128)} %get-tuple-element.43) | copy-start | bytes 4718596
  499.7 3.4 copy-start.19
  499.7 3.4 copy-start.20
  502.3 0.7 copy-start.26
  509.2 5.7 copy-start.27
  509.2 54.9 %all-to-all-start = ((bf16[4,64,2048]{2,1,0:T(8,128)(2,1)}), bf16[4,64,2048]{2,1,0:T(8,128)(2,1)}, u32[]{:S(2)}, u32[]{:S(2)}) async-start(bf16[4,64,2048]{2,1,0:T(8,128)(2,1)} %bitcast.15), calls=%async_computation.1 | async-start | bytes 2097152 | tf_op jit(solution)/shard_map/all_to_all | solution.py:1270
  561.7 4.7 copy-start.22
  566.3 1.1 copy-start.1
  (2 other events, 1.4 us)
Sparse Core Ops, SparseCore 0:
  11.0 176.3 all-gather.1
  319.7 182.1 reduce-scatter.1

commit v8 on v7

--- a/solution.py
+++ b/solution.py
@@ -422,63 +422,6 @@
         return decay * state + own[j, :, :part, :].astype(F32)
 
     lax.fori_loop(0, count, step, jnp.zeros(out.shape[1:], F32))
-
-
-def total_kernel(own, out, from_seq, part, from_head, send_a, recv_a, send_b, recv_b,
-                 send_c, recv_c, send_d, recv_d):
-    seq, head = lax.axis_size("seq"), lax.axis_size("head")
-    s, h = lax.axis_index("seq"), lax.axis_index("head")
-    greet(("seq", "head"))
-
-    def each(axis, me, count, src, dst, send, recv):
-        def copy(hop, index):
-            to = lax.rem(me + hop, count)
-            return push(src(to), dst(index), send.at[hop], recv.at[index], to, axis)
-
-        for hop in range(1, count):
-            copy(hop, me).start()
-        for hop in range(1, count):
-            copy(hop, lax.rem(me + hop, count)).wait_recv()
-        return [copy(hop, me).wait_send for hop in range(1, count)]
-
-    from_seq[s] = own[s]
-    sent = each("seq", s, seq, lambda to: own.at[to], lambda i: from_seq.at[i], send_a, recv_a)
-    part[...] = jnp.sum(from_seq[...], axis=0)
-    from_head[h] = part[h]
-    sent += each("head", h, head, lambda to: part.at[to], lambda i: from_head.at[i], send_b, recv_b)
-    out[s, h] = jnp.sum(from_head[...], axis=0)
-    sent += each("head", h, head, lambda _: out.at[s, h], lambda i: out.at[s, i], send_c, recv_c)
-    sent += each("seq", s, seq, lambda _: out.at[s], lambda i: out.at[i], send_d, recv_d)
-    for wait in sent:
-        wait()
-
-
-def total_of(parts):
-    seq, head = lax.axis_size("seq"), lax.axis_size("head")
-    flat = jnp.concatenate([p.reshape(-1) for p in parts])
-    deep = -(-flat.shape[0] // (seq * head * 1024)) * 8
-    flat = jnp.pad(flat, (0, seq * head * deep * 128 - flat.shape[0]))
-    vmem = pl.BlockSpec(memory_space=pltpu.VMEM)
-    dma = pltpu.SemaphoreType.DMA
-    shape = (seq, head, deep, 128)
-    whole = pl.pallas_call(
-        total_kernel,
-        out_shape=jax.ShapeDtypeStruct(shape, F32),
-        in_specs=[vmem],
-        out_specs=vmem,
-        scratch_shapes=[
-            pltpu.VMEM(shape, F32), pltpu.VMEM(shape[1:], F32), pltpu.VMEM(shape[1:], F32),
-        ]
-        + [dma((n,)) for n in (seq, seq, head, head, head, head, seq, seq)],
-        compiler_params=pltpu.CompilerParams(collective_id=4, has_side_effects=True),
-        cost_estimate=cost(15),
-        name="total",
-    )(flat.reshape(shape)).reshape(-1)
-    result, at = [], 0
-    for p in parts:
-        result.append(whole[at : at + p.size].reshape(p.shape))
-        at += p.size
-    return result
 
 
 def front_kernel(keep, qkv, decay, og, gain, rows_own, o_out, gated, through, kept_out, rows_all,
@@ -620,7 +563,7 @@
         compiler_params=pltpu.CompilerParams(
             collective_id=2, has_side_effects=True, vmem_limit_bytes=40 << 20
         ),
-        cost_estimate=cost(60),
+        cost_estimate=cost(90),
         name="attention_forward",
     )(keep, qkv, decays, og, gain, rows_own)
 
@@ -961,11 +904,13 @@
     )(keep, gated_own, og, o, qkv, decays, logits, through, gain, kept, parts)
 
 
-def finish_kernel(xn_in, proj_in, w_in, g_logits, ranked, up_own, rank_down,
-                  g_x, grad, g_down, g_up, g_bias,
+def finish_kernel(xn_in, proj_in, w_in, g_logits, ranked, up_own, rank_down, source, g_hidden,
+                  gain, g_ffn, g_head,
+                  g_x, grad, norm_sum, ffn_sum, head_sum, bias_sum, up_sum, down_sum,
                   turned, proj, w, outgoing, mine, paired, inbox, heads_in, parts, landed,
-                  slim_high, slim_low, in_sem, pair_send, pair_recv, send, recv, x_send, x_recv,
-                  p_sem, q_sem):
+                  slim_high, slim_low, small, small_in, small_part,
+                  small_heads, small_all, rows_sum, in_sem, pair_send, pair_recv, send, recv, x_send, x_recv,
+                  p_sem, q_sem, a_send, a_recv, b_send, b_recv, c_send, c_recv):
     h, head = lax.axis_index("head"), lax.axis_size("head")
     rows, width = g_x.shape
     deep = grad.shape[0] * head
@@ -1040,10 +985,6 @@
         for p in range(total.pieces):
             total.relay(head - 1 - h, p)
 
-    g_down[...] = mms((turned[...],), slim, (1, 0))
-    g_up[...] = mms(split(ranked[...]), logit_parts, (0, 0))
-    g_bias[...] = jnp.broadcast_to(jnp.sum(g_logits[...], axis=0, keepdims=True), g_bias.shape)
-
     thin = grad.shape[0]
 
     def to_head(hop, slot):
@@ -1051,16 +992,88 @@
         at = pl.ds(pl.multiple_of(to * thin, thin), thin)
         return push(mine.at[sums.own, at, :], heads_in.at[slot], x_send.at[hop], x_recv.at[slot], to)
 
-    for step in range(sums.levels):
+    sums.advance(0)
+
+    total.result(g_x)
+    rows_sum[...] = jnp.zeros_like(rows_sum)
+    band = rows_sum.shape[0]
+
+    def norm_rows(r, _):
+        at = pl.ds(pl.multiple_of(r * band, band), band)
+        x = source[at, :].astype(F32)
+        inv = lax.rsqrt(jnp.mean(x * x, axis=-1, keepdims=True) + 1e-6)
+        plain, g = x * inv, g_x[at, :]
+        scaled = g * gain[...]
+        inner = jnp.mean(scaled * plain, axis=-1, keepdims=True)
+        rows_sum[...] += g * plain
+        g_x[at, :] = g_hidden[at, :] + inv * (scaled - plain * inner)
+        return 0
+
+    lax.fori_loop(0, rows // band, norm_rows, 0)
+    rank, dk = up_own.shape
+    low, keys = rank // 2, up_sum.shape[1]
+    g_down = mms(slim, (turned[...],), (0, 1))
+    g_up = mms(split(ranked[...]), logit_parts, (0, 0))
+    small[...] = jnp.zeros_like(small)
+    small[:low, :width] = g_down[:low]
+    small[:low, width:] = g_down[low:]
+    own_keys = pl.multiple_of(h * dk, dk)
+    small[low:, pl.ds(own_keys, dk)] = g_up[:low]
+    small[low:, pl.ds(keys + own_keys, dk)] = g_up[low:]
+    small[low : low + 1, width:] = jnp.sum(rows_sum[...], axis=0, keepdims=True)
+    small[low + 1 : low + 2, width:] = g_ffn[...]
+    small[low + 2 : low + 3, width : width + g_head.shape[1]] = g_head[0:1, :]
+    small[low + 3 : low + 4, pl.ds(width + own_keys, dk)] = jnp.sum(
+        g_logits[...], axis=0, keepdims=True
+    )
+    s, seq = lax.axis_index("seq"), lax.axis_size("seq")
+    wide = small.shape[1] // seq
+
+    def piece(ref, i):
+        return ref.at[:, pl.ds(pl.multiple_of(i * wide, wide), wide)]
+
+    def begin_small(axis, me, count, copy):
+        for hop in range(1, count):
+            copy(hop, me, lax.rem(me + hop, count)).start()
+
+    def end_small(axis, me, count, copy):
+        for hop in range(1, count):
+            other = lax.rem(me + hop, count)
+            copy(hop, other, other).wait_recv()
+
+    def scatter(hop, slot, to):
+        return push(
+            piece(small, to), small_in.at[slot], a_send.at[hop], a_recv.at[slot], to, "seq"
+        )
+
+    def between(hop, slot, to):
+        return push(small_part, small_heads.at[slot], b_send.at[hop], b_recv.at[slot], to)
+
+    def spread(hop, slot, to):
+        return push(
+            small_part, piece(small_all, slot), c_send.at[hop], c_recv.at[slot], to, "seq"
+        )
+
+    begin_small("seq", s, seq, scatter)
+    small_in[s] = small[:, pl.ds(pl.multiple_of(s * wide, wide), wide)]
+    for step in range(1, sums.levels):
         sums.advance(step)
     for hop in range(1, head):
         to_head(hop, h).start()
     own_rows = pl.ds(pl.multiple_of(h * thin, thin), thin)
     heads_in[h] = mine[sums.own, own_rows, :]
-    total.result(g_x)
+    end_small("seq", s, seq, scatter)
+    small_part[...] = jnp.sum(small_in[...], axis=0)
+    begin_small("head", h, head, between)
+    small_heads[h] = small_part[...]
+    end_small("head", h, head, between)
+    for hop in range(1, head):
+        between(hop, h, lax.rem(h + hop, head)).wait_send()
+    small_part[...] = jnp.sum(small_heads[...], axis=0)
+    begin_small("seq", s, seq, spread)
+    small_all[:, pl.ds(pl.multiple_of(s * wide, wide), wide)] = small_part[...]
     for hop in range(1, head):
         to_head(hop, lax.rem(h + hop, head)).wait_recv()
-    dk = g_up.shape[1]
     dv = mine.shape[2] // 2 - dk
     for j in range(head):
         at, start = 0, 0
@@ -1069,13 +1082,27 @@
                 j, :, at : at + size
             ].astype(F32)
             at, start = at + size, start + head * size
+    end_small("seq", s, seq, spread)
+    down_sum[:low, :] = small_all[:low, :width]
+    down_sum[low:, :] = small_all[:low, width:]
+    up_sum[:low, :] = small_all[low:, :keys]
+    up_sum[low:, :] = small_all[low:, keys : 2 * keys]
+    norm_sum[...] = small_all[low : low + 1, width:]
+    ffn_sum[...] = small_all[low + 1 : low + 2, width:]
+    head_sum[...] = small_all[low + 2 : low + 3, width : width + head_sum.shape[1]]
+    bias_sum[...] = small_all[low + 3 : low + 4, width : width + keys]
+    for hop in range(1, seq):
+        scatter(hop, s, lax.rem(s + hop, seq)).wait_send()
+        spread(hop, s, lax.rem(s + hop, seq)).wait_send()
     sums.finish(lambda k: outgoing.at[k])
     for hop in range(1, head):
         to_head(hop, h).wait_send()
     total.finish()
 
 
-def finish(xn, g_proj, w_in, g_logits, ranked, up_own, rank_down):
+def finish(
+    xn, g_proj, w_in, g_logits, ranked, up_own, rank_down, source, g_hidden, gain, g_ffn, g_head
+):
     seq, head = lax.axis_size("seq"), lax.axis_size("head")
     group, width = xn.shape
     columns, rank = w_in.shape[1], ranked.shape[1]
@@ -1091,27 +1118,35 @@
         out_shape=(
             jax.ShapeDtypeStruct((rows, width), F32),
             jax.ShapeDtypeStruct((deep // head, columns * head), F32),
-            jax.ShapeDtypeStruct((width, rank), F32),
-            jax.ShapeDtypeStruct((rank, dk), F32),
-            jax.ShapeDtypeStruct((8, dk), F32),
+            jax.ShapeDtypeStruct((1, width), F32),
+            jax.ShapeDtypeStruct((1, width), F32),
+            jax.ShapeDtypeStruct((1, g_head.shape[1]), F32),
+            jax.ShapeDtypeStruct((1, dk * head), F32),
+            jax.ShapeDtypeStruct((rank, dk * head), F32),
+            jax.ShapeDtypeStruct((rank, width), F32),
         ),
-        in_specs=[anywhere] * 3 + [vmem] * 4,
-        out_specs=(vmem,) * 5,
+        in_specs=[anywhere] * 3 + [vmem] * 9,
+        out_specs=(vmem,) * 8,
         scratch_shapes=[
             pltpu.VMEM((width, group), BF16), pltpu.VMEM(g_proj.shape, BF16),
             pltpu.VMEM(w_in.shape, BF16), blocks(pairs, columns), blocks(pairs, columns),
             blocks(pairs, columns), blocks(pairs - 1, columns), ends(columns),
             pltpu.VMEM((group, width), BF16), pltpu.VMEM((group + rows, width), BF16),
             pltpu.VMEM(ranked.shape, BF16), pltpu.VMEM(ranked.shape, BF16),
+            pltpu.VMEM((rank, 2 * width), F32), pltpu.VMEM((seq, rank, 2 * width // seq), F32),
+            pltpu.VMEM((rank, 2 * width // seq), F32),
+            pltpu.VMEM((head, rank, 2 * width // seq), F32),
+            pltpu.VMEM((rank, 2 * width), F32), pltpu.VMEM((16, width), F32),
             dma((3,)), dma((pairs,)), dma((pairs,)), moves, moves, dma((head,)), dma((head,)),
             dma((head, 4)), dma((head + 1, 4)),
+            dma((seq,)), dma((seq,)), dma((head,)), dma((head,)), dma((seq,)), dma((seq,)),
         ],
         compiler_params=pltpu.CompilerParams(
             collective_id=5, has_side_effects=True, vmem_limit_bytes=60 << 20
         ),
-        cost_estimate=cost(60),
+        cost_estimate=cost(95),
         name="finish",
-    )(xn, g_proj, w_in, g_logits, ranked, up_own, rank_down)
+    )(xn, g_proj, w_in, g_logits, ranked, up_own, rank_down, source, g_hidden, gain, g_ffn, g_head)
 
 
 def weight_grad_kernel(left, right, *rest):
@@ -1249,23 +1284,13 @@
     )
     output = (hidden + ffn_out).astype(BF16)
     g_proj, g_logits = g_proj_b.reshape(group, proj_width), g_logits_b.reshape(group, dk)
-    g_xn, grad_in, g_rank_down, g_rank_up, g_bias = finish(
-        xn, g_proj, w_in, g_logits, ranked, up_own, rank_down
+    input_grad, grad_in, *small, g_rank_down = finish(
+        xn, g_proj, w_in, g_logits, ranked, up_own, rank_down, tokens.reshape(micro * rows, width),
+        g_hidden, norm_gain.reshape(1, width), g_ffn_gain.reshape(1, width), g_head_gain,
     )
-    inv_in = rms(source, 1e-6)
-    back_in, g_norm_gain = norm_back(g_xn, norm_gain, source * inv_in, inv_in)
-    input_grad = g_hidden + back_in
-
-    g_rank_up = lax.dynamic_update_slice_in_dim(
-        jnp.zeros(rank_up.shape, F32), g_rank_up, head * dk, 1
-    )
-    g_bias = lax.dynamic_update_slice_in_dim(
-        jnp.zeros(gate_bias.shape, F32), g_bias[0], head * dk, 0
-    )
-    small = total_of(
-        [g_norm_gain, g_ffn_gain, g_head_gain[0], g_rank_down, g_rank_up, g_bias]
-    )
+    g_norm_gain, g_ffn_gain, g_head_gain, g_bias, g_rank_up = small
     slab = width // (seq * heads)
+    grad_in, grads = lax.optimization_barrier((grad_in, grads))
     grad_ffn = grads[:, vals:]
     grad_out = lax.all_to_all(
         grads[:, :vals].reshape(heads, slab, vals), "head", split_axis=0, concat_axis=0, tiled=True
@@ -1278,7 +1303,12 @@
         grad_out,
         grad_ffn[:, : 2 * hidden_units].astype(F32).reshape(-1, 2, hidden_units),
         grad_ffn[:, 2 * hidden_units :].astype(F32),
-        *small,
+        g_norm_gain.reshape(norm_gain.shape),
+        g_ffn_gain.reshape(ffn_gain.shape),
+        g_head_gain.reshape(head_gain.shape),
+        g_rank_down.T,
+        g_rank_up,
+        g_bias.reshape(gate_bias.shape),
     )
 
 

time: 584 us -> 566 us (0.969)
  Pallas kernels: 478 us -> 457 us
  waiting for transfers between devices: 0.04 us -> 18.1 us
  local copies, waits for them, and re-layouts: 32.1 us -> 24.1 us
  other arithmetic: 21.7 us -> 14.5 us
    pallas_call x1 -> x0, Pallas kernels: 33.7 us -> none  [total_of(): pl.pallas_call(total_kernel, out_shape=jax.ShapeDtypeStruct(shape, F32),...]
    all_to_all x1, waiting for transfers between devices: 0.01 us -> 18 us  [on_device(): lax.all_to_all(grads[:, :vals].reshape(heads, slab, vals), 'head', split_...]
    pallas_call x1, Pallas kernels: 92.1 us -> 105 us  [finish(): pl.pallas_call(finish_kernel, out_shape=(jax.ShapeDtypeStruct((rows, widt...]
    slice x8 -> x0, local copies, waits for them, and re-layouts: 7.9 us -> none  [the longest x6 6.48 us: total_of(): result.append(whole[at:at + p.size].reshape(p.shape))]
    unnamed x72 -> x76, local copies, waits for them, and re-layouts: 11 us -> 15 us
  transfers between devices with their start and end apart: 3 -> 3, of which waited for: 0 -> 1; matrix products, arithmetic and copies ran while one was open for 9% -> 5% of each run, Pallas kernels for 62% -> 61%
where the time goes in v8:
time: 566 us; the launch traced here: 557 us
  Pallas kernels  457 us (81%)
  local copies, waits for them, and re-layouts  24.1 us (4%)
  matrix products  22.4 us (4%)
  waiting for transfers between devices  18.1 us (3%)
  between operations  14.9 us (3%)
  other arithmetic  14.5 us (3%)
  starting transfers between devices  6.2 us (1%)
    pallas_call x1, Pallas kernels, feed_forward(): pl.pallas_call(functools.partial(ffn_kernel, count), out_shape=(jax.Shape...  109 us
    pallas_call x1, Pallas kernels, finish(): pl.pallas_call(finish_kernel, out_shape=(jax.ShapeDtypeStruct((rows, widt...  105 us
    pallas_call x1, Pallas kernels, attention_forward(): pl.pallas_call(front_kernel, out_shape=(jax.ShapeDtypeStruct((blocks, mic...  90.5 us
    pallas_call x1, Pallas kernels, attention_back(): pl.pallas_call(back_kernel, out_shape=(jax.ShapeDtypeStruct((blocks, micr...  73.3 us
    pallas_call x1, Pallas kernels, gather_norm(): pl.pallas_call(gather_norm_kernel, out_shape=(jax.ShapeDtypeStruct((count...  69.2 us
    dot_general x6, matrix products, dot(): lax.dot_general(a, b, (((contract[0],), (contract[1],)), ((), ())), preci...  22.4 us
    all_to_all x1, waiting for transfers between devices, on_device(): lax.all_to_all(grads[:, :vals].reshape(heads, slab, vals), 'head', split_...  18 us
    unnamed x76, local copies, waits for them, and re-layouts  15 us
  transfers between devices with their start and end apart: 3, of which 1 were waited for; matrix products, arithmetic and copies ran while one was open for 5% of the time, Pallas kernels for 61%

profile of v8, /device:TPU:0, one launch (start us, length us, event | category | flops | bytes accessed | tf_op | source)
XLA Modules:
  0.0 556.8 jit_solution(5162419003704253247)
XLA Ops:
  7.3 1.6 copy.29
  9.1 1.8 pad_maximum_fusion
  12.4 1.1 constant_dynamic-slice_fusion.4
  13.5 1.1 constant_dynamic-slice_fusion.2
  14.7 69.2 %gather_norm.1 = (bf16[768,2048]{1,0:T(8,128)(2,1)S(1)}, bf16[2048,1536]{1,0:T(8,128)(2,1)S(1)}) custom-call(bf16[192,2048]{1,0:T(8,128)(2,1)S(1)} %bitcast.39, f32[1,2048]{1,0:T(1,128)S(1)} %bitcast.45, bf16[256,1536]{1,0:T(8,128)(2,1)S(1)} %pad_maximum_fusion.1.shard), custom_call_target="tpu_custom_call" | custom-call | bytes 150000000 | tf_op jit(solution)/shard_map/gather_norm/pallas_call | solution.py:363
  84.8 2.7 fusion.19
  87.5 1.8 fusion.12
  89.4 3.4 fusion.14
  92.9 90.5 %attention_forward.1 = (f32[4,3,64,512]{3,2,1,0:T(8,128)S(1)}, bf16[192,2048]{1,0:T(8,128)(2,1)S(1)}, bf16[8,3,16,256]{3,2,1,0:T(8,128)(2,1)S(1)}, f32[4,3,512,256]{3,2,1,0:T(8,128)}, bf16[768,2048]{1,0:T(8,128)(2,1)S(1)}) custom-call(f32[4,3,1,256]{3,2,1,0:T(1,128)S(1)} %broadcast_in_dim.2.keep, bf16[4,3,64,1024]{3,2,1,0:T(8,128)(2,1)S(1)} %bitcast.36, ...), custom_call_target="tpu_custom_call" | custom-call | bytes 270000000 | tf_op jit(solution)/shard_map/attention_forward/pallas_call | solution.py:544
  183.5 1.2 copy-done.5
  184.6 1.6 copy-done.8
  186.3 1.1 copy-done.11
  188.1 6.4 %multiply_reduce_fusion.2 = (f32[192]{0:T(256)S(1)}, f32[192,2048]{1,0:T(8,128)S(1)}) fusion(bf16[192,2048]{1,0:T(8,128)(2,1)S(1)} %get-tuple-element.38.right, bf16[2048,6272]{1,0:T(8,128)(2,1)} %all-gather.2.cloned.1.call-done.w, bf16[192,2048]{1,0:T(8,128)(2,1)S(1)} %bitcast.40), kind=kOutput, calls=%fused_computation.19 | convolution fusion | flops 1612185344 | bytes 11535104 | tf_op jit(solution)/shard_map/dot_general | solution.py:1200
  194.5 1.1 multiply_convert_fusion.x_own
  195.6 108.9 %feed_forward.1 = (f32[192,2048]{1,0:T(8,128)}, bf16[4,192,2048]{2,1,0:T(8,128)(2,1)}, bf16[2048,6272]{1,0:T(8,128)(2,1)}) custom-call(bf16[192,2048]{1,0:T(8,128)(2,1)} %multiply_convert_fusion.x_own, bf16[768,2048]{1,0:T(8,128)(2,1)} %copy-done.8, bf16[2048,6272]{1,0:T(8,128)(2,1)} %all-gather.2.cloned.1.call-done.w), custom_call_target="tpu_custom_call" | custom-call | bytes 300000000 | tf_op jit(solution)/shard_map/feed_forward/pallas_call | solution.py:687
  304.6 2.6 multiply_reduce_fusion
  307.2 1.6 fusion.20
  308.8 10.0 %weight_grad.1 = bf16[2048,6272]{1,0:T(8,128)(2,1)} custom-call(bf16[192,2048]{1,0:T(8,128)(2,1)S(1)} %get-tuple-element.62.left, bf16[192,2048]{1,0:T(8,128)(2,1)S(1)} %get-tuple-element.38.right, bf16[2048,6272]{1,0:T(8,128)(2,1)} %get-tuple-element.51.rest_0_), custom_call_target="tpu_custom_call", output_to_operand_aliasing={{}: (2, {})} | custom-call | flops 1610612736 | bytes 9961472 | tf_op jit(solution)/shard_map/weight_grad/pallas_call | solution.py:1167
  319.8 1.0 copy.28.rank_down
  320.8 7.1 %fusion.9.gated_own = bf16[192,2048]{1,0:T(8,128)(2,1)} fusion(bf16[192,2048]{1,0:T(8,128)(2,1)S(1)} %get-tuple-element.62.left, bf16[2048,6272]{1,0:T(8,128)(2,1)} %all-gather.2.cloned.1.call-done.w), kind=kOutput, calls=%fused_computation.8 | convolution fusion | flops 1611005952 | bytes 9961472 | tf_op jit(solution)/shard_map/dot_general | solution.py:1200
  327.9 73.3 %attention_back.1 = (bf16[4,3,64,1536]{3,2,1,0:T(8,128)(2,1)}, f32[4,3,64,256]{3,2,1,0:T(8,128)}, f32[8,512]{1,0:T(8,128)}, f32[192,2048]{1,0:T(8,128)}) custom-call(f32[4,3,1,256]{3,2,1,0:T(1,128)} %copy-done.14, bf16[192,2048]{1,0:T(8,128)(2,1)} %fusion.9.gated_own, f32[4,3,64,512]{3,2,1,0:T(8,128)} %bitcast.35, f32[4,3,64,512]{3,2,1,0:T(8,128)} %copy-done.11, ...), custom_call_target="tpu_custom_call" | custom-call | bytes 240000000 | tf_op jit(solution)/shard_map/attention_back/pallas_call | solution.py:876
  401.2 105.0 %finish.1 = (f32[192,2048]{1,0:T(8,128)}, f32[64,6144]{1,0:T(8,128)}, f32[1,2048]{1,0:T(1,128)}, f32[1,2048]{1,0:T(1,128)}, f32[1,512]{1,0:T(1,128)}, /*index=5*...) custom-call(bf16[768,2048]{1,0:T(8,128)(2,1)} %copy-done.2, bf16[768,1536]{1,0:T(8,128)(2,1)} %bitcast.50, ...), custom_call_target="tpu_custom_call" | custom-call | bytes 285000000 | tf_op jit(solution)/shard_map/finish/pallas_call | solution.py:1116
  506.2 2.3 slice.24
  508.5 6.1 %all-to-all-start = ((bf16[4,64,2048]{2,1,0:T(8,128)(2,1)}), bf16[4,64,2048]{2,1,0:T(8,128)(2,1)}, u32[]{:S(2)}, u32[]{:S(2)}) async-start(bf16[4,64,2048]{2,1,0:T(8,128)(2,1)} %bitcast.15), calls=%async_computation.1 | async-start | bytes 2097152 | tf_op jit(solution)/shard_map/all_to_all | solution.py:1295
  514.6 1.1 add_convert_fusion
  515.7 1.5 slice_convert_fusion
  517.2 2.8 reshape.146
  520.0 2.4 slice_convert_fusion.1
  522.4 18.0 %all-to-all-done = bf16[4,64,2048]{2,1,0:T(8,128)(2,1)} async-done(((bf16[4,64,2048]{2,1,0:T(8,128)(2,1)}), bf16[4,64,2048]{2,1,0:T(8,128)(2,1)}, u32[]{:S(2)}, u32[]{:S(2)}) %all-to-all-start) | async-done | bytes 1048608 | tf_op jit(solution)/shard_map/all_to_all | solution.py:1295
  540.5 2.2 convert_reduce_fusion
  542.7 1.1 copy.39
  544.7 1.1 copy.40
  (85 shorter events, 9.1 us)
Async XLA Ops:
  7.2 76.7 %copy-start = (f32[16,1024]{1,0:T(8,128)S(1)}, f32[16,1024]{1,0:T(8,128)}, u32[]{:S(2)}) copy-start(f32[16,1024]{1,0:T(8,128)} %param.24) | copy-start | bytes 196612
  7.2 1.7 copy-start.21
  7.2 1.9 copy-start.22
  7.2 180.9 %all-gather.2.cloned.1.call-start = ((), (), s32[]{:S(2)}) async-start(), calls=%async_computation.2 | async-start | bytes 28901376 | tf_op jit(solution)/shard_map/all_gather | solution.py:1192
  10.9 495.3 %reduce-scatter.2.cloned.1.call-start = ((), (), s32[]{:S(2)}) async-start(), calls=%async_computation.3 | async-start | bytes 28901376 | tf_op jit(solution)/shard_map/reduce_scatter | solution.py:1196
  12.4 2.2 copy-start.6
  12.4 2.2 copy-start.15
  14.6 69.3 %copy-start.23 = (bf16[2048,16]{0,1:T(8,128)(2,1)S(1)}, bf16[2048,16]{0,1:T(8,128)(2,1)}, u32[]{:S(2)}) copy-start(bf16[2048,16]{0,1:T(8,128)(2,1)} %param.23) | copy-start | bytes 196612
  83.8 5.5 copy-start.2
  83.8 5.5 copy-start.3
  83.9 5.5 copy-start.26
  87.5 5.4 copy-start.12
  89.4 3.5 copy-start.4
  89.4 3.5 copy-start.9
  89.4 3.5 copy-start.16
  92.9 90.6 %copy-start.14 = (f32[4,3,1,256]{3,2,1,0:T(1,128)}, f32[4,3,1,256]{3,2,1,0:T(1,128)S(1)}, u32[]{:S(2)}) copy-start(f32[4,3,1,256]{3,2,1,0:T(1,128)S(1)} %broadcast_in_dim.2.keep) | copy-start | bytes 36868
  92.9 95.2 %copy-start.7 = (bf16[3,64,2048]{2,1,0:T(8,128)(2,1)S(1)}, bf16[3,64,2048]{2,1,0:T(8,128)(2,1)}, u32[]{:S(2)}) copy-start(bf16[3,64,2048]{2,1,0:T(8,128)(2,1)} %param.13) | copy-start | bytes 2359300
  183.4 1.2 copy-start.5
  184.6 1.6 copy-start.8
  188.1 6.4 %copy-start.25 = (f32[2048]{0:T(1024)S(1)}, f32[2048]{0:T(1024)}, u32[]{:S(2)}) copy-start(f32[2048]{0:T(1024)} %param.21) | copy-start | bytes 24580
  304.5 2.7 copy-start.10
  304.6 2.7 copy-start.17
  508.5 6.1 %copy-start.20 = (f32[192,2048]{1,0:T(8,128)S(1)}, f32[192,2048]{1,0:T(8,128)}, u32[]{:S(2)}) copy-start(f32[192,2048]{1,0:T(8,128)} %get-tuple-element.45) | copy-start | bytes 4718596
  508.5 32.0 %all-to-all-start = ((bf16[4,64,2048]{2,1,0:T(8,128)(2,1)}), bf16[4,64,2048]{2,1,0:T(8,128)(2,1)}, u32[]{:S(2)}, u32[]{:S(2)}) async-start(bf16[4,64,2048]{2,1,0:T(8,128)(2,1)} %bitcast.15), calls=%async_computation.1 | async-start | bytes 2097152 | tf_op jit(solution)/shard_map/all_to_all | solution.py:1295
  520.0 22.7 %copy-start.19 = (f32[192,2048]{1,0:T(8,128)S(1)}, f32[192,2048]{1,0:T(8,128)}, u32[]{:S(2)}) copy-start(f32[192,2048]{1,0:T(8,128)} %get-tuple-element.49) | copy-start | bytes 4718596
  542.7 2.0 copy-start.18
  542.7 6.8 %copy-start.1 = (f32[16,1024]{1,0:T(8,128)S(1)}, f32[16,1024]{1,0:T(8,128)}, u32[]{:S(2)}) copy-start(f32[16,1024]{1,0:T(8,128)} %param.24) | copy-start | bytes 196612
  544.7 1.8 copy-start.28
  544.7 2.4 copy-start.32
  544.7 3.0 copy-start.24
  544.7 3.6 copy-start.27
  544.7 4.2 copy-start.30
  (4 other events, 3.7 us)
Sparse Core Ops, SparseCore 0:
  11.0 176.3 all-gather.1
  319.0 185.8 reduce-scatter.1

commit v9 on v8

--- a/solution.py
+++ b/solution.py
@@ -381,11 +381,12 @@
 
 
 def swap_slices(own, got, send, recv):
-    me, count = lax.axis_index("seq"), lax.axis_size("seq")
+    side = lax.rem(lax.axis_index("seq"), 2)
+    me, count = lax.axis_index("seq") // 2, lax.axis_size("seq") // 2
 
     def copy(hop, index):
         to = lax.rem(me + hop, count)
-        return push(own.at[to], got.at[index], send.at[hop], recv.at[index], to, "seq")
+        return push(own.at[to], got.at[index], send.at[hop], recv.at[index], 2 * to + side, "seq")
 
     def start(hop, _):
         copy(hop, me).start()
@@ -410,6 +411,16 @@
         lax.fori_loop(1, count, wait_send, 0)
 
     return begin, end, drain
+
+
+def to_mate(src, dst, send, recv):
+    s = lax.axis_index("seq")
+    return push(src, dst, send, recv, s + 1 - 2 * lax.rem(s, 2), "seq")
+
+
+def sided(own, mate):
+    first = lax.rem(lax.axis_index("seq"), 2) == 0
+    return jnp.where(first, own, mate), jnp.where(first, mate, own)
 
 
 def scan_states(reverse, own, through, out):
@@ -424,9 +435,11 @@
     lax.fori_loop(0, count, step, jnp.zeros(out.shape[1:], F32))
 
 
-def front_kernel(keep, qkv, decay, og, gain, rows_own, o_out, gated, through, kept_out, rows_all,
-                 kept, runs, state, sending, got, scanned, before, leaving,
-                 here_sem, go, come, s_send, s_recv, b_send, b_recv, z_send, z_recv, k_sem):
+def front_kernel(keep, qkv, decay, og, gain, rows_own,
+                 o_out, gated, through, pair_through, kept_out, rows_all,
+                 kept, runs, state, sending, got, scanned, before, leaving, mate_out, mate_in,
+                 back_out, back_in, first_state,
+                 here_sem, go, come, s_send, s_recv, b_send, b_recv, z_send, z_recv, k_sem, m_sem):
     h, head = lax.axis_index("head"), lax.axis_size("head")
     count, micro, rows, dk = decay.shape
     dv = og.shape[-1]
@@ -454,14 +467,35 @@
             alive[m] = alive[m] * keep[b, m]
     tail = sending.shape[2] - part
     at = lax.broadcasted_iota(jnp.int32, (tail, dk), 0)
+    half = dv // 2
+    side = lax.rem(lax.axis_index("seq"), 2)
+    own_half = pl.ds(pl.multiple_of(side * half, half), half)
+    mate_half = pl.ds(pl.multiple_of((1 - side) * half, half), half)
+
+    def as_rows(value):
+        high, low = split(value)
+        return jnp.where(at == 0, high.astype(F32), jnp.where(at == 1, low.astype(F32), 0.0))
+
+    own_rows = [as_rows(jnp.exp(passed[m]) * alive[m]) for m in range(micro)]
     for m in range(micro):
-        high, low = split(jnp.exp(passed[m]) * alive[m])
-        extra = jnp.where(
-            at == 0, high.astype(F32), jnp.where(at == 1, low.astype(F32), 0.0)
-        ).astype(BF16)
+        mate_out[m, :half, :] = state[m, mate_half, :].astype(BF16)
+        mate_out[m, half:, :] = own_rows[m].astype(BF16)
+    swap = to_mate(mate_out, mate_in, m_sem.at[0], m_sem.at[1])
+    swap.start()
+    swap.wait_recv()
+    first_through = []
+    for m in range(micro):
+        firsts, seconds = sided(own_rows[m], mate_in[m, half:, :].astype(F32))
+        pair_through[0, m], pair_through[1, m] = firsts.astype(BF16), seconds.astype(BF16)
+        first, second = firsts[0:1] + firsts[1:2], seconds[0:1] + seconds[1:2]
+        first_through.append(first)
+        start, after = sided(state[m, own_half, :], mate_in[m, :half, :].astype(F32))
+        first_state[m] = start
+        pair = second * start + after
+        both = as_rows(first * second).astype(BF16)
         for i in range(slices):
-            sending[i, m, :part, :] = state[m, i * part : (i + 1) * part, :].astype(BF16)
-            sending[i, m, part:, :] = extra
+            sending[i, m, :part, :] = pair[i * part : (i + 1) * part, :].astype(BF16)
+            sending[i, m, part:, :] = both
     begin, end, drain = swap_slices(sending, got, s_send, s_recv)
     begin()
     causal = lower_ones(rows)
@@ -484,8 +518,16 @@
     begin_back()
     line.receive(2, near_order(h, head, 2))
     end_back()
-    for i in range(slices):
-        state[:, i * part : (i + 1) * part, :] = before[i].astype(F32)
+    for m in range(micro):
+        entry = before[:, m].astype(F32).reshape(half, dk)
+        own, mate = sided(entry, first_through[m] * entry + first_state[m])
+        state[m, own_half, :] = own
+        back_out[m] = mate.astype(BF16)
+    swap_back = to_mate(back_out, back_in, m_sem.at[2], m_sem.at[3])
+    swap_back.start()
+    swap_back.wait_recv()
+    for m in range(micro):
+        state[m, mate_half, :] = back_in[m].astype(F32)
 
     def to_owner(b):
         columns = gated.at[:, pl.ds(pl.multiple_of(h * dv, dv), dv)]
@@ -529,6 +571,8 @@
     line.finish()
     drain()
     drain_back()
+    swap.wait_send()
+    swap_back.wait_send()
 
 
 def attention_forward(keep, qkv, decays, og, gain, rows_own):
@@ -536,29 +580,34 @@
     dk, dv = decays.shape[-1], og.shape[-1]
     head, seq = lax.axis_size("head"), lax.axis_size("seq")
     assert blocks == head and head == 4
-    part, tail = dv // seq, 16
+    pairs, half, tail = seq // 2, dv // 2, 16
+    part = half // pairs
     own_rows = micro * rows
     vmem, anywhere = pl.BlockSpec(memory_space=pltpu.VMEM), pl.BlockSpec(memory_space=pl.ANY)
     dma = pltpu.SemaphoreType.DMA
-    states, wider = (seq, micro, part, dk), (seq, micro, part + tail, dk)
+    states, wider = (pairs, micro, part, dk), (pairs, micro, part + tail, dk)
     return pl.pallas_call(
         front_kernel,
         out_shape=(
             jax.ShapeDtypeStruct((blocks, micro, rows, dv), F32),
             jax.ShapeDtypeStruct((own_rows, head * dv), BF16),
-            jax.ShapeDtypeStruct((seq, micro, tail, dk), BF16),
+            jax.ShapeDtypeStruct((pairs, micro, tail, dk), BF16),
+            jax.ShapeDtypeStruct((2, micro, tail, dk), BF16),
             jax.ShapeDtypeStruct((blocks, micro, dv, dk), F32),
             jax.ShapeDtypeStruct((head * rows_own.shape[0], rows_own.shape[1]), BF16),
         ),
         in_specs=[vmem] * 5 + [anywhere],
-        out_specs=(vmem,) * 3 + (anywhere,) * 2,
+        out_specs=(vmem,) * 4 + (anywhere,) * 2,
         scratch_shapes=[
             pltpu.VMEM((blocks, micro, dv, dk), F32), pltpu.VMEM((blocks, micro, rows, dk), F32),
             pltpu.VMEM((micro, dv, dk), F32), pltpu.VMEM(wider, BF16), pltpu.VMEM(wider, BF16),
             pltpu.VMEM(states, BF16), pltpu.VMEM(states, BF16),
             pltpu.VMEM((blocks, own_rows, dv), BF16),
-            dma(()), dma((head + 1,)), dma((head,)), dma((seq,)), dma((seq,)), dma((seq,)),
-            dma((seq,)), dma((head,)), dma((head,)), dma((blocks,)),
+            pltpu.VMEM((micro, half + tail, dk), BF16), pltpu.VMEM((micro, half + tail, dk), BF16),
+            pltpu.VMEM((micro, half, dk), BF16), pltpu.VMEM((micro, half, dk), BF16),
+            pltpu.VMEM((micro, half, dk), F32),
+            dma(()), dma((head + 1,)), dma((head,)), dma((pairs,)), dma((pairs,)), dma((pairs,)),
+            dma((pairs,)), dma((head,)), dma((head,)), dma((blocks,)), dma((4,)),
         ],
         compiler_params=pltpu.CompilerParams(
             collective_id=2, has_side_effects=True, vmem_limit_bytes=40 << 20
@@ -715,10 +764,12 @@
     )(x_own, c_all, w)
 
 
-def back_kernel(keep, gated_own, og, o_in, qkv, decay, logits, through, gain, kept_in, parts_in,
+def back_kernel(keep, gated_own, og, o_in, qkv, decay, logits, through, pair_through, gain,
+                kept_in, parts_in,
                 g_proj, g_logits, g_gain, f_out,
                 gated_all, go, runs, g_queried, g_keyed, g_values, pulls, weights, kept,
-                parts, landed, state, sending, got, scanned, after, in_sem, z_send, z_recv, s_send, s_recv, b_send, b_recv, p_sem, q_sem):
+                parts, landed, state, sending, got, scanned, after, mate_out, mate_in,
+                back_out, back_in, second_state, m_sem, in_sem, z_send, z_recv, s_send, s_recv, b_send, b_recv, p_sem, q_sem):
     h, head = lax.axis_index("head"), lax.axis_size("head")
     count, micro, rows, dk = decay.shape
     dv = og.shape[-1]
@@ -780,8 +831,21 @@
         return 0
 
     lax.fori_loop(0, head, gates, 0)
-    for i in range(slices):
-        sending[i] = state[:, i * part : (i + 1) * part, :].astype(BF16)
+    half = dv // 2
+    side = lax.rem(lax.axis_index("seq"), 2)
+    own_half = pl.ds(pl.multiple_of(side * half, half), half)
+    mate_half = pl.ds(pl.multiple_of((1 - side) * half, half), half)
+    mate_out[...] = state[:, mate_half, :].astype(BF16)
+    swap = to_mate(mate_out, mate_in, m_sem.at[0], m_sem.at[1])
+    swap.start()
+    swap.wait_recv()
+    passes = pair_through[:, :, 0:1, :].astype(F32) + pair_through[:, :, 1:2, :].astype(F32)
+    for m in range(micro):
+        start, later_state = sided(state[m, own_half, :], mate_in[m].astype(F32))
+        second_state[m] = later_state
+        pair = passes[0, m] * later_state + start
+        for i in range(slices):
+            sending[i, m] = pair[i * part : (i + 1) * part, :].astype(BF16)
     begin, end, drain = swap_slices(sending, got, s_send, s_recv)
     begin()
     for load in loads:
@@ -819,8 +883,18 @@
             total.relay(head - 1 - h, p)
 
     end_back()
-    for i in range(slices):
-        state[:, i * part : (i + 1) * part, :] = after[i].astype(F32)
+    for m in range(micro):
+        leave = after[:, m].astype(F32).reshape(half, dk)
+        firsts = passes[1, m] * leave + second_state[m]
+        own, _ = sided(firsts, leave)
+        mate, _ = sided(leave, firsts)
+        state[m, own_half, :] = own
+        back_out[m] = mate.astype(BF16)
+    swap_back = to_mate(back_out, back_in, m_sem.at[2], m_sem.at[3])
+    swap_back.start()
+    swap_back.wait_recv()
+    for m in range(micro):
+        state[m, mate_half, :] = back_in[m].astype(F32)
 
     def across(step, _):
         b = count - 1 - step
@@ -858,12 +932,14 @@
     total.finish()
     drain()
     drain_back()
+    swap.wait_send()
+    swap_back.wait_send()
     for hop in range(1, head):
         to_head(hop, h).wait_send()
 
 
 def attention_back(
-    keep, gated_own, og, o, qkv, decays, logits, through, gain, kept, parts
+    keep, gated_own, og, o, qkv, decays, logits, through, pair_through, gain, kept, parts
 ):
     blocks, micro, rows, width = qkv.shape
     dk, dv = decays.shape[-1], og.shape[-1]
@@ -872,7 +948,9 @@
     vmem, anywhere = pl.BlockSpec(memory_space=pltpu.VMEM), pl.BlockSpec(memory_space=pl.ANY)
     dma = pltpu.SemaphoreType.DMA
     blocked = lambda w, kind: pltpu.VMEM((blocks, micro, rows, w), kind)
-    states = (seq, micro, dv // seq, dk)
+    pairs, half = seq // 2, dv // 2
+    states = (pairs, micro, half // pairs, dk)
+    halves = (micro, half, dk)
     return pl.pallas_call(
         back_kernel,
         out_shape=(
@@ -881,7 +959,7 @@
             jax.ShapeDtypeStruct((8, dv), F32),
             jax.ShapeDtypeStruct((own_rows, parts.shape[1]), F32),
         ),
-        in_specs=[vmem] * 9 + [anywhere] * 2,
+        in_specs=[vmem] * 10 + [anywhere] * 2,
         out_specs=(vmem,) * 4,
         scratch_shapes=[
             pltpu.VMEM((blocks, micro * rows, dv), BF16), blocked(dv, F32), blocked(dk, F32),
@@ -892,19 +970,21 @@
             pltpu.VMEM((parts.shape[0] + own_rows, parts.shape[1]), BF16),
             pltpu.VMEM((micro, dv, dk), F32),
             pltpu.VMEM(states, BF16), pltpu.VMEM(states, BF16), pltpu.VMEM(states, BF16),
-            pltpu.VMEM(states, BF16),
-            dma((2,)), dma((head,)), dma((head,)), dma((seq,)), dma((seq,)), dma((seq,)),
-            dma((seq,)), dma((head, 4)), dma((head + 1, 4)),
+            pltpu.VMEM(states, BF16), pltpu.VMEM(halves, BF16), pltpu.VMEM(halves, BF16),
+            pltpu.VMEM(halves, BF16), pltpu.VMEM(halves, BF16), pltpu.VMEM(halves, F32), dma((4,)),
+            dma((2,)), dma((head,)), dma((head,)), dma((pairs,)), dma((pairs,)), dma((pairs,)),
+            dma((pairs,)), dma((head, 4)), dma((head + 1, 4)),
         ],
         compiler_params=pltpu.CompilerParams(
             collective_id=3, has_side_effects=True, vmem_limit_bytes=60 << 20
         ),
         cost_estimate=cost(80),
         name="attention_back",
-    )(keep, gated_own, og, o, qkv, decays, logits, through, gain, kept, parts)
-
-
-def finish_kernel(xn_in, proj_in, w_in, g_logits, ranked, up_own, rank_down, source, g_hidden,
+    )(keep, gated_own, og, o, qkv, decays, logits, through, pair_through, gain, kept,
+      parts)
+
+
+def finish_kernel(xn_in, proj_in, w_in, g_logits, ranked, up_own, rank_down, source,
                   gain, g_ffn, g_head,
                   g_x, grad, norm_sum, ffn_sum, head_sum, bias_sum, up_sum, down_sum,
                   turned, proj, w, outgoing, mine, paired, inbox, heads_in, parts, landed,
@@ -1006,7 +1086,7 @@
         scaled = g * gain[...]
         inner = jnp.mean(scaled * plain, axis=-1, keepdims=True)
         rows_sum[...] += g * plain
-        g_x[at, :] = g_hidden[at, :] + inv * (scaled - plain * inner)
+        g_x[at, :] = inv * (scaled - plain * inner)
         return 0
 
     lax.fori_loop(0, rows // band, norm_rows, 0)
@@ -1078,9 +1158,7 @@
     for j in range(head):
         at, start = 0, 0
         for size in (dk, dk, dv, dv):
-            grad[:, start + j * size : start + (j + 1) * size] = heads_in[
-                j, :, at : at + size
-            ].astype(F32)
+            grad[:, start + j * size : start + (j + 1) * size] = heads_in[j, :, at : at + size]
             at, start = at + size, start + head * size
     end_small("seq", s, seq, spread)
     down_sum[:low, :] = small_all[:low, :width]
@@ -1101,7 +1179,7 @@
 
 
 def finish(
-    xn, g_proj, w_in, g_logits, ranked, up_own, rank_down, source, g_hidden, gain, g_ffn, g_head
+    xn, g_proj, w_in, g_logits, ranked, up_own, rank_down, source, gain, g_ffn, g_head
 ):
     seq, head = lax.axis_size("seq"), lax.axis_size("head")
     group, width = xn.shape
@@ -1117,7 +1195,7 @@
         finish_kernel,
         out_shape=(
             jax.ShapeDtypeStruct((rows, width), F32),
-            jax.ShapeDtypeStruct((deep // head, columns * head), F32),
+            jax.ShapeDtypeStruct((deep // head, columns * head), BF16),
             jax.ShapeDtypeStruct((1, width), F32),
             jax.ShapeDtypeStruct((1, width), F32),
             jax.ShapeDtypeStruct((1, g_head.shape[1]), F32),
@@ -1125,7 +1203,7 @@
             jax.ShapeDtypeStruct((rank, dk * head), F32),
             jax.ShapeDtypeStruct((rank, width), F32),
         ),
-        in_specs=[anywhere] * 3 + [vmem] * 9,
+        in_specs=[anywhere] * 3 + [vmem] * 8,
         out_specs=(vmem,) * 8,
         scratch_shapes=[
             pltpu.VMEM((width, group), BF16), pltpu.VMEM(g_proj.shape, BF16),
@@ -1146,7 +1224,7 @@
         ),
         cost_estimate=cost(95),
         name="finish",
-    )(xn, g_proj, w_in, g_logits, ranked, up_own, rank_down, source, g_hidden, gain, g_ffn, g_head)
+    )(xn, g_proj, w_in, g_logits, ranked, up_own, rank_down, source, gain, g_ffn, g_head)
 
 
 def weight_grad_kernel(left, right, *rest):
@@ -1262,7 +1340,7 @@
     qkv_b, og_b, decays_b = blocks(qkv), blocks(og), blocks(decays)
     gain_row = head_gain.reshape(1, dv)
     keep = 1.0 - jnp.broadcast_to(starts.T[:, :, None, None], (heads, micro, 1, dk)).astype(F32)
-    o_b, gated, through, kept, all_cot = attention_forward(
+    o_b, gated, through, pair_through, kept, all_cot = attention_forward(
         keep, qkv_b, decays_b, og_b, gain_row, cotangent.reshape(micro * rows, width)
     )
 
@@ -1277,18 +1355,19 @@
     back_ffn, g_ffn_gain = norm_back(g_h2, ffn_gain, plain_ffn, inv_ffn)
     g_hidden = cotangent.astype(F32).reshape(micro * rows, width) + back_ffn
     g_mixed = g_hidden.astype(BF16)
-    grads = scatter_grad(weight_grad(g_mixed, gated, grads, later.shape[1], 0, dv))
+    grads = scatter_grad(weight_grad(g_mixed, gated, grads, later.shape[1], 0, vals))
     g_gated = dot(g_mixed, w_out, (1, 0)).astype(BF16)
     g_proj_b, g_logits_b, g_head_gain, ffn_out = attention_back(
-        keep, g_gated, og_b, o_b, qkv_b, decays_b, blocks(logits), through, gain_row, kept, ffn_part.reshape(group, width),
+        keep, g_gated, og_b, o_b, qkv_b, decays_b, blocks(logits), through, pair_through, gain_row, kept, ffn_part.reshape(group, width),
     )
     output = (hidden + ffn_out).astype(BF16)
     g_proj, g_logits = g_proj_b.reshape(group, proj_width), g_logits_b.reshape(group, dk)
-    input_grad, grad_in, *small, g_rank_down = finish(
+    back_in, grad_in, *small, g_rank_down = finish(
         xn, g_proj, w_in, g_logits, ranked, up_own, rank_down, tokens.reshape(micro * rows, width),
-        g_hidden, norm_gain.reshape(1, width), g_ffn_gain.reshape(1, width), g_head_gain,
+        norm_gain.reshape(1, width), g_ffn_gain.reshape(1, width), g_head_gain,
     )
     g_norm_gain, g_ffn_gain, g_head_gain, g_bias, g_rank_up = small
+    input_grad = g_hidden + back_in
     slab = width // (seq * heads)
     grad_in, grads = lax.optimization_barrier((grad_in, grads))
     grad_ffn = grads[:, vals:]
@@ -1299,7 +1378,7 @@
     return (
         output.reshape(tokens.shape),
         input_grad.reshape(tokens.shape),
-        grad_in,
+        grad_in.astype(F32),
         grad_out,
         grad_ffn[:, : 2 * hidden_units].astype(F32).reshape(-1, 2, hidden_units),
         grad_ffn[:, 2 * hidden_units :].astype(F32),

time: 566 us -> 552 us (0.975)
  Pallas kernels: 457 us -> 444 us
    pallas_call x1, Pallas kernels: 90.5 us -> 84.3 us  [attention_forward(): pl.pallas_call(front_kernel, out_shape=(jax.ShapeDtypeStruct((blocks, mic...]
  transfers between devices with their start and end apart: 3 -> 3, of which waited for: 1 -> 1; matrix products, arithmetic and copies ran while one was open for 5% -> 6% of each run, Pallas kernels for 61% -> 62%
where the time goes in v9:
time: 552 us; the launch traced here: 543 us
  Pallas kernels  444 us (80%)
  matrix products  22.8 us (4%)
  local copies, waits for them, and re-layouts  21.5 us (4%)
  other arithmetic  19.4 us (4%)
  between operations  14.9 us (3%)
  waiting for transfers between devices  13.9 us (3%)
  starting transfers between devices  7.26 us (1%)
    pallas_call x1, Pallas kernels, finish(): pl.pallas_call(finish_kernel, out_shape=(jax.ShapeDtypeStruct((rows, widt...  107 us
    pallas_call x1, Pallas kernels, feed_forward(): pl.pallas_call(functools.partial(ffn_kernel, count), out_shape=(jax.Shape...  103 us
    pallas_call x1, Pallas kernels, attention_forward(): pl.pallas_call(front_kernel, out_shape=(jax.ShapeDtypeStruct((blocks, mic...  84.3 us
    pallas_call x1, Pallas kernels, attention_back(): pl.pallas_call(back_kernel, out_shape=(jax.ShapeDtypeStruct((blocks, micr...  74.3 us
    pallas_call x1, Pallas kernels, gather_norm(): pl.pallas_call(gather_norm_kernel, out_shape=(jax.ShapeDtypeStruct((count...  69.2 us
    dot_general x6, matrix products, dot(): lax.dot_general(a, b, (((contract[0],), (contract[1],)), ((), ())), preci...  22.8 us
    all_to_all x1, waiting for transfers between devices, on_device(): lax.all_to_all(grads[:, :vals].reshape(heads, slab, vals), 'head', split_...  13.8 us
    unnamed x76, local copies, waits for them, and re-layouts  12.4 us
  transfers between devices with their start and end apart: 3, of which 1 were waited for; matrix products, arithmetic and copies ran while one was open for 6% of the time, Pallas kernels for 62%

profile of v9, /device:TPU:0, one launch (start us, length us, event | category | flops | bytes accessed | tf_op | source)
XLA Modules:
  0.0 543.5 jit_solution(5448935269051660561)
XLA Ops:
  7.3 1.6 copy.29
  9.1 1.8 pad_maximum_fusion
  12.4 1.1 constant_dynamic-slice_fusion.4
  13.5 1.1 constant_dynamic-slice_fusion.2
  14.7 69.2 %gather_norm.1 = (bf16[768,2048]{1,0:T(8,128)(2,1)S(1)}, bf16[2048,1536]{1,0:T(8,128)(2,1)S(1)}) custom-call(bf16[192,2048]{1,0:T(8,128)(2,1)S(1)} %bitcast.43, f32[1,2048]{1,0:T(1,128)S(1)} %bitcast.48, bf16[256,1536]{1,0:T(8,128)(2,1)S(1)} %pad_maximum_fusion.1.shard), custom_call_target="tpu_custom_call" | custom-call | bytes 150000000 | tf_op jit(solution)/shard_map/gather_norm/pallas_call | solution.py:363
  84.8 2.7 fusion.19
  87.5 1.8 fusion.12
  89.4 3.4 fusion.14
  92.9 84.3 %attention_forward.1 = (f32[4,3,64,512]{3,2,1,0:T(8,128)S(1)}, bf16[192,2048]{1,0:T(8,128)(2,1)S(1)}, bf16[4,3,16,256]{3,2,1,0:T(8,128)(2,1)S(1)}, bf16[2,3,16,2...) custom-call(f32[4,3,1,256]{3,2,1,0:T(1,128)S(1)} %broadcast_in_dim.2.keep, ...), custom_call_target="tpu_custom_call" | custom-call | bytes 270000000 | tf_op jit(solution)/shard_map/attention_forward/pallas_call | solution.py:589
  177.3 1.2 copy-done.7
  178.4 1.7 copy-done.8
  180.1 1.1 copy-done.11
  182.5 6.4 %multiply_reduce_fusion.2 = (f32[192]{0:T(256)S(1)}, f32[192,2048]{1,0:T(8,128)S(1)}) fusion(bf16[192,2048]{1,0:T(8,128)(2,1)S(1)} %get-tuple-element.39.right, bf16[2048,6272]{1,0:T(8,128)(2,1)} %all-gather.2.cloned.1.call-done.w, bf16[192,2048]{1,0:T(8,128)(2,1)S(1)} %bitcast.44), kind=kOutput, calls=%fused_computation.19 | convolution fusion | flops 1612185344 | bytes 11535104 | tf_op jit(solution)/shard_map/dot_general | solution.py:1278
  188.9 1.3 multiply_convert_fusion.x_own
  190.2 103.3 %feed_forward.1 = (f32[192,2048]{1,0:T(8,128)}, bf16[4,192,2048]{2,1,0:T(8,128)(2,1)}, bf16[2048,6272]{1,0:T(8,128)(2,1)}) custom-call(bf16[192,2048]{1,0:T(8,128)(2,1)} %multiply_convert_fusion.x_own, bf16[768,2048]{1,0:T(8,128)(2,1)} %copy-done.8, bf16[2048,6272]{1,0:T(8,128)(2,1)} %all-gather.2.cloned.1.call-done.w), custom_call_target="tpu_custom_call" | custom-call | bytes 300000000 | tf_op jit(solution)/shard_map/feed_forward/pallas_call | solution.py:736
  293.5 2.6 multiply_reduce_fusion
  296.1 1.9 fusion.21.left
  298.1 5.2 weight_grad.1
  303.3 0.9 copy.27.ranked
  304.2 1.0 copy.28.rank_down
  305.2 7.6 %fusion.9.gated_own = bf16[192,2048]{1,0:T(8,128)(2,1)} fusion(bf16[192,2048]{1,0:T(8,128)(2,1)S(1)} %fusion.21.left, bf16[2048,6272]{1,0:T(8,128)(2,1)} %all-gather.2.cloned.1.call-done.w), kind=kOutput, calls=%fused_computation.8 | convolution fusion | flops 1611005952 | bytes 9961472 | tf_op jit(solution)/shard_map/dot_general | solution.py:1278
  312.8 74.3 %attention_back.1 = (bf16[4,3,64,1536]{3,2,1,0:T(8,128)(2,1)}, f32[4,3,64,256]{3,2,1,0:T(8,128)}, f32[8,512]{1,0:T(8,128)}, f32[192,2048]{1,0:T(8,128)}) custom-call(f32[4,3,1,256]{3,2,1,0:T(1,128)} %copy-done.13, bf16[192,2048]{1,0:T(8,128)(2,1)} %fusion.9.gated_own, f32[4,3,64,512]{3,2,1,0:T(8,128)} %bitcast.39, f32[4,3,64,512]{3,2,1,0:T(8,128)} %copy-done.11, ...), custom_call_target="tpu_custom_call" | custom-call | bytes 240000000 | tf_op jit(solution)/shard_map/attention_back/pallas_call | solution.py:954
  387.1 107.5 %finish.1 = (f32[192,2048]{1,0:T(8,128)}, bf16[64,6144]{1,0:T(8,128)(2,1)}, f32[1,2048]{1,0:T(1,128)}, f32[1,2048]{1,0:T(1,128)}, f32[1,512]{1,0:T(1,128)}, /*in...) custom-call(bf16[768,2048]{1,0:T(8,128)(2,1)} %copy-done.2, bf16[768,1536]{1,0:T(8,128)(2,1)} %bitcast.53, ...), custom_call_target="tpu_custom_call" | custom-call | bytes 285000000 | tf_op jit(solution)/shard_map/finish/pallas_call | solution.py:1194
  494.7 2.3 slice.24
  497.0 7.2 %all-to-all-start = ((bf16[4,64,2048]{2,1,0:T(8,128)(2,1)}), bf16[4,64,2048]{2,1,0:T(8,128)(2,1)}, u32[]{:S(2)}, u32[]{:S(2)}) async-start(bf16[4,64,2048]{2,1,0:T(8,128)(2,1)} %bitcast.15), calls=%async_computation.1 | async-start | bytes 2097152 | tf_op jit(solution)/shard_map/all_to_all | solution.py:1374
  504.1 4.4 fusion.20
  508.5 1.2 convert_element_type.45
  509.7 1.5 slice_convert_fusion
  511.3 2.8 reshape.146
  514.1 2.4 slice_convert_fusion.1
  516.5 13.8 %all-to-all-done = bf16[4,64,2048]{2,1,0:T(8,128)(2,1)} async-done(((bf16[4,64,2048]{2,1,0:T(8,128)(2,1)}), bf16[4,64,2048]{2,1,0:T(8,128)(2,1)}, u32[]{:S(2)}, u32[]{:S(2)}) %all-to-all-start) | async-done | bytes 1048608 | tf_op jit(solution)/shard_map/all_to_all | solution.py:1374
  530.3 2.2 convert_reduce_fusion
  (86 shorter events, 7.9 us)
Async XLA Ops:
  7.2 76.6 %copy-start = (f32[16,1024]{1,0:T(8,128)S(1)}, f32[16,1024]{1,0:T(8,128)}, u32[]{:S(2)}) copy-start(f32[16,1024]{1,0:T(8,128)} %param.24) | copy-start | bytes 196612
  7.2 1.7 copy-start.21
  7.2 1.9 copy-start.23
  7.2 175.3 %all-gather.2.cloned.1.call-start = ((), (), s32[]{:S(2)}) async-start(), calls=%async_computation.2 | async-start | bytes 28901376 | tf_op jit(solution)/shard_map/all_gather | solution.py:1270
  10.9 483.7 %reduce-scatter.2.cloned.1.call-start = ((), (), s32[]{:S(2)}) async-start(), calls=%async_computation.3 | async-start | bytes 28901376 | tf_op jit(solution)/shard_map/reduce_scatter | solution.py:1274
  12.4 2.2 copy-start.9
  12.4 2.2 copy-start.16
  14.6 69.3 %copy-start.24 = (bf16[2048,16]{0,1:T(8,128)(2,1)S(1)}, bf16[2048,16]{0,1:T(8,128)(2,1)}, u32[]{:S(2)}) copy-start(bf16[2048,16]{0,1:T(8,128)(2,1)} %param.23) | copy-start | bytes 196612
  83.8 5.5 %copy-start.2 = (bf16[768,2048]{1,0:T(8,128)(2,1)}, bf16[768,2048]{1,0:T(8,128)(2,1)S(1)}, u32[]{:S(2)}) copy-start(bf16[768,2048]{1,0:T(8,128)(2,1)S(1)} %get-tuple-element.37.xn_in) | copy-start | bytes 9437188
  83.8 5.5 %copy-start.5 = (bf16[2048,1536]{1,0:T(8,128)(2,1)}, bf16[2048,1536]{1,0:T(8,128)(2,1)S(1)}, u32[]{:S(2)}) copy-start(bf16[2048,1536]{1,0:T(8,128)(2,1)S(1)} %get-tuple-element.38.w_in) | copy-start | bytes 18874372
  83.9 5.5 %copy-start.28 = (f32[16,256]{1,0:T(8,128)}, f32[16,256]{1,0:T(8,128)S(1)}, u32[]{:S(2)}) copy-start(f32[16,256]{1,0:T(8,128)S(1)} %constant_dynamic-slice_fusion.up_own) | copy-start | bytes 49156
  87.5 5.3 copy-start.12
  89.3 3.5 copy-start.6
  89.3 3.5 copy-start.3
  89.4 3.5 copy-start.17
  92.9 84.4 %copy-start.13 = (f32[4,3,1,256]{3,2,1,0:T(1,128)}, f32[4,3,1,256]{3,2,1,0:T(1,128)S(1)}, u32[]{:S(2)}) copy-start(f32[4,3,1,256]{3,2,1,0:T(1,128)S(1)} %broadcast_in_dim.2.keep) | copy-start | bytes 36868
  92.9 89.6 %copy-start.10 = (bf16[3,64,2048]{2,1,0:T(8,128)(2,1)S(1)}, bf16[3,64,2048]{2,1,0:T(8,128)(2,1)}, u32[]{:S(2)}) copy-start(bf16[3,64,2048]{2,1,0:T(8,128)(2,1)} %param.13) | copy-start | bytes 2359300
  178.4 1.7 copy-start.8
  182.5 6.5 %copy-start.26 = (f32[2048]{0:T(1024)S(1)}, f32[2048]{0:T(1024)}, u32[]{:S(2)}) copy-start(f32[2048]{0:T(1024)} %param.21) | copy-start | bytes 24580
  188.9 104.6 %copy-start.18 = (f32[192,2048]{1,0:T(8,128)}, f32[192,2048]{1,0:T(8,128)S(1)}, u32[]{:S(2)}) copy-start(f32[192,2048]{1,0:T(8,128)S(1)} %get-tuple-element.73) | copy-start | bytes 4718596
  293.5 2.7 copy-start.4
  293.5 2.7 copy-start.20
  497.0 7.2 %copy-start.19 = (f32[192,2048]{1,0:T(8,128)S(1)}, f32[192,2048]{1,0:T(8,128)}, u32[]{:S(2)}) copy-start(f32[192,2048]{1,0:T(8,128)} %copy-done.18) | copy-start | bytes 4718596
  497.0 33.3 %all-to-all-start = ((bf16[4,64,2048]{2,1,0:T(8,128)(2,1)}), bf16[4,64,2048]{2,1,0:T(8,128)(2,1)}, u32[]{:S(2)}, u32[]{:S(2)}) async-start(bf16[4,64,2048]{2,1,0:T(8,128)(2,1)} %bitcast.15), calls=%async_computation.1 | async-start | bytes 2097152 | tf_op jit(solution)/shard_map/all_to_all | solution.py:1374
  504.1 4.4 copy-start.22
  511.3 24.9 %copy-start.1 = (f32[16,1024]{1,0:T(8,128)S(1)}, f32[16,1024]{1,0:T(8,128)}, u32[]{:S(2)}) copy-start(f32[16,1024]{1,0:T(8,128)} %param.24) | copy-start | bytes 196612
  514.1 18.4 %copy-start.30 = (f32[1,2048]{1,0:T(1,128)S(1)}, f32[1,2048]{1,0:T(1,128)}, u32[]{:S(2)}) copy-start(f32[1,2048]{1,0:T(1,128)} %get-tuple-element.56) | copy-start | bytes 24580
  514.1 19.0 %copy-start.29 = (f32[1,2048]{1,0:T(1,128)S(1)}, f32[1,2048]{1,0:T(1,128)}, u32[]{:S(2)}) copy-start(f32[1,2048]{1,0:T(1,128)} %get-tuple-element.57) | copy-start | bytes 24580
  514.1 19.6 %copy-start.33 = (f32[1,512]{1,0:T(1,128)S(1)}, f32[1,512]{1,0:T(1,128)}, u32[]{:S(2)}) copy-start(f32[1,512]{1,0:T(1,128)} %get-tuple-element.58) | copy-start | bytes 6148
  514.1 20.2 %copy-start.25 = (f32[16,2048]{1,0:T(8,128)S(1)}, f32[16,2048]{1,0:T(8,128)}, u32[]{:S(2)}) copy-start(f32[16,2048]{1,0:T(8,128)} %get-tuple-element.59) | copy-start | bytes 393220
  514.1 20.9 %copy-start.27 = (f32[16,1024]{1,0:T(8,128)S(1)}, f32[16,1024]{1,0:T(8,128)}, u32[]{:S(2)}) copy-start(f32[16,1024]{1,0:T(8,128)} %get-tuple-element.96) | copy-start | bytes 196612
  514.1 21.5 %copy-start.31 = (f32[1,1024]{1,0:T(1,128)S(1)}, f32[1,1024]{1,0:T(1,128)}, u32[]{:S(2)}) copy-start(f32[1,1024]{1,0:T(1,128)} %get-tuple-element.61) | copy-start | bytes 12292
  (5 other events, 4.2 us)
Sparse Core Ops, SparseCore 0:
  11.0 166.8 all-gather.1
  303.4 180.0 reduce-scatter.1

commit v10 on v9

--- a/solution.py
+++ b/solution.py
@@ -85,44 +85,56 @@
 class Line:
     def __init__(self, own, all_rows, send, recv):
         self.own, self.all, self.send, self.recv = own, all_rows, send, recv
-        self.z, self.count, self.rows = lax.axis_index("head"), lax.axis_size("head"), own.shape[0]
-        z, count = self.z, self.count
-        self.right = push(own, self.at(z), send.at[0], recv.at[z], lax.rem(z + 1, count))
-        self.left = push(own, self.at(z), send.at[1], recv.at[z], lax.rem(z + count - 1, count))
-
-    def chunk(self, b):
-        return pl.ds(pl.multiple_of(b * self.rows, self.rows), self.rows)
+        self.z, self.count = lax.axis_index("head"), lax.axis_size("head")
+        self.rows, self.parts = own.shape[0], recv.shape[1]
+        self.deep = self.rows // self.parts
 
     def at(self, b):
-        return self.all.at[self.chunk(b)]
+        return self.all.at[pl.ds(pl.multiple_of(b * self.rows, self.rows), self.rows)]
+
+    def part(self, b, p):
+        start = b * self.rows + p * self.deep
+        return self.all.at[pl.ds(pl.multiple_of(start, self.deep), self.deep)]
+
+    def first(self, way, p):
+        to = lax.rem(self.z + (1 if way == 0 else self.count - 1), self.count)
+        src = self.own.at[pl.ds(p * self.deep, self.deep)]
+        return push(
+            src, self.part(self.z, p), self.send.at[way, p], self.recv.at[self.z, p], to
+        )
+
+    def each_first(self, act):
+        for p in range(self.parts):
+            pl.when(self.z < self.count - 1)(lambda p=p: act(self.first(0, p)))
+            pl.when(self.z > 0)(lambda p=p: act(self.first(1, p)))
 
     def start(self):
-        pl.when(self.z < self.count - 1)(self.right.start)
-        pl.when(self.z > 0)(self.left.start)
-
-    def passing(self, i, b):
+        self.each_first(lambda copy: copy.start())
+
+    def passing(self, i, b, p):
         z, count = self.z, self.count
         to = jnp.where(b < z, z + 1, z - 1)
         going = ((b < z) & (z < count - 1)) | ((b > z) & (z > 0))
         copy = push(
-            self.at(b), self.at(b), self.send.at[i + 1], self.recv.at[b], lax.rem(to + count, count)
+            self.part(b, p), self.part(b, p), self.send.at[i + 1, p], self.recv.at[b, p],
+            lax.rem(to + count, count),
         )
         return copy, going
 
-    def receive(self, i, b):
-        copy, going = self.passing(i, b)
+    def receive(self, i, b, p=0):
+        copy, going = self.passing(i, b, p)
         copy.wait_recv()
         pl.when(going)(copy.start)
 
     def finish(self):
         def sent(i, _):
-            copy, going = self.passing(i, near_order(self.z, self.count, i))
-            pl.when(going)(copy.wait_send)
+            for p in range(self.parts):
+                copy, going = self.passing(i, near_order(self.z, self.count, i), p)
+                pl.when(going)(copy.wait_send)
             return 0
 
         lax.fori_loop(1, self.count, sent, 0)
-        pl.when(self.z < self.count - 1)(self.right.wait_send)
-        pl.when(self.z > 0)(self.left.wait_send)
+        self.each_first(lambda copy: copy.wait_send())
 
 
 class LineSum:
@@ -369,7 +381,7 @@
         in_specs=[vmem, vmem, anywhere],
         out_specs=(vmem, anywhere),
         scratch_shapes=[
-            pltpu.VMEM((count * rows, width), BF16), dma(()), dma((count + 1,)), dma((count,)),
+            pltpu.VMEM((count * rows, width), BF16), dma(()), dma((count + 1, 1)), dma((count, 1)),
             dma(()), dma((seq // 2,)), dma((seq // 2,)), dma((seq,)),
         ],
         compiler_params=pltpu.CompilerParams(
@@ -606,7 +618,7 @@
             pltpu.VMEM((micro, half + tail, dk), BF16), pltpu.VMEM((micro, half + tail, dk), BF16),
             pltpu.VMEM((micro, half, dk), BF16), pltpu.VMEM((micro, half, dk), BF16),
             pltpu.VMEM((micro, half, dk), F32),
-            dma(()), dma((head + 1,)), dma((head,)), dma((pairs,)), dma((pairs,)), dma((pairs,)),
+            dma(()), dma((head + 1, 1)), dma((head, 1)), dma((pairs,)), dma((pairs,)), dma((pairs,)),
             dma((pairs,)), dma((head,)), dma((head,)), dma((blocks,)), dma((4,)),
         ],
         compiler_params=pltpu.CompilerParams(
@@ -645,12 +657,16 @@
 
     total = LineSum(parts, landed, p_sem, q_sem, rows)
 
-    def step(i, _):
+    halves = x_sem.shape[1]
+    deep = rows // halves
+    each = total.pieces // halves
+
+    def step(t, _):
+        i, half = t // halves, lax.rem(t, halves)
         b = near_order(z, count, i)
-
-        pl.when(i > 0)(lambda: line.receive(i, b))
-
-        at = chunk(b)
+        pl.when(i > 0)(lambda: line.receive(i, b, half))
+        start = b * rows + half * deep
+        at = pl.ds(pl.multiple_of(start, deep), deep)
         x = xs[at, :]
         lin[0] = jnp.dot(x, wv[:, :hidden], preferred_element_type=F32)
         lin[1] = jnp.dot(x, wv[:, hidden : 2 * hidden], preferred_element_type=F32)
@@ -659,7 +675,7 @@
 
         def act_rows(r, _):
             here = pl.ds(pl.multiple_of(r * band, band), band)
-            there = pl.ds(pl.multiple_of(b * rows + r * band, band), band)
+            there = pl.ds(pl.multiple_of(start + r * band, band), band)
             gate, up, g_product = lin[0, here, :], lin[1, here, :], lin[2, here, :]
             sig = sigmoid(gate)
             gated = gate * sig
@@ -668,17 +684,17 @@
             act[there, 2 * hidden :] = (gated * up).astype(BF16)
             return 0
 
-        lax.fori_loop(0, rows // band, act_rows, 0)
+        lax.fori_loop(0, deep // band, act_rows, 0)
         parts[at, :] = mm(act[at, : 2 * hidden], wv[:, : 2 * hidden], (1, 1), None).astype(BF16)
 
         @pl.when((i > 0) & jnp.logical_not(total.inner))
         def _():
-            for p in range(total.pieces):
-                total.onward(b, p).start()
+            for p in range(each):
+                total.onward(b, half * each + p).start()
 
         return 0
 
-    lax.fori_loop(0, count, step, 0)
+    lax.fori_loop(0, count * halves, step, 0)
 
     high = tiles.shape[1]
     steps = width // high
@@ -747,13 +763,13 @@
             pltpu.VMEM((group, width), BF16),
             pltpu.VMEM((group, width), BF16),
             pltpu.VMEM((group, 3 * hidden), BF16),
-            pltpu.VMEM((3, rows, hidden), F32),
+            pltpu.VMEM((3, rows // 2, hidden), F32),
             pltpu.VMEM((group, width), BF16),
             pltpu.VMEM((group + rows, width), BF16),
             pltpu.VMEM((width, group), BF16),
             pltpu.VMEM((width, group), BF16),
             pltpu.VMEM((2, width // 4, hidden), BF16),
-            dma((3,)), dma((2,)), dma((count + 1,)), dma((count,)),
+            dma((3,)), dma((2,)), dma((count + 1, 2)), dma((count, 2)),
             dma((count, 4)), dma((count + 1, 4)), dma((2,)),
         ],
         compiler_params=pltpu.CompilerParams(
@@ -831,6 +847,9 @@
         return 0
 
     lax.fori_loop(0, head, gates, 0)
+    loads[0].wait()
+    total = LineSum(parts, landed, p_sem, q_sem, f_out.shape[0])
+    total.send_all()
     half = dv // 2
     side = lax.rem(lax.axis_index("seq"), 2)
     own_half = pl.ds(pl.multiple_of(side * half, half), half)
@@ -848,10 +867,7 @@
             sending[i, m] = pair[i * part : (i + 1) * part, :].astype(BF16)
     begin, end, drain = swap_slices(sending, got, s_send, s_recv)
     begin()
-    for load in loads:
-        load.wait()
-    total = LineSum(parts, landed, p_sem, q_sem, f_out.shape[0])
-    total.send_all()
+    loads[1].wait()
 
     def inside(b, _):
         for m in range(micro):

time: 552 us -> 548 us (level)
    pallas_call x1, Pallas kernels: 103 us -> 109 us  [feed_forward(): pl.pallas_call(functools.partial(ffn_kernel, count), out_shape=(jax.Shape...]
  transfers between devices with their start and end apart: 3 -> 3, of which waited for: 1 -> 2; matrix products, arithmetic and copies ran while one was open for 6% -> 6% of each run, Pallas kernels for 62% -> 61%
where the time goes in v10:
time: 548 us; the launch traced here: 540 us
  Pallas kernels  442 us (81%)
  matrix products  22.2 us (4%)
  local copies, waits for them, and re-layouts  21.5 us (4%)
  other arithmetic  19.4 us (4%)
  between operations  14.9 us (3%)
  waiting for transfers between devices  14.6 us (3%)
    pallas_call x1, Pallas kernels, feed_forward(): pl.pallas_call(functools.partial(ffn_kernel, count), out_shape=(jax.Shape...  109 us
    pallas_call x1, Pallas kernels, finish(): pl.pallas_call(finish_kernel, out_shape=(jax.ShapeDtypeStruct((rows, widt...  102 us
    pallas_call x1, Pallas kernels, attention_forward(): pl.pallas_call(front_kernel, out_shape=(jax.ShapeDtypeStruct((blocks, mic...  84.3 us
    pallas_call x1, Pallas kernels, attention_back(): pl.pallas_call(back_kernel, out_shape=(jax.ShapeDtypeStruct((blocks, micr...  71.7 us
    pallas_call x1, Pallas kernels, gather_norm(): pl.pallas_call(gather_norm_kernel, out_shape=(jax.ShapeDtypeStruct((count...  69.2 us
    dot_general x6, matrix products, dot(): lax.dot_general(a, b, (((contract[0],), (contract[1],)), ((), ())), preci...  22.2 us
    all_to_all x1, waiting for transfers between devices, on_device(): lax.all_to_all(grads[:, :vals].reshape(heads, slab, vals), 'head', split_...  14.3 us
    unnamed x76, local copies, waits for them, and re-layouts  12.4 us
  transfers between devices with their start and end apart: 3, of which 2 were waited for; matrix products, arithmetic and copies ran while one was open for 6% of the time, Pallas kernels for 61%

profile of v10, /device:TPU:0, one launch (start us, length us, event | category | flops | bytes accessed | tf_op | source)
XLA Modules:
  0.0 539.7 jit_solution(12906775925014111798)
XLA Ops:
  7.3 1.6 copy.29
  9.1 1.8 pad_maximum_fusion
  12.4 1.1 constant_dynamic-slice_fusion.4
  13.5 1.1 constant_dynamic-slice_fusion.2
  14.7 69.2 %gather_norm.1 = (bf16[768,2048]{1,0:T(8,128)(2,1)S(1)}, bf16[2048,1536]{1,0:T(8,128)(2,1)S(1)}) custom-call(bf16[192,2048]{1,0:T(8,128)(2,1)S(1)} %bitcast.43, f32[1,2048]{1,0:T(1,128)S(1)} %bitcast.48, bf16[256,1536]{1,0:T(8,128)(2,1)S(1)} %pad_maximum_fusion.1.shard), custom_call_target="tpu_custom_call" | custom-call | bytes 150000000 | tf_op jit(solution)/shard_map/gather_norm/pallas_call | solution.py:375
  84.8 2.7 fusion.19
  87.5 1.8 fusion.12
  89.4 3.4 fusion.14
  92.9 84.3 %attention_forward.1 = (f32[4,3,64,512]{3,2,1,0:T(8,128)S(1)}, bf16[192,2048]{1,0:T(8,128)(2,1)S(1)}, bf16[4,3,16,256]{3,2,1,0:T(8,128)(2,1)S(1)}, bf16[2,3,16,2...) custom-call(f32[4,3,1,256]{3,2,1,0:T(1,128)S(1)} %broadcast_in_dim.2.keep, ...), custom_call_target="tpu_custom_call" | custom-call | bytes 270000000 | tf_op jit(solution)/shard_map/attention_forward/pallas_call | solution.py:601
  177.3 1.2 copy-done.7
  178.4 1.7 copy-done.8
  180.1 1.1 copy-done.11
  182.5 6.4 %multiply_reduce_fusion.2 = (f32[192]{0:T(256)S(1)}, f32[192,2048]{1,0:T(8,128)S(1)}) fusion(bf16[192,2048]{1,0:T(8,128)(2,1)S(1)} %get-tuple-element.39.right, bf16[2048,6272]{1,0:T(8,128)(2,1)} %all-gather.2.cloned.1.call-done.w, bf16[192,2048]{1,0:T(8,128)(2,1)S(1)} %bitcast.44), kind=kOutput, calls=%fused_computation.19 | convolution fusion | flops 1612185344 | bytes 11535104 | tf_op jit(solution)/shard_map/dot_general | solution.py:1294
  188.9 1.3 multiply_convert_fusion.x_own
  190.2 109.1 %feed_forward.1 = (f32[192,2048]{1,0:T(8,128)}, bf16[4,192,2048]{2,1,0:T(8,128)(2,1)}, bf16[2048,6272]{1,0:T(8,128)(2,1)}) custom-call(bf16[192,2048]{1,0:T(8,128)(2,1)} %multiply_convert_fusion.x_own, bf16[768,2048]{1,0:T(8,128)(2,1)} %copy-done.8, bf16[2048,6272]{1,0:T(8,128)(2,1)} %all-gather.2.cloned.1.call-done.w), custom_call_target="tpu_custom_call" | custom-call | bytes 300000000 | tf_op jit(solution)/shard_map/feed_forward/pallas_call | solution.py:752
  299.4 2.6 multiply_reduce_fusion
  302.0 1.9 fusion.21.left
  303.9 5.2 weight_grad.1
  309.2 0.9 copy.27.ranked
  310.1 1.0 copy.28.rank_down
  311.1 7.0 %fusion.9.gated_own = bf16[192,2048]{1,0:T(8,128)(2,1)} fusion(bf16[192,2048]{1,0:T(8,128)(2,1)S(1)} %fusion.21.left, bf16[2048,6272]{1,0:T(8,128)(2,1)} %all-gather.2.cloned.1.call-done.w), kind=kOutput, calls=%fused_computation.8 | convolution fusion | flops 1611005952 | bytes 9961472 | tf_op jit(solution)/shard_map/dot_general | solution.py:1294
  318.1 71.7 %attention_back.1 = (bf16[4,3,64,1536]{3,2,1,0:T(8,128)(2,1)}, f32[4,3,64,256]{3,2,1,0:T(8,128)}, f32[8,512]{1,0:T(8,128)}, f32[192,2048]{1,0:T(8,128)}) custom-call(f32[4,3,1,256]{3,2,1,0:T(1,128)} %copy-done.13, bf16[192,2048]{1,0:T(8,128)(2,1)} %fusion.9.gated_own, f32[4,3,64,512]{3,2,1,0:T(8,128)} %bitcast.39, f32[4,3,64,512]{3,2,1,0:T(8,128)} %copy-done.11, ...), custom_call_target="tpu_custom_call" | custom-call | bytes 240000000 | tf_op jit(solution)/shard_map/attention_back/pallas_call | solution.py:970
  389.7 102.2 %finish.1 = (f32[192,2048]{1,0:T(8,128)}, bf16[64,6144]{1,0:T(8,128)(2,1)}, f32[1,2048]{1,0:T(1,128)}, f32[1,2048]{1,0:T(1,128)}, f32[1,512]{1,0:T(1,128)}, /*in...) custom-call(bf16[768,2048]{1,0:T(8,128)(2,1)} %copy-done.2, bf16[768,1536]{1,0:T(8,128)(2,1)} %bitcast.53, ...), custom_call_target="tpu_custom_call" | custom-call | bytes 285000000 | tf_op jit(solution)/shard_map/finish/pallas_call | solution.py:1210
  492.2 2.3 slice.24
  494.5 5.4 all-to-all-start
  499.8 4.4 fusion.20
  504.2 1.2 convert_element_type.45
  505.4 1.5 slice_convert_fusion
  507.0 2.8 reshape.146
  509.8 2.4 slice_convert_fusion.1
  512.2 14.3 %all-to-all-done = bf16[4,64,2048]{2,1,0:T(8,128)(2,1)} async-done(((bf16[4,64,2048]{2,1,0:T(8,128)(2,1)}), bf16[4,64,2048]{2,1,0:T(8,128)(2,1)}, u32[]{:S(2)}, u32[]{:S(2)}) %all-to-all-start) | async-done | bytes 1048608 | tf_op jit(solution)/shard_map/all_to_all | solution.py:1390
  526.5 2.2 convert_reduce_fusion
  (86 shorter events, 8.1 us)
Async XLA Ops:
  7.2 76.6 %copy-start = (f32[16,1024]{1,0:T(8,128)S(1)}, f32[16,1024]{1,0:T(8,128)}, u32[]{:S(2)}) copy-start(f32[16,1024]{1,0:T(8,128)} %param.24) | copy-start | bytes 196612
  7.2 1.7 copy-start.21
  7.2 1.9 copy-start.23
  7.2 175.3 %all-gather.2.cloned.1.call-start = ((), (), s32[]{:S(2)}) async-start(), calls=%async_computation.2 | async-start | bytes 28901376 | tf_op jit(solution)/shard_map/all_gather | solution.py:1286
  10.9 481.2 %reduce-scatter.2.cloned.1.call-start = ((), (), s32[]{:S(2)}) async-start(), calls=%async_computation.3 | async-start | bytes 28901376 | tf_op jit(solution)/shard_map/reduce_scatter | solution.py:1290
  12.4 2.2 copy-start.9
  12.4 2.2 copy-start.16
  14.6 69.3 %copy-start.24 = (bf16[2048,16]{0,1:T(8,128)(2,1)S(1)}, bf16[2048,16]{0,1:T(8,128)(2,1)}, u32[]{:S(2)}) copy-start(bf16[2048,16]{0,1:T(8,128)(2,1)} %param.23) | copy-start | bytes 196612
  83.8 5.5 %copy-start.2 = (bf16[768,2048]{1,0:T(8,128)(2,1)}, bf16[768,2048]{1,0:T(8,128)(2,1)S(1)}, u32[]{:S(2)}) copy-start(bf16[768,2048]{1,0:T(8,128)(2,1)S(1)} %get-tuple-element.37.xn_in) | copy-start | bytes 9437188
  83.8 5.5 %copy-start.5 = (bf16[2048,1536]{1,0:T(8,128)(2,1)}, bf16[2048,1536]{1,0:T(8,128)(2,1)S(1)}, u32[]{:S(2)}) copy-start(bf16[2048,1536]{1,0:T(8,128)(2,1)S(1)} %get-tuple-element.38.w_in) | copy-start | bytes 18874372
  83.9 5.5 %copy-start.28 = (f32[16,256]{1,0:T(8,128)}, f32[16,256]{1,0:T(8,128)S(1)}, u32[]{:S(2)}) copy-start(f32[16,256]{1,0:T(8,128)S(1)} %constant_dynamic-slice_fusion.up_own) | copy-start | bytes 49156
  87.5 5.3 copy-start.12
  89.3 3.5 copy-start.6
  89.3 3.5 copy-start.3
  89.4 3.5 copy-start.17
  92.9 84.4 %copy-start.13 = (f32[4,3,1,256]{3,2,1,0:T(1,128)}, f32[4,3,1,256]{3,2,1,0:T(1,128)S(1)}, u32[]{:S(2)}) copy-start(f32[4,3,1,256]{3,2,1,0:T(1,128)S(1)} %broadcast_in_dim.2.keep) | copy-start | bytes 36868
  92.9 89.6 %copy-start.10 = (bf16[3,64,2048]{2,1,0:T(8,128)(2,1)S(1)}, bf16[3,64,2048]{2,1,0:T(8,128)(2,1)}, u32[]{:S(2)}) copy-start(bf16[3,64,2048]{2,1,0:T(8,128)(2,1)} %param.13) | copy-start | bytes 2359300
  178.4 1.7 copy-start.8
  182.5 6.5 %copy-start.26 = (f32[2048]{0:T(1024)S(1)}, f32[2048]{0:T(1024)}, u32[]{:S(2)}) copy-start(f32[2048]{0:T(1024)} %param.21) | copy-start | bytes 24580
  188.9 110.4 %copy-start.18 = (f32[192,2048]{1,0:T(8,128)}, f32[192,2048]{1,0:T(8,128)S(1)}, u32[]{:S(2)}) copy-start(f32[192,2048]{1,0:T(8,128)S(1)} %get-tuple-element.73) | copy-start | bytes 4718596
  299.3 2.7 copy-start.4
  299.3 2.7 copy-start.20
  494.5 5.4 copy-start.19
  494.5 32.1 %all-to-all-start = ((bf16[4,64,2048]{2,1,0:T(8,128)(2,1)}), bf16[4,64,2048]{2,1,0:T(8,128)(2,1)}, u32[]{:S(2)}, u32[]{:S(2)}) async-start(bf16[4,64,2048]{2,1,0:T(8,128)(2,1)} %bitcast.15), calls=%async_computation.1 | async-start | bytes 2097152 | tf_op jit(solution)/shard_map/all_to_all | solution.py:1390
  499.8 4.4 copy-start.22
  507.0 25.4 %copy-start.1 = (f32[16,1024]{1,0:T(8,128)S(1)}, f32[16,1024]{1,0:T(8,128)}, u32[]{:S(2)}) copy-start(f32[16,1024]{1,0:T(8,128)} %param.24) | copy-start | bytes 196612
  509.8 19.0 %copy-start.30 = (f32[1,2048]{1,0:T(1,128)S(1)}, f32[1,2048]{1,0:T(1,128)}, u32[]{:S(2)}) copy-start(f32[1,2048]{1,0:T(1,128)} %get-tuple-element.56) | copy-start | bytes 24580
  509.8 19.6 %copy-start.29 = (f32[1,2048]{1,0:T(1,128)S(1)}, f32[1,2048]{1,0:T(1,128)}, u32[]{:S(2)}) copy-start(f32[1,2048]{1,0:T(1,128)} %get-tuple-element.57) | copy-start | bytes 24580
  509.8 20.2 %copy-start.33 = (f32[1,512]{1,0:T(1,128)S(1)}, f32[1,512]{1,0:T(1,128)}, u32[]{:S(2)}) copy-start(f32[1,512]{1,0:T(1,128)} %get-tuple-element.58) | copy-start | bytes 6148
  509.8 20.7 %copy-start.25 = (f32[16,2048]{1,0:T(8,128)S(1)}, f32[16,2048]{1,0:T(8,128)}, u32[]{:S(2)}) copy-start(f32[16,2048]{1,0:T(8,128)} %get-tuple-element.59) | copy-start | bytes 393220
  509.8 21.4 %copy-start.27 = (f32[16,1024]{1,0:T(8,128)S(1)}, f32[16,1024]{1,0:T(8,128)}, u32[]{:S(2)}) copy-start(f32[16,1024]{1,0:T(8,128)} %get-tuple-element.96) | copy-start | bytes 196612
  509.8 22.0 %copy-start.31 = (f32[1,1024]{1,0:T(1,128)S(1)}, f32[1,1024]{1,0:T(1,128)}, u32[]{:S(2)}) copy-start(f32[1,1024]{1,0:T(1,128)} %get-tuple-element.61) | copy-start | bytes 12292
  (5 other events, 4.2 us)
Sparse Core Ops, SparseCore 0:
  11.0 166.8 all-gather.1
  309.3 182.8 reduce-scatter.1

commit v11 on v10

--- a/solution.py
+++ b/solution.py
@@ -763,13 +763,13 @@
             pltpu.VMEM((group, width), BF16),
             pltpu.VMEM((group, width), BF16),
             pltpu.VMEM((group, 3 * hidden), BF16),
-            pltpu.VMEM((3, rows // 2, hidden), F32),
+            pltpu.VMEM((3, rows, hidden), F32),
             pltpu.VMEM((group, width), BF16),
             pltpu.VMEM((group + rows, width), BF16),
             pltpu.VMEM((width, group), BF16),
             pltpu.VMEM((width, group), BF16),
             pltpu.VMEM((2, width // 4, hidden), BF16),
-            dma((3,)), dma((2,)), dma((count + 1, 2)), dma((count, 2)),
+            dma((3,)), dma((2,)), dma((count + 1, 1)), dma((count, 1)),
             dma((count, 4)), dma((count + 1, 4)), dma((2,)),
         ],
         compiler_params=pltpu.CompilerParams(

time: 548 us -> 542 us (0.989)
  Pallas kernels: 442 us -> 436 us
    pallas_call x1, Pallas kernels: 109 us -> 103 us  [feed_forward(): pl.pallas_call(functools.partial(ffn_kernel, count), out_shape=(jax.Shape...]
  transfers between devices with their start and end apart: 3 -> 3, of which waited for: 2 -> 1; matrix products, arithmetic and copies ran while one was open for 6% -> 6% of each run, Pallas kernels for 61% -> 61%
where the time goes in v11:
time: 542 us; the launch traced here: 533 us
  Pallas kernels  436 us (80%)
  matrix products  22.8 us (4%)
  local copies, waits for them, and re-layouts  21.5 us (4%)
  other arithmetic  19.4 us (4%)
  between operations  14.9 us (3%)
  waiting for transfers between devices  14.1 us (3%)
    pallas_call x1, Pallas kernels, feed_forward(): pl.pallas_call(functools.partial(ffn_kernel, count), out_shape=(jax.Shape...  103 us
    pallas_call x1, Pallas kernels, finish(): pl.pallas_call(finish_kernel, out_shape=(jax.ShapeDtypeStruct((rows, widt...  102 us
    pallas_call x1, Pallas kernels, attention_forward(): pl.pallas_call(front_kernel, out_shape=(jax.ShapeDtypeStruct((blocks, mic...  84.3 us
    pallas_call x1, Pallas kernels, attention_back(): pl.pallas_call(back_kernel, out_shape=(jax.ShapeDtypeStruct((blocks, micr...  72.2 us
    pallas_call x1, Pallas kernels, gather_norm(): pl.pallas_call(gather_norm_kernel, out_shape=(jax.ShapeDtypeStruct((count...  69.2 us
    dot_general x6, matrix products, dot(): lax.dot_general(a, b, (((contract[0],), (contract[1],)), ((), ())), preci...  22.8 us
    all_to_all x1, waiting for transfers between devices, on_device(): lax.all_to_all(grads[:, :vals].reshape(heads, slab, vals), 'head', split_...  14 us
    unnamed x76, local copies, waits for them, and re-layouts  12.4 us
  transfers between devices with their start and end apart: 3, of which 1 were waited for; matrix products, arithmetic and copies ran while one was open for 6% of the time, Pallas kernels for 61%

profile of v11, /device:TPU:0, one launch (start us, length us, event | category | flops | bytes accessed | tf_op | source)
XLA Modules:
  0.0 533.5 jit_solution(12355573719719677411)
XLA Ops:
  7.3 1.6 copy.29
  9.1 1.8 pad_maximum_fusion
  12.4 1.1 constant_dynamic-slice_fusion.4
  13.5 1.1 constant_dynamic-slice_fusion.2
  14.7 69.2 %gather_norm.1 = (bf16[768,2048]{1,0:T(8,128)(2,1)S(1)}, bf16[2048,1536]{1,0:T(8,128)(2,1)S(1)}) custom-call(bf16[192,2048]{1,0:T(8,128)(2,1)S(1)} %bitcast.43, f32[1,2048]{1,0:T(1,128)S(1)} %bitcast.48, bf16[256,1536]{1,0:T(8,128)(2,1)S(1)} %pad_maximum_fusion.1.shard), custom_call_target="tpu_custom_call" | custom-call | bytes 150000000 | tf_op jit(solution)/shard_map/gather_norm/pallas_call | solution.py:375
  84.8 2.7 fusion.19
  87.5 1.8 fusion.12
  89.4 3.4 fusion.14
  92.9 84.3 %attention_forward.1 = (f32[4,3,64,512]{3,2,1,0:T(8,128)S(1)}, bf16[192,2048]{1,0:T(8,128)(2,1)S(1)}, bf16[4,3,16,256]{3,2,1,0:T(8,128)(2,1)S(1)}, bf16[2,3,16,2...) custom-call(f32[4,3,1,256]{3,2,1,0:T(1,128)S(1)} %broadcast_in_dim.2.keep, ...), custom_call_target="tpu_custom_call" | custom-call | bytes 270000000 | tf_op jit(solution)/shard_map/attention_forward/pallas_call | solution.py:601
  177.3 1.2 copy-done.7
  178.4 1.7 copy-done.8
  180.1 1.1 copy-done.11
  182.5 6.4 %multiply_reduce_fusion.2 = (f32[192]{0:T(256)S(1)}, f32[192,2048]{1,0:T(8,128)S(1)}) fusion(bf16[192,2048]{1,0:T(8,128)(2,1)S(1)} %get-tuple-element.39.right, bf16[2048,6272]{1,0:T(8,128)(2,1)} %all-gather.2.cloned.1.call-done.w, bf16[192,2048]{1,0:T(8,128)(2,1)S(1)} %bitcast.44), kind=kOutput, calls=%fused_computation.19 | convolution fusion | flops 1612185344 | bytes 11535104 | tf_op jit(solution)/shard_map/dot_general | solution.py:1294
  188.9 1.3 multiply_convert_fusion.x_own
  190.2 103.3 %feed_forward.1 = (f32[192,2048]{1,0:T(8,128)}, bf16[4,192,2048]{2,1,0:T(8,128)(2,1)}, bf16[2048,6272]{1,0:T(8,128)(2,1)}) custom-call(bf16[192,2048]{1,0:T(8,128)(2,1)} %multiply_convert_fusion.x_own, bf16[768,2048]{1,0:T(8,128)(2,1)} %copy-done.8, bf16[2048,6272]{1,0:T(8,128)(2,1)} %all-gather.2.cloned.1.call-done.w), custom_call_target="tpu_custom_call" | custom-call | bytes 300000000 | tf_op jit(solution)/shard_map/feed_forward/pallas_call | solution.py:752
  293.5 2.6 multiply_reduce_fusion
  296.1 1.9 fusion.21.left
  298.1 5.2 weight_grad.1
  303.3 0.9 copy.27.ranked
  304.2 1.0 copy.28.rank_down
  305.2 7.6 %fusion.9.gated_own = bf16[192,2048]{1,0:T(8,128)(2,1)} fusion(bf16[192,2048]{1,0:T(8,128)(2,1)S(1)} %fusion.21.left, bf16[2048,6272]{1,0:T(8,128)(2,1)} %all-gather.2.cloned.1.call-done.w), kind=kOutput, calls=%fused_computation.8 | convolution fusion | flops 1611005952 | bytes 9961472 | tf_op jit(solution)/shard_map/dot_general | solution.py:1294
  312.8 72.2 %attention_back.1 = (bf16[4,3,64,1536]{3,2,1,0:T(8,128)(2,1)}, f32[4,3,64,256]{3,2,1,0:T(8,128)}, f32[8,512]{1,0:T(8,128)}, f32[192,2048]{1,0:T(8,128)}) custom-call(f32[4,3,1,256]{3,2,1,0:T(1,128)} %copy-done.13, bf16[192,2048]{1,0:T(8,128)(2,1)} %fusion.9.gated_own, f32[4,3,64,512]{3,2,1,0:T(8,128)} %bitcast.39, f32[4,3,64,512]{3,2,1,0:T(8,128)} %copy-done.11, ...), custom_call_target="tpu_custom_call" | custom-call | bytes 240000000 | tf_op jit(solution)/shard_map/attention_back/pallas_call | solution.py:970
  385.1 102.1 %finish.1 = (f32[192,2048]{1,0:T(8,128)}, bf16[64,6144]{1,0:T(8,128)(2,1)}, f32[1,2048]{1,0:T(1,128)}, f32[1,2048]{1,0:T(1,128)}, f32[1,512]{1,0:T(1,128)}, /*in...) custom-call(bf16[768,2048]{1,0:T(8,128)(2,1)} %copy-done.2, bf16[768,1536]{1,0:T(8,128)(2,1)} %bitcast.53, ...), custom_call_target="tpu_custom_call" | custom-call | bytes 285000000 | tf_op jit(solution)/shard_map/finish/pallas_call | solution.py:1210
  487.2 2.3 slice.24
  489.5 4.4 all-to-all-start
  493.9 4.4 fusion.20
  498.3 1.2 convert_element_type.45
  499.5 1.5 slice_convert_fusion
  501.1 2.8 reshape.146
  503.9 2.4 slice_convert_fusion.1
  506.3 14.0 %all-to-all-done = bf16[4,64,2048]{2,1,0:T(8,128)(2,1)} async-done(((bf16[4,64,2048]{2,1,0:T(8,128)(2,1)}), bf16[4,64,2048]{2,1,0:T(8,128)(2,1)}, u32[]{:S(2)}, u32[]{:S(2)}) %all-to-all-start) | async-done | bytes 1048608 | tf_op jit(solution)/shard_map/all_to_all | solution.py:1390
  520.3 2.2 convert_reduce_fusion
  (86 shorter events, 7.9 us)
Async XLA Ops:
  7.2 76.6 %copy-start = (f32[16,1024]{1,0:T(8,128)S(1)}, f32[16,1024]{1,0:T(8,128)}, u32[]{:S(2)}) copy-start(f32[16,1024]{1,0:T(8,128)} %param.24) | copy-start | bytes 196612
  7.2 1.7 copy-start.21
  7.2 1.9 copy-start.23
  7.2 175.3 %all-gather.2.cloned.1.call-start = ((), (), s32[]{:S(2)}) async-start(), calls=%async_computation.2 | async-start | bytes 28901376 | tf_op jit(solution)/shard_map/all_gather | solution.py:1286
  10.9 476.3 %reduce-scatter.2.cloned.1.call-start = ((), (), s32[]{:S(2)}) async-start(), calls=%async_computation.3 | async-start | bytes 28901376 | tf_op jit(solution)/shard_map/reduce_scatter | solution.py:1290
  12.4 2.2 copy-start.9
  12.4 2.2 copy-start.16
  14.6 69.3 %copy-start.24 = (bf16[2048,16]{0,1:T(8,128)(2,1)S(1)}, bf16[2048,16]{0,1:T(8,128)(2,1)}, u32[]{:S(2)}) copy-start(bf16[2048,16]{0,1:T(8,128)(2,1)} %param.23) | copy-start | bytes 196612
  83.8 5.5 %copy-start.2 = (bf16[768,2048]{1,0:T(8,128)(2,1)}, bf16[768,2048]{1,0:T(8,128)(2,1)S(1)}, u32[]{:S(2)}) copy-start(bf16[768,2048]{1,0:T(8,128)(2,1)S(1)} %get-tuple-element.37.xn_in) | copy-start | bytes 9437188
  83.8 5.5 %copy-start.5 = (bf16[2048,1536]{1,0:T(8,128)(2,1)}, bf16[2048,1536]{1,0:T(8,128)(2,1)S(1)}, u32[]{:S(2)}) copy-start(bf16[2048,1536]{1,0:T(8,128)(2,1)S(1)} %get-tuple-element.38.w_in) | copy-start | bytes 18874372
  83.9 5.5 %copy-start.28 = (f32[16,256]{1,0:T(8,128)}, f32[16,256]{1,0:T(8,128)S(1)}, u32[]{:S(2)}) copy-start(f32[16,256]{1,0:T(8,128)S(1)} %constant_dynamic-slice_fusion.up_own) | copy-start | bytes 49156
  87.5 5.3 %copy-start.12 = (bf16[768,256]{1,0:T(8,128)(2,1)}, bf16[768,256]{1,0:T(8,128)(2,1)S(1)}, u32[]{:S(2)}) copy-start(bf16[768,256]{1,0:T(8,128)(2,1)S(1)} %get-tuple-element.70) | copy-start | bytes 1179652
  89.3 3.5 copy-start.6
  89.3 3.5 copy-start.3
  89.4 3.5 copy-start.17
  92.9 84.4 %copy-start.13 = (f32[4,3,1,256]{3,2,1,0:T(1,128)}, f32[4,3,1,256]{3,2,1,0:T(1,128)S(1)}, u32[]{:S(2)}) copy-start(f32[4,3,1,256]{3,2,1,0:T(1,128)S(1)} %broadcast_in_dim.2.keep) | copy-start | bytes 36868
  92.9 89.6 %copy-start.10 = (bf16[3,64,2048]{2,1,0:T(8,128)(2,1)S(1)}, bf16[3,64,2048]{2,1,0:T(8,128)(2,1)}, u32[]{:S(2)}) copy-start(bf16[3,64,2048]{2,1,0:T(8,128)(2,1)} %param.13) | copy-start | bytes 2359300
  178.4 1.7 copy-start.8
  182.5 6.5 %copy-start.26 = (f32[2048]{0:T(1024)S(1)}, f32[2048]{0:T(1024)}, u32[]{:S(2)}) copy-start(f32[2048]{0:T(1024)} %param.21) | copy-start | bytes 24580
  188.9 104.6 %copy-start.18 = (f32[192,2048]{1,0:T(8,128)}, f32[192,2048]{1,0:T(8,128)S(1)}, u32[]{:S(2)}) copy-start(f32[192,2048]{1,0:T(8,128)S(1)} %get-tuple-element.73) | copy-start | bytes 4718596
  293.5 2.7 copy-start.4
  293.5 2.7 copy-start.20
  489.5 4.4 copy-start.19
  489.5 30.8 %all-to-all-start = ((bf16[4,64,2048]{2,1,0:T(8,128)(2,1)}), bf16[4,64,2048]{2,1,0:T(8,128)(2,1)}, u32[]{:S(2)}, u32[]{:S(2)}) async-start(bf16[4,64,2048]{2,1,0:T(8,128)(2,1)} %bitcast.15), calls=%async_computation.1 | async-start | bytes 2097152 | tf_op jit(solution)/shard_map/all_to_all | solution.py:1390
  493.9 4.4 copy-start.22
  501.1 25.1 %copy-start.1 = (f32[16,1024]{1,0:T(8,128)S(1)}, f32[16,1024]{1,0:T(8,128)}, u32[]{:S(2)}) copy-start(f32[16,1024]{1,0:T(8,128)} %param.24) | copy-start | bytes 196612
  503.9 18.6 %copy-start.30 = (f32[1,2048]{1,0:T(1,128)S(1)}, f32[1,2048]{1,0:T(1,128)}, u32[]{:S(2)}) copy-start(f32[1,2048]{1,0:T(1,128)} %get-tuple-element.56) | copy-start | bytes 24580
  503.9 19.2 %copy-start.29 = (f32[1,2048]{1,0:T(1,128)S(1)}, f32[1,2048]{1,0:T(1,128)}, u32[]{:S(2)}) copy-start(f32[1,2048]{1,0:T(1,128)} %get-tuple-element.57) | copy-start | bytes 24580
  503.9 19.8 %copy-start.33 = (f32[1,512]{1,0:T(1,128)S(1)}, f32[1,512]{1,0:T(1,128)}, u32[]{:S(2)}) copy-start(f32[1,512]{1,0:T(1,128)} %get-tuple-element.58) | copy-start | bytes 6148
  503.9 20.4 %copy-start.25 = (f32[16,2048]{1,0:T(8,128)S(1)}, f32[16,2048]{1,0:T(8,128)}, u32[]{:S(2)}) copy-start(f32[16,2048]{1,0:T(8,128)} %get-tuple-element.59) | copy-start | bytes 393220
  503.9 21.1 %copy-start.27 = (f32[16,1024]{1,0:T(8,128)S(1)}, f32[16,1024]{1,0:T(8,128)}, u32[]{:S(2)}) copy-start(f32[16,1024]{1,0:T(8,128)} %get-tuple-element.96) | copy-start | bytes 196612
  503.9 21.7 %copy-start.31 = (f32[1,1024]{1,0:T(1,128)S(1)}, f32[1,1024]{1,0:T(1,128)}, u32[]{:S(2)}) copy-start(f32[1,1024]{1,0:T(1,128)} %get-tuple-element.61) | copy-start | bytes 12292
  (5 other events, 4.2 us)
Sparse Core Ops, SparseCore 0:
  11.0 166.8 all-gather.1
  303.4 176.9 reduce-scatter.1

commit v12 on v11

--- a/solution.py
+++ b/solution.py
@@ -622,7 +622,7 @@
             dma((pairs,)), dma((head,)), dma((head,)), dma((blocks,)), dma((4,)),
         ],
         compiler_params=pltpu.CompilerParams(
-            collective_id=2, has_side_effects=True, vmem_limit_bytes=40 << 20
+            collective_id=2, has_side_effects=True, vmem_limit_bytes=60 << 20
         ),
         cost_estimate=cost(90),
         name="attention_forward",
@@ -639,7 +639,9 @@
 
     weights = [
         pltpu.make_async_copy(
-            w.at[:, pl.ds(k * hidden, hidden)], wv.at[:, pl.ds(k * hidden, hidden)], w_sem.at[k]
+            w.at[:, pl.ds(w.shape[1] + (k - 3) * hidden, hidden)],
+            wv.at[:, pl.ds(k * hidden, hidden)],
+            w_sem.at[k],
         )
         for k in range(3)
     ]
@@ -1282,6 +1284,30 @@
     )(left, right, *given)
 
 
+def product_kernel(left, right, out):
+    out[...] = jnp.dot(left[...], right[...], preferred_element_type=F32).astype(BF16)
+
+
+def rows_by_columns(left, right, columns):
+    rows, depth = left.shape
+    tile = 512
+    return pl.pallas_call(
+        product_kernel,
+        out_shape=jax.ShapeDtypeStruct((rows, columns), BF16),
+        grid=(columns // tile,),
+        in_specs=[
+            pl.BlockSpec((rows, depth), lambda j: (0, 0)),
+            pl.BlockSpec((depth, tile), lambda j: (0, j)),
+        ],
+        out_specs=pl.BlockSpec((rows, tile), lambda j: (0, j)),
+        compiler_params=pltpu.CompilerParams(
+            dimension_semantics=("arbitrary",), vmem_limit_bytes=32 << 20
+        ),
+        cost_estimate=cost(5),
+        name="product",
+    )(left, right)
+
+
 def gather_weight(w):
     return lax.all_gather(w, "seq", axis=0, tiled=True)
 
@@ -1334,10 +1360,10 @@
     )
     later = gather_weight(
         jnp.concatenate(
-            [gate_up.reshape(gate_up.shape[0], 2 * hidden_units), down_proj, mix_out], axis=1
+            [mix_out, gate_up.reshape(gate_up.shape[0], 2 * hidden_units), down_proj], axis=1
         )
     )
-    w_out = later[:, 3 * hidden_units :]
+    w_out = later[:, :vals]
     up_own = own_columns(rank_up, 0, dk)
     bias_own = lax.dynamic_slice_in_dim(gate_bias, head * dk, dk, 0)
 
@@ -1372,7 +1398,7 @@
     g_hidden = cotangent.astype(F32).reshape(micro * rows, width) + back_ffn
     g_mixed = g_hidden.astype(BF16)
     grads = scatter_grad(weight_grad(g_mixed, gated, grads, later.shape[1], 0, vals))
-    g_gated = dot(g_mixed, w_out, (1, 0)).astype(BF16)
+    g_gated = rows_by_columns(g_mixed, later, vals)
     g_proj_b, g_logits_b, g_head_gain, ffn_out = attention_back(
         keep, g_gated, og_b, o_b, qkv_b, decays_b, blocks(logits), through, pair_through, gain_row, kept, ffn_part.reshape(group, width),
     )

time: 542 us -> 545 us (level)
  Pallas kernels: 436 us -> 448 us
    pallas_call x0 -> x1, Pallas kernels: none -> 6.85 us  [rows_by_columns(): pl.pallas_call(product_kernel, out_shape=jax.ShapeDtypeStruct((rows, colu...]
    dot_general x6 -> x5, matrix products: 22.8 us -> 17.9 us  [dot(): lax.dot_general(a, b, (((contract[0],), (contract[1],)), ((), ())), preci...]
    unnamed x76 -> x58, local copies, waits for them, and re-layouts: 12.4 us -> 8.7 us
  transfers between devices with their start and end apart: 3 -> 3, of which waited for: 1 -> 1; matrix products, arithmetic and copies ran while one was open for 6% -> 5% of each run, Pallas kernels for 61% -> 63%
where the time goes in v12:
time: 545 us; the launch traced here: 535 us
  Pallas kernels  448 us (82%)
  local copies, waits for them, and re-layouts  18.4 us (3%)
  matrix products  17.9 us (3%)
  other arithmetic  17.6 us (3%)
  between operations  14.8 us (3%)
  waiting for transfers between devices  14.3 us (3%)
    pallas_call x1, Pallas kernels, feed_forward(): pl.pallas_call(functools.partial(ffn_kernel, count), out_shape=(jax.Shape...  104 us
    pallas_call x1, Pallas kernels, finish(): pl.pallas_call(finish_kernel, out_shape=(jax.ShapeDtypeStruct((rows, widt...  103 us
    pallas_call x1, Pallas kernels, attention_forward(): pl.pallas_call(front_kernel, out_shape=(jax.ShapeDtypeStruct((blocks, mic...  88 us
    pallas_call x1, Pallas kernels, attention_back(): pl.pallas_call(back_kernel, out_shape=(jax.ShapeDtypeStruct((blocks, micr...  71.5 us
    pallas_call x1, Pallas kernels, gather_norm(): pl.pallas_call(gather_norm_kernel, out_shape=(jax.ShapeDtypeStruct((count...  69.2 us
    dot_general x5, matrix products, dot(): lax.dot_general(a, b, (((contract[0],), (contract[1],)), ((), ())), preci...  17.9 us
    all_to_all x1, waiting for transfers between devices, on_device(): lax.all_to_all(grads[:, :vals].reshape(heads, slab, vals), 'head', split_...  14.3 us
  transfers between devices with their start and end apart: 3, of which 1 were waited for; matrix products, arithmetic and copies ran while one was open for 5% of the time, Pallas kernels for 63%

profile of v12, /device:TPU:0, one launch (start us, length us, event | category | flops | bytes accessed | tf_op | source)
XLA Modules:
  0.0 535.0 jit_solution(15885496867217427796)
XLA Ops:
  7.3 1.6 copy.29
  9.1 1.8 pad_maximum_fusion
  11.7 0.8 dynamic_slice.23
  12.4 1.1 constant_dynamic-slice_fusion.4
  13.5 1.1 constant_dynamic-slice_fusion.2
  14.6 69.2 %gather_norm.1 = (bf16[768,2048]{1,0:T(8,128)(2,1)S(1)}, bf16[2048,1536]{1,0:T(8,128)(2,1)S(1)}) custom-call(bf16[192,2048]{1,0:T(8,128)(2,1)S(1)} %bitcast.37, f32[1,2048]{1,0:T(1,128)S(1)} %bitcast.40, bf16[256,1536]{1,0:T(8,128)(2,1)S(1)} %pad_maximum_fusion.1.shard), custom_call_target="tpu_custom_call" | custom-call | bytes 150000000 | tf_op jit(solution)/shard_map/gather_norm/pallas_call | solution.py:375
  83.9 0.9 fusion.17
  84.8 2.9 fusion.14
  87.7 2.9 fusion.7
  90.6 4.5 fusion.9
  95.1 0.7 broadcast_in_dim.2.keep
  95.8 88.0 %attention_forward.1 = (f32[4,3,64,512]{3,2,1,0:T(8,128)}, bf16[192,2048]{1,0:T(8,128)(2,1)}, bf16[4,3,16,256]{3,2,1,0:T(8,128)(2,1)}, bf16[2,3,16,256]{3,2,1,0:...) custom-call(f32[4,3,1,256]{3,2,1,0:T(1,128)} %broadcast_in_dim.2.keep, ...), custom_call_target="tpu_custom_call" | custom-call | bytes 270000000 | tf_op jit(solution)/shard_map/attention_forward/pallas_call | solution.py:601
  183.8 6.7 %multiply_reduce_fusion.2 = (f32[192]{0:T(256)S(1)}, f32[192,2048]{1,0:T(8,128)S(1)}) fusion(bf16[192,2048]{1,0:T(8,128)(2,1)} %get-tuple-element.39.right, bf16[2048,6272]{1,0:T(8,128)(2,1)} %all-gather.2.cloned.1.call-done.w.right, bf16[192,2048]{1,0:T(8,128)(2,1)S(1)} %bitcast.38), kind=kOutput, calls=%fused_computation.16 | convolution fusion | flops 1612185344 | bytes 11535104 | tf_op jit(solution)/shard_map/dot_general | solution.py:1320
  190.5 1.1 multiply_convert_fusion.x_own
  191.6 103.7 %feed_forward.1 = (f32[192,2048]{1,0:T(8,128)}, bf16[4,192,2048]{2,1,0:T(8,128)(2,1)}, bf16[2048,6272]{1,0:T(8,128)(2,1)}) custom-call(bf16[192,2048]{1,0:T(8,128)(2,1)} %multiply_convert_fusion.x_own, bf16[768,2048]{1,0:T(8,128)(2,1)} %get-tuple-element.40.c_all, bf16[2048,6272]{1,0:T(8,128)(2,1)} %all-gather.2.cloned.1.call-done.w.right), custom_call_target="tpu_custom_call" | custom-call | bytes 300000000 | tf_op jit(solution)/shard_map/feed_forward/pallas_call | solution.py:754
  295.3 2.6 multiply_reduce_fusion
  299.1 5.1 weight_grad.1
  304.2 0.9 copy.27.ranked
  305.2 1.0 copy.28.rank_down
  306.2 6.8 %product.1.gated_own = bf16[192,2048]{1,0:T(8,128)(2,1)S(1)} custom-call(bf16[192,2048]{1,0:T(8,128)(2,1)S(1)} %fusion.16.left, bf16[2048,6272]{1,0:T(8,128)(2,1)} %all-gather.2.cloned.1.call-done.w.right), custom_call_target="tpu_custom_call" | custom-call | bytes 15000000 | tf_op jit(solution)/shard_map/product/pallas_call | solution.py:1294
  313.0 0.9 copy-done.6
  313.9 71.5 %attention_back.1 = (bf16[4,3,64,1536]{3,2,1,0:T(8,128)(2,1)}, f32[4,3,64,256]{3,2,1,0:T(8,128)}, f32[8,512]{1,0:T(8,128)}, f32[192,2048]{1,0:T(8,128)}) custom-call(f32[4,3,1,256]{3,2,1,0:T(1,128)} %broadcast_in_dim.2.keep, bf16[192,2048]{1,0:T(8,128)(2,1)} %copy-done.6, f32[4,3,64,512]{3,2,1,0:T(8,128)} %bitcast.43, ...), custom_call_target="tpu_custom_call" | custom-call | bytes 240000000 | tf_op jit(solution)/shard_map/attention_back/pallas_call | solution.py:972
  385.4 103.3 %finish.1 = (f32[192,2048]{1,0:T(8,128)}, bf16[64,6144]{1,0:T(8,128)(2,1)}, f32[1,2048]{1,0:T(1,128)}, f32[1,2048]{1,0:T(1,128)}, f32[1,512]{1,0:T(1,128)}, /*in...) custom-call(bf16[768,2048]{1,0:T(8,128)(2,1)} %copy-done.2, bf16[768,1536]{1,0:T(8,128)(2,1)} %bitcast.49, ...), custom_call_target="tpu_custom_call" | custom-call | bytes 285000000 | tf_op jit(solution)/shard_map/finish/pallas_call | solution.py:1212
  488.7 2.3 slice.24
  491.0 4.4 all-to-all-start
  495.5 4.1 fusion.15
  499.6 1.2 convert_element_type.41
  500.8 1.5 slice_convert_fusion
  502.4 2.8 reshape.146
  505.2 2.4 slice_convert_fusion.1
  507.6 14.3 %all-to-all-done = bf16[4,64,2048]{2,1,0:T(8,128)(2,1)} async-done(((bf16[4,64,2048]{2,1,0:T(8,128)(2,1)}), bf16[4,64,2048]{2,1,0:T(8,128)(2,1)}, u32[]{:S(2)}, u32[]{:S(2)}) %all-to-all-start) | async-done | bytes 1048608 | tf_op jit(solution)/shard_map/all_to_all | solution.py:1416
  521.8 2.2 convert_reduce_fusion
  (68 shorter events, 6.0 us)
Async XLA Ops:
  7.2 76.6 %copy-start = (f32[16,1024]{1,0:T(8,128)S(1)}, f32[16,1024]{1,0:T(8,128)}, u32[]{:S(2)}) copy-start(f32[16,1024]{1,0:T(8,128)} %param.24) | copy-start | bytes 196612
  7.2 1.7 copy-start.14
  7.2 1.9 copy-start.12
  7.2 176.6 %all-gather.2.cloned.1.call-start = ((), (), s32[]{:S(2)}) async-start(), calls=%async_computation.2 | async-start | bytes 28901376 | tf_op jit(solution)/shard_map/all_gather | solution.py:1312
  10.9 0.7 copy-start.23
  10.9 477.8 %reduce-scatter.2.cloned.1.call-start = ((), (), s32[]{:S(2)}) async-start(), calls=%async_computation.3 | async-start | bytes 28901376 | tf_op jit(solution)/shard_map/reduce_scatter | solution.py:1316
  12.4 2.2 copy-start.4
  12.4 2.2 copy-start.8
  14.6 69.3 %copy-start.15 = (bf16[2048,16]{0,1:T(8,128)(2,1)S(1)}, bf16[2048,16]{0,1:T(8,128)(2,1)}, u32[]{:S(2)}) copy-start(bf16[2048,16]{0,1:T(8,128)(2,1)} %param.23) | copy-start | bytes 196612
  83.8 6.8 %copy-start.2 = (bf16[768,2048]{1,0:T(8,128)(2,1)}, bf16[768,2048]{1,0:T(8,128)(2,1)S(1)}, u32[]{:S(2)}) copy-start(bf16[768,2048]{1,0:T(8,128)(2,1)S(1)} %get-tuple-element.37.xn_in) | copy-start | bytes 9437188
  83.8 6.8 %copy-start.3 = (bf16[2048,1536]{1,0:T(8,128)(2,1)}, bf16[2048,1536]{1,0:T(8,128)(2,1)S(1)}, u32[]{:S(2)}) copy-start(bf16[2048,1536]{1,0:T(8,128)(2,1)S(1)} %get-tuple-element.38.w_in) | copy-start | bytes 18874372
  83.9 6.8 %copy-start.19 = (f32[16,256]{1,0:T(8,128)}, f32[16,256]{1,0:T(8,128)S(1)}, u32[]{:S(2)}) copy-start(f32[16,256]{1,0:T(8,128)S(1)} %constant_dynamic-slice_fusion.up_own) | copy-start | bytes 49156
  95.8 88.0 %copy-start.5 = (bf16[3,64,2048]{2,1,0:T(8,128)(2,1)S(1)}, bf16[3,64,2048]{2,1,0:T(8,128)(2,1)}, u32[]{:S(2)}) copy-start(bf16[3,64,2048]{2,1,0:T(8,128)(2,1)} %param.13) | copy-start | bytes 2359300
  183.8 6.7 %copy-start.17 = (f32[2048]{0:T(1024)S(1)}, f32[2048]{0:T(1024)}, u32[]{:S(2)}) copy-start(f32[2048]{0:T(1024)} %param.21) | copy-start | bytes 24580
  295.3 2.7 copy-start.9
  295.3 2.7 copy-start.11
  298.0 1.1 copy-start.7
  313.0 0.9 copy-start.6
  491.0 4.4 copy-start.10
  491.0 30.8 %all-to-all-start = ((bf16[4,64,2048]{2,1,0:T(8,128)(2,1)}), bf16[4,64,2048]{2,1,0:T(8,128)(2,1)}, u32[]{:S(2)}, u32[]{:S(2)}) async-start(bf16[4,64,2048]{2,1,0:T(8,128)(2,1)} %bitcast.47), calls=%async_computation.1 | async-start | bytes 2097152 | tf_op jit(solution)/shard_map/all_to_all | solution.py:1416
  495.4 4.1 copy-start.13
  502.4 25.4 %copy-start.1 = (f32[16,1024]{1,0:T(8,128)S(1)}, f32[16,1024]{1,0:T(8,128)}, u32[]{:S(2)}) copy-start(f32[16,1024]{1,0:T(8,128)} %param.24) | copy-start | bytes 196612
  505.2 18.9 %copy-start.21 = (f32[1,2048]{1,0:T(1,128)S(1)}, f32[1,2048]{1,0:T(1,128)}, u32[]{:S(2)}) copy-start(f32[1,2048]{1,0:T(1,128)} %get-tuple-element.56) | copy-start | bytes 24580
  505.2 19.5 %copy-start.20 = (f32[1,2048]{1,0:T(1,128)S(1)}, f32[1,2048]{1,0:T(1,128)}, u32[]{:S(2)}) copy-start(f32[1,2048]{1,0:T(1,128)} %get-tuple-element.57) | copy-start | bytes 24580
  505.2 20.1 %copy-start.24 = (f32[1,512]{1,0:T(1,128)S(1)}, f32[1,512]{1,0:T(1,128)}, u32[]{:S(2)}) copy-start(f32[1,512]{1,0:T(1,128)} %get-tuple-element.58) | copy-start | bytes 6148
  505.2 20.7 %copy-start.16 = (f32[16,2048]{1,0:T(8,128)S(1)}, f32[16,2048]{1,0:T(8,128)}, u32[]{:S(2)}) copy-start(f32[16,2048]{1,0:T(8,128)} %get-tuple-element.59) | copy-start | bytes 393220
  505.2 21.3 %copy-start.18 = (f32[16,1024]{1,0:T(8,128)S(1)}, f32[16,1024]{1,0:T(8,128)}, u32[]{:S(2)}) copy-start(f32[16,1024]{1,0:T(8,128)} %get-tuple-element.96) | copy-start | bytes 196612
  505.2 21.9 %copy-start.22 = (f32[1,1024]{1,0:T(1,128)S(1)}, f32[1,1024]{1,0:T(1,128)}, u32[]{:S(2)}) copy-start(f32[1,1024]{1,0:T(1,128)} %get-tuple-element.61) | copy-start | bytes 12292
Sparse Core Ops, SparseCore 0:
  11.0 166.8 all-gather.1
  304.4 176.8 reduce-scatter.1

commit v13 on v11

--- a/solution.py
+++ b/solution.py
@@ -296,7 +296,7 @@
 
 
 def gather_norm_kernel(own, gain, shard, normed, rows_of_all, rows_all, here_sem, send, recv,
-                       w_sem, w_peer, w_pair, w_recv):
+                       w_sem, w_send, w_recv, w_pair, w_pair_recv):
     z, count, rows = lax.axis_index("head"), lax.axis_size("head"), own.shape[0]
     greet(("seq", "head"))
     line = Line(own, rows_all, send, recv)
@@ -304,40 +304,61 @@
     here = pltpu.make_async_copy(own, line.at(z), here_sem)
     here.start()
 
-    s, deep = lax.axis_index("seq"), shard.shape[0]
+    s, deep, half = lax.axis_index("seq"), shard.shape[0], shard.shape[1] // 2
     side, pairs, own_pair = lax.rem(s, 2), lax.axis_size("seq") // 2, s // 2
-    partner = s + 1 - 2 * side
-
-    def shard_at(i):
-        return rows_of_all.at[pl.ds(pl.multiple_of(i * deep, deep), deep)]
-
-    def to_peer(k):
-        return push(shard, shard_at(s), w_peer.at[k], w_recv.at[s], 2 * k + side, "seq")
-
-    def from_peer(k):
-        i = 2 * k + side
-        return push(shard, shard_at(i), w_peer.at[k], w_recv.at[i], partner, "seq")
-
-    def to_partner(k):
-        i = 2 * k + side
-        return push(shard_at(i), shard_at(i), w_pair.at[k], w_recv.at[i], partner, "seq")
-
-    def from_partner(k):
-        i = 2 * k + 1 - side
-        return push(shard_at(i), shard_at(i), w_pair.at[k], w_recv.at[i], partner, "seq")
-
-    mine = pltpu.make_async_copy(shard, shard_at(s), w_sem)
+    levels = pairs.bit_length() - 1
+    assert pairs == 1 << levels
+    orders = list(range(levels)), list(reversed(range(levels)))
+
+    def bit(level):
+        return lax.rem(own_pair // (1 << level), 2) * (1 << level)
+
+    def block(k, of_side):
+        return pl.ds(pl.multiple_of((2 * k + of_side) * deep, deep), deep)
+
+    def across(part, step):
+        level = orders[part][step]
+        return own_pair + (1 << level) - 2 * bit(level)
+
+    def known(part, step, start):
+        done = orders[part][:step]
+        base = start - sum((bit(d) for d in done), 0)
+        for c in range(1 << step):
+            yield base + sum(((c >> n) & 1) << d for n, d in enumerate(done))
+
+    def hop(part, step, k):
+        at = rows_of_all.at[block(k, side), pl.ds(part * half, half)]
+        to = 2 * across(part, step) + side
+        return push(at, at, w_send.at[part, step, k], w_recv.at[part, k], to, "seq")
+
+    def begin(step):
+        for part in range(2):
+            for k in known(part, step, own_pair):
+                hop(part, step, k).start()
+
+    def advance(step):
+        for part in range(2):
+            for k in known(part, step, across(part, step)):
+                hop(part, step, k).wait_recv()
+        if step + 1 < levels:
+            begin(step + 1)
+
+    def to_partner(k, of_side):
+        at = rows_of_all.at[block(k, of_side)]
+        return push(at, at, w_pair.at[k], w_pair_recv.at[k], s + 1 - 2 * side, "seq")
+
+    mine = pltpu.make_async_copy(shard, rows_of_all.at[block(own_pair, side)], w_sem)
     mine.start()
-    for k in range(pairs):
-        pl.when(own_pair != k)(to_peer(k).start)
     mine.wait()
-    to_partner(own_pair).start()
+    begin(0)
+    to_partner(own_pair, side).start()
     here.wait()
     band = 16
 
     def step(i, _):
         b = near_order(z, count, i)
         pl.when(i > 0)(lambda: line.receive(i, b))
+        pl.when(i == 1)(lambda: advance(0))
 
         def norm(r, _):
             at = pl.ds(pl.multiple_of(b * rows + r * band, band), band)
@@ -350,18 +371,18 @@
         return 0
 
     lax.fori_loop(0, count, step, 0)
+    for later in range(1, levels):
+        advance(later)
     for k in range(pairs):
-
-        @pl.when(own_pair != k)
-        def _():
-            from_peer(k).wait_recv()
-            to_partner(k).start()
-
+        pl.when(own_pair != k)(to_partner(k, side).start)
     for k in range(pairs):
-        from_partner(k).wait_recv()
+        to_partner(k, 1 - side).wait_recv()
     for k in range(pairs):
-        to_partner(k).wait_send()
-        pl.when(own_pair != k)(to_peer(k).wait_send)
+        to_partner(k, side).wait_send()
+    for part in range(2):
+        for late in range(levels):
+            for k in known(part, late, own_pair):
+                hop(part, late, k).wait_send()
     line.finish()
 
 
@@ -382,7 +403,8 @@
         out_specs=(vmem, anywhere),
         scratch_shapes=[
             pltpu.VMEM((count * rows, width), BF16), dma(()), dma((count + 1, 1)), dma((count, 1)),
-            dma(()), dma((seq // 2,)), dma((seq // 2,)), dma((seq,)),
+            dma(()), dma((2, (seq // 2).bit_length() - 1, seq // 2)), dma((2, seq // 2)),
+            dma((seq // 2,)), dma((seq // 2,)),
         ],
         compiler_params=pltpu.CompilerParams(
             collective_id=1, has_side_effects=True, vmem_limit_bytes=32 << 20

time: 542 us -> 533 us (0.983)
  Pallas kernels: 436 us -> 428 us
    pallas_call x1, Pallas kernels: 84.3 us -> 78.2 us  [attention_forward(): pl.pallas_call(front_kernel, out_shape=(jax.ShapeDtypeStruct((blocks, mic...]
where the time goes in v13:
time: 533 us; the launch traced here: 525 us
  Pallas kernels  428 us (80%)
  matrix products  22.7 us (4%)
  local copies, waits for them, and re-layouts  21.5 us (4%)
  other arithmetic  19.4 us (4%)
  between operations  14.9 us (3%)
  waiting for transfers between devices  14.1 us (3%)
    pallas_call x1, Pallas kernels, feed_forward(): pl.pallas_call(functools.partial(ffn_kernel, count), out_shape=(jax.Shape...  103 us
    pallas_call x1, Pallas kernels, finish(): pl.pallas_call(finish_kernel, out_shape=(jax.ShapeDtypeStruct((rows, widt...  103 us
    pallas_call x1, Pallas kernels, attention_forward(): pl.pallas_call(front_kernel, out_shape=(jax.ShapeDtypeStruct((blocks, mic...  78.2 us
    pallas_call x1, Pallas kernels, attention_back(): pl.pallas_call(back_kernel, out_shape=(jax.ShapeDtypeStruct((blocks, micr...  72.2 us
    pallas_call x1, Pallas kernels, gather_norm(): pl.pallas_call(gather_norm_kernel, out_shape=(jax.ShapeDtypeStruct((count...  66.7 us
    dot_general x6, matrix products, dot(): lax.dot_general(a, b, (((contract[0],), (contract[1],)), ((), ())), preci...  22.7 us
    all_to_all x1, waiting for transfers between devices, on_device(): lax.all_to_all(grads[:, :vals].reshape(heads, slab, vals), 'head', split_...  14 us
    unnamed x76, local copies, waits for them, and re-layouts  12.4 us
  transfers between devices with their start and end apart: 3, of which 1 were waited for; matrix products, arithmetic and copies ran while one was open for 6% of the time, Pallas kernels for 61%

profile of v13, /device:TPU:0, one launch (start us, length us, event | category | flops | bytes accessed | tf_op | source)
XLA Modules:
  0.0 525.3 jit_solution(10585087834608851151)
XLA Ops:
  7.3 1.6 copy.29
  9.1 1.8 pad_maximum_fusion
  12.4 1.1 constant_dynamic-slice_fusion.4
  13.5 1.1 constant_dynamic-slice_fusion.2
  14.7 66.7 %gather_norm.1 = (bf16[768,2048]{1,0:T(8,128)(2,1)S(1)}, bf16[2048,1536]{1,0:T(8,128)(2,1)S(1)}) custom-call(bf16[192,2048]{1,0:T(8,128)(2,1)S(1)} %bitcast.43, f32[1,2048]{1,0:T(1,128)S(1)} %bitcast.48, bf16[256,1536]{1,0:T(8,128)(2,1)S(1)} %pad_maximum_fusion.1.shard), custom_call_target="tpu_custom_call" | custom-call | bytes 150000000 | tf_op jit(solution)/shard_map/gather_norm/pallas_call | solution.py:396
  81.4 0.9 fusion.22
  82.3 2.7 fusion.19
  85.0 1.8 fusion.12
  86.9 3.4 fusion.14
  90.4 78.2 %attention_forward.1 = (f32[4,3,64,512]{3,2,1,0:T(8,128)S(1)}, bf16[192,2048]{1,0:T(8,128)(2,1)S(1)}, bf16[4,3,16,256]{3,2,1,0:T(8,128)(2,1)S(1)}, bf16[2,3,16,2...) custom-call(f32[4,3,1,256]{3,2,1,0:T(1,128)S(1)} %broadcast_in_dim.2.keep, ...), custom_call_target="tpu_custom_call" | custom-call | bytes 270000000 | tf_op jit(solution)/shard_map/attention_forward/pallas_call | solution.py:623
  168.6 1.2 copy-done.7
  169.8 1.7 copy-done.8
  171.5 1.1 copy-done.11
  173.9 6.4 %multiply_reduce_fusion.2 = (f32[192]{0:T(256)S(1)}, f32[192,2048]{1,0:T(8,128)S(1)}) fusion(bf16[192,2048]{1,0:T(8,128)(2,1)S(1)} %get-tuple-element.39.right, bf16[2048,6272]{1,0:T(8,128)(2,1)} %all-gather.2.cloned.1.call-done.w, bf16[192,2048]{1,0:T(8,128)(2,1)S(1)} %bitcast.44), kind=kOutput, calls=%fused_computation.19 | convolution fusion | flops 1612185344 | bytes 11535104 | tf_op jit(solution)/shard_map/dot_general | solution.py:1316
  180.3 1.3 multiply_convert_fusion.x_own
  181.6 103.4 %feed_forward.1 = (f32[192,2048]{1,0:T(8,128)}, bf16[4,192,2048]{2,1,0:T(8,128)(2,1)}, bf16[2048,6272]{1,0:T(8,128)(2,1)}) custom-call(bf16[192,2048]{1,0:T(8,128)(2,1)} %multiply_convert_fusion.x_own, bf16[768,2048]{1,0:T(8,128)(2,1)} %copy-done.8, bf16[2048,6272]{1,0:T(8,128)(2,1)} %all-gather.2.cloned.1.call-done.w), custom_call_target="tpu_custom_call" | custom-call | bytes 300000000 | tf_op jit(solution)/shard_map/feed_forward/pallas_call | solution.py:774
  285.1 2.6 multiply_reduce_fusion
  287.7 1.9 fusion.21.left
  289.6 5.2 weight_grad.1
  295.8 1.0 copy.28.rank_down
  296.8 7.5 %fusion.9.gated_own = bf16[192,2048]{1,0:T(8,128)(2,1)} fusion(bf16[192,2048]{1,0:T(8,128)(2,1)S(1)} %fusion.21.left, bf16[2048,6272]{1,0:T(8,128)(2,1)} %all-gather.2.cloned.1.call-done.w), kind=kOutput, calls=%fused_computation.8 | convolution fusion | flops 1611005952 | bytes 9961472 | tf_op jit(solution)/shard_map/dot_general | solution.py:1316
  304.3 72.2 %attention_back.1 = (bf16[4,3,64,1536]{3,2,1,0:T(8,128)(2,1)}, f32[4,3,64,256]{3,2,1,0:T(8,128)}, f32[8,512]{1,0:T(8,128)}, f32[192,2048]{1,0:T(8,128)}) custom-call(f32[4,3,1,256]{3,2,1,0:T(1,128)} %copy-done.13, bf16[192,2048]{1,0:T(8,128)(2,1)} %fusion.9.gated_own, f32[4,3,64,512]{3,2,1,0:T(8,128)} %bitcast.39, f32[4,3,64,512]{3,2,1,0:T(8,128)} %copy-done.11, ...), custom_call_target="tpu_custom_call" | custom-call | bytes 240000000 | tf_op jit(solution)/shard_map/attention_back/pallas_call | solution.py:992
  376.4 102.5 %finish.1 = (f32[192,2048]{1,0:T(8,128)}, bf16[64,6144]{1,0:T(8,128)(2,1)}, f32[1,2048]{1,0:T(1,128)}, f32[1,2048]{1,0:T(1,128)}, f32[1,512]{1,0:T(1,128)}, /*in...) custom-call(bf16[768,2048]{1,0:T(8,128)(2,1)} %copy-done.2, bf16[768,1536]{1,0:T(8,128)(2,1)} %bitcast.53, ...), custom_call_target="tpu_custom_call" | custom-call | bytes 285000000 | tf_op jit(solution)/shard_map/finish/pallas_call | solution.py:1232
  479.0 2.3 slice.24
  481.3 4.4 all-to-all-start
  485.7 4.4 fusion.20
  490.1 1.2 convert_element_type.45
  491.3 1.5 slice_convert_fusion
  492.9 2.8 reshape.146
  495.7 2.4 slice_convert_fusion.1
  498.1 14.0 %all-to-all-done = bf16[4,64,2048]{2,1,0:T(8,128)(2,1)} async-done(((bf16[4,64,2048]{2,1,0:T(8,128)(2,1)}), bf16[4,64,2048]{2,1,0:T(8,128)(2,1)}, u32[]{:S(2)}, u32[]{:S(2)}) %all-to-all-start) | async-done | bytes 1048608 | tf_op jit(solution)/shard_map/all_to_all | solution.py:1412
  512.1 2.2 convert_reduce_fusion
  (86 shorter events, 7.9 us)
Async XLA Ops:
  7.2 74.2 %copy-start = (f32[16,1024]{1,0:T(8,128)S(1)}, f32[16,1024]{1,0:T(8,128)}, u32[]{:S(2)}) copy-start(f32[16,1024]{1,0:T(8,128)} %param.24) | copy-start | bytes 196612
  7.2 1.7 copy-start.21
  7.2 1.9 copy-start.23
  7.2 166.6 %all-gather.2.cloned.1.call-start = ((), (), s32[]{:S(2)}) async-start(), calls=%async_computation.2 | async-start | bytes 28901376 | tf_op jit(solution)/shard_map/all_gather | solution.py:1308
  10.9 468.1 %reduce-scatter.2.cloned.1.call-start = ((), (), s32[]{:S(2)}) async-start(), calls=%async_computation.3 | async-start | bytes 28901376 | tf_op jit(solution)/shard_map/reduce_scatter | solution.py:1312
  12.4 2.2 copy-start.9
  12.4 2.2 copy-start.16
  14.6 66.8 %copy-start.24 = (bf16[2048,16]{0,1:T(8,128)(2,1)S(1)}, bf16[2048,16]{0,1:T(8,128)(2,1)}, u32[]{:S(2)}) copy-start(bf16[2048,16]{0,1:T(8,128)(2,1)} %param.23) | copy-start | bytes 196612
  81.3 5.5 %copy-start.2 = (bf16[768,2048]{1,0:T(8,128)(2,1)}, bf16[768,2048]{1,0:T(8,128)(2,1)S(1)}, u32[]{:S(2)}) copy-start(bf16[768,2048]{1,0:T(8,128)(2,1)S(1)} %get-tuple-element.37.xn_in) | copy-start | bytes 9437188
  81.3 5.5 %copy-start.5 = (bf16[2048,1536]{1,0:T(8,128)(2,1)}, bf16[2048,1536]{1,0:T(8,128)(2,1)S(1)}, u32[]{:S(2)}) copy-start(bf16[2048,1536]{1,0:T(8,128)(2,1)S(1)} %get-tuple-element.38.w_in) | copy-start | bytes 18874372
  81.4 5.5 %copy-start.28 = (f32[16,256]{1,0:T(8,128)}, f32[16,256]{1,0:T(8,128)S(1)}, u32[]{:S(2)}) copy-start(f32[16,256]{1,0:T(8,128)S(1)} %constant_dynamic-slice_fusion.up_own) | copy-start | bytes 49156
  85.0 5.3 %copy-start.12 = (bf16[768,256]{1,0:T(8,128)(2,1)}, bf16[768,256]{1,0:T(8,128)(2,1)S(1)}, u32[]{:S(2)}) copy-start(bf16[768,256]{1,0:T(8,128)(2,1)S(1)} %get-tuple-element.70) | copy-start | bytes 1179652
  86.8 3.5 copy-start.6
  86.9 3.5 copy-start.3
  86.9 3.5 copy-start.17
  90.4 78.3 %copy-start.13 = (f32[4,3,1,256]{3,2,1,0:T(1,128)}, f32[4,3,1,256]{3,2,1,0:T(1,128)S(1)}, u32[]{:S(2)}) copy-start(f32[4,3,1,256]{3,2,1,0:T(1,128)S(1)} %broadcast_in_dim.2.keep) | copy-start | bytes 36868
  90.4 83.4 %copy-start.10 = (bf16[3,64,2048]{2,1,0:T(8,128)(2,1)S(1)}, bf16[3,64,2048]{2,1,0:T(8,128)(2,1)}, u32[]{:S(2)}) copy-start(bf16[3,64,2048]{2,1,0:T(8,128)(2,1)} %param.13) | copy-start | bytes 2359300
  169.8 1.7 copy-start.8
  173.9 6.5 %copy-start.26 = (f32[2048]{0:T(1024)S(1)}, f32[2048]{0:T(1024)}, u32[]{:S(2)}) copy-start(f32[2048]{0:T(1024)} %param.21) | copy-start | bytes 24580
  180.3 104.8 %copy-start.18 = (f32[192,2048]{1,0:T(8,128)}, f32[192,2048]{1,0:T(8,128)S(1)}, u32[]{:S(2)}) copy-start(f32[192,2048]{1,0:T(8,128)S(1)} %get-tuple-element.73) | copy-start | bytes 4718596
  285.1 2.7 copy-start.4
  285.1 2.7 copy-start.20
  481.3 4.4 copy-start.19
  481.3 30.8 %all-to-all-start = ((bf16[4,64,2048]{2,1,0:T(8,128)(2,1)}), bf16[4,64,2048]{2,1,0:T(8,128)(2,1)}, u32[]{:S(2)}, u32[]{:S(2)}) async-start(bf16[4,64,2048]{2,1,0:T(8,128)(2,1)} %bitcast.15), calls=%async_computation.1 | async-start | bytes 2097152 | tf_op jit(solution)/shard_map/all_to_all | solution.py:1412
  485.7 4.4 copy-start.22
  492.9 25.1 %copy-start.1 = (f32[16,1024]{1,0:T(8,128)S(1)}, f32[16,1024]{1,0:T(8,128)}, u32[]{:S(2)}) copy-start(f32[16,1024]{1,0:T(8,128)} %param.24) | copy-start | bytes 196612
  495.7 18.6 %copy-start.30 = (f32[1,2048]{1,0:T(1,128)S(1)}, f32[1,2048]{1,0:T(1,128)}, u32[]{:S(2)}) copy-start(f32[1,2048]{1,0:T(1,128)} %get-tuple-element.56) | copy-start | bytes 24580
  495.7 19.2 %copy-start.29 = (f32[1,2048]{1,0:T(1,128)S(1)}, f32[1,2048]{1,0:T(1,128)}, u32[]{:S(2)}) copy-start(f32[1,2048]{1,0:T(1,128)} %get-tuple-element.57) | copy-start | bytes 24580
  495.7 19.8 %copy-start.33 = (f32[1,512]{1,0:T(1,128)S(1)}, f32[1,512]{1,0:T(1,128)}, u32[]{:S(2)}) copy-start(f32[1,512]{1,0:T(1,128)} %get-tuple-element.58) | copy-start | bytes 6148
  495.7 20.4 %copy-start.25 = (f32[16,2048]{1,0:T(8,128)S(1)}, f32[16,2048]{1,0:T(8,128)}, u32[]{:S(2)}) copy-start(f32[16,2048]{1,0:T(8,128)} %get-tuple-element.59) | copy-start | bytes 393220
  495.7 21.1 %copy-start.27 = (f32[16,1024]{1,0:T(8,128)S(1)}, f32[16,1024]{1,0:T(8,128)}, u32[]{:S(2)}) copy-start(f32[16,1024]{1,0:T(8,128)} %get-tuple-element.96) | copy-start | bytes 196612
  495.7 21.7 %copy-start.31 = (f32[1,1024]{1,0:T(1,128)S(1)}, f32[1,1024]{1,0:T(1,128)}, u32[]{:S(2)}) copy-start(f32[1,1024]{1,0:T(1,128)} %get-tuple-element.61) | copy-start | bytes 12292
  (5 other events, 4.2 us)
Sparse Core Ops, SparseCore 0:
  11.0 158.3 all-gather.1
  295.0 176.6 reduce-scatter.1

commit v14 on v13

--- a/solution.py
+++ b/solution.py
@@ -486,9 +486,10 @@
     here.start()
 
     state[...] = jnp.zeros_like(state)
-    passed = [jnp.zeros((1, dk), F32)] * micro
-    alive = [jnp.ones((1, dk), F32)] * micro
-    for b in range(count):
+
+    def gather(b, carry):
+        passed, alive = carry
+        later_passed, later_alive = [], []
         for m in range(micro):
             run = running(decay[b, m])
             runs[b, m] = run
@@ -497,8 +498,14 @@
             fresh = mms((qkv[b, m, :, 2 * dk :],), split(carried), (0, 0))
             kept[b, m] = fresh
             state[m] = jnp.exp(last) * (state[m] * keep[b, m]) + fresh
-            passed[m] = passed[m] + last
-            alive[m] = alive[m] * keep[b, m]
+            later_passed.append(passed[m] + last)
+            later_alive.append(alive[m] * keep[b, m])
+        return later_passed, later_alive
+
+    passed, alive = lax.fori_loop(
+        0, count, gather,
+        ([jnp.zeros((1, dk), F32)] * micro, [jnp.ones((1, dk), F32)] * micro),
+    )
     tail = sending.shape[2] - part
     at = lax.broadcasted_iota(jnp.int32, (tail, dk), 0)
     half = dv // 2
@@ -832,15 +839,21 @@
     gated_all[h] = gated_own[:, pl.ds(pl.multiple_of(h * dv, dv), dv)]
 
     causal = lower_ones(rows)
-    before = [jnp.zeros((1, dk), F32)] * micro
-    alive = [jnp.ones((1, dk), F32)] * micro
-    for b in range(count):
+
+    def reach(b, carry):
+        before, alive = carry
+        later_before, later_alive = [], []
         for m in range(micro):
             run = running(decay[b, m])
             runs[b, m] = run
-            alive[m] = alive[m] * keep[b, m]
-            weights[b, m] = jnp.exp(before[m]) * alive[m]
-            before[m] = before[m] + run[rows - 1 : rows, :]
+            later_alive.append(alive[m] * keep[b, m])
+            weights[b, m] = jnp.exp(before[m]) * later_alive[m]
+            later_before.append(before[m] + run[rows - 1 : rows, :])
+        return later_before, later_alive
+
+    lax.fori_loop(
+        0, count, reach, ([jnp.zeros((1, dk), F32)] * micro, [jnp.ones((1, dk), F32)] * micro)
+    )
     g_gain[...] = jnp.zeros_like(g_gain)
     state[...] = jnp.zeros_like(state)
 

time: 533 us -> 534 us (level)
  no operation moved by 1% of the time
where the time goes in v14:
time: 534 us; the launch traced here: 526 us
  Pallas kernels  429 us (80%)
  matrix products  22.8 us (4%)
  local copies, waits for them, and re-layouts  21.5 us (4%)
  other arithmetic  19.4 us (4%)
  between operations  14.9 us (3%)
  waiting for transfers between devices  14.1 us (3%)
    pallas_call x1, Pallas kernels, feed_forward(): pl.pallas_call(functools.partial(ffn_kernel, count), out_shape=(jax.Shape...  104 us
    pallas_call x1, Pallas kernels, finish(): pl.pallas_call(finish_kernel, out_shape=(jax.ShapeDtypeStruct((rows, widt...  103 us
    pallas_call x1, Pallas kernels, attention_forward(): pl.pallas_call(front_kernel, out_shape=(jax.ShapeDtypeStruct((blocks, mic...  78 us
    pallas_call x1, Pallas kernels, attention_back(): pl.pallas_call(back_kernel, out_shape=(jax.ShapeDtypeStruct((blocks, micr...  72.1 us
    pallas_call x1, Pallas kernels, gather_norm(): pl.pallas_call(gather_norm_kernel, out_shape=(jax.ShapeDtypeStruct((count...  66.7 us
    dot_general x6, matrix products, dot(): lax.dot_general(a, b, (((contract[0],), (contract[1],)), ((), ())), preci...  22.8 us
    all_to_all x1, waiting for transfers between devices, on_device(): lax.all_to_all(grads[:, :vals].reshape(heads, slab, vals), 'head', split_...  14 us
    unnamed x76, local copies, waits for them, and re-layouts  12.4 us
  transfers between devices with their start and end apart: 3, of which 1 were waited for; matrix products, arithmetic and copies ran while one was open for 6% of the time, Pallas kernels for 61%

profile of v14, /device:TPU:0, one launch (start us, length us, event | category | flops | bytes accessed | tf_op | source)
XLA Modules:
  0.0 526.0 jit_solution(9538470967787438898)
XLA Ops:
  7.3 1.6 copy.29
  9.1 1.8 pad_maximum_fusion
  12.4 1.1 constant_dynamic-slice_fusion.4
  13.5 1.1 constant_dynamic-slice_fusion.2
  14.7 66.7 %gather_norm.1 = (bf16[768,2048]{1,0:T(8,128)(2,1)S(1)}, bf16[2048,1536]{1,0:T(8,128)(2,1)S(1)}) custom-call(bf16[192,2048]{1,0:T(8,128)(2,1)S(1)} %bitcast.43, f32[1,2048]{1,0:T(1,128)S(1)} %bitcast.48, bf16[256,1536]{1,0:T(8,128)(2,1)S(1)} %pad_maximum_fusion.1.shard), custom_call_target="tpu_custom_call" | custom-call | bytes 150000000 | tf_op jit(solution)/shard_map/gather_norm/pallas_call | solution.py:396
  81.4 0.9 fusion.22
  82.3 2.7 fusion.19
  85.0 1.8 fusion.12
  86.9 3.4 fusion.14
  90.4 78.0 %attention_forward.1 = (f32[4,3,64,512]{3,2,1,0:T(8,128)S(1)}, bf16[192,2048]{1,0:T(8,128)(2,1)S(1)}, bf16[4,3,16,256]{3,2,1,0:T(8,128)(2,1)S(1)}, bf16[2,3,16,2...) custom-call(f32[4,3,1,256]{3,2,1,0:T(1,128)S(1)} %broadcast_in_dim.2.keep, ...), custom_call_target="tpu_custom_call" | custom-call | bytes 270000000 | tf_op jit(solution)/shard_map/attention_forward/pallas_call | solution.py:630
  168.5 1.2 copy-done.7
  169.6 1.7 copy-done.8
  171.3 1.1 copy-done.11
  173.7 6.4 %multiply_reduce_fusion.2 = (f32[192]{0:T(256)S(1)}, f32[192,2048]{1,0:T(8,128)S(1)}) fusion(bf16[192,2048]{1,0:T(8,128)(2,1)S(1)} %get-tuple-element.39.right, bf16[2048,6272]{1,0:T(8,128)(2,1)} %all-gather.2.cloned.1.call-done.w, bf16[192,2048]{1,0:T(8,128)(2,1)S(1)} %bitcast.44), kind=kOutput, calls=%fused_computation.19 | convolution fusion | flops 1612185344 | bytes 11535104 | tf_op jit(solution)/shard_map/dot_general | solution.py:1329
  180.2 1.3 multiply_convert_fusion.x_own
  181.4 103.6 %feed_forward.1 = (f32[192,2048]{1,0:T(8,128)}, bf16[4,192,2048]{2,1,0:T(8,128)(2,1)}, bf16[2048,6272]{1,0:T(8,128)(2,1)}) custom-call(bf16[192,2048]{1,0:T(8,128)(2,1)} %multiply_convert_fusion.x_own, bf16[768,2048]{1,0:T(8,128)(2,1)} %copy-done.8, bf16[2048,6272]{1,0:T(8,128)(2,1)} %all-gather.2.cloned.1.call-done.w), custom_call_target="tpu_custom_call" | custom-call | bytes 300000000 | tf_op jit(solution)/shard_map/feed_forward/pallas_call | solution.py:781
  285.1 2.6 multiply_reduce_fusion
  287.7 1.9 fusion.21.left
  289.6 5.2 weight_grad.1
  295.8 1.0 copy.28.rank_down
  296.8 7.5 %fusion.9.gated_own = bf16[192,2048]{1,0:T(8,128)(2,1)} fusion(bf16[192,2048]{1,0:T(8,128)(2,1)S(1)} %fusion.21.left, bf16[2048,6272]{1,0:T(8,128)(2,1)} %all-gather.2.cloned.1.call-done.w), kind=kOutput, calls=%fused_computation.8 | convolution fusion | flops 1611005952 | bytes 9961472 | tf_op jit(solution)/shard_map/dot_general | solution.py:1329
  304.3 72.1 %attention_back.1 = (bf16[4,3,64,1536]{3,2,1,0:T(8,128)(2,1)}, f32[4,3,64,256]{3,2,1,0:T(8,128)}, f32[8,512]{1,0:T(8,128)}, f32[192,2048]{1,0:T(8,128)}) custom-call(f32[4,3,1,256]{3,2,1,0:T(1,128)} %copy-done.13, bf16[192,2048]{1,0:T(8,128)(2,1)} %fusion.9.gated_own, f32[4,3,64,512]{3,2,1,0:T(8,128)} %bitcast.39, f32[4,3,64,512]{3,2,1,0:T(8,128)} %copy-done.11, ...), custom_call_target="tpu_custom_call" | custom-call | bytes 240000000 | tf_op jit(solution)/shard_map/attention_back/pallas_call | solution.py:1005
  376.5 103.2 %finish.1 = (f32[192,2048]{1,0:T(8,128)}, bf16[64,6144]{1,0:T(8,128)(2,1)}, f32[1,2048]{1,0:T(1,128)}, f32[1,2048]{1,0:T(1,128)}, f32[1,512]{1,0:T(1,128)}, /*in...) custom-call(bf16[768,2048]{1,0:T(8,128)(2,1)} %copy-done.2, bf16[768,1536]{1,0:T(8,128)(2,1)} %bitcast.53, ...), custom_call_target="tpu_custom_call" | custom-call | bytes 285000000 | tf_op jit(solution)/shard_map/finish/pallas_call | solution.py:1245
  479.7 2.3 slice.24
  482.0 4.4 all-to-all-start
  486.4 4.4 fusion.20
  490.8 1.2 convert_element_type.45
  492.0 1.5 slice_convert_fusion
  493.6 2.8 reshape.146
  496.4 2.4 slice_convert_fusion.1
  498.8 14.0 %all-to-all-done = bf16[4,64,2048]{2,1,0:T(8,128)(2,1)} async-done(((bf16[4,64,2048]{2,1,0:T(8,128)(2,1)}), bf16[4,64,2048]{2,1,0:T(8,128)(2,1)}, u32[]{:S(2)}, u32[]{:S(2)}) %all-to-all-start) | async-done | bytes 1048608 | tf_op jit(solution)/shard_map/all_to_all | solution.py:1425
  512.8 2.2 convert_reduce_fusion
  (86 shorter events, 7.9 us)
Async XLA Ops:
  7.2 74.2 %copy-start = (f32[16,1024]{1,0:T(8,128)S(1)}, f32[16,1024]{1,0:T(8,128)}, u32[]{:S(2)}) copy-start(f32[16,1024]{1,0:T(8,128)} %param.24) | copy-start | bytes 196612
  7.2 1.7 copy-start.21
  7.2 1.9 copy-start.23
  7.2 166.5 %all-gather.2.cloned.1.call-start = ((), (), s32[]{:S(2)}) async-start(), calls=%async_computation.2 | async-start | bytes 28901376 | tf_op jit(solution)/shard_map/all_gather | solution.py:1321
  10.9 468.8 %reduce-scatter.2.cloned.1.call-start = ((), (), s32[]{:S(2)}) async-start(), calls=%async_computation.3 | async-start | bytes 28901376 | tf_op jit(solution)/shard_map/reduce_scatter | solution.py:1325
  12.4 2.2 copy-start.9
  12.4 2.2 copy-start.16
  14.6 66.8 %copy-start.24 = (bf16[2048,16]{0,1:T(8,128)(2,1)S(1)}, bf16[2048,16]{0,1:T(8,128)(2,1)}, u32[]{:S(2)}) copy-start(bf16[2048,16]{0,1:T(8,128)(2,1)} %param.23) | copy-start | bytes 196612
  81.3 5.5 %copy-start.2 = (bf16[768,2048]{1,0:T(8,128)(2,1)}, bf16[768,2048]{1,0:T(8,128)(2,1)S(1)}, u32[]{:S(2)}) copy-start(bf16[768,2048]{1,0:T(8,128)(2,1)S(1)} %get-tuple-element.37.xn_in) | copy-start | bytes 9437188
  81.3 5.5 %copy-start.5 = (bf16[2048,1536]{1,0:T(8,128)(2,1)}, bf16[2048,1536]{1,0:T(8,128)(2,1)S(1)}, u32[]{:S(2)}) copy-start(bf16[2048,1536]{1,0:T(8,128)(2,1)S(1)} %get-tuple-element.38.w_in) | copy-start | bytes 18874372
  81.4 5.5 %copy-start.28 = (f32[16,256]{1,0:T(8,128)}, f32[16,256]{1,0:T(8,128)S(1)}, u32[]{:S(2)}) copy-start(f32[16,256]{1,0:T(8,128)S(1)} %constant_dynamic-slice_fusion.up_own) | copy-start | bytes 49156
  85.0 5.3 %copy-start.12 = (bf16[768,256]{1,0:T(8,128)(2,1)}, bf16[768,256]{1,0:T(8,128)(2,1)S(1)}, u32[]{:S(2)}) copy-start(bf16[768,256]{1,0:T(8,128)(2,1)S(1)} %get-tuple-element.70) | copy-start | bytes 1179652
  86.8 3.5 copy-start.6
  86.9 3.5 copy-start.3
  86.9 3.5 copy-start.17
  90.4 78.1 %copy-start.13 = (f32[4,3,1,256]{3,2,1,0:T(1,128)}, f32[4,3,1,256]{3,2,1,0:T(1,128)S(1)}, u32[]{:S(2)}) copy-start(f32[4,3,1,256]{3,2,1,0:T(1,128)S(1)} %broadcast_in_dim.2.keep) | copy-start | bytes 36868
  90.4 83.3 %copy-start.10 = (bf16[3,64,2048]{2,1,0:T(8,128)(2,1)S(1)}, bf16[3,64,2048]{2,1,0:T(8,128)(2,1)}, u32[]{:S(2)}) copy-start(bf16[3,64,2048]{2,1,0:T(8,128)(2,1)} %param.13) | copy-start | bytes 2359300
  169.6 1.7 copy-start.8
  173.7 6.5 %copy-start.26 = (f32[2048]{0:T(1024)S(1)}, f32[2048]{0:T(1024)}, u32[]{:S(2)}) copy-start(f32[2048]{0:T(1024)} %param.21) | copy-start | bytes 24580
  180.1 104.9 %copy-start.18 = (f32[192,2048]{1,0:T(8,128)}, f32[192,2048]{1,0:T(8,128)S(1)}, u32[]{:S(2)}) copy-start(f32[192,2048]{1,0:T(8,128)S(1)} %get-tuple-element.73) | copy-start | bytes 4718596
  285.1 2.7 copy-start.4
  285.1 2.7 copy-start.20
  482.0 4.4 copy-start.19
  482.0 30.8 %all-to-all-start = ((bf16[4,64,2048]{2,1,0:T(8,128)(2,1)}), bf16[4,64,2048]{2,1,0:T(8,128)(2,1)}, u32[]{:S(2)}, u32[]{:S(2)}) async-start(bf16[4,64,2048]{2,1,0:T(8,128)(2,1)} %bitcast.15), calls=%async_computation.1 | async-start | bytes 2097152 | tf_op jit(solution)/shard_map/all_to_all | solution.py:1425
  486.4 4.4 copy-start.22
  493.6 25.1 %copy-start.1 = (f32[16,1024]{1,0:T(8,128)S(1)}, f32[16,1024]{1,0:T(8,128)}, u32[]{:S(2)}) copy-start(f32[16,1024]{1,0:T(8,128)} %param.24) | copy-start | bytes 196612
  496.4 18.6 %copy-start.30 = (f32[1,2048]{1,0:T(1,128)S(1)}, f32[1,2048]{1,0:T(1,128)}, u32[]{:S(2)}) copy-start(f32[1,2048]{1,0:T(1,128)} %get-tuple-element.56) | copy-start | bytes 24580
  496.4 19.2 %copy-start.29 = (f32[1,2048]{1,0:T(1,128)S(1)}, f32[1,2048]{1,0:T(1,128)}, u32[]{:S(2)}) copy-start(f32[1,2048]{1,0:T(1,128)} %get-tuple-element.57) | copy-start | bytes 24580
  496.4 19.8 %copy-start.33 = (f32[1,512]{1,0:T(1,128)S(1)}, f32[1,512]{1,0:T(1,128)}, u32[]{:S(2)}) copy-start(f32[1,512]{1,0:T(1,128)} %get-tuple-element.58) | copy-start | bytes 6148
  496.4 20.4 %copy-start.25 = (f32[16,2048]{1,0:T(8,128)S(1)}, f32[16,2048]{1,0:T(8,128)}, u32[]{:S(2)}) copy-start(f32[16,2048]{1,0:T(8,128)} %get-tuple-element.59) | copy-start | bytes 393220
  496.4 21.1 %copy-start.27 = (f32[16,1024]{1,0:T(8,128)S(1)}, f32[16,1024]{1,0:T(8,128)}, u32[]{:S(2)}) copy-start(f32[16,1024]{1,0:T(8,128)} %get-tuple-element.96) | copy-start | bytes 196612
  496.4 21.7 %copy-start.31 = (f32[1,1024]{1,0:T(1,128)S(1)}, f32[1,1024]{1,0:T(1,128)}, u32[]{:S(2)}) copy-start(f32[1,1024]{1,0:T(1,128)} %get-tuple-element.61) | copy-start | bytes 12292
  (5 other events, 4.2 us)
Sparse Core Ops, SparseCore 0:
  11.0 158.3 all-gather.1
  295.0 176.5 reduce-scatter.1

commit v15 on v14

--- a/solution.py
+++ b/solution.py
@@ -668,7 +668,9 @@
 
     weights = [
         pltpu.make_async_copy(
-            w.at[:, pl.ds(k * hidden, hidden)], wv.at[:, pl.ds(k * hidden, hidden)], w_sem.at[k]
+            w.at[:, pl.ds(w.shape[1] + (k - 3) * hidden, hidden)],
+            wv.at[:, pl.ds(k * hidden, hidden)],
+            w_sem.at[k],
         )
         for k in range(3)
     ]
@@ -1317,6 +1319,44 @@
     )(left, right, *given)
 
 
+def product_kernel(left, right, out, total):
+    part = jnp.dot(left[...], right[...], preferred_element_type=F32)
+    step, last = pl.program_id(0), pl.num_programs(0) - 1
+
+    @pl.when(step == 0)
+    def _():
+        total[...] = part
+
+    @pl.when((step > 0) & (step < last))
+    def _():
+        total[...] += part
+
+    @pl.when(step == last)
+    def _():
+        out[...] = (total[...] + part).astype(BF16)
+
+
+def rows_by_columns(left, right, columns):
+    rows, depth = left.shape
+    tile = depth // 4
+    return pl.pallas_call(
+        product_kernel,
+        out_shape=jax.ShapeDtypeStruct((rows, columns), BF16),
+        grid=(depth // tile,),
+        in_specs=[
+            pl.BlockSpec((rows, tile), lambda j: (0, j)),
+            pl.BlockSpec((tile, columns), lambda j: (j, 0)),
+        ],
+        out_specs=pl.BlockSpec((rows, columns), lambda j: (0, 0)),
+        scratch_shapes=[pltpu.VMEM((rows, columns), F32)],
+        compiler_params=pltpu.CompilerParams(
+            dimension_semantics=("arbitrary",), vmem_limit_bytes=32 << 20
+        ),
+        cost_estimate=cost(5),
+        name="product",
+    )(left, right)
+
+
 def gather_weight(w):
     return lax.all_gather(w, "seq", axis=0, tiled=True)
 
@@ -1369,10 +1409,10 @@
     )
     later = gather_weight(
         jnp.concatenate(
-            [gate_up.reshape(gate_up.shape[0], 2 * hidden_units), down_proj, mix_out], axis=1
+            [mix_out, gate_up.reshape(gate_up.shape[0], 2 * hidden_units), down_proj], axis=1
         )
     )
-    w_out = later[:, 3 * hidden_units :]
+    w_out = later[:, :vals]
     up_own = own_columns(rank_up, 0, dk)
     bias_own = lax.dynamic_slice_in_dim(gate_bias, head * dk, dk, 0)
 
@@ -1407,7 +1447,7 @@
     g_hidden = cotangent.astype(F32).reshape(micro * rows, width) + back_ffn
     g_mixed = g_hidden.astype(BF16)
     grads = scatter_grad(weight_grad(g_mixed, gated, grads, later.shape[1], 0, vals))
-    g_gated = dot(g_mixed, w_out, (1, 0)).astype(BF16)
+    g_gated = rows_by_columns(g_mixed, later, vals)
     g_proj_b, g_logits_b, g_head_gain, ffn_out = attention_back(
         keep, g_gated, og_b, o_b, qkv_b, decays_b, blocks(logits), through, pair_through, gain_row, kept, ffn_part.reshape(group, width),
     )

time: 534 us -> 536 us (level)
  matrix products: 22.8 us -> 15.2 us
  Pallas kernels: 429 us -> 435 us
    dot_general x6 -> x5, matrix products: 22.8 us -> 15.2 us  [dot(): lax.dot_general(a, b, (((contract[0],), (contract[1],)), ((), ())), preci...]
    pallas_call x0 -> x1, Pallas kernels: none -> 7.17 us  [rows_by_columns(): pl.pallas_call(product_kernel, out_shape=jax.ShapeDtypeStruct((rows, colu...]
    unnamed x76 -> x78, local copies, waits for them, and re-layouts: 12.4 us -> 13.3 us
  transfers between devices with their start and end apart: 3 -> 3, of which waited for: 1 -> 1; matrix products, arithmetic and copies ran while one was open for 6% -> 5% of each run, Pallas kernels for 61% -> 62%
where the time goes in v15:
time: 536 us; the launch traced here: 526 us
  Pallas kernels  435 us (81%)
  local copies, waits for them, and re-layouts  22.4 us (4%)
  other arithmetic  19.4 us (4%)
  matrix products  15.2 us (3%)
  between operations  14.9 us (3%)
  waiting for transfers between devices  13.9 us (3%)
    pallas_call x1, Pallas kernels, feed_forward(): pl.pallas_call(functools.partial(ffn_kernel, count), out_shape=(jax.Shape...  104 us
    pallas_call x1, Pallas kernels, finish(): pl.pallas_call(finish_kernel, out_shape=(jax.ShapeDtypeStruct((rows, widt...  102 us
    pallas_call x1, Pallas kernels, attention_forward(): pl.pallas_call(front_kernel, out_shape=(jax.ShapeDtypeStruct((blocks, mic...  78 us
    pallas_call x1, Pallas kernels, attention_back(): pl.pallas_call(back_kernel, out_shape=(jax.ShapeDtypeStruct((blocks, micr...  71.6 us
    pallas_call x1, Pallas kernels, gather_norm(): pl.pallas_call(gather_norm_kernel, out_shape=(jax.ShapeDtypeStruct((count...  66.7 us
    dot_general x5, matrix products, dot(): lax.dot_general(a, b, (((contract[0],), (contract[1],)), ((), ())), preci...  15.2 us
    all_to_all x1, waiting for transfers between devices, on_device(): lax.all_to_all(grads[:, :vals].reshape(heads, slab, vals), 'head', split_...  13.8 us
    unnamed x78, local copies, waits for them, and re-layouts  13.3 us
  transfers between devices with their start and end apart: 3, of which 1 were waited for; matrix products, arithmetic and copies ran while one was open for 5% of the time, Pallas kernels for 62%

profile of v15, /device:TPU:0, one launch (start us, length us, event | category | flops | bytes accessed | tf_op | source)
XLA Modules:
  0.0 525.6 jit_solution(1456969570523096231)
XLA Ops:
  7.3 1.6 copy.29
  9.1 1.8 pad_maximum_fusion
  12.4 1.1 constant_dynamic-slice_fusion.4
  13.5 1.1 constant_dynamic-slice_fusion.2
  14.7 66.7 %gather_norm.1 = (bf16[768,2048]{1,0:T(8,128)(2,1)S(1)}, bf16[2048,1536]{1,0:T(8,128)(2,1)S(1)}) custom-call(bf16[192,2048]{1,0:T(8,128)(2,1)S(1)} %bitcast.42, f32[1,2048]{1,0:T(1,128)S(1)} %bitcast.47, bf16[256,1536]{1,0:T(8,128)(2,1)S(1)} %pad_maximum_fusion.1.shard), custom_call_target="tpu_custom_call" | custom-call | bytes 150000000 | tf_op jit(solution)/shard_map/gather_norm/pallas_call | solution.py:396
  81.4 0.9 fusion.17
  82.3 2.7 fusion.14
  85.0 1.8 fusion.7
  86.9 3.4 fusion.9
  90.4 78.0 %attention_forward.1 = (f32[4,3,64,512]{3,2,1,0:T(8,128)S(1)}, bf16[192,2048]{1,0:T(8,128)(2,1)S(1)}, bf16[4,3,16,256]{3,2,1,0:T(8,128)(2,1)S(1)}, bf16[2,3,16,2...) custom-call(f32[4,3,1,256]{3,2,1,0:T(1,128)S(1)} %broadcast_in_dim.2.keep, ...), custom_call_target="tpu_custom_call" | custom-call | bytes 270000000 | tf_op jit(solution)/shard_map/attention_forward/pallas_call | solution.py:630
  168.4 1.2 copy-done.7
  169.6 1.6 copy-done.8
  171.2 1.1 copy-done.12
  173.6 6.4 %multiply_reduce_fusion.2 = (f32[192]{0:T(256)S(1)}, f32[192,2048]{1,0:T(8,128)S(1)}) fusion(bf16[192,2048]{1,0:T(8,128)(2,1)S(1)} %get-tuple-element.39.right, bf16[2048,6272]{1,0:T(8,128)(2,1)} %all-gather.2.cloned.1.call-done.w.right, bf16[192,2048]{1,0:T(8,128)(2,1)S(1)} %bitcast.43), kind=kOutput, calls=%fused_computation.16 | convolution fusion | flops 1612185344 | bytes 11535104 | tf_op jit(solution)/shard_map/dot_general | solution.py:1369
  180.1 1.3 multiply_convert_fusion.x_own
  181.4 103.6 %feed_forward.1 = (f32[192,2048]{1,0:T(8,128)}, bf16[4,192,2048]{2,1,0:T(8,128)(2,1)}, bf16[2048,6272]{1,0:T(8,128)(2,1)}) custom-call(bf16[192,2048]{1,0:T(8,128)(2,1)} %multiply_convert_fusion.x_own, bf16[768,2048]{1,0:T(8,128)(2,1)} %copy-done.8, bf16[2048,6272]{1,0:T(8,128)(2,1)} %all-gather.2.cloned.1.call-done.w.right), custom_call_target="tpu_custom_call" | custom-call | bytes 300000000 | tf_op jit(solution)/shard_map/feed_forward/pallas_call | solution.py:783
  285.0 2.6 multiply_reduce_fusion
  287.6 1.9 fusion.16.left
  289.5 5.1 weight_grad.1
  295.5 1.0 copy.28.rank_down
  296.5 7.2 %product.1.gated_own = bf16[192,2048]{1,0:T(8,128)(2,1)S(1)} custom-call(bf16[192,2048]{1,0:T(8,128)(2,1)S(1)} %fusion.16.left, bf16[2048,6272]{1,0:T(8,128)(2,1)} %all-gather.2.cloned.1.call-done.w.right), custom_call_target="tpu_custom_call" | custom-call | bytes 15000000 | tf_op jit(solution)/shard_map/product/pallas_call | solution.py:1342
  304.6 71.6 %attention_back.1 = (bf16[4,3,64,1536]{3,2,1,0:T(8,128)(2,1)}, f32[4,3,64,256]{3,2,1,0:T(8,128)}, f32[8,512]{1,0:T(8,128)}, f32[192,2048]{1,0:T(8,128)}) custom-call(f32[4,3,1,256]{3,2,1,0:T(1,128)} %copy-done.14, bf16[192,2048]{1,0:T(8,128)(2,1)} %copy-done.11, f32[4,3,64,512]{3,2,1,0:T(8,128)} %bitcast.38, f32[4,3,64,512]{3,2,1,0:T(8,128)} %copy-done.12, ...), custom_call_target="tpu_custom_call" | custom-call | bytes 240000000 | tf_op jit(solution)/shard_map/attention_back/pallas_call | solution.py:1007
  376.2 102.5 %finish.1 = (f32[192,2048]{1,0:T(8,128)}, bf16[64,6144]{1,0:T(8,128)(2,1)}, f32[1,2048]{1,0:T(1,128)}, f32[1,2048]{1,0:T(1,128)}, f32[1,512]{1,0:T(1,128)}, /*in...) custom-call(bf16[768,2048]{1,0:T(8,128)(2,1)} %copy-done.2, bf16[768,1536]{1,0:T(8,128)(2,1)} %bitcast.52, ...), custom_call_target="tpu_custom_call" | custom-call | bytes 285000000 | tf_op jit(solution)/shard_map/finish/pallas_call | solution.py:1247
  478.7 2.3 slice.24
  481.0 5.2 all-to-all-start
  486.2 4.4 fusion.15
  490.6 1.2 convert_element_type.41
  491.8 1.5 slice_convert_fusion
  493.4 2.8 reshape.146
  496.2 2.4 slice_convert_fusion.1
  498.6 13.8 %all-to-all-done = bf16[4,64,2048]{2,1,0:T(8,128)(2,1)} async-done(((bf16[4,64,2048]{2,1,0:T(8,128)(2,1)}), bf16[4,64,2048]{2,1,0:T(8,128)(2,1)}, u32[]{:S(2)}, u32[]{:S(2)}) %all-to-all-start) | async-done | bytes 1048608 | tf_op jit(solution)/shard_map/all_to_all | solution.py:1465
  512.4 2.2 convert_reduce_fusion
  (88 shorter events, 8.8 us)
Async XLA Ops:
  7.2 74.2 %copy-start = (f32[16,1024]{1,0:T(8,128)S(1)}, f32[16,1024]{1,0:T(8,128)}, u32[]{:S(2)}) copy-start(f32[16,1024]{1,0:T(8,128)} %param.24) | copy-start | bytes 196612
  7.2 1.7 copy-start.24
  7.2 1.9 copy-start.22
  7.2 166.4 %all-gather.2.cloned.1.call-start = ((), (), s32[]{:S(2)}) async-start(), calls=%async_computation.2 | async-start | bytes 28901376 | tf_op jit(solution)/shard_map/all_gather | solution.py:1361
  10.9 467.8 %reduce-scatter.2.cloned.1.call-start = ((), (), s32[]{:S(2)}) async-start(), calls=%async_computation.3 | async-start | bytes 28901376 | tf_op jit(solution)/shard_map/reduce_scatter | solution.py:1365
  12.4 2.2 copy-start.9
  12.4 2.2 copy-start.17
  14.6 66.8 %copy-start.25 = (bf16[2048,16]{0,1:T(8,128)(2,1)S(1)}, bf16[2048,16]{0,1:T(8,128)(2,1)}, u32[]{:S(2)}) copy-start(bf16[2048,16]{0,1:T(8,128)(2,1)} %param.23) | copy-start | bytes 196612
  81.3 5.5 %copy-start.2 = (bf16[768,2048]{1,0:T(8,128)(2,1)}, bf16[768,2048]{1,0:T(8,128)(2,1)S(1)}, u32[]{:S(2)}) copy-start(bf16[768,2048]{1,0:T(8,128)(2,1)S(1)} %get-tuple-element.37.xn_in) | copy-start | bytes 9437188
  81.4 5.5 %copy-start.5 = (bf16[2048,1536]{1,0:T(8,128)(2,1)}, bf16[2048,1536]{1,0:T(8,128)(2,1)S(1)}, u32[]{:S(2)}) copy-start(bf16[2048,1536]{1,0:T(8,128)(2,1)S(1)} %get-tuple-element.38.w_in) | copy-start | bytes 18874372
  81.4 5.4 %copy-start.29 = (f32[16,256]{1,0:T(8,128)}, f32[16,256]{1,0:T(8,128)S(1)}, u32[]{:S(2)}) copy-start(f32[16,256]{1,0:T(8,128)S(1)} %constant_dynamic-slice_fusion.up_own) | copy-start | bytes 49156
  85.0 5.3 %copy-start.13 = (bf16[768,256]{1,0:T(8,128)(2,1)}, bf16[768,256]{1,0:T(8,128)(2,1)S(1)}, u32[]{:S(2)}) copy-start(bf16[768,256]{1,0:T(8,128)(2,1)S(1)} %get-tuple-element.70) | copy-start | bytes 1179652
  86.8 3.5 copy-start.6
  86.9 3.5 copy-start.3
  86.9 3.5 copy-start.18
  90.4 78.0 %copy-start.14 = (f32[4,3,1,256]{3,2,1,0:T(1,128)}, f32[4,3,1,256]{3,2,1,0:T(1,128)S(1)}, u32[]{:S(2)}) copy-start(f32[4,3,1,256]{3,2,1,0:T(1,128)S(1)} %broadcast_in_dim.2.keep) | copy-start | bytes 36868
  90.4 83.2 %copy-start.10 = (bf16[3,64,2048]{2,1,0:T(8,128)(2,1)S(1)}, bf16[3,64,2048]{2,1,0:T(8,128)(2,1)}, u32[]{:S(2)}) copy-start(bf16[3,64,2048]{2,1,0:T(8,128)(2,1)} %param.13) | copy-start | bytes 2359300
  169.6 1.7 copy-start.8
  173.6 6.4 %copy-start.27 = (f32[2048]{0:T(1024)S(1)}, f32[2048]{0:T(1024)}, u32[]{:S(2)}) copy-start(f32[2048]{0:T(1024)} %param.21) | copy-start | bytes 24580
  180.1 104.9 %copy-start.19 = (f32[192,2048]{1,0:T(8,128)}, f32[192,2048]{1,0:T(8,128)S(1)}, u32[]{:S(2)}) copy-start(f32[192,2048]{1,0:T(8,128)S(1)} %get-tuple-element.73) | copy-start | bytes 4718596
  284.9 2.7 copy-start.4
  285.0 2.7 copy-start.21
  481.0 5.2 copy-start.20
  481.0 31.4 %all-to-all-start = ((bf16[4,64,2048]{2,1,0:T(8,128)(2,1)}), bf16[4,64,2048]{2,1,0:T(8,128)(2,1)}, u32[]{:S(2)}, u32[]{:S(2)}) async-start(bf16[4,64,2048]{2,1,0:T(8,128)(2,1)} %bitcast.15), calls=%async_computation.1 | async-start | bytes 2097152 | tf_op jit(solution)/shard_map/all_to_all | solution.py:1465
  486.2 4.4 copy-start.23
  493.4 24.9 %copy-start.1 = (f32[16,1024]{1,0:T(8,128)S(1)}, f32[16,1024]{1,0:T(8,128)}, u32[]{:S(2)}) copy-start(f32[16,1024]{1,0:T(8,128)} %param.24) | copy-start | bytes 196612
  496.2 18.4 %copy-start.31 = (f32[1,2048]{1,0:T(1,128)S(1)}, f32[1,2048]{1,0:T(1,128)}, u32[]{:S(2)}) copy-start(f32[1,2048]{1,0:T(1,128)} %get-tuple-element.56) | copy-start | bytes 24580
  496.2 19.0 %copy-start.30 = (f32[1,2048]{1,0:T(1,128)S(1)}, f32[1,2048]{1,0:T(1,128)}, u32[]{:S(2)}) copy-start(f32[1,2048]{1,0:T(1,128)} %get-tuple-element.57) | copy-start | bytes 24580
  496.2 19.6 %copy-start.34 = (f32[1,512]{1,0:T(1,128)S(1)}, f32[1,512]{1,0:T(1,128)}, u32[]{:S(2)}) copy-start(f32[1,512]{1,0:T(1,128)} %get-tuple-element.58) | copy-start | bytes 6148
  496.2 20.2 %copy-start.26 = (f32[16,2048]{1,0:T(8,128)S(1)}, f32[16,2048]{1,0:T(8,128)}, u32[]{:S(2)}) copy-start(f32[16,2048]{1,0:T(8,128)} %get-tuple-element.59) | copy-start | bytes 393220
  496.2 20.9 %copy-start.28 = (f32[16,1024]{1,0:T(8,128)S(1)}, f32[16,1024]{1,0:T(8,128)}, u32[]{:S(2)}) copy-start(f32[16,1024]{1,0:T(8,128)} %get-tuple-element.96) | copy-start | bytes 196612
  496.2 21.5 %copy-start.32 = (f32[1,1024]{1,0:T(1,128)S(1)}, f32[1,1024]{1,0:T(1,128)}, u32[]{:S(2)}) copy-start(f32[1,1024]{1,0:T(1,128)} %get-tuple-element.61) | copy-start | bytes 12292
  (6 other events, 5.1 us)
Sparse Core Ops, SparseCore 0:
  11.0 158.3 all-gather.1
  294.8 177.6 reduce-scatter.1
